TPU v7x, 256 devices: a whole 4x4x8 slice. The times are simulated.
256 devices in a mesh: req: 64 (over z, y, core), head: 4 (over x).
Axes of the slice: x: 4, y: 4, z: 8, core: 2. Of those that a mesh axis runs over, the one named last changes fastest.
Arguments:
- residual: bfloat16 [1024, 2048], P('req'), may hold values from -5.2 to 5.2
- queries: bfloat16 [1024, 1024], P('req', 'head'), may hold values from -5.5 to 5.5
- new_kv: bfloat16 [1024, 2, 1024], P('req', None, 'head'), may hold values from -4.5 to 4.5
- kv_cache: bfloat16 [8192, 2, 32, 1024], P('req', None, None, 'head'), may hold values from -131 to 131
- lengths: int32 [1024], replicated, may hold values from 2 to 16384, as said below
- slot_request: int32 [8192], P('req'), may hold values from 0 to 1023, as said below
- slot_page: int32 [8192], P('req'), may hold values from 0 to 511, as said below
- slot_used: int32 [8192], P('req'), may hold values from 0 to 1
- out_weight: bfloat16 [1024, 2048], P('head'), may hold values from -0.1875 to 0.1875
- norm_gain: float32 [2048], replicated, may hold values from 0.25 to 1.75
- routes: int32 [1024, 8], P('req'), may hold values from 0 to 63, all different within a row; in each aligned block of 16 rows (0 to 15, 16 to 31, ...) at most 4 rows name the same one
- route_weights: float32 [1024, 8], P('req'), may hold values from 0.05 to 0.5
- w_gate: bfloat16 [64, 2048, 1024], P('req', None, 'head'), may hold values from -0.125 to 0.125
- w_up: bfloat16 [64, 2048, 1024], P('req', None, 'head'), may hold values from -0.125 to 0.125
- w_down: bfloat16 [64, 1024, 2048], P('req', 'head'), may hold values from -0.1875 to 0.1875
- next_gain: float32 [2048], replicated, may hold values from 0.25 to 1.75
- next_weight: bfloat16 [2048, 3, 1024], P(None, None, 'head'), may hold values from -0.125 to 0.125
Outputs:
- stream: bfloat16 [1024, 2048], P('req', 'head')
- next_qkv: bfloat16 [1024, 3, 1024], P('req', None, 'head')
Inputs may be any that keep to these rules, and one draw needn't show every extreme that they name: Request r has cached positions 0 to lengths[r] - 1, held in pages 0 to ceil(lengths[r] / 32) - 1; some request is 16384 long. `slot_request`: each page of every request lies in exactly one slot with slot_used 1; unused slots hold request 0. `slot_page`: unused slots hold page 0. `routes`: within the rows of one index of req at most 4 rows name the same expert.
All inputs are finite; a program needn't handle non-finite values.
Results may differ from a plain program's by a relative error of at most 0.025.
Values may be sent and summed in bfloat16 or wider, within the bound.
No kernel may reach another device: no remote copies, remote signals or barrier semaphores. Data moves between devices by JAX's collectives and lax.ppermute only.
A program may use at most 64 MiB of HBM per device.

v0:
```python
import math

import jax
import jax.numpy as jnp
from jax import lax
from jax.sharding import PartitionSpec as P

HD = 128
EXP_DEV = 1


norm_eps = 1e-06
floor_value = -1e30


def norm_whole(rows_in, gain):
    wide_rows = rows_in.astype(jnp.float32)
    mean_square = jnp.mean(wide_rows * wide_rows, axis=1, keepdims=True)
    return (wide_rows * lax.rsqrt(mean_square + norm_eps) * gain).astype(jnp.bfloat16)


def route_tables(routes, route_weights, expert_total, capacity):
    row_count, pick_count = routes.shape
    flat_routes = routes.reshape(row_count * pick_count)
    hit_table = (flat_routes[:, None] == jnp.arange(expert_total, dtype=jnp.int32)[None, :]).astype(
        jnp.int32
    )
    before = jnp.cumsum(hit_table, axis=0) - hit_table
    slot_rank = jnp.sum(before * hit_table, axis=1)
    target = flat_routes * capacity + slot_rank
    lookup = (
        target[:, None] == jnp.arange(expert_total * capacity, dtype=jnp.int32)[None, :]
    ).astype(jnp.float32)
    lookup = lookup.reshape(row_count, pick_count, expert_total * capacity)
    pick_map = jnp.sum(lookup, axis=1)
    blend_map = jnp.sum(lookup * route_weights[:, :, None], axis=1)
    return (pick_map, blend_map)


def expert_block(arrived, w_gate, w_up, w_down):
    gate_out = jnp.einsum("secd,edf->secf", arrived, w_gate, preferred_element_type=jnp.float32)
    upward = jnp.einsum("secd,edf->secf", arrived, w_up, preferred_element_type=jnp.float32)
    inner_act = (jax.nn.silu(gate_out) * upward).astype(jnp.bfloat16)
    return jnp.einsum("secf,efd->secd", inner_act, w_down, preferred_element_type=jnp.float32)


def local(
    residual,
    queries,
    new_kv,
    kv_cache,
    lengths,
    slot_request,
    slot_page,
    slot_used,
    out_weight,
    norm_gain,
    routes,
    route_weights,
    w_gate,
    w_up,
    w_down,
    next_gain,
    next_weight,
):
    req_rows, row_width = queries.shape
    head_count = row_width // HD
    slot_count = kv_cache.shape[0]
    page_len = kv_cache.shape[2]
    model_width = residual.shape[1]
    req_count = lax.axis_size("req")
    head_total = lax.axis_size("head")
    score_scale = 1.0 / math.sqrt(HD)
    first_row = lax.axis_index("req") * req_rows
    everyone = lax.all_gather(queries, "req", axis=0, tiled=True)
    total_req = everyone.shape[0]
    chosen = everyone[slot_request].reshape(slot_count, head_count, HD)
    key_rows = kv_cache[:, 0].reshape(slot_count, page_len, head_count, HD)
    value_rows = kv_cache[:, 1].reshape(slot_count, page_len, head_count, HD)
    scores = (
        jnp.einsum("sphd,shd->sph", key_rows, chosen, preferred_element_type=jnp.float32)
        * score_scale
    )
    position = slot_page[:, None] * page_len + jnp.arange(page_len, dtype=jnp.int32)[None, :]
    valid = (slot_used[:, None] == 1) & (position < lengths[slot_request][:, None])
    masked = jnp.where(valid[:, :, None], scores, floor_value)
    slot_peak = jnp.max(masked, axis=1)
    member = slot_request[None, :] == jnp.arange(total_req, dtype=jnp.int32)[:, None]
    local_peak = jnp.max(jnp.where(member[:, :, None], slot_peak[None], floor_value), axis=1)
    fresh_key = new_kv[:, 0].reshape(req_rows, head_count, HD)
    fresh_value = new_kv[:, 1].astype(jnp.float32).reshape(req_rows, head_count, HD)
    own_query = queries.reshape(req_rows, head_count, HD)
    own_score = (
        jnp.einsum("rhd,rhd->rh", own_query, fresh_key, preferred_element_type=jnp.float32)
        * score_scale
    )
    placed_score = lax.dynamic_update_slice(
        jnp.full((total_req, head_count), floor_value, jnp.float32), own_score, (first_row, 0)
    )
    peak_score = lax.pmax(jnp.maximum(local_peak, placed_score), "req")
    weights = jnp.where(
        valid[:, :, None], jnp.exp(masked - peak_score[slot_request][:, None, :]), 0.0
    ).astype(jnp.bfloat16)
    slot_numer = jnp.einsum(
        "sph,sphd->shd", weights, value_rows, preferred_element_type=jnp.float32
    ).reshape(slot_count, row_width)
    slot_denom = jnp.sum(weights.astype(jnp.float32), axis=1)
    member_float = member.astype(jnp.float32)
    numerator = jnp.dot(member_float, slot_numer, precision=lax.Precision.HIGHEST)
    denominator = jnp.dot(member_float, slot_denom, precision=lax.Precision.HIGHEST)
    numerator, denominator = (
        lax.psum_scatter(numerator, "req", scatter_dimension=0, tiled=True),
        lax.psum_scatter(denominator, "req", scatter_dimension=0, tiled=True),
    )
    own_peak = lax.dynamic_slice_in_dim(peak_score, first_row, req_rows, 0)
    new_lift = jnp.exp(own_score - own_peak)
    mixed_rows = (
        numerator.reshape(req_rows, head_count, HD) + new_lift[:, :, None] * fresh_value
    ) / (denominator + new_lift)[:, :, None]
    attended = mixed_rows.reshape(req_rows, row_width).astype(jnp.bfloat16)
    partial_out = jnp.dot(attended, out_weight, preferred_element_type=jnp.float32)
    expert_total = EXP_DEV * req_count
    pick_count = routes.shape[1]
    capacity = min(
        req_rows, max(2, 2 * ((req_rows * pick_count + expert_total - 1) // expert_total))
    )
    slot_cells = expert_total * capacity
    pick_map, blend_map = route_tables(routes, route_weights, expert_total, capacity)
    pick_bf = pick_map.astype(jnp.bfloat16)
    slice_width = model_width // head_total
    first_col = lax.axis_index("head") * slice_width
    attn_out = lax.psum(partial_out.astype(jnp.bfloat16), "head").astype(jnp.float32)
    hidden_state = (residual.astype(jnp.float32) + attn_out).astype(jnp.bfloat16)
    normed = norm_whole(hidden_state, norm_gain)
    buffer = jnp.einsum("rc,rd->cd", pick_bf, normed, preferred_element_type=jnp.float32).astype(
        jnp.bfloat16
    )
    buffer = buffer.reshape(req_count, EXP_DEV, capacity, model_width)
    expert_part = expert_block(
        lax.all_to_all(buffer, "req", split_axis=0, concat_axis=0, tiled=True), w_gate, w_up, w_down
    )
    expert_sum = lax.psum(expert_part.astype(jnp.bfloat16), "head")
    returned = lax.all_to_all(expert_sum, "req", split_axis=0, concat_axis=0, tiled=True)
    moe_sum = jnp.dot(
        blend_map,
        returned.reshape(slot_cells, model_width).astype(jnp.float32),
        precision=lax.Precision.HIGHEST,
    )
    stream_full = (hidden_state.astype(jnp.float32) + moe_sum).astype(jnp.bfloat16)
    next_normed = norm_whole(stream_full, next_gain)
    stream_out = lax.dynamic_slice_in_dim(stream_full, first_col, slice_width, 1)
    next_qkv = jnp.einsum(
        "td,dcf->tcf", next_normed, next_weight, preferred_element_type=jnp.float32
    ).astype(jnp.bfloat16)
    return (stream_out, next_qkv)


def solution(mesh):
    placed = (
        P("req", None),
        P("req", "head"),
        P("req", None, "head"),
        P("req", None, None, "head"),
        P(),
        P("req"),
        P("req"),
        P("req"),
        P("head", None),
        P(),
        P("req", None),
        P("req", None),
        P("req", None, "head"),
        P("req", None, "head"),
        P("req", "head", None),
        P(),
        P(None, None, "head"),
    )
    return jax.shard_map(
        local,
        mesh=mesh,
        in_specs=placed,
        out_specs=(P("req", "head"), P("req", None, "head")),
        check_vma=False,
    )
```

profile of v0, /device:TPU:1, one launch (start us, length us, event | category | flops | bytes accessed | tf_op | source)
XLA Modules:
  0.0 685.3 jit_solution(6370104238343383896)
XLA Ops:
  7.2 0.8 compare_select_fusion
  8.0 0.8 iota_compare_fusion
  8.9 59.8 %all_gather.3 = bf16[1024,256]{1,0:T(8,128)(2,1)} all-gather(bf16[16,256]{1,0:T(8,128)(2,1)} %param.18), channel_id=1, replica_groups=mesh['req'=64,'head'=4] {'req'}, dimensions={0}, use_global_device_ids=true | all-gather | bytes 532480 | tf_op jit(solution)/shard_map/all_gather | solution.py:75
  68.7 0.7 reshape.163
  69.4 1.9 gather_fusion.1
  71.2 0.7 reshape.212
  71.9 4.6 fusion.59
  76.5 4.0 reshape_squeeze.9
  80.5 2.9 fusion.4
  83.4 0.1 copy.55
  83.5 1.0 gather_fusion
  84.6 0.4 select_reduce_fusion
  84.9 1.0 copy.43
  86.0 0.1 fusion.52
  86.2 1.9 max.5
  88.1 247.3 %pmax.7 = f32[1024,2]{1,0:T(8,128)} all-reduce(f32[1024,2]{1,0:T(8,128)} %max.5), channel_id=1, replica_groups=mesh['req'=64,'head'=4] {'req'}, use_global_device_ids=true, to_apply=%region_2.3 | all-reduce | flops 2048 | bytes 16384 | tf_op jit(solution)/shard_map/pmax | solution.py:100
  335.4 1.7 gather_fusion.2
  337.2 0.1 copy.60
  337.3 4.0 reshape_squeeze.11
  341.3 2.3 fusion.2
  343.6 1.6 fusion.21
  345.4 0.1 eq.58
  345.5 0.1 fusion.45
  345.6 0.2 reduce_window_sum.11
  345.7 0.2 select_reduce_fusion.2
  346.1 0.6 dynamic-slice
  347.3 0.3 fusion.20
  347.7 131.4 %all-reduce = f32[1024,2]{0,1:T(2,128)S(1)} all-reduce(f32[1024,2]{0,1:T(2,128)S(1)} %fusion.20), channel_id=3, replica_groups=mesh['req'=64,'head'=4] {'req'}, use_global_device_ids=true, to_apply=%region_5.6.clone | all-reduce | flops 2048 | bytes 16384
  479.2 0.7 fusion.58
  479.9 1.2 reduce-scatter.3.cloned.1.call-done
  481.3 2.1 convolution_convert_fusion.2
  483.5 0.1 convert_reduce_fusion
  483.7 47.0 %all-reduce.4.cloned.1.call-done = bf16[16,2048]{1,0:T(8,128)(2,1)} async-done(((bf16[16,2048]{1,0:T(8,128)(2,1)}), bf16[16,2048]{1,0:T(8,128)(2,1)}) %all-reduce.4.cloned.1.call-update) | async-done | bytes 65552 | tf_op jit(solution)/shard_map/psum | solution.py:132
  530.7 1.0 fusion.32
  531.7 2.3 convolution_convert_fusion.1
  534.0 2.3 reshape.165
  536.3 40.8 %all_to_all.10 = bf16[64,1,4,2048]{3,2,1,0:T(4,128)(2,1)S(1)} all-to-all(bf16[64,1,4,2048]{3,2,1,0:T(4,128)(2,1)} %bitcast.123), channel_id=1, replica_groups=mesh['req'=64,'head'=4] {'req'}, dimensions={0} | all-to-all | bytes 2097152 | tf_op jit(solution)/shard_map/all_to_all | solution.py:140
  577.1 1.0 copy-done.2
  578.1 1.3 convolution_bitcast_fusion.1
  579.4 4.2 fusion
  583.6 45.9 %all-reduce.6.cloned.1.call-done = bf16[64,1,4,2048]{3,0,2,1:T(8,128)(2,1)} async-done(((bf16[64,1,4,2048]{3,0,2,1:T(8,128)(2,1)}), bf16[64,1,4,2048]{3,0,2,1:T(8,128)(2,1)}) %all-reduce.6.cloned.1.call-update) | async-done | bytes 1048592 | tf_op jit(solution)/shard_map/psum | solution.py:142
  629.5 3.1 copy.52
  632.6 12.4 %all-to-all-start.1 = ((bf16[64,1,4,2048]{3,2,1,0:T(4,128)(2,1)}), bf16[64,1,4,2048]{3,2,1,0:T(4,128)(2,1)}, u32[]{:S(2)}, u32[]{:S(2)}) async-start(bf16[64,1,4,2048]{3,2,1,0:T(4,128)(2,1)} %copy.52), calls=%async_computation.2 | async-start | bytes 2097152 | tf_op jit(solution)/shard_map/all_to_all | solution.py:143
  645.0 27.9 %all-to-all-done.1 = bf16[64,1,4,2048]{3,2,1,0:T(4,128)(2,1)} async-done(((bf16[64,1,4,2048]{3,2,1,0:T(4,128)(2,1)}), bf16[64,1,4,2048]{3,2,1,0:T(4,128)(2,1)}, u32[]{:S(2)}, u32[]{:S(2)}) %all-to-all-start.1) | async-done | bytes 1048608 | tf_op jit(solution)/shard_map/all_to_all | solution.py:143
  672.9 2.2 reshape.171
  675.1 1.9 fusion.29
  677.0 0.6 constant_dynamic-slice_fusion
  677.6 1.2 convolution_convert_fusion.3
  (56 shorter events, 1.1 us)
Async XLA Ops:
  7.2 670.4 %copy-start = (bf16[2048,3,256]{2,0,1:T(8,128)(2,1)S(1)}, bf16[2048,3,256]{2,0,1:T(8,128)(2,1)}, u32[]{:S(2)}) copy-start(bf16[2048,3,256]{2,0,1:T(8,128)(2,1)} %param.33) | copy-start | bytes 9437188
  7.2 474.0 %reduce-scatter.3.cloned.1.call-start = ((), (), s32[]{:S(2)}) async-start(), calls=%async_computation.3 | async-start | bytes 1064960 | tf_op jit(solution)/shard_map/reduce_scatter | solution.py:112
  80.5 3.0 copy-start.1
  80.5 4.0 copy-start.12
  80.5 4.0 copy-start.13
  80.5 5.5 copy-start.5
  341.3 2.3 copy-start.10
  341.3 4.0 copy-start.8
  341.3 4.7 copy-start.9
  341.3 4.8 copy-start.14
  343.6 187.1 %copy-start.3 = (bf16[16,2048]{1,0:T(8,128)(2,1)S(1)}, bf16[16,2048]{1,0:T(8,128)(2,1)}, u32[]{:S(2)}) copy-start(bf16[16,2048]{1,0:T(8,128)(2,1)} %param.17) | copy-start | bytes 196612
  343.6 188.1 %copy-start.6 = (f32[2048]{0:T(1024)S(1)}, f32[2048]{0:T(1024)}, u32[]{:S(2)}) copy-start(f32[2048]{0:T(1024)} %param.26) | copy-start | bytes 24580
  345.2 185.5 %all-reduce.4.cloned.1.call-start = ((), (), s32[]{:S(2)}) async-start(), calls=%async_computation.4 | async-start | bytes 131072 | tf_op jit(solution)/shard_map/psum | solution.py:132
  483.5 146.0 %all-reduce.6.cloned.1.call-start = ((), (), s32[]{:S(2)}) async-start(), calls=%async_computation.5 | async-start | bytes 2097152 | tf_op jit(solution)/shard_map/psum | solution.py:142
  536.3 41.8 %copy-start.11 = (bf16[1,2048,256]{2,1,0:T(8,128)(2,1)S(1)}, bf16[1,2048,256]{2,1,0:T(8,128)(2,1)}, u32[]{:S(2)}) copy-start(bf16[1,2048,256]{2,1,0:T(8,128)(2,1)} %param.29) | copy-start | bytes 3145732
  577.1 1.0 copy-start.2
  632.6 42.5 %copy-start.4 = (bf16[16,2048]{1,0:T(8,128)(2,1)S(1)}, bf16[16,2048]{1,0:T(8,128)(2,1)}, u32[]{:S(2)}) copy-start(bf16[16,2048]{1,0:T(8,128)(2,1)} %all-reduce.4.cloned.1.call-done) | copy-start | bytes 196612
  632.6 40.3 %all-to-all-start.1 = ((bf16[64,1,4,2048]{3,2,1,0:T(4,128)(2,1)}), bf16[64,1,4,2048]{3,2,1,0:T(4,128)(2,1)}, u32[]{:S(2)}, u32[]{:S(2)}) async-start(bf16[64,1,4,2048]{3,2,1,0:T(4,128)(2,1)} %copy.52), calls=%async_computation.2 | async-start | bytes 2097152 | tf_op jit(solution)/shard_map/all_to_all | solution.py:143
  645.0 32.6 %copy-start.7 = (f32[2048]{0:T(1024)S(1)}, f32[2048]{0:T(1024)}, u32[]{:S(2)}) copy-start(f32[2048]{0:T(1024)} %param.32) | copy-start | bytes 24580
Sparse Core Ops, SparseCore 0:
  345.3 135.7 reduce-scatter.2
  483.6 47.0 all-reduce.3
  583.8 45.7 all-reduce.5
where the time goes:
time: 686 us; the launch traced here: 685 us
  blocking collectives  479 us (70%)
  waiting for transfers between devices  122 us (18%)
  local copies, waits for them, and re-layouts  30.3 us (4%)
  matrix products  20 us (3%)
  between operations  14.6 us (2%)
  starting transfers between devices  12.5 us (2%)
    pmax x1, blocking collectives, local(): peak_score = lax.pmax(jnp.maximum(local_peak, placed_score), 'req')  247 us
    unnamed x1, blocking collectives  131 us
    all_gather x1, blocking collectives, local(): everyone = lax.all_gather(queries, 'req', axis=0, tiled=True)  59.8 us
    psum x1, waiting for transfers between devices, local(): lax.psum(partial_out.astype(jnp.bfloat16), 'head').astype(jnp.float32)  47 us
    psum x1, waiting for transfers between devices, local(): expert_sum = lax.psum(expert_part.astype(jnp.bfloat16), 'head')  45.9 us
    all_to_all x1, blocking collectives, local(): lax.all_to_all(buffer, 'req', split_axis=0, concat_axis=0, tiled=True)  40.8 us
    all_to_all x1, waiting for transfers between devices, local(): lax.all_to_all(expert_sum, 'req', split_axis=0, concat_axis=0, tiled=True)  27.9 us
  transfers between devices with their start and end apart: 4, of which 4 were waited for; matrix products, arithmetic and copies ran while one was open for 0% of the time, Pallas kernels for 0%

commit v1 on v0

v1 whole, which is shorter than its diff:
```python
import functools
import math

import jax
import jax.numpy as jnp
from jax import lax
from jax.experimental import pallas as pl
from jax.experimental.pallas import tpu as pltpu
from jax.sharding import Mesh, PartitionSpec as P

HD = 128
EPS = 1e-06
FLOOR = -(2.0**99)
SCALE = 1.0 / math.sqrt(HD)
F32 = jnp.float32
BF16 = jnp.bfloat16
REQ = ("z", "y", "c")
VLIM = pltpu.CompilerParams(vmem_limit_bytes=40 * 1024 * 1024)


def iota(shape, dim):
    return lax.broadcasted_iota(jnp.int32, shape, dim)


def core_id():
    return lax.axis_index("c")


def head_id():
    return lax.axis_index("head")


def dot(a, b):
    return jnp.dot(a, b, preferred_element_type=F32)


def hi_lo(x):
    hi = x.astype(BF16)
    return hi, (x - hi.astype(F32)).astype(BF16)


def attn_kernel(sr_ref, sp_ref, su_ref, len_ref, qa_ref, qb_ref, kv_ref, out_ref, kv_buf, n_scr, m_scr, l_scr, sems):
    slots = kv_ref.shape[0]
    page = kv_ref.shape[2]
    total = len_ref.shape[1]
    half = total // 2
    chunks = sems.shape[0]
    per = slots // chunks
    copies = [
        pltpu.make_async_copy(kv_ref.at[pl.ds(i * per, per)], kv_buf.at[pl.ds(i * per, per)], sems.at[i])
        for i in range(chunks)
    ]
    for copy in copies:
        copy.start()
    core = core_id()
    req = sr_ref[...]
    place = jnp.where((req // 16) % 2 == core, 0, half) + (req // 32) * 16 + req % 16
    eye = iota((slots, slots), 0) == iota((slots, slots), 1)

    def to_col(row):
        return jnp.sum(jnp.where(eye, row.astype(F32), 0.0), axis=1, keepdims=True)

    def to_row(wide):
        return jnp.sum(jnp.where(eye, wide, 0.0), axis=0, keepdims=True)

    req_row = req.astype(F32)
    req_col = to_col(req)
    place_row = place.astype(F32)
    place_col = to_col(place)
    lane_total = iota((slots, total), 1).astype(F32)
    len_col = jnp.sum(jnp.where(req_col == lane_total, len_ref[...].astype(F32), 0.0), axis=1, keepdims=True)
    count = jnp.clip(len_col - to_col(sp_ref[...]) * page, 0.0, float(page))
    count = jnp.where(to_col(su_ref[...]) == 1.0, count, 0.0)
    pick = jnp.where(place_col == lane_total, 1.0, 0.0).astype(BF16)
    chosen = dot(pick[:, :half], qa_ref[...]) + dot(pick[:, half:], qb_ref[...])

    low_lanes = iota((8, 2 * HD), 1) < HD
    rel = iota((16, 8 * page), 1) - (iota((16, 8 * page), 0) % 8) * page
    rel = rel.astype(F32)
    for b in range(slots // 8):
        if (b * 8) % per == 0:
            copies[b * 8 // per].wait()
        q8 = chosen[b * 8 : b * 8 + 8]
        q16 = jnp.concatenate([jnp.where(low_lanes, q8, 0.0), jnp.where(low_lanes, 0.0, q8)], axis=0).astype(BF16)
        keys = kv_buf[b * 8 : b * 8 + 8, 0].reshape(8 * page, 2 * HD)
        vals = kv_buf[b * 8 : b * 8 + 8, 1].reshape(8 * page, 2 * HD)
        s = lax.dot_general(q16, keys, (((1,), (1,)), ((), ())), preferred_element_type=F32) * SCALE
        c8 = count[b * 8 : b * 8 + 8]
        ok = (rel >= 0.0) & (rel < jnp.concatenate([c8, c8], axis=0))
        s = jnp.where(ok, s, FLOOR)
        m = jnp.max(s, axis=1, keepdims=True)
        w = jnp.where(ok, jnp.exp(s - m), 0.0).astype(BF16)
        l = jnp.sum(w.astype(F32), axis=1, keepdims=True)
        n = dot(w, vals)
        for h in range(2):
            n_scr[h, b * 8 : b * 8 + 8, :] = n[8 * h : 8 * h + 8, HD * h : HD * h + HD]
            m_scr[h, b * 8 : b * 8 + 8, :] = jnp.broadcast_to(m[8 * h : 8 * h + 8], (8, slots))
            l_scr[h, b * 8 : b * 8 + 8, :] = jnp.broadcast_to(l[8 * h : 8 * h + 8], (8, slots))

    same = req_col == req_row
    slot_row = iota((slots, slots), 1).astype(F32)
    first = jnp.min(jnp.where(same, slot_row, 9999.0), axis=1, keepdims=True)
    leader = first == iota((slots, 1), 0).astype(F32)
    spread = jnp.where(iota((total, slots), 0).astype(F32) == place_row, 1.0, 0.0).astype(BF16)
    stat = []
    for h in range(2):
        m_wide = m_scr[h]
        m_ref = jnp.max(jnp.where(same, to_row(m_wide), FLOOR), axis=1, keepdims=True)
        m_ref = m_ref.astype(BF16).astype(F32)
        lift = jnp.exp(m_wide - m_ref)
        n_hi, n_lo = hi_lo(n_scr[h] * lift)
        l_sum = jnp.sum(jnp.where(same, to_row(l_scr[h] * lift), 0.0), axis=1, keepdims=True)
        out = (dot(spread, n_hi) + dot(spread, n_lo)).astype(BF16)
        out_ref[:, :, 16 * h : 16 * h + 16, :] = out.reshape(2, half // 16, 16, HD)
        l_hi = l_sum.astype(BF16).astype(F32)
        stat.append((m_ref, l_hi, l_sum - l_hi))
    lane = iota((slots, HD), 1)
    group = lane // 16
    board = jnp.zeros((slots, HD), F32)
    for h in range(2):
        for i in range(3):
            board = jnp.where(group == 2 * i + h, stat[h][i], board)
    mine = (lane % 16).astype(F32) == to_col(req % 16)
    board = jnp.where(mine & leader, board, 0.0).astype(BF16)
    spread16 = jnp.where(iota((total, slots), 0) // 16 == place // 16, 1.0, 0.0).astype(BF16)
    out_ref[:, :, 32:48, :] = dot(spread16, board).astype(BF16).reshape(2, half // 16, 16, HD)


def attend_pages(slot_request, slot_page, slot_used, lengths, qa, qb, kv_cache):
    slots = kv_cache.shape[0]
    total = lengths.shape[0]
    vm = pl.BlockSpec(memory_space=pltpu.VMEM)
    return pl.pallas_call(
        attn_kernel,
        name="attend_pages",
        out_shape=jax.ShapeDtypeStruct((2, total // 32, 48, HD), BF16),
        in_specs=[vm] * 6 + [pl.BlockSpec(memory_space=pl.ANY)],
        out_specs=vm,
        scratch_shapes=[
            pltpu.VMEM(kv_cache.shape, BF16),
            pltpu.VMEM((2, slots, HD), F32),
            pltpu.VMEM((2, slots, slots), F32),
            pltpu.VMEM((2, slots, slots), F32),
            pltpu.SemaphoreType.DMA((8,)),
        ],
        compiler_params=VLIM,
    )(
        slot_request.reshape(1, slots),
        slot_page.reshape(1, slots),
        slot_used.reshape(1, slots),
        lengths.reshape(1, total),
        qa.reshape(total // 2, 2 * HD),
        qb.reshape(total // 2, 2 * HD),
        kv_cache,
    )


def read_stats(board, h):
    lane, row = iota(board.shape, 2), iota(board.shape, 1) + 16 * h
    m = jnp.sum(jnp.where(lane == row, board, 0.0), axis=2, keepdims=True)
    l = jnp.sum(jnp.where((lane == row + 32) | (lane == row + 64), board, 0.0), axis=2, keepdims=True)
    return jnp.where(l > 0.0, m, FLOOR), l


def owner_kernel(part_ref, q_ref, nkv_ref, w_ref, *outs):
    board = part_ref[:, 32:48, :].astype(F32)
    q = q_ref[...].astype(F32)
    nkv = nkv_ref[...].astype(F32)
    att = []
    for h in range(2):
        m, l = read_stats(board, h)
        own = jnp.sum(q[:, HD * h : HD * h + HD] * nkv[:, HD * h : HD * h + HD], axis=1, keepdims=True) * SCALE
        top = jnp.maximum(jnp.max(m, axis=0), own)
        lift = jnp.exp(m - top[None])
        n = jnp.sum(part_ref[:, 16 * h : 16 * h + 16, :].astype(F32) * lift, axis=0)
        den = jnp.sum(l * lift, axis=0)
        new = jnp.exp(own - top)
        v = nkv[:, 2 * HD + HD * h : 2 * HD + HD * h + HD]
        att.append((n + new * v) / (den + new))
    attended = jnp.concatenate(att, axis=1).astype(BF16)
    head = head_id()
    width = outs[0].shape[1]
    for k in range(4):
        first = pl.multiple_of(((head + k) % 4) * width, width)
        outs[k][...] = dot(attended, w_ref[:, pl.ds(first, width)]).astype(BF16)


def owner_part(parts, queries, nkv, out_weight):
    rows = queries.shape[0]
    width = out_weight.shape[1] // 4
    vm = pl.BlockSpec(memory_space=pltpu.VMEM)
    return pl.pallas_call(
        owner_kernel,
        name="owner_part",
        out_shape=[jax.ShapeDtypeStruct((rows, width), BF16)] * 4,
        in_specs=[vm] * 4,
        out_specs=[vm] * 4,
        compiler_params=VLIM,
    )(parts, queries, nkv, out_weight)


def rank_of(hit):
    rows = hit.shape[0]
    before = jnp.where(iota((rows, rows), 0) > iota((rows, rows), 1), 1.0, 0.0).astype(BF16)
    return dot(before, hit.astype(BF16))


def dispatch_kernel(p0, p1, p2, p3, res_ref, routes_ref, hid_ref, disp_ref):
    width = hid_ref.shape[1]
    first = pl.multiple_of(head_id() * width, width)
    acc = p0[...].astype(F32) + p1[...].astype(F32) + p2[...].astype(F32) + p3[...].astype(F32)
    hid = (res_ref[:, pl.ds(first, width)].astype(F32) + acc).astype(BF16)
    hid_ref[...] = hid
    rows, picks = routes_ref.shape
    routes = routes_ref[...]
    cells = disp_ref.shape[0] * 8
    lane = iota((rows, cells), 1)
    hit = jnp.zeros((rows, cells), F32)
    for k in range(picks):
        hit = hit + jnp.where(routes[:, k : k + 1] == lane // 8, 1.0, 0.0)
    hit = jnp.where(rank_of(hit) == (lane % 4).astype(F32), hit, 0.0)
    left = lane % 8 < 4
    pick = jnp.concatenate([jnp.where(left, hit, 0.0), jnp.where(left, 0.0, hit)], axis=0).astype(BF16)
    both = jnp.concatenate([hid[:, : width // 2], hid[:, width // 2 :]], axis=0)
    out = lax.dot_general(pick, both, (((0,), (0,)), ((), ())), preferred_element_type=F32)
    disp_ref[...] = out.astype(BF16).reshape(disp_ref.shape)


def dispatch(parts, residual, routes, experts):
    rows, width = parts[0].shape
    vm = pl.BlockSpec(memory_space=pltpu.VMEM)
    return pl.pallas_call(
        dispatch_kernel,
        name="dispatch",
        out_shape=[
            jax.ShapeDtypeStruct((rows, width), BF16),
            jax.ShapeDtypeStruct((experts, 8, width // 2), BF16),
        ],
        in_specs=[vm] * 6,
        out_specs=[vm] * 2,
        compiler_params=VLIM,
    )(*parts, residual, routes)


def unfold(x):
    n, _, w = x.shape
    x = x.reshape(n // 2, 2, 8, w)
    a, b = x[:, 0], x[:, 1]
    top = iota(a.shape, 1) < 4
    left = jnp.where(top, a, pltpu.roll(b, 4, 1))
    right = jnp.where(top, pltpu.roll(a, 4, 1), b)
    return left.reshape(n * 4, w), right.reshape(n * 4, w)


def fold(left, right):
    rows, w = left.shape
    left, right = left.reshape(rows // 8, 8, w), right.reshape(rows // 8, 8, w)
    top = iota(left.shape, 1) < 4
    a = jnp.where(top, left, pltpu.roll(right, 4, 1))
    b = jnp.where(top, pltpu.roll(left, 4, 1), right)
    return a, b


def gate_kernel(x0, x1, x2, x3, gain_ref, wg_ref, wu_ref, inner_ref, xs):
    head = head_id()
    w = x0.shape[2]
    total = jnp.zeros((inner_ref.shape[0], 1), F32)
    for k, x in enumerate((x0, x1, x2, x3)):
        for f, part in enumerate(unfold(x[...].astype(F32))):
            xs[2 * k + f] = part
            total = total + jnp.sum(part * part, axis=1, keepdims=True)
    scale = lax.rsqrt(total / (8 * w) + EPS)
    gate = jnp.zeros(inner_ref.shape, F32)
    up = jnp.zeros(inner_ref.shape, F32)
    for k in range(4):
        for f in range(2):
            first = pl.multiple_of(((head + 4 - k) % 4) * 2 * w + f * w, w)
            normed = (xs[2 * k + f] * scale * gain_ref[:, pl.ds(first, w)]).astype(BF16)
            gate = gate + dot(normed, wg_ref[pl.ds(first, w), :])
            up = up + dot(normed, wu_ref[pl.ds(first, w), :])
    inner_ref[...] = (gate / (1.0 + jnp.exp(-gate)) * up).astype(BF16)


def gate_up(xs, gain, w_gate, w_up):
    n, _, w = xs[0].shape
    eff = w_gate.shape[1]
    vm = pl.BlockSpec(memory_space=pltpu.VMEM)
    return pl.pallas_call(
        gate_kernel,
        name="gate_up",
        out_shape=jax.ShapeDtypeStruct((n * 4, eff), BF16),
        in_specs=[vm] * 7,
        out_specs=vm,
        scratch_shapes=[pltpu.VMEM((8, n * 4, w), F32)],
        compiler_params=VLIM,
    )(*xs, gain.reshape(1, -1), w_gate, w_up)


def down_kernel(i0, i1, i2, i3, w_ref, out_ref, w_buf, sem):
    head = head_id()
    eff = i0.shape[1]
    width = w_buf.shape[1]
    cols = pl.ds(pl.multiple_of(head * width, width), width)
    copy = pltpu.make_async_copy(w_ref.at[:, cols], w_buf, sem)
    copy.start()
    copy.wait()
    acc = jnp.zeros((i0.shape[0], width), F32)
    for k, x in enumerate((i0, i1, i2, i3)):
        first = pl.multiple_of(((head + 4 - k) % 4) * eff, eff)
        acc = acc + dot(x[...], w_buf[pl.ds(first, eff), :])
    a, b = fold(acc[:, : width // 2], acc[:, width // 2 :])
    out_ref[:, 0] = a.astype(BF16)
    out_ref[:, 1] = b.astype(BF16)


def down(inners, w_down):
    rows, eff = inners[0].shape
    width = w_down.shape[1] // 4
    vm = pl.BlockSpec(memory_space=pltpu.VMEM)
    out = pl.pallas_call(
        down_kernel,
        name="down",
        out_shape=jax.ShapeDtypeStruct((rows // 8, 2, 8, width // 2), BF16),
        in_specs=[vm] * 4 + [pl.BlockSpec(memory_space=pl.ANY)],
        out_specs=vm,
        scratch_shapes=[pltpu.VMEM((w_down.shape[0], width), BF16), pltpu.SemaphoreType.DMA],
        compiler_params=VLIM,
    )(*inners, w_down)
    return out.reshape(rows // 4, 8, width // 2)


def blend_kernel(y_ref, hid_ref, routes_ref, rw_ref, out_ref):
    rows, picks = routes_ref.shape
    routes, share = routes_ref[...], rw_ref[...]
    cells = y_ref.shape[0] * 4
    lane = iota((rows, cells), 1)
    hit = jnp.zeros((rows, cells), F32)
    mix = jnp.zeros((rows, cells), F32)
    for k in range(picks):
        on = routes[:, k : k + 1] == lane // 4
        hit = hit + jnp.where(on, 1.0, 0.0)
        mix = mix + jnp.where(on, share[:, k : k + 1], 0.0)
    mix = jnp.where(rank_of(hit) == (lane % 4).astype(F32), mix, 0.0)
    m_hi, m_lo = hi_lo(mix)
    w = y_ref.shape[2]
    for f, part in enumerate(unfold(y_ref[...].astype(F32))):
        part = part.astype(BF16)
        hid = hid_ref[:, f * w : f * w + w].astype(F32)
        out_ref[:, f * w : f * w + w] = (hid + (dot(m_hi, part) + dot(m_lo, part))).astype(BF16)


def blend(returned, hidden, routes, route_weights):
    vm = pl.BlockSpec(memory_space=pltpu.VMEM)
    return pl.pallas_call(
        blend_kernel,
        name="blend",
        out_shape=jax.ShapeDtypeStruct(hidden.shape, BF16),
        in_specs=[vm] * 4,
        out_specs=vm,
        compiler_params=VLIM,
    )(returned, hidden, routes, route_weights)


def norm_kernel(s0, s1, s2, s3, gain_ref, out_ref):
    head = head_id()
    w = s0.shape[1]
    parts = [s[...].astype(F32) for s in (s0, s1, s2, s3)]
    total = sum(jnp.sum(p * p, axis=1, keepdims=True) for p in parts)
    scale = lax.rsqrt(total / (4 * w) + EPS)
    for k, p in enumerate(parts):
        cols = pl.ds(pl.multiple_of(((head + 4 - k) % 4) * w, w), w)
        out_ref[:, cols] = (p * scale * gain_ref[:, cols]).astype(BF16)


def norm_parts(parts, gain):
    rows, w = parts[0].shape
    vm = pl.BlockSpec(memory_space=pltpu.VMEM)
    return pl.pallas_call(
        norm_kernel,
        name="norm_parts",
        out_shape=jax.ShapeDtypeStruct((rows, 4 * w), BF16),
        in_specs=[vm] * 5,
        out_specs=vm,
        compiler_params=VLIM,
    )(*parts, gain.reshape(1, -1))


def from_heads(x):
    n = lax.axis_size("head")
    return [x] + [lax.ppermute(x, "head", [(i, (i + k) % n) for i in range(n)]) for k in range(1, n)]


def to_heads(xs):
    n = lax.axis_size("head")
    return [xs[0]] + [lax.ppermute(xs[k], "head", [(i, (i + k) % n) for i in range(n)]) for k in range(1, n)]


def swap_core(x):
    return lax.ppermute(x, "c", [(0, 1), (1, 0)])


def local(
    residual, queries, new_kv, kv_cache, lengths, slot_request, slot_page, slot_used, out_weight,
    norm_gain, routes, route_weights, w_gate, w_up, w_down, next_gain, next_weight,
):
    rows = queries.shape[0]
    experts = lax.axis_size(REQ)
    chips = experts // 2
    w_down_all = lax.all_gather(w_down.reshape(w_down.shape[1:]), "head", axis=0, tiled=True)
    nkv = new_kv.reshape(rows, -1)
    qa = lax.all_to_all(jnp.broadcast_to(queries[None], (chips,) + queries.shape), ("z", "y"), 0, 0, tiled=True)
    qb = swap_core(qa)
    parts = attend_pages(slot_request, slot_page, slot_used, lengths, qa, qb, kv_cache)
    core = lax.axis_index("c")
    both = jnp.where(core == 0, jnp.stack([parts[0], parts[1]], 1), jnp.stack([parts[1], parts[0]], 1))
    both = both.reshape((experts,) + parts.shape[2:])
    arrived = lax.all_to_all(both, REQ, 0, 0, tiled=True)
    shares = to_heads(owner_part(arrived, queries, nkv, out_weight))
    hidden, disp = dispatch(shares, residual, routes, experts)
    tokens = lax.all_to_all(disp, REQ, 0, 0, tiled=True)
    inner = gate_up(from_heads(tokens), norm_gain, w_gate[0], w_up[0])
    expert_out = down(from_heads(inner), w_down_all)
    returned = lax.all_to_all(expert_out, REQ, 0, 0, tiled=True)
    stream = blend(returned, hidden, routes, route_weights)
    normed = norm_parts(from_heads(stream), next_gain)
    next_qkv = jnp.einsum("td,dcf->tcf", normed, next_weight, preferred_element_type=F32).astype(BF16)
    return stream, next_qkv


def solution(mesh):
    split = Mesh(mesh.devices.reshape(8, 4, 2, 4), ("z", "y", "c", "head"))
    placed = (
        P(REQ, None),
        P(REQ, "head"),
        P(REQ, None, "head"),
        P(REQ, None, None, "head"),
        P(),
        P(REQ),
        P(REQ),
        P(REQ),
        P("head", None),
        P(),
        P(REQ, None),
        P(REQ, None),
        P(REQ, None, "head"),
        P(REQ, None, "head"),
        P(REQ, "head", None),
        P(),
        P(None, None, "head"),
    )
    return jax.shard_map(
        local,
        mesh=split,
        in_specs=placed,
        out_specs=(P(REQ, "head"), P(REQ, None, "head")),
        check_vma=False,
    )
```

time: 686 us -> 179 us (0.26)
  blocking collectives: 479 us -> 43.5 us
  waiting for transfers between devices: 122 us -> 59.5 us
  matrix products: 20 us -> 1.13 us
  starting transfers between devices: 12.5 us -> 28.8 us
  Pallas kernels: 0 us -> 13.7 us
  local copies, waits for them, and re-layouts: 30.3 us -> 17.1 us
    pmax x1 -> x0, blocking collectives: 247 us -> none  [local(): peak_score = lax.pmax(jnp.maximum(local_peak, placed_score), 'req')]
    unnamed x1 -> x0, blocking collectives: 131 us -> none
    psum x2 -> x0, waiting for transfers between devices: 92.9 us -> none  [the longest x1 47 us: local(): lax.psum(partial_out.astype(jnp.bfloat16), 'head').astype(jnp.float32)]
    all_gather x1 -> x0, blocking collectives: 59.8 us -> none  [local(): everyone = lax.all_gather(queries, 'req', axis=0, tiled=True)]
    ppermute x0 -> x13, waiting for transfers between devices: none -> 23.5 us  [the longest x9 20.5 us: from_heads(): lax.ppermute(x, 'head', [(i, (i + k) % n) for i in range(n)])]
    dot_general x10 -> x1, matrix products: 20 us -> 1.13 us  [local(): jnp.einsum('td,dcf->tcf', normed, next_weight, preferred_element_type=F32)]
    ppermute x0 -> x13, starting transfers between devices: none -> 18.1 us  [the longest x9 10.7 us: from_heads(): lax.ppermute(x, 'head', [(i, (i + k) % n) for i in range(n)])]
    pallas_call x0 -> x7, Pallas kernels: none -> 13.7 us  [the longest x1 7.47 us: attend_pages(): pl.pallas_call(attn_kernel, name='attend_pages', out_shape=jax.ShapeDtype...]
  transfers between devices with their start and end apart: 4 -> 16, of which waited for: 4 -> 12; matrix products, arithmetic and copies ran while one was open for 0% -> 2% of each run, Pallas kernels for 0% -> 6%
where the time goes in v1:
time: 179 us; the launch traced here: 178 us
  waiting for transfers between devices  59.5 us (33%)
  blocking collectives  43.5 us (24%)
  starting transfers between devices  28.8 us (16%)
  local copies, waits for them, and re-layouts  17.1 us (10%)
  between operations  14.2 us (8%)
  Pallas kernels  13.7 us (8%)
    all_to_all x1, blocking collectives, local(): lax.all_to_all(jnp.broadcast_to(queries[None], (chips,) + queries.shape),...  23 us
    all_to_all x1, waiting for transfers between devices, local(): arrived = lax.all_to_all(both, REQ, 0, 0, tiled=True)  22.9 us
    ppermute x9, waiting for transfers between devices, from_heads(): lax.ppermute(x, 'head', [(i, (i + k) % n) for i in range(n)])  20.5 us
    all_to_all x1, blocking collectives, local(): tokens = lax.all_to_all(disp, REQ, 0, 0, tiled=True)  20.5 us
    unnamed x45, local copies, waits for them, and re-layouts  15.2 us
    all_to_all x1, waiting for transfers between devices, local(): returned = lax.all_to_all(expert_out, REQ, 0, 0, tiled=True)  12.4 us
    ppermute x9, starting transfers between devices, from_heads(): lax.ppermute(x, 'head', [(i, (i + k) % n) for i in range(n)])  10.7 us
    pallas_call x1, Pallas kernels, attend_pages(): pl.pallas_call(attn_kernel, name='attend_pages', out_shape=jax.ShapeDtype...  7.47 us
  transfers between devices with their start and end apart: 16, of which 12 were waited for; matrix products, arithmetic and copies ran while one was open for 2% of the time, Pallas kernels for 6%

profile of v1, /device:TPU:1, one launch (start us, length us, event | category | flops | bytes accessed | tf_op | source)
XLA Modules:
  0.0 178.1 jit_solution(11278023253489917213)
XLA Ops:
  7.2 0.7 all-gather.3.cloned.1.call-update
  7.9 0.9 broadcast_in_dim.2
  8.8 23.0 %all_to_all.20 = bf16[32,16,256]{2,1,0:T(8,128)(2,1)S(1)} all-to-all(bf16[32,16,256]{2,1,0:T(8,128)(2,1)S(1)} %broadcast_in_dim.2), channel_id=1, replica_groups=mesh['z'=8,'y'=4,'c'=2,'head'=4] {'z','y'}, dimensions={0} | all-to-all | bytes 524288 | tf_op jit(solution)/shard_map/all_to_all | solution.py:411
  31.9 2.5 %collective-permute-start = (bf16[32,16,256]{2,1,0:T(8,128)(2,1)S(1)}, bf16[32,16,256]{2,1,0:T(8,128)(2,1)}, u32[]{:S(2)}, u32[]{:S(2)}) collective-permute-start(bf16[32,16,256]{2,1,0:T(8,128)(2,1)S(1)} %all_to_all.20), channel_id=1, source_target_pairs={{0,4},{4,0},{1,5},{5,1},{2,6},{6,2},{3,7},{7,3},{8,12},{12,8},{9,1... | collective-permute-start | bytes 786440 | tf_op jit(solution)/shard_map/ppermute | solution.py:399
  34.3 1.3 collective-permute-done
  35.6 2.2 %copy-done.2 = bf16[128,2,32,256]{3,2,1,0:T(8,128)(2,1)S(1)} copy-done((bf16[128,2,32,256]{3,2,1,0:T(8,128)(2,1)S(1)}, bf16[128,2,32,256]{3,2,1,0:T(8,128)(2,1)}, u32[]{:S(2)}) %copy-start.2) | copy-done | bytes 4194328
  37.8 0.7 copy-done.15
  38.5 0.7 copy-done.16
  39.2 0.7 copy-done.17
  39.8 0.7 copy-done.18
  40.5 7.5 %attend_pages.1 = bf16[2,32,48,128]{3,2,1,0:T(8,128)(2,1)S(1)} custom-call(s32[1,128]{1,0:T(1,128)S(1)} %bitcast.31, s32[1,128]{1,0:T(1,128)S(1)} %bitcast.32, s32[1,128]{1,0:T(1,128)S(1)} %bitcast.33, s32[1,1024]{1,0:T(1,128)S(1)} %bitcast.30, bf16[512,256]{1,0:T(8,128)(2,1)S(1)} %bitcast.26, bf16[512,256]{1,0:T(8,128)(2,1)} %bitcast.5.qb_ref, ...), custom_call_target="tpu_custom_call" | custom-call | tf_op jit(solution)/shard_map/attend_pages/pallas_call | solution.py:133
  48.2 0.9 copy.19
  49.2 5.2 %all-to-all-start.1 = ((bf16[64,48,128]{2,1,0:T(8,128)(2,1)}), bf16[64,48,128]{2,1,0:T(8,128)(2,1)}, u32[]{:S(2)}, u32[]{:S(2)}) async-start(bf16[64,48,128]{2,1,0:T(8,128)(2,1)} %bitcast.34), calls=%async_computation.1 | async-start | bytes 1572864 | tf_op jit(solution)/shard_map/all_to_all | solution.py:417
  54.4 22.9 %all-to-all-done.1.part_ref = bf16[64,48,128]{2,1,0:T(8,128)(2,1)} async-done(((bf16[64,48,128]{2,1,0:T(8,128)(2,1)}), bf16[64,48,128]{2,1,0:T(8,128)(2,1)}, u32[]{:S(2)}, u32[]{:S(2)}) %all-to-all-start.1) | async-done | bytes 786464 | tf_op jit(solution)/shard_map/all_to_all | solution.py:417
  77.3 1.2 copy-done.5
  78.5 2.3 %owner_part.1 = (bf16[16,512]{1,0:T(8,128)(2,1)S(1)}, bf16[16,512]{1,0:T(8,128)(2,1)S(1)}, bf16[16,512]{1,0:T(8,128)(2,1)S(1)}, bf16[16,512]{1,0:T(8,128)(2,1)S(1)}) custom-call(bf16[64,48,128]{2,1,0:T(8,128)(2,1)} %all-to-all-done.1.part_ref, bf16[16,256]{1,0:T(8,128)(2,1)S(1)} %copy-done.10, bf16[16,512]{1,0:T(8,128)(2,1)S(1)} %bitcast.27, ...), custom_call_target="tpu_custom_call" | custom-call | tf_op jit(solution)/shard_map/owner_part/pallas_call | solution.py:192
  80.8 1.3 collective-permute-start.1
  82.1 2.5 %collective-permute-start.2 = (bf16[16,512]{1,0:T(8,128)(2,1)S(1)}, bf16[16,512]{1,0:T(8,128)(2,1)S(1)}, u32[]{:S(2)}, u32[]{:S(2)}) collective-permute-start(bf16[16,512]{1,0:T(8,128)(2,1)S(1)} %get-tuple-element.10), channel_id=1, source_target_pairs={{0,2},{1,3},{2,0},{3,1},{4,6},{5,7},{6,4},{7,5},{8,10},{9,11},{10,... | collective-permute-start | bytes 49160 | tf_op jit(solution)/shard_map/ppermute | solution.py:395
  84.6 1.1 collective-permute-start.3
  86.2 1.3 collective-permute-done.3.p3
  87.5 0.5 dispatch.1
  88.0 0.6 copy-done.11
  88.6 20.5 %all_to_all.21.x0 = bf16[64,8,256]{2,1,0:T(8,128)(2,1)S(1)} all-to-all(bf16[64,8,256]{2,1,0:T(8,128)(2,1)S(1)} %get-tuple-element.12), channel_id=1, replica_groups=mesh['z'=8,'y'=4,'c'=2,'head'=4] {'z','y','c'}, dimensions={0} | all-to-all | bytes 524288 | tf_op jit(solution)/shard_map/all_to_all | solution.py:420
  109.0 3.5 %collective-permute-start.5 = (bf16[64,8,256]{2,1,0:T(8,128)(2,1)S(1)}, bf16[64,8,256]{2,1,0:T(8,128)(2,1)S(1)}, u32[]{:S(2)}, u32[]{:S(2)}) collective-permute-start(bf16[64,8,256]{2,1,0:T(8,128)(2,1)S(1)} %all_to_all.21.x0), channel_id=1, source_target_pairs={{0,2},{1,3},{2,0},{3,1},{4,6},{5,7},{6,4},{7,5},{8,10},{9,11},{10,... | collective-permute-start | bytes 786440 | tf_op jit(solution)/shard_map/ppermute | solution.py:390
  112.6 5.3 %collective-permute-done.4.x1 = bf16[64,8,256]{2,1,0:T(8,128)(2,1)S(1)} collective-permute-done((bf16[64,8,256]{2,1,0:T(8,128)(2,1)S(1)}, bf16[64,8,256]{2,1,0:T(8,128)(2,1)S(1)}, u32[]{:S(2)}, u32[]{:S(2)}) %collective-permute-start.4) | collective-permute-done | bytes 262176 | tf_op jit(solution)/shard_map/ppermute | solution.py:390
  117.9 6.5 %collective-permute-done.5.x2 = bf16[64,8,256]{2,1,0:T(8,128)(2,1)S(1)} collective-permute-done((bf16[64,8,256]{2,1,0:T(8,128)(2,1)S(1)}, bf16[64,8,256]{2,1,0:T(8,128)(2,1)S(1)}, u32[]{:S(2)}, u32[]{:S(2)}) %collective-permute-start.5) | collective-permute-done | bytes 262176 | tf_op jit(solution)/shard_map/ppermute | solution.py:390
  124.4 1.2 copy-done.3
  125.6 1.2 copy-done.4
  126.8 1.1 gate_up.1.i0
  127.9 1.2 collective-permute-start.7
  129.1 3.0 %collective-permute-start.8 = (bf16[256,256]{1,0:T(8,128)(2,1)S(1)}, bf16[256,256]{1,0:T(8,128)(2,1)S(1)}, u32[]{:S(2)}, u32[]{:S(2)}) collective-permute-start(bf16[256,256]{1,0:T(8,128)(2,1)S(1)} %gate_up.1.i0), channel_id=1, source_target_pairs={{0,2},{1,3},{2,0},{3,1},{4,6},{5,7},{6,4},{7,5},{8,10},{9,11},{10,... | collective-permute-start | bytes 393224 | tf_op jit(solution)/shard_map/ppermute | solution.py:390
  132.1 1.2 collective-permute-done.7.i1
  133.2 4.7 %collective-permute-done.8.i2 = bf16[256,256]{1,0:T(8,128)(2,1)S(1)} collective-permute-done((bf16[256,256]{1,0:T(8,128)(2,1)S(1)}, bf16[256,256]{1,0:T(8,128)(2,1)S(1)}, u32[]{:S(2)}, u32[]{:S(2)}) %collective-permute-start.8) | collective-permute-done | bytes 131104 | tf_op jit(solution)/shard_map/ppermute | solution.py:390
  138.0 0.6 copy-done.6
  138.6 2.2 %copy-done.1 = bf16[1,1024,2048]{2,1,0:T(8,128)(2,1)S(1)} copy-done((bf16[1,1024,2048]{2,1,0:T(8,128)(2,1)S(1)}, bf16[1,1024,2048]{2,1,0:T(8,128)(2,1)}, u32[]{:S(2)}) %copy-start.1) | copy-done | bytes 4194328
  140.8 0.9 copy-done.7
  141.7 1.3 down.1
  143.0 5.5 %all-to-all-start.3 = ((bf16[64,8,256]{2,1,0:T(8,128)(2,1)}), bf16[64,8,256]{2,1,0:T(8,128)(2,1)S(1)}, u32[]{:S(2)}, u32[]{:S(2)}) async-start(bf16[64,8,256]{2,1,0:T(8,128)(2,1)} %bitcast.13), calls=%async_computation.3 | async-start | bytes 524288 | tf_op jit(solution)/shard_map/all_to_all | solution.py:423
  148.6 0.8 copy.22.rw_ref
  149.3 12.4 %all-to-all-done.3.y_ref = bf16[64,8,256]{2,1,0:T(8,128)(2,1)S(1)} async-done(((bf16[64,8,256]{2,1,0:T(8,128)(2,1)}), bf16[64,8,256]{2,1,0:T(8,128)(2,1)S(1)}, u32[]{:S(2)}, u32[]{:S(2)}) %all-to-all-start.3) | async-done | bytes 262176 | tf_op jit(solution)/shard_map/all_to_all | solution.py:423
  161.7 0.7 copy-done.12
  162.5 1.0 blend.1.s0
  163.5 3.0 %collective-permute-start.11 = (bf16[16,512]{1,0:T(8,128)(2,1)}, bf16[16,512]{1,0:T(8,128)(2,1)S(1)}, u32[]{:S(2)}, u32[]{:S(2)}) collective-permute-start(bf16[16,512]{1,0:T(8,128)(2,1)} %blend.1.s0), channel_id=1, source_target_pairs={{0,2},{1,3},{2,0},{3,1},{4,6},{5,7},{6,4},{7,5},{8,10},{9,11},{10,... | collective-permute-start | bytes 49160 | tf_op jit(solution)/shard_map/ppermute | solution.py:390
  166.5 0.9 collective-permute-done.10.s1
  167.4 0.6 collective-permute-done.11.s2
  168.0 1.3 collective-permute-done.12.s3
  169.3 0.7 copy-done.8
  170.1 1.1 convolution_convert_fusion
  (44 shorter events, 1.0 us)
Async XLA Ops:
  7.2 163.0 %copy-start = (bf16[2048,3,256]{2,0,1:T(8,128)(2,1)S(1)}, bf16[2048,3,256]{2,0,1:T(8,128)(2,1)}, u32[]{:S(2)}) copy-start(bf16[2048,3,256]{2,0,1:T(8,128)(2,1)} %param.33) | copy-start | bytes 9437188
  7.2 131.5 %all-gather.3.cloned.1.call-start = ((), (), s32[]{:S(2)}) async-start(), calls=%async_computation.4 | async-start | bytes 5242880 | tf_op jit(solution)/shard_map/all_gather | solution.py:409
  31.9 3.7 %collective-permute-start = (bf16[32,16,256]{2,1,0:T(8,128)(2,1)S(1)}, bf16[32,16,256]{2,1,0:T(8,128)(2,1)}, u32[]{:S(2)}, u32[]{:S(2)}) collective-permute-start(bf16[32,16,256]{2,1,0:T(8,128)(2,1)S(1)} %all_to_all.20), channel_id=1, source_target_pairs={{0,4},{4,0},{1,5},{5,1},{2,6},{6,2},{3,7},{7,3},{8,12},{12,8},{9,1... | collective-permute-start | bytes 786440 | tf_op jit(solution)/shard_map/ppermute | solution.py:399
  35.6 2.2 %copy-start.2 = (bf16[128,2,32,256]{3,2,1,0:T(8,128)(2,1)S(1)}, bf16[128,2,32,256]{3,2,1,0:T(8,128)(2,1)}, u32[]{:S(2)}) copy-start(bf16[128,2,32,256]{3,2,1,0:T(8,128)(2,1)} %kv_ref.1) | copy-start | bytes 12582916
  37.8 0.7 copy-start.15
  38.5 0.7 copy-start.16
  39.2 0.7 copy-start.17
  39.8 0.7 copy-start.18
  48.0 6.4 %copy-start.19 = (bf16[16,2,256]{2,1,0:T(2,128)(2,1)S(1)}, bf16[16,2,256]{2,1,0:T(2,128)(2,1)}, u32[]{:S(2)}) copy-start(bf16[16,2,256]{2,1,0:T(2,128)(2,1)} %param.19) | copy-start | bytes 49156
  48.0 29.3 %copy-start.10 = (bf16[16,256]{1,0:T(8,128)(2,1)S(1)}, bf16[16,256]{1,0:T(8,128)(2,1)}, u32[]{:S(2)}) copy-start(bf16[16,256]{1,0:T(8,128)(2,1)} %q_ref.1) | copy-start | bytes 24580
  48.0 37.7 %copy-start.20 = (s32[16,8]{0,1:T(8,128)S(1)}, s32[16,8]{0,1:T(8,128)}, u32[]{:S(2)}) copy-start(s32[16,8]{0,1:T(8,128)} %param.27) | copy-start | bytes 1540
  48.1 39.4 %copy-start.9 = (bf16[16,2048]{1,0:T(8,128)(2,1)S(1)}, bf16[16,2048]{1,0:T(8,128)(2,1)}, u32[]{:S(2)}) copy-start(bf16[16,2048]{1,0:T(8,128)(2,1)} %res_ref.1) | copy-start | bytes 196612
  48.2 76.2 %copy-start.13 = (f32[2048]{0:T(1024)S(1)}, f32[2048]{0:T(1024)}, u32[]{:S(2)}) copy-start(f32[2048]{0:T(1024)} %param.26) | copy-start | bytes 24580
  49.2 28.1 %all-to-all-start.1 = ((bf16[64,48,128]{2,1,0:T(8,128)(2,1)}), bf16[64,48,128]{2,1,0:T(8,128)(2,1)}, u32[]{:S(2)}, u32[]{:S(2)}) async-start(bf16[64,48,128]{2,1,0:T(8,128)(2,1)} %bitcast.34), calls=%async_computation.1 | async-start | bytes 1572864 | tf_op jit(solution)/shard_map/all_to_all | solution.py:417
  77.3 1.2 copy-start.5
  80.8 5.0 %collective-permute-start.1 = (bf16[16,512]{1,0:T(8,128)(2,1)S(1)}, bf16[16,512]{1,0:T(8,128)(2,1)S(1)}, u32[]{:S(2)}, u32[]{:S(2)}) collective-permute-start(bf16[16,512]{1,0:T(8,128)(2,1)S(1)} %get-tuple-element.9), channel_id=1, source_target_pairs={{0,1},{1,2},{2,3},{3,0},{4,5},{5,6},{6,7},{7,4},{8,9},{9,10},{10,1... | collective-permute-start | bytes 49160 | tf_op jit(solution)/shard_map/ppermute | solution.py:395
  82.1 4.1 %collective-permute-start.2 = (bf16[16,512]{1,0:T(8,128)(2,1)S(1)}, bf16[16,512]{1,0:T(8,128)(2,1)S(1)}, u32[]{:S(2)}, u32[]{:S(2)}) collective-permute-start(bf16[16,512]{1,0:T(8,128)(2,1)S(1)} %get-tuple-element.10), channel_id=1, source_target_pairs={{0,2},{1,3},{2,0},{3,1},{4,6},{5,7},{6,4},{7,5},{8,10},{9,11},{10,... | collective-permute-start | bytes 49160 | tf_op jit(solution)/shard_map/ppermute | solution.py:395
  84.6 2.9 %collective-permute-start.3 = (bf16[16,512]{1,0:T(8,128)(2,1)S(1)}, bf16[16,512]{1,0:T(8,128)(2,1)S(1)}, u32[]{:S(2)}, u32[]{:S(2)}) collective-permute-start(bf16[16,512]{1,0:T(8,128)(2,1)S(1)} %get-tuple-element.11), channel_id=1, source_target_pairs={{0,3},{1,0},{2,1},{3,2},{4,7},{5,4},{6,5},{7,6},{8,11},{9,8},{10,9... | collective-permute-start | bytes 49160 | tf_op jit(solution)/shard_map/ppermute | solution.py:395
  88.0 0.6 copy-start.11
  109.0 8.9 %collective-permute-start.4 = (bf16[64,8,256]{2,1,0:T(8,128)(2,1)S(1)}, bf16[64,8,256]{2,1,0:T(8,128)(2,1)S(1)}, u32[]{:S(2)}, u32[]{:S(2)}) collective-permute-start(bf16[64,8,256]{2,1,0:T(8,128)(2,1)S(1)} %all_to_all.21.x0), channel_id=1, source_target_pairs={{0,1},{1,2},{2,3},{3,0},{4,5},{5,6},{6,7},{7,4},{8,9},{9,10},{10,1... | collective-permute-start | bytes 786440 | tf_op jit(solution)/shard_map/ppermute | solution.py:390
  109.0 15.3 %collective-permute-start.5 = (bf16[64,8,256]{2,1,0:T(8,128)(2,1)S(1)}, bf16[64,8,256]{2,1,0:T(8,128)(2,1)S(1)}, u32[]{:S(2)}, u32[]{:S(2)}) collective-permute-start(bf16[64,8,256]{2,1,0:T(8,128)(2,1)S(1)} %all_to_all.21.x0), channel_id=1, source_target_pairs={{0,2},{1,3},{2,0},{3,1},{4,6},{5,7},{6,4},{7,5},{8,10},{9,11},{10,... | collective-permute-start | bytes 786440 | tf_op jit(solution)/shard_map/ppermute | solution.py:390
  112.6 11.8 %collective-permute-start.6 = (bf16[64,8,256]{2,1,0:T(8,128)(2,1)S(1)}, bf16[64,8,256]{2,1,0:T(8,128)(2,1)S(1)}, u32[]{:S(2)}, u32[]{:S(2)}) collective-permute-start(bf16[64,8,256]{2,1,0:T(8,128)(2,1)S(1)} %all_to_all.21.x0), channel_id=1, source_target_pairs={{0,3},{1,0},{2,1},{3,2},{4,7},{5,4},{6,5},{7,6},{8,11},{9,8},{10,9... | collective-permute-start | bytes 786440 | tf_op jit(solution)/shard_map/ppermute | solution.py:390
  124.4 1.2 copy-start.3
  125.6 1.2 copy-start.4
  126.8 42.5 %copy-start.14 = (f32[2048]{0:T(1024)S(1)}, f32[2048]{0:T(1024)}, u32[]{:S(2)}) copy-start(f32[2048]{0:T(1024)} %param.32) | copy-start | bytes 24580
  127.9 5.3 %collective-permute-start.7 = (bf16[256,256]{1,0:T(8,128)(2,1)S(1)}, bf16[256,256]{1,0:T(8,128)(2,1)S(1)}, u32[]{:S(2)}, u32[]{:S(2)}) collective-permute-start(bf16[256,256]{1,0:T(8,128)(2,1)S(1)} %gate_up.1.i0), channel_id=1, source_target_pairs={{0,1},{1,2},{2,3},{3,0},{4,5},{5,6},{6,7},{7,4},{8,9},{9,10},{10,1... | collective-permute-start | bytes 393224 | tf_op jit(solution)/shard_map/ppermute | solution.py:390
  129.1 8.9 %collective-permute-start.8 = (bf16[256,256]{1,0:T(8,128)(2,1)S(1)}, bf16[256,256]{1,0:T(8,128)(2,1)S(1)}, u32[]{:S(2)}, u32[]{:S(2)}) collective-permute-start(bf16[256,256]{1,0:T(8,128)(2,1)S(1)} %gate_up.1.i0), channel_id=1, source_target_pairs={{0,2},{1,3},{2,0},{3,1},{4,6},{5,7},{6,4},{7,5},{8,10},{9,11},{10,... | collective-permute-start | bytes 393224 | tf_op jit(solution)/shard_map/ppermute | solution.py:390
  132.1 5.9 %collective-permute-start.9 = (bf16[256,256]{1,0:T(8,128)(2,1)S(1)}, bf16[256,256]{1,0:T(8,128)(2,1)S(1)}, u32[]{:S(2)}, u32[]{:S(2)}) collective-permute-start(bf16[256,256]{1,0:T(8,128)(2,1)S(1)} %gate_up.1.i0), channel_id=1, source_target_pairs={{0,3},{1,0},{2,1},{3,2},{4,7},{5,4},{6,5},{7,6},{8,11},{9,8},{10,9... | collective-permute-start | bytes 393224 | tf_op jit(solution)/shard_map/ppermute | solution.py:390
  138.0 0.7 copy-start.6
  138.6 2.2 %copy-start.1 = (bf16[1,1024,2048]{2,1,0:T(8,128)(2,1)S(1)}, bf16[1,1024,2048]{2,1,0:T(8,128)(2,1)}, u32[]{:S(2)}) copy-start(bf16[1,1024,2048]{2,1,0:T(8,128)(2,1)} %all-gather.3.cloned.1.call-done) | copy-start | bytes 12582916
  140.8 0.9 copy-start.7
  143.0 18.7 %all-to-all-start.3 = ((bf16[64,8,256]{2,1,0:T(8,128)(2,1)}), bf16[64,8,256]{2,1,0:T(8,128)(2,1)S(1)}, u32[]{:S(2)}, u32[]{:S(2)}) async-start(bf16[64,8,256]{2,1,0:T(8,128)(2,1)} %bitcast.13), calls=%async_computation.3 | async-start | bytes 524288 | tf_op jit(solution)/shard_map/all_to_all | solution.py:423
  161.7 0.7 copy-start.12
  163.4 4.0 %collective-permute-start.10 = (bf16[16,512]{1,0:T(8,128)(2,1)}, bf16[16,512]{1,0:T(8,128)(2,1)S(1)}, u32[]{:S(2)}, u32[]{:S(2)}) collective-permute-start(bf16[16,512]{1,0:T(8,128)(2,1)} %blend.1.s0), channel_id=1, source_target_pairs={{0,1},{1,2},{2,3},{3,0},{4,5},{5,6},{6,7},{7,4},{8,9},{9,10},{10,1... | collective-permute-start | bytes 49160 | tf_op jit(solution)/shard_map/ppermute | solution.py:390
  163.5 4.5 %collective-permute-start.11 = (bf16[16,512]{1,0:T(8,128)(2,1)}, bf16[16,512]{1,0:T(8,128)(2,1)S(1)}, u32[]{:S(2)}, u32[]{:S(2)}) collective-permute-start(bf16[16,512]{1,0:T(8,128)(2,1)} %blend.1.s0), channel_id=1, source_target_pairs={{0,2},{1,3},{2,0},{3,1},{4,6},{5,7},{6,4},{7,5},{8,10},{9,11},{10,... | collective-permute-start | bytes 49160 | tf_op jit(solution)/shard_map/ppermute | solution.py:390
  166.5 2.8 %collective-permute-start.12 = (bf16[16,512]{1,0:T(8,128)(2,1)}, bf16[16,512]{1,0:T(8,128)(2,1)S(1)}, u32[]{:S(2)}, u32[]{:S(2)}) collective-permute-start(bf16[16,512]{1,0:T(8,128)(2,1)} %blend.1.s0), channel_id=1, source_target_pairs={{0,3},{1,0},{2,1},{3,2},{4,7},{5,4},{6,5},{7,6},{8,11},{9,8},{10,9... | collective-permute-start | bytes 49160 | tf_op jit(solution)/shard_map/ppermute | solution.py:390
  169.3 0.7 copy-start.8
Sparse Core Ops, SparseCore 0:
  9.8 54.5 all-gather.2

commit v2 on v1

v2 whole, which is shorter than its diff:
```python
import functools
import math

import jax
import jax.numpy as jnp
from jax import lax
from jax.experimental import pallas as pl
from jax.experimental.pallas import tpu as pltpu
from jax.sharding import Mesh, PartitionSpec as P

HD = 128
EPS = 1e-06
FLOOR = -(2.0**99)
SCALE = 1.0 / math.sqrt(HD)
F32 = jnp.float32
BF16 = jnp.bfloat16
REQ = ("z", "y", "c")
VLIM = pltpu.CompilerParams(vmem_limit_bytes=24 * 1024 * 1024)
VM = pl.BlockSpec(memory_space=pltpu.VMEM)


class Pending:
    def __init__(self, buf, copy):
        self.buf, self.copy, self.done = buf, copy, False

    def get(self):
        if not self.done:
            self.copy.wait()
            self.done = True
        return self.buf


def run(body, name, outs, near, far, scratch=(), after=(), moves=()):
    nn, nf, na, nm = len(near), len(far), len(after), len(moves)
    parts = 4

    def kernel(*refs):
        ins, refs = refs[: nn + nf + na + nm], refs[nn + nf + na + nm :]
        outputs, moved, rest = refs[: len(outs)], refs[len(outs) : len(outs) + nm], refs[len(outs) + nm :]
        bufs, sems, move_sems, own = rest[:nf], rest[nf], rest[nf + 1], rest[nf + 2 :]
        copies = [pltpu.make_async_copy(ins[nn + i], bufs[i], sems.at[i]) for i in range(nf)]
        for copy in copies:
            copy.start()
        pending = [Pending(b, c) for b, c in zip(bufs, copies)]
        moving = []
        for i in range(nm):
            rows = moved[i].shape[0] // parts
            for j in range(parts):
                src, dst = ins[nn + nf + na + i].at[pl.ds(j * rows, rows)], moved[i].at[pl.ds(j * rows, rows)]
                moving.append(pltpu.make_async_copy(src, dst, move_sems.at[parts * i + j]))
        for copy in moving:
            copy.start()
        body(ins[:nn], pending, outputs, own)
        for p in pending:
            p.get()
        for copy in moving:
            copy.wait()

    def pin(xs):
        return [pltpu.with_memory_space_constraint(x, pltpu.HBM) for x in xs]

    hbm, any_space = pl.BlockSpec(memory_space=pltpu.HBM), pl.BlockSpec(memory_space=pl.ANY)
    return pl.pallas_call(
        kernel,
        name=name,
        out_shape=list(outs) + [sds(x.shape, x.dtype) for x in moves],
        in_specs=[VM] * nn + [hbm] * nf + [any_space] * na + [hbm] * nm,
        out_specs=[VM] * (len(outs) + nm),
        scratch_shapes=[pltpu.VMEM(x.shape, x.dtype) for x in far]
        + [pltpu.SemaphoreType.DMA((max(nf, 1),)), pltpu.SemaphoreType.DMA((max(nm * parts, 1),))]
        + list(scratch),
        compiler_params=VLIM,
    )(*near, *pin(far), *after, *pin(moves))


def sds(shape, dtype):
    return jax.ShapeDtypeStruct(shape, dtype)


def iota(shape, dim):
    return lax.broadcasted_iota(jnp.int32, shape, dim)


def core_id():
    return lax.axis_index("c")


def head_id():
    return lax.axis_index("head")


def dot(a, b):
    return jnp.dot(a, b, preferred_element_type=F32)


def hi_lo(x):
    hi = x.astype(BF16)
    return hi, (x - hi.astype(F32)).astype(BF16)


def tables_body(near, far, outs, own, page):
    pick_ref, count_ref, same_ref, mine_ref, spread_ref, spread16_ref = outs
    req = far[0].get()[...]
    slots, total = pick_ref.shape
    half = total // 2
    place = jnp.where((req // 16) % 2 == core_id(), 0, half) + (req // 32) * 16 + req % 16
    spread_ref[...] = jnp.where(iota((total, slots), 0) == place, 1.0, 0.0).astype(BF16)
    spread16_ref[...] = jnp.where(iota((total, slots), 0) // 16 == place // 16, 1.0, 0.0).astype(BF16)
    eye = iota((slots, slots), 0) == iota((slots, slots), 1)

    def to_col(row):
        return jnp.sum(jnp.where(eye, row.astype(F32), 0.0), axis=1, keepdims=True)

    req_col = to_col(req)
    same = req_col == req.astype(F32)
    same_ref[...] = jnp.where(same, 1.0, 0.0)
    slot_row = iota((slots, slots), 1).astype(F32)
    first = jnp.min(jnp.where(same, slot_row, 9999.0), axis=1, keepdims=True)
    leader = first == iota((slots, 1), 0).astype(F32)
    mine = (iota((slots, HD), 1) % 16).astype(F32) == to_col(req % 16)
    mine_ref[...] = jnp.where(mine & leader, 1.0, 0.0)
    lane_total = iota((slots, total), 1).astype(F32)
    pick_ref[...] = jnp.where(to_col(place) == lane_total, 1.0, 0.0).astype(BF16)
    lengths = far[3].get()[...].astype(F32)
    len_col = jnp.sum(jnp.where(req_col == lane_total, lengths, 0.0), axis=1, keepdims=True)
    count = jnp.clip(len_col - to_col(far[1].get()[...]) * page, 0.0, float(page))
    count = jnp.where(to_col(far[2].get()[...]) == 1.0, count, 0.0)
    count_ref[...] = jnp.broadcast_to(count, (slots, HD))


def slot_tables(slot_request, slot_page, slot_used, lengths, kv_cache, after):
    slots = kv_cache.shape[0]
    total = lengths.shape[0]
    return run(
        functools.partial(tables_body, page=kv_cache.shape[2]),
        "slot_tables",
        [
            sds((slots, total), BF16),
            sds((slots, HD), F32),
            sds((slots, slots), F32),
            sds((slots, HD), F32),
            sds((total, slots), BF16),
            sds((total, slots), BF16),
        ],
        [],
        [slot_request.reshape(1, slots), slot_page.reshape(1, slots), slot_used.reshape(1, slots), lengths.reshape(1, total)],
        after=[after],
        moves=[kv_cache],
    )


def attn_kernel(pick_ref, count_ref, same_ref, mine_ref, spread_ref, spread16_ref, kv_ref, qa_ref, qb_ref, keep_ref, send_ref, n_scr, m_scr, l_scr):
    slots = kv_ref.shape[0]
    page = kv_ref.shape[2]
    half = qa_ref.shape[0]
    chosen = dot(pick_ref[:, :half], qa_ref[...]) + dot(pick_ref[:, half:], qb_ref[...])
    low_lanes = iota((8, 2 * HD), 1) < HD
    rel = iota((16, 8 * page), 1) - (iota((16, 8 * page), 0) % 8) * page
    rel = rel.astype(F32)
    for b in range(slots // 8):
        q8 = chosen[b * 8 : b * 8 + 8]
        q16 = jnp.concatenate([jnp.where(low_lanes, q8, 0.0), jnp.where(low_lanes, 0.0, q8)], axis=0).astype(BF16)
        keys = kv_ref[b * 8 : b * 8 + 8, 0].reshape(8 * page, 2 * HD)
        vals = kv_ref[b * 8 : b * 8 + 8, 1].reshape(8 * page, 2 * HD)
        s = lax.dot_general(q16, keys, (((1,), (1,)), ((), ())), preferred_element_type=F32) * SCALE
        c8 = count_ref[b * 8 : b * 8 + 8, :1]
        ok = (rel >= 0.0) & (rel < jnp.concatenate([c8, c8], axis=0))
        s = jnp.where(ok, s, FLOOR)
        m = jnp.max(s, axis=1, keepdims=True)
        w = jnp.where(ok, jnp.exp(s - m), 0.0).astype(BF16)
        l = jnp.sum(w.astype(F32), axis=1, keepdims=True)
        n = dot(w, vals)
        for h in range(2):
            n_scr[h, b * 8 : b * 8 + 8, :] = n[8 * h : 8 * h + 8, HD * h : HD * h + HD]
            m_scr[h, b * 8 : b * 8 + 8, :] = jnp.broadcast_to(m[8 * h : 8 * h + 8], (8, slots))
            l_scr[h, b * 8 : b * 8 + 8, :] = jnp.broadcast_to(l[8 * h : 8 * h + 8], (8, slots))

    eye = iota((slots, slots), 0) == iota((slots, slots), 1)
    same = same_ref[...] > 0.0

    def to_row(wide):
        return jnp.sum(jnp.where(eye, wide, 0.0), axis=0, keepdims=True)

    group = iota((slots, HD), 1) // 16
    board = jnp.zeros((slots, HD), F32)
    for h in range(2):
        m_wide = m_scr[h]
        m_ref = jnp.max(jnp.where(same, to_row(m_wide), FLOOR), axis=1, keepdims=True)
        m_ref = m_ref.astype(BF16).astype(F32)
        lift = jnp.exp(m_wide - m_ref)
        n_hi, n_lo = hi_lo(n_scr[h] * lift)
        l_sum = jnp.sum(jnp.where(same, to_row(l_scr[h] * lift), 0.0), axis=1, keepdims=True)
        out = (dot(spread_ref[...], n_hi) + dot(spread_ref[...], n_lo)).astype(BF16)
        keep_ref[:, 16 * h : 16 * h + 16, :] = out[:half].reshape(half // 16, 16, HD)
        send_ref[:, 16 * h : 16 * h + 16, :] = out[half:].reshape(half // 16, 16, HD)
        l_hi = l_sum.astype(BF16).astype(F32)
        for i, stat in enumerate((m_ref, l_hi, l_sum - l_hi)):
            board = jnp.where(group == 2 * i + h, stat, board)
    board = jnp.where(mine_ref[...] > 0.0, board, 0.0).astype(BF16)
    out = dot(spread16_ref[...], board).astype(BF16)
    keep_ref[:, 32:48, :] = out[:half].reshape(half // 16, 16, HD)
    send_ref[:, 32:48, :] = out[half:].reshape(half // 16, 16, HD)


def attend_pages(tables, qa, qb):
    slots, total = tables[0].shape
    return pl.pallas_call(
        attn_kernel,
        name="attend_pages",
        out_shape=[jax.ShapeDtypeStruct((total // 32, 48, HD), BF16)] * 2,
        in_specs=[VM] * 9,
        out_specs=[VM] * 2,
        scratch_shapes=[
            pltpu.VMEM((2, slots, HD), F32),
            pltpu.VMEM((2, slots, slots), F32),
            pltpu.VMEM((2, slots, slots), F32),
        ],
        compiler_params=VLIM,
    )(*tables, qa.reshape(total // 2, 2 * HD), qb.reshape(total // 2, 2 * HD))


def merge_body(near, far, outs, own):
    (a_ref, b_ref), out_ref = near, outs[0]
    a, b = a_ref[:, 32:48, :].astype(F32), b_ref[:, 32:48, :].astype(F32)
    lane, row = iota(a.shape, 2), iota(a.shape, 1)
    board = jnp.zeros(a.shape, F32)
    for h in range(2):
        (ma, la), (mb, lb) = read_stats(a, h), read_stats(b, h)
        m = jnp.maximum(ma, mb)
        fa, fb = jnp.exp(ma - m), jnp.exp(mb - m)
        rows = slice(16 * h, 16 * h + 16)
        out_ref[:, rows, :] = (a_ref[:, rows, :].astype(F32) * fa + b_ref[:, rows, :].astype(F32) * fb).astype(BF16)
        l = la * fa + lb * fb
        l_hi = l.astype(BF16).astype(F32)
        for i, stat in enumerate((m, l_hi, l - l_hi)):
            board = jnp.where(lane == row + 32 * i + 16 * h, stat, board)
    out_ref[:, 32:48, :] = board.astype(BF16)


def merge(a, b, after):
    return run(merge_body, "merge", [sds(a.shape, BF16)], [a, b], [], after=[after])[0]


def fetch(after, *arrays):
    return run(lambda *_: None, "fetch", [], [], [], after=[after], moves=arrays)


def column_kernel(w_ref, after_ref, out_ref, sem):
    width = out_ref.shape[1]
    cols = pl.ds(pl.multiple_of(head_id() * width, width), width)
    copy = pltpu.make_async_copy(w_ref.at[:, cols], out_ref, sem)
    copy.start()
    copy.wait()


def fetch_columns(after, w):
    return pl.pallas_call(
        column_kernel,
        name="fetch_columns",
        out_shape=sds((w.shape[0], w.shape[1] // 4), w.dtype),
        in_specs=[pl.BlockSpec(memory_space=pltpu.HBM), pl.BlockSpec(memory_space=pl.ANY)],
        out_specs=VM,
        scratch_shapes=[pltpu.SemaphoreType.DMA],
        compiler_params=VLIM,
    )(pltpu.with_memory_space_constraint(w, pltpu.HBM), after)


def read_stats(board, h):
    lane, row = iota(board.shape, 2), iota(board.shape, 1) + 16 * h
    m = jnp.sum(jnp.where(lane == row, board, 0.0), axis=2, keepdims=True)
    l = jnp.sum(jnp.where((lane == row + 32) | (lane == row + 64), board, 0.0), axis=2, keepdims=True)
    return jnp.where(l > 0.0, m, FLOOR), l


def owner_body(near, far, outs, own_scratch):
    part_ref, w_ref = near
    board = part_ref[:, 32:48, :].astype(F32)
    q = far[0].get()[...].astype(F32)
    nkv = far[1].get()[...].astype(F32)
    nkv = jnp.concatenate([nkv[:, 0, :], nkv[:, 1, :]], axis=1)
    att = []
    for h in range(2):
        m, l = read_stats(board, h)
        own = jnp.sum(q[:, HD * h : HD * h + HD] * nkv[:, HD * h : HD * h + HD], axis=1, keepdims=True) * SCALE
        top = jnp.maximum(jnp.max(m, axis=0), own)
        lift = jnp.exp(m - top[None])
        n = jnp.sum(part_ref[:, 16 * h : 16 * h + 16, :].astype(F32) * lift, axis=0)
        den = jnp.sum(l * lift, axis=0)
        new = jnp.exp(own - top)
        v = nkv[:, 2 * HD + HD * h : 2 * HD + HD * h + HD]
        att.append((n + new * v) / (den + new))
    attended = jnp.concatenate(att, axis=1).astype(BF16)
    head = head_id()
    width = outs[0].shape[1]
    for k in range(4):
        first = pl.multiple_of(((head + k) % 4) * width, width)
        outs[k][...] = dot(attended, w_ref[:, pl.ds(first, width)]).astype(BF16)


def owner_part(parts, queries, new_kv, out_weight):
    rows = queries.shape[0]
    width = out_weight.shape[1] // 4
    return run(owner_body, "owner_part", [sds((rows, width), BF16)] * 4, [parts, out_weight], [queries, new_kv])


def flip(x, terms):
    n = x.shape[1]
    eye = jnp.where(iota((n, n), 0) == iota((n, n), 1), 1.0, 0.0).astype(BF16)
    x = x.astype(F32)
    out = jnp.zeros((n, x.shape[0]), F32)
    for _ in range(terms):
        part = x.astype(BF16)
        out = out + lax.dot_general(eye, part, (((1,), (1,)), ((), ())), preferred_element_type=F32)
        x = x - part.astype(F32)
    return out


def rank_of(hit):
    rows = hit.shape[0]
    before = jnp.where(iota((rows, rows), 0) > iota((rows, rows), 1), 1.0, 0.0).astype(BF16)
    return dot(before, hit.astype(BF16))


def dispatch_body(near, far, outs, own):
    hid_ref, disp_ref = outs
    rows, width = hid_ref.shape
    first = pl.multiple_of(head_id() * width, width)
    acc = sum(p[...].astype(F32) for p in near)
    routes = flip(far[1].get()[...], 1)
    cells = disp_ref.shape[0] * 8
    lane = iota((rows, cells), 1)
    expert = (lane // 8).astype(F32)
    hit = jnp.zeros((rows, cells), F32)
    for k in range(routes.shape[1]):
        hit = hit + jnp.where(routes[:, k : k + 1] == expert, 1.0, 0.0)
    hit = jnp.where(rank_of(hit) == (lane % 4).astype(F32), hit, 0.0)
    left = lane % 8 < 4
    pick = jnp.concatenate([jnp.where(left, hit, 0.0), jnp.where(left, 0.0, hit)], axis=0).astype(BF16)
    hid = (far[0].get()[:, pl.ds(first, width)].astype(F32) + acc).astype(BF16)
    hid_ref[...] = hid
    both = jnp.concatenate([hid[:, : width // 2], hid[:, width // 2 :]], axis=0)
    out = lax.dot_general(pick, both, (((0,), (0,)), ((), ())), preferred_element_type=F32)
    disp_ref[...] = out.astype(BF16).reshape(disp_ref.shape)


def dispatch(parts, residual, routes, experts):
    rows, width = parts[0].shape
    outs = [sds((rows, width), BF16), sds((experts, 8, width // 2), BF16)]
    return run(dispatch_body, "dispatch", outs, parts, [residual, routes.T])


def unfold(x):
    n, _, w = x.shape
    x = x.reshape(n // 2, 2, 8, w)
    a, b = x[:, 0], x[:, 1]
    top = iota(a.shape, 1) < 4
    left = jnp.where(top, a, pltpu.roll(b, 4, 1))
    right = jnp.where(top, pltpu.roll(a, 4, 1), b)
    return left.reshape(n * 4, w), right.reshape(n * 4, w)


def fold(left, right):
    rows, w = left.shape
    left, right = left.reshape(rows // 8, 8, w), right.reshape(rows // 8, 8, w)
    top = iota(left.shape, 1) < 4
    a = jnp.where(top, left, pltpu.roll(right, 4, 1))
    b = jnp.where(top, pltpu.roll(left, 4, 1), right)
    return a, b


def gate_body(near, far, outs, own):
    inner_ref, xs = outs[0], own[0]
    wg_ref, wu_ref = near[4:]
    head = head_id()
    w = near[0].shape[2]
    total = jnp.zeros((inner_ref.shape[0], 1), F32)
    for k in range(4):
        for f, part in enumerate(unfold(near[k][...].astype(F32))):
            xs[2 * k + f] = part
            total = total + jnp.sum(part * part, axis=1, keepdims=True)
    scale = lax.rsqrt(total / (8 * w) + EPS)
    gain_ref = far[0].get()
    gate = jnp.zeros(inner_ref.shape, F32)
    up = jnp.zeros(inner_ref.shape, F32)
    for k in range(4):
        for f in range(2):
            first = pl.multiple_of(((head + 4 - k) % 4) * 2 * w + f * w, w)
            normed = (xs[2 * k + f] * scale * gain_ref[:, pl.ds(first, w)]).astype(BF16)
            gate = gate + dot(normed, wg_ref[pl.ds(first, w), :])
            up = up + dot(normed, wu_ref[pl.ds(first, w), :])
    inner_ref[...] = (gate / (1.0 + jnp.exp(-gate)) * up).astype(BF16)


def gate_up(xs, gain, w_gate, w_up):
    n, _, w = xs[0].shape
    out = sds((n * 4, w_gate.shape[1]), BF16)
    scratch = [pltpu.VMEM((8, n * 4, w), F32)]
    return run(gate_body, "gate_up", [out], [*xs, w_gate, w_up], [gain.reshape(1, -1)], scratch)[0]


def down_body(near, far, outs, own):
    w_ref, out_ref = near[4], outs[0]
    head = head_id()
    rows, eff = near[0].shape
    width = w_ref.shape[1]
    acc = jnp.zeros((rows, width), F32)
    for k in range(4):
        first = pl.multiple_of(((head + 4 - k) % 4) * eff, eff)
        acc = acc + dot(near[k][...], w_ref[pl.ds(first, eff), :])
    a, b = fold(acc[:, : width // 2], acc[:, width // 2 :])
    out_ref[:, 0] = a.astype(BF16)
    out_ref[:, 1] = b.astype(BF16)


def down(inners, w_cols):
    rows = inners[0].shape[0]
    width = w_cols.shape[1]
    out = run(down_body, "down", [sds((rows // 8, 2, 8, width // 2), BF16)], [*inners, w_cols], [])[0]
    return out.reshape(rows // 4, 8, width // 2)


def blend_body(near, far, outs, own):
    y_ref, out_ref = near[0], outs[0]
    rows = out_ref.shape[0]
    routes, share = flip(far[1].get()[...], 1), flip(far[2].get()[...], 3)
    cells = y_ref.shape[0] * 4
    lane = iota((rows, cells), 1)
    expert = (lane // 4).astype(F32)
    hit = jnp.zeros((rows, cells), F32)
    mix = jnp.zeros((rows, cells), F32)
    for k in range(routes.shape[1]):
        on = routes[:, k : k + 1] == expert
        hit = hit + jnp.where(on, 1.0, 0.0)
        mix = mix + jnp.where(on, share[:, k : k + 1], 0.0)
    mix = jnp.where(rank_of(hit) == (lane % 4).astype(F32), mix, 0.0)
    m_hi, m_lo = hi_lo(mix)
    w = y_ref.shape[2]
    hid_ref = far[0].get()
    for f, part in enumerate(unfold(y_ref[...].astype(F32))):
        part = part.astype(BF16)
        hid = hid_ref[:, f * w : f * w + w].astype(F32)
        out_ref[:, f * w : f * w + w] = (hid + (dot(m_hi, part) + dot(m_lo, part))).astype(BF16)


def blend(returned, hidden, routes, route_weights):
    out = sds(hidden.shape, BF16)
    return run(blend_body, "blend", [out], [returned], [hidden, routes.T, route_weights.T])[0]


def norm_body(near, far, outs, own):
    head = head_id()
    w = near[0].shape[1]
    parts = [s[...].astype(F32) for s in (far[1].get(), *near)]
    total = sum(jnp.sum(p * p, axis=1, keepdims=True) for p in parts)
    scale = lax.rsqrt(total / (4 * w) + EPS)
    gain_ref = far[0].get()
    for k, p in enumerate(parts):
        cols = pl.ds(pl.multiple_of(((head + 4 - k) % 4) * w, w), w)
        outs[0][:, cols] = (p * scale * gain_ref[:, cols]).astype(BF16)


def norm_parts(parts, gain):
    rows, w = parts[0].shape
    return run(norm_body, "norm_parts", [sds((rows, 4 * w), BF16)], parts[1:], [gain.reshape(1, -1), parts[0]])[0]


def from_heads(x):
    n = lax.axis_size("head")
    return [x] + [lax.ppermute(x, "head", [(i, (i + k) % n) for i in range(n)]) for k in range(1, n)]


def to_heads(xs):
    n = lax.axis_size("head")
    return [xs[0]] + [lax.ppermute(xs[k], "head", [(i, (i + k) % n) for i in range(n)]) for k in range(1, n)]


def swap_core(x):
    return lax.ppermute(x, "c", [(0, 1), (1, 0)])


def local(
    residual, queries, new_kv, kv_cache, lengths, slot_request, slot_page, slot_used, out_weight,
    norm_gain, routes, route_weights, w_gate, w_up, w_down, next_gain, next_weight,
):
    rows = queries.shape[0]
    experts = lax.axis_size(REQ)
    chips = experts // 2
    w_down_all = lax.all_gather(w_down.reshape(w_down.shape[1:]), "head", axis=0, tiled=True)
    spread = jnp.broadcast_to(queries[None], (chips,) + queries.shape)
    qa = lax.all_to_all(spread, ("z", "y"), 0, 0, tiled=True)
    tables = slot_tables(slot_request, slot_page, slot_used, lengths, kv_cache, qa)
    keep, send = attend_pages(tables, qa, swap_core(qa))
    out_weight = fetch(send, out_weight)[0]
    arrived = lax.all_to_all(merge(keep, swap_core(send), out_weight), ("z", "y"), 0, 0, tiled=True)
    shares = to_heads(owner_part(arrived, queries, new_kv, out_weight))
    hidden, disp = dispatch(shares, residual, routes, experts)
    tokens = lax.all_to_all(disp, REQ, 0, 0, tiled=True)
    w_gate, w_up = fetch(tokens, w_gate[0], w_up[0])
    inner = gate_up(from_heads(tokens), norm_gain, w_gate, w_up)
    w_cols = fetch_columns(inner, w_down_all)
    expert_out = down(from_heads(inner), w_cols)
    returned = lax.all_to_all(expert_out, REQ, 0, 0, tiled=True)
    stream = blend(returned, hidden, routes, route_weights)
    normed = norm_parts(from_heads(stream), next_gain)
    next_qkv = jnp.einsum("td,dcf->tcf", normed, next_weight, preferred_element_type=F32).astype(BF16)
    return stream, next_qkv


def solution(mesh):
    split = Mesh(mesh.devices.reshape(8, 4, 2, 4), ("z", "y", "c", "head"))
    placed = (
        P(REQ, None),
        P(REQ, "head"),
        P(REQ, None, "head"),
        P(REQ, None, None, "head"),
        P(),
        P(REQ),
        P(REQ),
        P(REQ),
        P("head", None),
        P(),
        P(REQ, None),
        P(REQ, None),
        P(REQ, None, "head"),
        P(REQ, None, "head"),
        P(REQ, "head", None),
        P(),
        P(None, None, "head"),
    )
    return jax.shard_map(
        local,
        mesh=split,
        in_specs=placed,
        out_specs=(P(REQ, "head"), P(REQ, None, "head")),
        check_vma=False,
    )
```

time: 179 us -> 157 us (0.88)
  waiting for transfers between devices: 59.5 us -> 21.4 us
  blocking collectives: 43.5 us -> 80.3 us
  local copies, waits for them, and re-layouts: 17.1 us -> 0.93 us
  starting transfers between devices: 28.8 us -> 17.8 us
  Pallas kernels: 13.7 us -> 20.7 us
    all_to_all x1 -> x3, blocking collectives: 23 us -> 59.5 us  [the longest x1 23 us: local(): qa = lax.all_to_all(spread, ('z', 'y'), 0, 0, tiled=True)]
    all_to_all x2 -> x0, waiting for transfers between devices: 35.3 us -> none  [the longest x1 22.9 us: local(): arrived = lax.all_to_all(both, REQ, 0, 0, tiled=True)]
    unnamed x45 -> x4, local copies, waits for them, and re-layouts: 15.2 us -> 0.02 us
    all_to_all x2 -> x0, starting transfers between devices: 10.7 us -> none  [the longest x1 5.52 us: local(): returned = lax.all_to_all(expert_out, REQ, 0, 0, tiled=True)]
    pallas_call x7 -> x12, Pallas kernels: 13.7 us -> 20.7 us  [the longest x10 14.5 us: run(): pl.pallas_call(kernel, name=name, out_shape=list(outs) + [sds(x.shape, x....]
  transfers between devices with their start and end apart: 16 -> 15, of which waited for: 12 -> 9; matrix products, arithmetic and copies ran while one was open for 2% -> 1% of each run, Pallas kernels for 6% -> 11%
where the time goes in v2:
time: 157 us
  blocking collectives  80.3 us (51%)
  waiting for transfers between devices  21.4 us (14%)
  Pallas kernels  20.7 us (13%)
  starting transfers between devices  17.8 us (11%)
  between operations  14.2 us (9%)
    all_to_all x1, blocking collectives, local(): qa = lax.all_to_all(spread, ('z', 'y'), 0, 0, tiled=True)  23 us
    all_to_all x1, blocking collectives, local(): tokens = lax.all_to_all(disp, REQ, 0, 0, tiled=True)  20.8 us
    ppermute x9, waiting for transfers between devices, from_heads(): lax.ppermute(x, 'head', [(i, (i + k) % n) for i in range(n)])  18.7 us
    all_to_all x1, blocking collectives, local(): returned = lax.all_to_all(expert_out, REQ, 0, 0, tiled=True)  18.4 us
    all_to_all x1, blocking collectives, local(): lax.all_to_all(merge(keep, swap_core(send), out_weight), ('z', 'y'), 0, 0...  18.1 us
    pallas_call x10, Pallas kernels, run(): pl.pallas_call(kernel, name=name, out_shape=list(outs) + [sds(x.shape, x....  14.5 us
    ppermute x9, starting transfers between devices, from_heads(): lax.ppermute(x, 'head', [(i, (i + k) % n) for i in range(n)])  10.3 us
    pallas_call x1, Pallas kernels, attend_pages(): pl.pallas_call(attn_kernel, name='attend_pages', out_shape=[jax.ShapeDtyp...  4.96 us
  transfers between devices with their start and end apart: 15, of which 9 were waited for; matrix products, arithmetic and copies ran while one was open for 1% of the time, Pallas kernels for 11%

profile of v2, /device:TPU:1, one launch (start us, length us, event | category | flops | bytes accessed | tf_op | source)
XLA Modules:
  0.0 156.6 jit_solution(12807166403498739371)
XLA Ops:
  7.2 0.0 copy-start
  7.2 0.0 all-gather.3.cloned.1.call-start
  7.2 0.7 all-gather.3.cloned.1.call-update
  7.9 0.9 broadcast_in_dim.2
  8.8 23.0 %all_to_all.20.refs_4_ = bf16[32,16,256]{2,1,0:T(8,128)(2,1)S(1)} all-to-all(bf16[32,16,256]{2,1,0:T(8,128)(2,1)S(1)} %broadcast_in_dim.2), channel_id=1, replica_groups=mesh['z'=8,'y'=4,'c'=2,'head'=4] {'z','y'}, dimensions={0} | all-to-all | bytes 524288 | tf_op jit(solution)/shard_map/all_to_all | solution.py:490
  31.9 2.5 %collective-permute-start = (bf16[32,16,256]{2,1,0:T(8,128)(2,1)S(1)}, bf16[32,16,256]{2,1,0:T(8,128)(2,1)S(1)}, u32[]{:S(2)}, u32[]{:S(2)}) collective-permute-start(bf16[32,16,256]{2,1,0:T(8,128)(2,1)S(1)} %all_to_all.20.refs_4_), channel_id=1, source_target_pairs={{0,4},{4,0},{1,5},{5,1},{2,6},{6,2},{3,7},{7,3},{8,12},{12,8},{9,1... | collective-permute-start | bytes 786440 | tf_op jit(solution)/shard_map/ppermute | solution.py:478
  34.3 2.3 %slot_tables.1 = (bf16[128,1024]{1,0:T(8,128)(2,1)S(1)}, f32[128,128]{1,0:T(8,128)S(1)}, f32[128,128]{1,0:T(8,128)S(1)}, f32[128,128]{1,0:T(8,128)S(1)}, bf16[10...) custom-call(s32[1,128]{1,0:T(1,128)} %bitcast.30, s32[1,128]{1,0:T(1,128)} %bitcast.31, ...), custom_call_target="tpu_custom_call" | custom-call | tf_op jit(solution)/shard_map/slot_tables/pallas_call | solution.py:63
  36.7 5.0 %attend_pages.1 = (bf16[32,48,128]{2,1,0:T(8,128)(2,1)S(1)}, bf16[32,48,128]{2,1,0:T(8,128)(2,1)S(1)}) custom-call(bf16[128,1024]{1,0:T(8,128)(2,1)S(1)} %get-tuple-element.19.pick_ref, f32[128,128]{1,0:T(8,128)S(1)} %get-tuple-element.20.count_ref, f32[128,128]{1,0:T(8,128)S(1)} %get-tuple-element.21.same_ref, f32[128,128]{1,0:T(8,128)S(1)} %get-tuple-element.22.mine_ref, ...), custom_call_target="tpu_custom_call" | custom-call | tf_op jit(solution)/shard_map/attend_pages/pallas_call | solution.py:207
  41.6 0.1 collective-permute-start.1
  41.8 1.2 fetch.2.refs_2_.refs_1_
  43.0 0.4 collective-permute-done.1.refs_1_
  43.4 0.9 merge.1
  44.4 18.1 %all_to_all.21.refs_0_ = bf16[32,48,128]{2,1,0:T(8,128)(2,1)S(1)} all-to-all(bf16[32,48,128]{2,1,0:T(8,128)(2,1)S(1)} %merge.1), channel_id=1, replica_groups=mesh['z'=8,'y'=4,'c'=2,'head'=4] {'z','y'}, dimensions={0} | all-to-all | bytes 786432 | tf_op jit(solution)/shard_map/all_to_all | solution.py:494
  62.5 1.5 owner_part.1
  64.0 1.3 collective-permute-start.2
  65.3 2.4 %collective-permute-start.3 = (bf16[16,512]{1,0:T(8,128)(2,1)S(1)}, bf16[16,512]{1,0:T(8,128)(2,1)S(1)}, u32[]{:S(2)}, u32[]{:S(2)}) collective-permute-start(bf16[16,512]{1,0:T(8,128)(2,1)S(1)} %get-tuple-element.30), channel_id=1, source_target_pairs={{0,2},{1,3},{2,0},{3,1},{4,6},{5,7},{6,4},{7,5},{8,10},{9,11},{10,... | collective-permute-start | bytes 49160 | tf_op jit(solution)/shard_map/ppermute | solution.py:474
  67.7 1.2 collective-permute-start.4
  68.9 0.0 collective-permute-done.2.refs_1_
  68.9 0.5 collective-permute-done.3.refs_2_
  69.4 1.1 collective-permute-done.4.refs_3_
  70.5 1.4 dispatch.1
  71.8 0.0 copy-start.1
  71.8 20.8 %all_to_all.22.refs_0_ = bf16[64,8,256]{2,1,0:T(8,128)(2,1)S(1)} all-to-all(bf16[64,8,256]{2,1,0:T(8,128)(2,1)S(1)} %get-tuple-element.32), channel_id=1, replica_groups=mesh['z'=8,'y'=4,'c'=2,'head'=4] {'z','y','c'}, dimensions={0} | all-to-all | bytes 524288 | tf_op jit(solution)/shard_map/all_to_all | solution.py:497
  92.7 0.0 collective-permute-start.5
  92.7 3.5 %collective-permute-start.6 = (bf16[64,8,256]{2,1,0:T(8,128)(2,1)S(1)}, bf16[64,8,256]{2,1,0:T(8,128)(2,1)S(1)}, u32[]{:S(2)}, u32[]{:S(2)}) collective-permute-start(bf16[64,8,256]{2,1,0:T(8,128)(2,1)S(1)} %all_to_all.22.refs_0_), channel_id=1, source_target_pairs={{0,2},{1,3},{2,0},{3,1},{4,6},{5,7},{6,4},{7,5},{8,10},{9,11},{10,... | collective-permute-start | bytes 786440 | tf_op jit(solution)/shard_map/ppermute | solution.py:469
  96.2 0.0 collective-permute-start.7
  96.2 1.6 %fetch.3 = (bf16[2048,256]{1,0:T(8,128)(2,1)S(1)}, bf16[2048,256]{1,0:T(8,128)(2,1)S(1)}) custom-call(bf16[64,8,256]{2,1,0:T(8,128)(2,1)S(1)} %all_to_all.22.refs_0_, bf16[2048,256]{1,0:T(8,128)(2,1)} %bitcast.22, bf16[2048,256]{1,0:T(8,128)(2,1)} %bitcast.23), custom_call_target="tpu_custom_call" | custom-call | tf_op jit(solution)/shard_map/fetch/pallas_call | solution.py:63
  97.8 3.7 %collective-permute-done.5.refs_1_ = bf16[64,8,256]{2,1,0:T(8,128)(2,1)S(1)} collective-permute-done((bf16[64,8,256]{2,1,0:T(8,128)(2,1)S(1)}, bf16[64,8,256]{2,1,0:T(8,128)(2,1)S(1)}, u32[]{:S(2)}, u32[]{:S(2)}) %collective-permute-start.5) | collective-permute-done | bytes 262176 | tf_op jit(solution)/shard_map/ppermute | solution.py:469
  101.5 6.5 %collective-permute-done.6.refs_2_ = bf16[64,8,256]{2,1,0:T(8,128)(2,1)S(1)} collective-permute-done((bf16[64,8,256]{2,1,0:T(8,128)(2,1)S(1)}, bf16[64,8,256]{2,1,0:T(8,128)(2,1)S(1)}, u32[]{:S(2)}, u32[]{:S(2)}) %collective-permute-start.6) | collective-permute-done | bytes 262176 | tf_op jit(solution)/shard_map/ppermute | solution.py:469
  108.0 0.0 collective-permute-done.7.refs_3_
  108.0 1.5 gate_up.1.after_ref.refs_0_
  109.5 2.7 %collective-permute-start.10 = (bf16[256,256]{1,0:T(8,128)(2,1)S(1)}, bf16[256,256]{1,0:T(8,128)(2,1)S(1)}, u32[]{:S(2)}, u32[]{:S(2)}) collective-permute-start(bf16[256,256]{1,0:T(8,128)(2,1)S(1)} %gate_up.1.after_ref.refs_0_), channel_id=1, source_target_pairs={{0,3},{1,0},{2,1},{3,2},{4,7},{5,4},{6,5},{7,6},{8,11},{9,8},{10,9... | collective-permute-start | bytes 393224 | tf_op jit(solution)/shard_map/ppermute | solution.py:469
  112.2 0.0 collective-permute-start.8
  112.2 1.3 collective-permute-start.9
  113.5 1.2 fetch_columns.1.refs_4_
  114.7 0.0 collective-permute-done.10.refs_3_
  114.8 6.1 %collective-permute-done.8.refs_1_ = bf16[256,256]{1,0:T(8,128)(2,1)S(1)} collective-permute-done((bf16[256,256]{1,0:T(8,128)(2,1)S(1)}, bf16[256,256]{1,0:T(8,128)(2,1)S(1)}, u32[]{:S(2)}, u32[]{:S(2)}) %collective-permute-start.8) | collective-permute-done | bytes 131104 | tf_op jit(solution)/shard_map/ppermute | solution.py:469
  120.9 1.4 down.1
  122.3 18.4 %all_to_all.23.refs_0_ = bf16[64,8,256]{2,1,0:T(8,128)(2,1)S(1)} all-to-all(bf16[64,8,256]{2,1,0:T(8,128)(2,1)S(1)} %bitcast.19), channel_id=1, replica_groups=mesh['z'=8,'y'=4,'c'=2,'head'=4] {'z','y','c'}, dimensions={0} | all-to-all | bytes 524288 | tf_op jit(solution)/shard_map/all_to_all | solution.py:502
  140.7 1.9 %blend.1.refs_4_ = bf16[16,512]{1,0:T(8,128)(2,1)} custom-call(bf16[64,8,256]{2,1,0:T(8,128)(2,1)S(1)} %all_to_all.23.refs_0_, bf16[16,512]{1,0:T(8,128)(2,1)} %copy-done.1, s32[8,16]{1,0:T(8,128)} %bitcast.25, f32[8,16]{1,0:T(8,128)} %bitcast.29), custom_call_target="tpu_custom_call" | custom-call | tf_op jit(solution)/shard_map/blend/pallas_call | solution.py:63
  142.6 0.1 collective-permute-start.11
  142.7 1.5 collective-permute-start.12
  144.2 1.1 collective-permute-start.13
  145.3 1.3 collective-permute-done.11.refs_0_
  146.7 0.4 collective-permute-done.12.refs_1_
  147.1 0.7 collective-permute-done.13.refs_2_
  147.7 0.9 norm_parts.1
  148.6 1.1 convolution_convert_fusion
  (5 shorter events, 0.0 us)
Async XLA Ops:
  7.2 141.4 %copy-start = (bf16[2048,3,256]{2,0,1:T(8,128)(2,1)S(1)}, bf16[2048,3,256]{2,0,1:T(8,128)(2,1)}, u32[]{:S(2)}) copy-start(bf16[2048,3,256]{2,0,1:T(8,128)(2,1)} %param.33) | copy-start | bytes 9437188
  7.2 106.3 %all-gather.3.cloned.1.call-start = ((), (), s32[]{:S(2)}) async-start(), calls=%async_computation.4 | async-start | bytes 5242880 | tf_op jit(solution)/shard_map/all_gather | solution.py:488
  31.9 4.8 %collective-permute-start = (bf16[32,16,256]{2,1,0:T(8,128)(2,1)S(1)}, bf16[32,16,256]{2,1,0:T(8,128)(2,1)S(1)}, u32[]{:S(2)}, u32[]{:S(2)}) collective-permute-start(bf16[32,16,256]{2,1,0:T(8,128)(2,1)S(1)} %all_to_all.20.refs_4_), channel_id=1, source_target_pairs={{0,4},{4,0},{1,5},{5,1},{2,6},{6,2},{3,7},{7,3},{8,12},{12,8},{9,1... | collective-permute-start | bytes 786440 | tf_op jit(solution)/shard_map/ppermute | solution.py:478
  41.6 1.8 %collective-permute-start.1 = (bf16[32,48,128]{2,1,0:T(8,128)(2,1)S(1)}, bf16[32,48,128]{2,1,0:T(8,128)(2,1)S(1)}, u32[]{:S(2)}, u32[]{:S(2)}) collective-permute-start(bf16[32,48,128]{2,1,0:T(8,128)(2,1)S(1)} %get-tuple-element.27.refs_0_), channel_id=1, source_target_pairs={{0,4},{4,0},{1,5},{5,1},{2,6},{6,2},{3,7},{7,3},{8,12},{12,8},{9,1... | collective-permute-start | bytes 1179656 | tf_op jit(solution)/shard_map/ppermute | solution.py:478
  64.0 4.9 %collective-permute-start.2 = (bf16[16,512]{1,0:T(8,128)(2,1)S(1)}, bf16[16,512]{1,0:T(8,128)(2,1)S(1)}, u32[]{:S(2)}, u32[]{:S(2)}) collective-permute-start(bf16[16,512]{1,0:T(8,128)(2,1)S(1)} %get-tuple-element.29), channel_id=1, source_target_pairs={{0,1},{1,2},{2,3},{3,0},{4,5},{5,6},{6,7},{7,4},{8,9},{9,10},{10,1... | collective-permute-start | bytes 49160 | tf_op jit(solution)/shard_map/ppermute | solution.py:474
  65.3 4.1 %collective-permute-start.3 = (bf16[16,512]{1,0:T(8,128)(2,1)S(1)}, bf16[16,512]{1,0:T(8,128)(2,1)S(1)}, u32[]{:S(2)}, u32[]{:S(2)}) collective-permute-start(bf16[16,512]{1,0:T(8,128)(2,1)S(1)} %get-tuple-element.30), channel_id=1, source_target_pairs={{0,2},{1,3},{2,0},{3,1},{4,6},{5,7},{6,4},{7,5},{8,10},{9,11},{10,... | collective-permute-start | bytes 49160 | tf_op jit(solution)/shard_map/ppermute | solution.py:474
  67.7 2.7 %collective-permute-start.4 = (bf16[16,512]{1,0:T(8,128)(2,1)S(1)}, bf16[16,512]{1,0:T(8,128)(2,1)S(1)}, u32[]{:S(2)}, u32[]{:S(2)}) collective-permute-start(bf16[16,512]{1,0:T(8,128)(2,1)S(1)} %get-tuple-element.31), channel_id=1, source_target_pairs={{0,3},{1,0},{2,1},{3,2},{4,7},{5,4},{6,5},{7,6},{8,11},{9,8},{10,9... | collective-permute-start | bytes 49160 | tf_op jit(solution)/shard_map/ppermute | solution.py:474
  71.8 24.4 %copy-start.1 = (bf16[16,512]{1,0:T(8,128)(2,1)}, bf16[16,512]{1,0:T(8,128)(2,1)S(1)}, u32[]{:S(2)}) copy-start(bf16[16,512]{1,0:T(8,128)(2,1)S(1)} %get-tuple-element.35.refs_1_) | copy-start | bytes 49156
  92.7 8.9 %collective-permute-start.5 = (bf16[64,8,256]{2,1,0:T(8,128)(2,1)S(1)}, bf16[64,8,256]{2,1,0:T(8,128)(2,1)S(1)}, u32[]{:S(2)}, u32[]{:S(2)}) collective-permute-start(bf16[64,8,256]{2,1,0:T(8,128)(2,1)S(1)} %all_to_all.22.refs_0_), channel_id=1, source_target_pairs={{0,1},{1,2},{2,3},{3,0},{4,5},{5,6},{6,7},{7,4},{8,9},{9,10},{10,1... | collective-permute-start | bytes 786440 | tf_op jit(solution)/shard_map/ppermute | solution.py:469
  92.7 15.3 %collective-permute-start.6 = (bf16[64,8,256]{2,1,0:T(8,128)(2,1)S(1)}, bf16[64,8,256]{2,1,0:T(8,128)(2,1)S(1)}, u32[]{:S(2)}, u32[]{:S(2)}) collective-permute-start(bf16[64,8,256]{2,1,0:T(8,128)(2,1)S(1)} %all_to_all.22.refs_0_), channel_id=1, source_target_pairs={{0,2},{1,3},{2,0},{3,1},{4,6},{5,7},{6,4},{7,5},{8,10},{9,11},{10,... | collective-permute-start | bytes 786440 | tf_op jit(solution)/shard_map/ppermute | solution.py:469
  96.2 11.8 %collective-permute-start.7 = (bf16[64,8,256]{2,1,0:T(8,128)(2,1)S(1)}, bf16[64,8,256]{2,1,0:T(8,128)(2,1)S(1)}, u32[]{:S(2)}, u32[]{:S(2)}) collective-permute-start(bf16[64,8,256]{2,1,0:T(8,128)(2,1)S(1)} %all_to_all.22.refs_0_), channel_id=1, source_target_pairs={{0,3},{1,0},{2,1},{3,2},{4,7},{5,4},{6,5},{7,6},{8,11},{9,8},{10,9... | collective-permute-start | bytes 786440 | tf_op jit(solution)/shard_map/ppermute | solution.py:469
  109.5 5.3 %collective-permute-start.10 = (bf16[256,256]{1,0:T(8,128)(2,1)S(1)}, bf16[256,256]{1,0:T(8,128)(2,1)S(1)}, u32[]{:S(2)}, u32[]{:S(2)}) collective-permute-start(bf16[256,256]{1,0:T(8,128)(2,1)S(1)} %gate_up.1.after_ref.refs_0_), channel_id=1, source_target_pairs={{0,3},{1,0},{2,1},{3,2},{4,7},{5,4},{6,5},{7,6},{8,11},{9,8},{10,9... | collective-permute-start | bytes 393224 | tf_op jit(solution)/shard_map/ppermute | solution.py:469
  112.2 8.7 %collective-permute-start.8 = (bf16[256,256]{1,0:T(8,128)(2,1)S(1)}, bf16[256,256]{1,0:T(8,128)(2,1)S(1)}, u32[]{:S(2)}, u32[]{:S(2)}) collective-permute-start(bf16[256,256]{1,0:T(8,128)(2,1)S(1)} %gate_up.1.after_ref.refs_0_), channel_id=1, source_target_pairs={{0,1},{1,2},{2,3},{3,0},{4,5},{5,6},{6,7},{7,4},{8,9},{9,10},{10,1... | collective-permute-start | bytes 393224 | tf_op jit(solution)/shard_map/ppermute | solution.py:469
  112.2 8.7 %collective-permute-start.9 = (bf16[256,256]{1,0:T(8,128)(2,1)S(1)}, bf16[256,256]{1,0:T(8,128)(2,1)}, u32[]{:S(2)}, u32[]{:S(2)}) collective-permute-start(bf16[256,256]{1,0:T(8,128)(2,1)S(1)} %gate_up.1.after_ref.refs_0_), channel_id=1, source_target_pairs={{0,2},{1,3},{2,0},{3,1},{4,6},{5,7},{6,4},{7,5},{8,10},{9,11},{10,... | collective-permute-start | bytes 393224 | tf_op jit(solution)/shard_map/ppermute | solution.py:469
  142.6 4.1 %collective-permute-start.11 = (bf16[16,512]{1,0:T(8,128)(2,1)}, bf16[16,512]{1,0:T(8,128)(2,1)S(1)}, u32[]{:S(2)}, u32[]{:S(2)}) collective-permute-start(bf16[16,512]{1,0:T(8,128)(2,1)} %blend.1.refs_4_), channel_id=1, source_target_pairs={{0,1},{1,2},{2,3},{3,0},{4,5},{5,6},{6,7},{7,4},{8,9},{9,10},{10,1... | collective-permute-start | bytes 49160 | tf_op jit(solution)/shard_map/ppermute | solution.py:469
  142.7 4.4 %collective-permute-start.12 = (bf16[16,512]{1,0:T(8,128)(2,1)}, bf16[16,512]{1,0:T(8,128)(2,1)S(1)}, u32[]{:S(2)}, u32[]{:S(2)}) collective-permute-start(bf16[16,512]{1,0:T(8,128)(2,1)} %blend.1.refs_4_), channel_id=1, source_target_pairs={{0,2},{1,3},{2,0},{3,1},{4,6},{5,7},{6,4},{7,5},{8,10},{9,11},{10,... | collective-permute-start | bytes 49160 | tf_op jit(solution)/shard_map/ppermute | solution.py:469
  144.2 3.5 %collective-permute-start.13 = (bf16[16,512]{1,0:T(8,128)(2,1)}, bf16[16,512]{1,0:T(8,128)(2,1)S(1)}, u32[]{:S(2)}, u32[]{:S(2)}) collective-permute-start(bf16[16,512]{1,0:T(8,128)(2,1)} %blend.1.refs_4_), channel_id=1, source_target_pairs={{0,3},{1,0},{2,1},{3,2},{4,7},{5,4},{6,5},{7,6},{8,11},{9,8},{10,9... | collective-permute-start | bytes 49160 | tf_op jit(solution)/shard_map/ppermute | solution.py:469
Sparse Core Ops, SparseCore 0:
  9.8 54.5 all-gather.2

commit v3 on v2

--- a/solution.py
+++ b/solution.py
@@ -98,6 +98,41 @@
     return hi, (x - hi.astype(F32)).astype(BF16)
 
 
+def hits(routes, expert):
+    hit = jnp.zeros(expert.shape, F32)
+    for k in range(routes.shape[1]):
+        hit = hit + jnp.where(routes[:, k : k + 1] == expert, 1.0, 0.0)
+    return hit
+
+
+def cell_map(routes, expert, lane):
+    hit = hits(routes, expert)
+    hit = jnp.where(rank_of(hit) == (lane % 4).astype(F32), hit, 0.0)
+    left = lane % 8 < 4
+    return jnp.concatenate([jnp.where(left, hit, 0.0), jnp.where(left, 0.0, hit)], axis=0).astype(BF16)
+
+
+def outset_body(near, far, outs, own):
+    chips, _, width = outs[0].shape
+    rows = far[0].buf.shape[0]
+    routes = flip(far[2].get()[...], 1)
+    lane = iota((rows, chips * 16), 1)
+    expert = (lane // 16) * 2 + (core_id() + (lane // 8) % 2) % 2
+    pick = cell_map(routes, expert.astype(F32), lane)
+    first = pl.multiple_of(head_id() * 2 * width, 2 * width)
+    res = far[1].get()
+    both = jnp.concatenate([res[:, pl.ds(first, width)], res[:, pl.ds(first + width, width)]], axis=0)
+    out = lax.dot_general(pick, both, (((0,), (0,)), ((), ())), preferred_element_type=F32)
+    outs[0][:, 16:32, :] = out.astype(BF16).reshape(chips, 16, width)
+    q = far[0].get()[...]
+    outs[0][:, 0:16, :] = jnp.broadcast_to(q[None], (chips,) + q.shape)
+
+
+def outset(queries, residual, routes, chips):
+    out = sds((chips, 32, queries.shape[1]), BF16)
+    return run(outset_body, "outset", [out], [], [queries, residual, routes.T])[0]
+
+
 def tables_body(near, far, outs, own, page):
     pick_ref, count_ref, same_ref, mine_ref, spread_ref, spread16_ref = outs
     req = far[0].get()[...]
@@ -144,16 +179,20 @@
         ],
         [],
         [slot_request.reshape(1, slots), slot_page.reshape(1, slots), slot_used.reshape(1, slots), lengths.reshape(1, total)],
-        after=[after],
+        after=after,
         moves=[kv_cache],
     )
 
 
-def attn_kernel(pick_ref, count_ref, same_ref, mine_ref, spread_ref, spread16_ref, kv_ref, qa_ref, qb_ref, keep_ref, send_ref, n_scr, m_scr, l_scr):
+def attn_kernel(pick_ref, count_ref, same_ref, mine_ref, spread_ref, spread16_ref, kv_ref, qa_ref, qb_ref, keep_ref, send_ref, res_ref, n_scr, m_scr, l_scr):
     slots = kv_ref.shape[0]
     page = kv_ref.shape[2]
-    half = qa_ref.shape[0]
-    chosen = dot(pick_ref[:, :half], qa_ref[...]) + dot(pick_ref[:, half:], qb_ref[...])
+    half = qa_ref.shape[0] * 16
+    qa, qb = (r[:, 0:16, :].reshape(half, 2 * HD) for r in (qa_ref, qb_ref))
+    chosen = dot(pick_ref[:, :half], qa) + dot(pick_ref[:, half:], qb)
+    core = core_id()
+    res_ref[:, core] = qa_ref[:, 16:24, :]
+    res_ref[:, 1 - core] = qb_ref[:, 24:32, :]
     low_lanes = iota((8, 2 * HD), 1) < HD
     rel = iota((16, 8 * page), 1) - (iota((16, 8 * page), 0) % 8) * page
     rel = rel.astype(F32)
@@ -207,16 +246,16 @@
     return pl.pallas_call(
         attn_kernel,
         name="attend_pages",
-        out_shape=[jax.ShapeDtypeStruct((total // 32, 48, HD), BF16)] * 2,
+        out_shape=[sds((total // 32, 48, HD), BF16)] * 2 + [sds((total // 32, 2, 8, 2 * HD), BF16)],
         in_specs=[VM] * 9,
-        out_specs=[VM] * 2,
+        out_specs=[VM] * 3,
         scratch_shapes=[
             pltpu.VMEM((2, slots, HD), F32),
             pltpu.VMEM((2, slots, slots), F32),
             pltpu.VMEM((2, slots, slots), F32),
         ],
         compiler_params=VLIM,
-    )(*tables, qa.reshape(total // 2, 2 * HD), qb.reshape(total // 2, 2 * HD))
+    )(*tables, qa, qb)
 
 
 def merge_body(near, far, outs, own):
@@ -237,32 +276,37 @@
     out_ref[:, 32:48, :] = board.astype(BF16)
 
 
-def merge(a, b, after):
-    return run(merge_body, "merge", [sds(a.shape, BF16)], [a, b], [], after=[after])[0]
+def merge(a, b):
+    return run(merge_body, "merge", [sds(a.shape, BF16)], [a, b], [])[0]
 
 
 def fetch(after, *arrays):
     return run(lambda *_: None, "fetch", [], [], [], after=[after], moves=arrays)
 
 
-def column_kernel(w_ref, after_ref, out_ref, sem):
-    width = out_ref.shape[1]
-    cols = pl.ds(pl.multiple_of(head_id() * width, width), width)
-    copy = pltpu.make_async_copy(w_ref.at[:, cols], out_ref, sem)
-    copy.start()
-    copy.wait()
-
-
-def fetch_columns(after, w):
+def split_kernel(w_ref, *refs):
+    outs, sems = refs[:4], refs[4]
+    width = outs[0].shape[1]
+    copies = []
+    for k in range(4):
+        cols = pl.ds(pl.multiple_of(((head_id() + k) % 4) * width, width), width)
+        copies.append(pltpu.make_async_copy(w_ref.at[:, cols], outs[k], sems.at[k]))
+    for copy in copies:
+        copy.start()
+    for copy in copies:
+        copy.wait()
+
+
+def split_columns(w):
     return pl.pallas_call(
-        column_kernel,
-        name="fetch_columns",
-        out_shape=sds((w.shape[0], w.shape[1] // 4), w.dtype),
-        in_specs=[pl.BlockSpec(memory_space=pltpu.HBM), pl.BlockSpec(memory_space=pl.ANY)],
-        out_specs=VM,
-        scratch_shapes=[pltpu.SemaphoreType.DMA],
+        split_kernel,
+        name="split_columns",
+        out_shape=[sds((w.shape[0], w.shape[1] // 4), w.dtype)] * 4,
+        in_specs=[pl.BlockSpec(memory_space=pltpu.HBM)],
+        out_specs=[VM] * 4,
+        scratch_shapes=[pltpu.SemaphoreType.DMA((4,))],
         compiler_params=VLIM,
-    )(pltpu.with_memory_space_constraint(w, pltpu.HBM), after)
+    )(pltpu.with_memory_space_constraint(w, pltpu.HBM))
 
 
 def read_stats(board, h):
@@ -273,7 +317,7 @@
 
 
 def owner_body(near, far, outs, own_scratch):
-    part_ref, w_ref = near
+    part_ref = near[0]
     board = part_ref[:, 32:48, :].astype(F32)
     q = far[0].get()[...].astype(F32)
     nkv = far[1].get()[...].astype(F32)
@@ -289,18 +333,19 @@
         new = jnp.exp(own - top)
         v = nkv[:, 2 * HD + HD * h : 2 * HD + HD * h + HD]
         att.append((n + new * v) / (den + new))
-    attended = jnp.concatenate(att, axis=1).astype(BF16)
-    head = head_id()
-    width = outs[0].shape[1]
-    for k in range(4):
-        first = pl.multiple_of(((head + k) % 4) * width, width)
-        outs[k][...] = dot(attended, w_ref[:, pl.ds(first, width)]).astype(BF16)
-
-
-def owner_part(parts, queries, new_kv, out_weight):
-    rows = queries.shape[0]
-    width = out_weight.shape[1] // 4
-    return run(owner_body, "owner_part", [sds((rows, width), BF16)] * 4, [parts, out_weight], [queries, new_kv])
+    att_ref, disp_ref = outs
+    att_ref[...] = jnp.concatenate(att, axis=1).astype(BF16)
+    rows = att_ref.shape[0]
+    lane = iota((rows, disp_ref.shape[0] * 8), 1)
+    pick = cell_map(flip(far[2].get()[...], 1), (lane // 8).astype(F32), lane)
+    both = jnp.concatenate(att, axis=0).astype(BF16)
+    out = lax.dot_general(pick, both, (((0,), (0,)), ((), ())), preferred_element_type=F32)
+    disp_ref[...] = out.astype(BF16).reshape(disp_ref.shape)
+
+
+def owner_part(parts, queries, new_kv, routes, experts):
+    outs = [sds(queries.shape, BF16), sds((experts, 8, HD), BF16)]
+    return run(owner_body, "owner_part", outs, [parts], [queries, new_kv, routes.T])
 
 
 def flip(x, terms):
@@ -321,34 +366,6 @@
     return dot(before, hit.astype(BF16))
 
 
-def dispatch_body(near, far, outs, own):
-    hid_ref, disp_ref = outs
-    rows, width = hid_ref.shape
-    first = pl.multiple_of(head_id() * width, width)
-    acc = sum(p[...].astype(F32) for p in near)
-    routes = flip(far[1].get()[...], 1)
-    cells = disp_ref.shape[0] * 8
-    lane = iota((rows, cells), 1)
-    expert = (lane // 8).astype(F32)
-    hit = jnp.zeros((rows, cells), F32)
-    for k in range(routes.shape[1]):
-        hit = hit + jnp.where(routes[:, k : k + 1] == expert, 1.0, 0.0)
-    hit = jnp.where(rank_of(hit) == (lane % 4).astype(F32), hit, 0.0)
-    left = lane % 8 < 4
-    pick = jnp.concatenate([jnp.where(left, hit, 0.0), jnp.where(left, 0.0, hit)], axis=0).astype(BF16)
-    hid = (far[0].get()[:, pl.ds(first, width)].astype(F32) + acc).astype(BF16)
-    hid_ref[...] = hid
-    both = jnp.concatenate([hid[:, : width // 2], hid[:, width // 2 :]], axis=0)
-    out = lax.dot_general(pick, both, (((0,), (0,)), ((), ())), preferred_element_type=F32)
-    disp_ref[...] = out.astype(BF16).reshape(disp_ref.shape)
-
-
-def dispatch(parts, residual, routes, experts):
-    rows, width = parts[0].shape
-    outs = [sds((rows, width), BF16), sds((experts, 8, width // 2), BF16)]
-    return run(dispatch_body, "dispatch", outs, parts, [residual, routes.T])
-
-
 def unfold(x):
     n, _, w = x.shape
     x = x.reshape(n // 2, 2, 8, w)
@@ -368,20 +385,32 @@
     return a, b
 
 
-def gate_body(near, far, outs, own):
-    inner_ref, xs = outs[0], own[0]
-    wg_ref, wu_ref = near[4:]
+def expert_body(near, far, outs, own):
+    inner_ref, hid_ref = outs
+    xs = own[0]
+    att, (wo_ref, wg_ref, wu_ref) = near[:4], near[4:]
+    gain, mine, res, own_res = far[0], far[1:5], far[5:9], far[9]
     head = head_id()
-    w = near[0].shape[2]
-    total = jnp.zeros((inner_ref.shape[0], 1), F32)
+    n = inner_ref.shape[0]
+    eff = 2 * HD
+    w = xs.shape[2]
+    att = [jnp.concatenate(unfold(a[...].astype(F32)), axis=1).astype(BF16) for a in att]
+    block = [pl.multiple_of(((head + 4 - k) % 4) * eff, eff) for k in range(4)]
+    total = jnp.zeros((n, 1), F32)
     for k in range(4):
-        for f, part in enumerate(unfold(near[k][...].astype(F32))):
+        pair = unfold(res[k].get()[...].astype(F32))
+        for f in range(2):
+            first = pl.multiple_of(((head + 4 - k) % 4) * 2 * w + f * w, w)
+            acc = dot(att[0], wo_ref[pl.ds(block[0], eff), pl.ds(first, w)])
+            for i in range(1, 4):
+                acc = acc + dot(att[i], wo_ref[pl.ds(block[i], eff), pl.ds(first, w)])
+            part = (pair[f] + acc).astype(BF16).astype(F32)
             xs[2 * k + f] = part
             total = total + jnp.sum(part * part, axis=1, keepdims=True)
     scale = lax.rsqrt(total / (8 * w) + EPS)
-    gain_ref = far[0].get()
-    gate = jnp.zeros(inner_ref.shape, F32)
-    up = jnp.zeros(inner_ref.shape, F32)
+    gain_ref = gain.get()
+    gate = jnp.zeros((n, wg_ref.shape[1]), F32)
+    up = jnp.zeros((n, wg_ref.shape[1]), F32)
     for k in range(4):
         for f in range(2):
             first = pl.multiple_of(((head + 4 - k) % 4) * 2 * w + f * w, w)
@@ -389,24 +418,25 @@
             gate = gate + dot(normed, wg_ref[pl.ds(first, w), :])
             up = up + dot(normed, wu_ref[pl.ds(first, w), :])
     inner_ref[...] = (gate / (1.0 + jnp.exp(-gate)) * up).astype(BF16)
-
-
-def gate_up(xs, gain, w_gate, w_up):
-    n, _, w = xs[0].shape
-    out = sds((n * 4, w_gate.shape[1]), BF16)
+    cols = pl.ds(pl.multiple_of(head * 2 * w, 2 * w), 2 * w)
+    acc = own_res.get()[:, cols].astype(F32)
+    acc = acc + sum(dot(mine[i].get()[...], wo_ref[pl.ds(block[i], eff), cols]) for i in range(4))
+    hid_ref[...] = acc.astype(BF16)
+
+
+def expert_rows(tokens, out_weight, w_gate, w_up, gain, mine, res, residual):
+    n, _, half = tokens[0].shape
+    w = res[0].shape[2]
+    outs = [sds((n * 4, w_gate.shape[1]), BF16), sds((residual.shape[0], 2 * w), BF16)]
     scratch = [pltpu.VMEM((8, n * 4, w), F32)]
-    return run(gate_body, "gate_up", [out], [*xs, w_gate, w_up], [gain.reshape(1, -1)], scratch)[0]
+    near = [*tokens, out_weight, w_gate, w_up]
+    return run(expert_body, "expert_rows", outs, near, [gain.reshape(1, -1), *mine, *res, residual], scratch)
 
 
 def down_body(near, far, outs, own):
-    w_ref, out_ref = near[4], outs[0]
-    head = head_id()
-    rows, eff = near[0].shape
-    width = w_ref.shape[1]
-    acc = jnp.zeros((rows, width), F32)
-    for k in range(4):
-        first = pl.multiple_of(((head + 4 - k) % 4) * eff, eff)
-        acc = acc + dot(near[k][...], w_ref[pl.ds(first, eff), :])
+    out_ref = outs[0]
+    acc = sum(dot(near[k][...], near[4 + k][...]) for k in range(4))
+    width = acc.shape[1]
     a, b = fold(acc[:, : width // 2], acc[:, width // 2 :])
     out_ref[:, 0] = a.astype(BF16)
     out_ref[:, 1] = b.astype(BF16)
@@ -414,8 +444,8 @@
 
 def down(inners, w_cols):
     rows = inners[0].shape[0]
-    width = w_cols.shape[1]
-    out = run(down_body, "down", [sds((rows // 8, 2, 8, width // 2), BF16)], [*inners, w_cols], [])[0]
+    width = w_cols[0].shape[1]
+    out = run(down_body, "down", [sds((rows // 8, 2, 8, width // 2), BF16)], [*inners, *w_cols], [])[0]
     return out.reshape(rows // 4, 8, width // 2)
 
 
@@ -426,13 +456,10 @@
     cells = y_ref.shape[0] * 4
     lane = iota((rows, cells), 1)
     expert = (lane // 4).astype(F32)
-    hit = jnp.zeros((rows, cells), F32)
     mix = jnp.zeros((rows, cells), F32)
     for k in range(routes.shape[1]):
-        on = routes[:, k : k + 1] == expert
-        hit = hit + jnp.where(on, 1.0, 0.0)
-        mix = mix + jnp.where(on, share[:, k : k + 1], 0.0)
-    mix = jnp.where(rank_of(hit) == (lane % 4).astype(F32), mix, 0.0)
+        mix = mix + jnp.where(routes[:, k : k + 1] == expert, share[:, k : k + 1], 0.0)
+    mix = jnp.where(rank_of(hits(routes, expert)) == (lane % 4).astype(F32), mix, 0.0)
     m_hi, m_lo = hi_lo(mix)
     w = y_ref.shape[2]
     hid_ref = far[0].get()
@@ -485,20 +512,20 @@
     rows = queries.shape[0]
     experts = lax.axis_size(REQ)
     chips = experts // 2
-    w_down_all = lax.all_gather(w_down.reshape(w_down.shape[1:]), "head", axis=0, tiled=True)
-    spread = jnp.broadcast_to(queries[None], (chips,) + queries.shape)
-    qa = lax.all_to_all(spread, ("z", "y"), 0, 0, tiled=True)
-    tables = slot_tables(slot_request, slot_page, slot_used, lengths, kv_cache, qa)
-    keep, send = attend_pages(tables, qa, swap_core(qa))
-    out_weight = fetch(send, out_weight)[0]
-    arrived = lax.all_to_all(merge(keep, swap_core(send), out_weight), ("z", "y"), 0, 0, tiled=True)
-    shares = to_heads(owner_part(arrived, queries, new_kv, out_weight))
-    hidden, disp = dispatch(shares, residual, routes, experts)
+    out_weight = lax.all_gather(out_weight, "head", axis=0, tiled=True)
+    qa = lax.all_to_all(outset(queries, residual, routes, chips), ("z", "y"), 0, 0, tiled=True)
+    w_cols = to_heads(split_columns(w_down[0]))
+    tables = slot_tables(slot_request, slot_page, slot_used, lengths, kv_cache, [qa])
+    keep, send, res = attend_pages(tables, qa, swap_core(qa))
+    res = from_heads(res.reshape(experts, 8, -1))
+    arrived = lax.all_to_all(merge(keep, swap_core(send)), ("z", "y"), 0, 0, tiled=True)
+    attended, disp = owner_part(arrived, queries, new_kv, routes, experts)
     tokens = lax.all_to_all(disp, REQ, 0, 0, tiled=True)
-    w_gate, w_up = fetch(tokens, w_gate[0], w_up[0])
-    inner = gate_up(from_heads(tokens), norm_gain, w_gate, w_up)
-    w_cols = fetch_columns(inner, w_down_all)
-    expert_out = down(from_heads(inner), w_cols)
+    mine = from_heads(attended)
+    tokens, res, mine, w_cols = lax.optimization_barrier((tokens, res, mine, w_cols))
+    out_weight, w_gate, w_up = fetch(tokens, out_weight, w_gate[0], w_up[0])
+    inner, hidden = expert_rows(from_heads(tokens), out_weight, w_gate, w_up, norm_gain, mine, res, residual)
+    expert_out = down(from_heads(inner), fetch(inner, *w_cols))
     returned = lax.all_to_all(expert_out, REQ, 0, 0, tiled=True)
     stream = blend(returned, hidden, routes, route_weights)
     normed = norm_parts(from_heads(stream), next_gain)

time: 157 us -> 157 us (level)
  blocking collectives: 80.3 us -> 46.4 us
  starting transfers between devices: 17.8 us -> 40.8 us
  Pallas kernels: 20.7 us -> 26.4 us
  local copies, waits for them, and re-layouts: 0.93 us -> 3.53 us
  waiting for transfers between devices: 21.4 us -> 23.5 us
    all_to_all x3 -> x1, blocking collectives: 61.9 us -> 28.1 us  [local(): lax.all_to_all(outset(queries, residual, routes, chips), ('z', 'y'), 0, 0...]
    all_to_all x0 -> x2, starting transfers between devices: none -> 16.1 us  [the longest x1 11.8 us: local(): tokens = lax.all_to_all(disp, REQ, 0, 0, tiled=True)]
    ppermute x9 -> x15, starting transfers between devices: 10.3 us -> 18 us  [from_heads(): lax.ppermute(x, 'head', [(i, (i + k) % n) for i in range(n)])]
    ppermute x9 -> x15, waiting for transfers between devices: 18.7 us -> 11.5 us  [from_heads(): lax.ppermute(x, 'head', [(i, (i + k) % n) for i in range(n)])]
    all_to_all x0 -> x2, waiting for transfers between devices: none -> 5.45 us  [the longest x1 5.45 us: local(): tokens = lax.all_to_all(disp, REQ, 0, 0, tiled=True)]
    pallas_call x10, Pallas kernels: 14.5 us -> 19.5 us  [run(): pl.pallas_call(kernel, name=name, out_shape=list(outs) + [sds(x.shape, x....]
    unnamed x4 -> x22, local copies, waits for them, and re-layouts: 0.02 us -> 3.53 us
    ppermute x3, waiting for transfers between devices: 1.58 us -> 4.18 us  [to_heads(): lax.ppermute(xs[k], 'head', [(i, (i + k) % n) for i in range(n)])]
  transfers between devices with their start and end apart: 15 -> 23, of which waited for: 9 -> 13; matrix products, arithmetic and copies ran while one was open for 1% -> 0% of each run, Pallas kernels for 11% -> 11%
where the time goes in v3:
time: 157 us; the launch traced here: 156 us
  blocking collectives  46.4 us (30%)
  starting transfers between devices  40.8 us (26%)
  Pallas kernels  26.4 us (17%)
  waiting for transfers between devices  23.5 us (15%)
  between operations  14.2 us (9%)
  local copies, waits for them, and re-layouts  3.53 us (2%)
    all_to_all x1, blocking collectives, local(): lax.all_to_all(outset(queries, residual, routes, chips), ('z', 'y'), 0, 0...  28.1 us
    pallas_call x10, Pallas kernels, run(): pl.pallas_call(kernel, name=name, out_shape=list(outs) + [sds(x.shape, x....  19.5 us
    all_to_all x1, blocking collectives, local(): returned = lax.all_to_all(expert_out, REQ, 0, 0, tiled=True)  18.3 us
    ppermute x15, starting transfers between devices, from_heads(): lax.ppermute(x, 'head', [(i, (i + k) % n) for i in range(n)])  18 us
    all_to_all x1, starting transfers between devices, local(): tokens = lax.all_to_all(disp, REQ, 0, 0, tiled=True)  11.8 us
    ppermute x15, waiting for transfers between devices, from_heads(): lax.ppermute(x, 'head', [(i, (i + k) % n) for i in range(n)])  11.5 us
    all_to_all x1, waiting for transfers between devices, local(): tokens = lax.all_to_all(disp, REQ, 0, 0, tiled=True)  5.45 us
    pallas_call x1, Pallas kernels, attend_pages(): pl.pallas_call(attn_kernel, name='attend_pages', out_shape=[sds((total //...  4.96 us
  transfers between devices with their start and end apart: 23, of which 13 were waited for; matrix products, arithmetic and copies ran while one was open for 0% of the time, Pallas kernels for 11%

profile of v3, /device:TPU:1, one launch (start us, length us, event | category | flops | bytes accessed | tf_op | source)
XLA Modules:
  0.0 156.1 jit_solution(4593978756288159490)
XLA Ops:
  7.2 0.7 all-gather.2.cloned.1.call-update
  7.9 1.6 %outset.1 = bf16[32,32,256]{2,1,0:T(8,128)(2,1)S(1)} custom-call(bf16[16,256]{1,0:T(8,128)(2,1)} %refs_1_.3, bf16[16,2048]{1,0:T(8,128)(2,1)} %refs_16_.1, s32[8,16]{1,0:T(8,128)} %bitcast.25), custom_call_target="tpu_custom_call" | custom-call | tf_op jit(solution)/shard_map/outset/pallas_call | solution.py:63
  9.5 28.1 %all_to_all.20.refs_4_.qa_ref = bf16[32,32,256]{2,1,0:T(8,128)(2,1)S(1)} all-to-all(bf16[32,32,256]{2,1,0:T(8,128)(2,1)S(1)} %outset.1), channel_id=1, replica_groups=mesh['z'=8,'y'=4,'c'=2,'head'=4] {'z','y'}, dimensions={0} | all-to-all | bytes 1048576 | tf_op jit(solution)/shard_map/all_to_all | solution.py:516
  37.6 2.4 %collective-permute-start = (bf16[32,32,256]{2,1,0:T(8,128)(2,1)S(1)}, bf16[32,32,256]{2,1,0:T(8,128)(2,1)S(1)}, u32[]{:S(2)}, u32[]{:S(2)}) collective-permute-start(bf16[32,32,256]{2,1,0:T(8,128)(2,1)S(1)} %all_to_all.20.refs_4_.qa_ref), channel_id=1, source_target_pairs={{0,4},{4,0},{1,5},{5,1},{2,6},{6,2},{3,7},{7,3},{8,12},{12,8},{9,1... | collective-permute-start | bytes 1572872 | tf_op jit(solution)/shard_map/ppermute | solution.py:505
  40.0 2.3 %slot_tables.1 = (bf16[128,1024]{1,0:T(8,128)(2,1)S(1)}, f32[128,128]{1,0:T(8,128)S(1)}, f32[128,128]{1,0:T(8,128)S(1)}, f32[128,128]{1,0:T(8,128)S(1)}, bf16[10...) custom-call(s32[1,128]{1,0:T(1,128)} %bitcast.32, s32[1,128]{1,0:T(1,128)} %bitcast.33, ...), custom_call_target="tpu_custom_call" | custom-call | tf_op jit(solution)/shard_map/slot_tables/pallas_call | solution.py:63
  42.4 5.0 %attend_pages.1 = (bf16[32,48,128]{2,1,0:T(8,128)(2,1)S(1)}, bf16[32,48,128]{2,1,0:T(8,128)(2,1)S(1)}, bf16[32,2,8,256]{3,2,1,0:T(8,128)(2,1)S(1)}) custom-call(bf16[128,1024]{1,0:T(8,128)(2,1)S(1)} %get-tuple-element.40.pick_ref, f32[128,128]{1,0:T(8,128)S(1)} %get-tuple-element.41.count_ref, f32[128,128]{1,0:T(8,128)S(1)} %get-tuple-element.42.same_ref, ...), custom_call_target="tpu_custom_call" | custom-call | tf_op jit(solution)/shard_map/attend_pages/pallas_call | solution.py:246
  47.4 0.7 copy-done.2
  48.1 1.7 %collective-permute-done.1.refs_1_ = bf16[32,48,128]{2,1,0:T(8,128)(2,1)S(1)} collective-permute-done((bf16[32,48,128]{2,1,0:T(8,128)(2,1)S(1)}, bf16[32,48,128]{2,1,0:T(8,128)(2,1)S(1)}, u32[]{:S(2)}, u32[]{:S(2)}) %collective-permute-start.1) | collective-permute-done | bytes 393248 | tf_op jit(solution)/shard_map/ppermute | solution.py:505
  49.8 0.9 merge.1
  50.7 0.8 copy-done.1
  51.5 4.4 %all-to-all-start.1 = ((bf16[32,48,128]{2,1,0:T(8,128)(2,1)}), bf16[32,48,128]{2,1,0:T(8,128)(2,1)S(1)}, u32[]{:S(2)}, u32[]{:S(2)}) async-start(bf16[32,48,128]{2,1,0:T(8,128)(2,1)} %copy-done.1), calls=%async_computation.1 | async-start | bytes 786432 | tf_op jit(solution)/shard_map/all_to_all | solution.py:521
  55.9 2.0 %split_columns.1 = (bf16[256,512]{1,0:T(8,128)(2,1)S(1)}, bf16[256,512]{1,0:T(8,128)(2,1)}, bf16[256,512]{1,0:T(8,128)(2,1)}, bf16[256,512]{1,0:T(8,128)(2,1)S(1)}) custom-call(bf16[256,2048]{1,0:T(8,128)(2,1)} %bitcast.24), custom_call_target="tpu_custom_call" | custom-call | tf_op jit(solution)/shard_map/split_columns/pallas_call | solution.py:301
  57.9 0.7 copy-done.3
  58.6 2.5 %collective-permute-start.10 = (bf16[256,512]{1,0:T(8,128)(2,1)S(1)}, bf16[256,512]{1,0:T(8,128)(2,1)S(1)}, u32[]{:S(2)}, u32[]{:S(2)}) collective-permute-start(bf16[256,512]{1,0:T(8,128)(2,1)S(1)} %get-tuple-element.55), channel_id=1, source_target_pairs={{0,3},{1,0},{2,1},{3,2},{4,7},{5,4},{6,5},{7,6},{8,11},{9,8},{10,9... | collective-permute-start | bytes 786440 | tf_op jit(solution)/shard_map/ppermute | solution.py:501
  61.1 1.7 %collective-permute-start.9 = (bf16[256,512]{1,0:T(8,128)(2,1)}, bf16[256,512]{1,0:T(8,128)(2,1)}, u32[]{:S(2)}, u32[]{:S(2)}) collective-permute-start(bf16[256,512]{1,0:T(8,128)(2,1)} %get-tuple-element.54), channel_id=1, source_target_pairs={{0,2},{1,3},{2,0},{3,1},{4,6},{5,7},{6,4},{7,5},{8,10},{9,11},{10,... | collective-permute-start | bytes 786440 | tf_op jit(solution)/shard_map/ppermute | solution.py:501
  62.8 1.5 collective-permute-start.2
  64.4 0.6 collective-permute-start.3
  65.0 4.2 %collective-permute-done.10.refs_4_ = bf16[256,512]{1,0:T(8,128)(2,1)S(1)} collective-permute-done((bf16[256,512]{1,0:T(8,128)(2,1)S(1)}, bf16[256,512]{1,0:T(8,128)(2,1)S(1)}, u32[]{:S(2)}, u32[]{:S(2)}) %collective-permute-start.10) | collective-permute-done | bytes 262176 | tf_op jit(solution)/shard_map/ppermute | solution.py:501
  69.2 0.7 copy-done.7
  69.9 0.6 collective-permute-start.4
  70.5 1.8 %owner_part.1 = (bf16[16,256]{1,0:T(8,128)(2,1)S(1)}, bf16[64,8,128]{2,1,0:T(8,128)(2,1)S(1)}) custom-call(bf16[32,48,128]{2,1,0:T(8,128)(2,1)S(1)} %all-to-all-done.1.refs_0_, bf16[16,256]{1,0:T(8,128)(2,1)} %refs_1_.3, bf16[16,2,256]{2,1,0:T(2,128)(2,1)} %refs_2_.1, s32[8,16]{1,0:T(8,128)} %bitcast.26), custom_call_target="tpu_custom_call" | custom-call | tf_op jit(solution)/shard_map/owner_part/pallas_call | solution.py:63
  72.3 0.7 copy-done.4
  73.0 11.8 %all-to-all-start.2 = ((bf16[64,8,128]{2,1,0:T(8,128)(2,1)}), bf16[64,8,128]{2,1,0:T(8,128)(2,1)S(1)}, u32[]{:S(2)}, u32[]{:S(2)}) async-start(bf16[64,8,128]{2,1,0:T(8,128)(2,1)} %copy-done.4), calls=%async_computation.2 | async-start | bytes 262144 | tf_op jit(solution)/shard_map/all_to_all | solution.py:523
  84.8 0.4 collective-permute-start.5
  85.2 2.4 %collective-permute-start.6 = (bf16[16,256]{1,0:T(8,128)(2,1)S(1)}, bf16[16,256]{1,0:T(8,128)(2,1)S(1)}, u32[]{:S(2)}, u32[]{:S(2)}) collective-permute-start(bf16[16,256]{1,0:T(8,128)(2,1)S(1)} %get-tuple-element.60.refs_8_), channel_id=1, source_target_pairs={{0,2},{1,3},{2,0},{3,1},{4,6},{5,7},{6,4},{7,5},{8,10},{9,11},{10,... | collective-permute-start | bytes 24584 | tf_op jit(solution)/shard_map/ppermute | solution.py:496
  87.6 0.8 collective-permute-start.7
  88.4 0.4 collective-permute-done.5.refs_9_
  88.8 0.7 collective-permute-done.6.refs_10_
  89.5 0.9 collective-permute-done.7.refs_11_
  90.4 5.5 %all-to-all-done.2.refs_0_ = bf16[64,8,128]{2,1,0:T(8,128)(2,1)S(1)} async-done(((bf16[64,8,128]{2,1,0:T(8,128)(2,1)}), bf16[64,8,128]{2,1,0:T(8,128)(2,1)S(1)}, u32[]{:S(2)}, u32[]{:S(2)}) %all-to-all-start.2) | async-done | bytes 131104 | tf_op jit(solution)/shard_map/all_to_all | solution.py:523
  96.2 2.4 %collective-permute-start.12 = (bf16[64,8,128]{2,1,0:T(8,128)(2,1)S(1)}, bf16[64,8,128]{2,1,0:T(8,128)(2,1)S(1)}, u32[]{:S(2)}, u32[]{:S(2)}) collective-permute-start(bf16[64,8,128]{2,1,0:T(8,128)(2,1)S(1)} %all-to-all-done.2.refs_0_), channel_id=1, source_target_pairs={{0,2},{1,3},{2,0},{3,1},{4,6},{5,7},{6,4},{7,5},{8,10},{9,11},{10,... | collective-permute-start | bytes 393224 | tf_op jit(solution)/shard_map/ppermute | solution.py:496
  98.6 0.8 collective-permute-start.13
  99.4 2.9 %fetch.2 = (bf16[1024,2048]{1,0:T(8,128)(2,1)S(1)}, bf16[2048,256]{1,0:T(8,128)(2,1)S(1)}, bf16[2048,256]{1,0:T(8,128)(2,1)S(1)}) custom-call(bf16[64,8,128]{2,1,0:T(8,128)(2,1)S(1)} %all-to-all-done.2.refs_0_, bf16[1024,2048]{1,0:T(8,128)(2,1)} %all-gather.2.cloned.1.call-done.refs_1_, bf16[2048,256]{1,0:T(8,128)(2,1)} %bitcast.22, bf16[2048,256]{1,0:T(8,128)(2,1)} %bitcast.23), custom_call_target="tpu_custom_call" | custom-call | tf_op jit(solution)/shard_map/fetch/pallas_call | solution.py:63
  102.3 2.3 %collective-permute-done.12.refs_2_ = bf16[64,8,128]{2,1,0:T(8,128)(2,1)S(1)} collective-permute-done((bf16[64,8,128]{2,1,0:T(8,128)(2,1)S(1)}, bf16[64,8,128]{2,1,0:T(8,128)(2,1)S(1)}, u32[]{:S(2)}, u32[]{:S(2)}) %collective-permute-start.12) | collective-permute-done | bytes 131104 | tf_op jit(solution)/shard_map/ppermute | solution.py:496
  104.9 5.3 %expert_rows.1 = (bf16[256,256]{1,0:T(8,128)(2,1)S(1)}, bf16[16,512]{1,0:T(8,128)(2,1)S(1)}) custom-call(bf16[64,8,128]{2,1,0:T(8,128)(2,1)S(1)} %all-to-all-done.2.refs_0_, bf16[64,8,128]{2,1,0:T(8,128)(2,1)S(1)} %collective-permute-done.11.refs_1_, bf16[64,8,128]{2,1,0:T(8,128)(2,1)S(1)} %collective-permute-done.12.refs_2_, ...), custom_call_target="tpu_custom_call" | custom-call | tf_op jit(solution)/shard_map/expert_rows/pallas_call | solution.py:63
  110.3 1.9 %collective-permute-start.14 = (bf16[256,256]{1,0:T(8,128)(2,1)S(1)}, bf16[256,256]{1,0:T(8,128)(2,1)S(1)}, u32[]{:S(2)}, u32[]{:S(2)}) collective-permute-start(bf16[256,256]{1,0:T(8,128)(2,1)S(1)} %get-tuple-element.68.refs_0_), channel_id=1, source_target_pairs={{0,1},{1,2},{2,3},{3,0},{4,5},{5,6},{6,7},{7,4},{8,9},{9,10},{10,1... | collective-permute-start | bytes 393224 | tf_op jit(solution)/shard_map/ppermute | solution.py:496
  112.2 2.7 %collective-permute-start.15 = (bf16[256,256]{1,0:T(8,128)(2,1)S(1)}, bf16[256,256]{1,0:T(8,128)(2,1)S(1)}, u32[]{:S(2)}, u32[]{:S(2)}) collective-permute-start(bf16[256,256]{1,0:T(8,128)(2,1)S(1)} %get-tuple-element.68.refs_0_), channel_id=1, source_target_pairs={{0,2},{1,3},{2,0},{3,1},{4,6},{5,7},{6,4},{7,5},{8,10},{9,11},{10,... | collective-permute-start | bytes 393224 | tf_op jit(solution)/shard_map/ppermute | solution.py:496
  114.9 1.4 fetch.3
  116.4 4.3 %collective-permute-done.15.refs_2_ = bf16[256,256]{1,0:T(8,128)(2,1)S(1)} collective-permute-done((bf16[256,256]{1,0:T(8,128)(2,1)S(1)}, bf16[256,256]{1,0:T(8,128)(2,1)S(1)}, u32[]{:S(2)}, u32[]{:S(2)}) %collective-permute-start.15) | collective-permute-done | bytes 131104 | tf_op jit(solution)/shard_map/ppermute | solution.py:496
  120.7 0.5 down.1
  121.2 18.3 %all_to_all.21.refs_0_ = bf16[64,8,256]{2,1,0:T(8,128)(2,1)S(1)} all-to-all(bf16[64,8,256]{2,1,0:T(8,128)(2,1)S(1)} %bitcast.17), channel_id=1, replica_groups=mesh['z'=8,'y'=4,'c'=2,'head'=4] {'z','y','c'}, dimensions={0} | all-to-all | bytes 524288 | tf_op jit(solution)/shard_map/all_to_all | solution.py:529
  139.5 1.9 %blend.1.refs_4_ = bf16[16,512]{1,0:T(8,128)(2,1)} custom-call(bf16[64,8,256]{2,1,0:T(8,128)(2,1)S(1)} %all_to_all.21.refs_0_, bf16[16,512]{1,0:T(8,128)(2,1)} %copy-done.5, s32[8,16]{1,0:T(8,128)} %bitcast.27, f32[8,16]{1,0:T(8,128)} %bitcast.31), custom_call_target="tpu_custom_call" | custom-call | tf_op jit(solution)/shard_map/blend/pallas_call | solution.py:63
  141.5 2.9 %collective-permute-start.18 = (bf16[16,512]{1,0:T(8,128)(2,1)}, bf16[16,512]{1,0:T(8,128)(2,1)S(1)}, u32[]{:S(2)}, u32[]{:S(2)}) collective-permute-start(bf16[16,512]{1,0:T(8,128)(2,1)} %blend.1.refs_4_), channel_id=1, source_target_pairs={{0,2},{1,3},{2,0},{3,1},{4,6},{5,7},{6,4},{7,5},{8,10},{9,11},{10,... | collective-permute-start | bytes 49160 | tf_op jit(solution)/shard_map/ppermute | solution.py:496
  144.8 0.7 collective-permute-done.17.refs_0_
  145.5 0.4 collective-permute-done.18.refs_1_
  145.9 1.3 collective-permute-done.19.refs_2_
  147.2 0.9 norm_parts.1
  148.1 1.1 convolution_convert_fusion
  (36 shorter events, 1.4 us)
Async XLA Ops:
  7.2 141.0 %copy-start = (bf16[2048,3,256]{2,0,1:T(8,128)(2,1)S(1)}, bf16[2048,3,256]{2,0,1:T(8,128)(2,1)}, u32[]{:S(2)}) copy-start(bf16[2048,3,256]{2,0,1:T(8,128)(2,1)} %param.33) | copy-start | bytes 9437188
  7.2 92.2 %all-gather.2.cloned.1.call-start = ((), (), s32[]{:S(2)}) async-start(), calls=%async_computation.4 | async-start | bytes 5242880 | tf_op jit(solution)/shard_map/all_gather | solution.py:515
  37.6 4.7 %collective-permute-start = (bf16[32,32,256]{2,1,0:T(8,128)(2,1)S(1)}, bf16[32,32,256]{2,1,0:T(8,128)(2,1)S(1)}, u32[]{:S(2)}, u32[]{:S(2)}) collective-permute-start(bf16[32,32,256]{2,1,0:T(8,128)(2,1)S(1)} %all_to_all.20.refs_4_.qa_ref), channel_id=1, source_target_pairs={{0,4},{4,0},{1,5},{5,1},{2,6},{6,2},{3,7},{7,3},{8,12},{12,8},{9,1... | collective-permute-start | bytes 1572872 | tf_op jit(solution)/shard_map/ppermute | solution.py:505
  47.3 0.7 copy-start.2
  48.1 1.7 %collective-permute-start.1 = (bf16[32,48,128]{2,1,0:T(8,128)(2,1)S(1)}, bf16[32,48,128]{2,1,0:T(8,128)(2,1)S(1)}, u32[]{:S(2)}, u32[]{:S(2)}) collective-permute-start(bf16[32,48,128]{2,1,0:T(8,128)(2,1)S(1)} %get-tuple-element.48), channel_id=1, source_target_pairs={{0,4},{4,0},{1,5},{5,1},{2,6},{6,2},{3,7},{7,3},{8,12},{12,8},{9,1... | collective-permute-start | bytes 1179656 | tf_op jit(solution)/shard_map/ppermute | solution.py:505
  50.7 0.8 copy-start.1
  51.5 19.0 %all-to-all-start.1 = ((bf16[32,48,128]{2,1,0:T(8,128)(2,1)}), bf16[32,48,128]{2,1,0:T(8,128)(2,1)S(1)}, u32[]{:S(2)}, u32[]{:S(2)}) async-start(bf16[32,48,128]{2,1,0:T(8,128)(2,1)} %copy-done.1), calls=%async_computation.1 | async-start | bytes 786432 | tf_op jit(solution)/shard_map/all_to_all | solution.py:521
  57.9 0.7 copy-start.3
  58.6 10.6 %collective-permute-start.10 = (bf16[256,512]{1,0:T(8,128)(2,1)S(1)}, bf16[256,512]{1,0:T(8,128)(2,1)S(1)}, u32[]{:S(2)}, u32[]{:S(2)}) collective-permute-start(bf16[256,512]{1,0:T(8,128)(2,1)S(1)} %get-tuple-element.55), channel_id=1, source_target_pairs={{0,3},{1,0},{2,1},{3,2},{4,7},{5,4},{6,5},{7,6},{8,11},{9,8},{10,9... | collective-permute-start | bytes 786440 | tf_op jit(solution)/shard_map/ppermute | solution.py:501
  61.1 23.6 %collective-permute-start.8 = (bf16[256,512]{1,0:T(8,128)(2,1)}, bf16[256,512]{1,0:T(8,128)(2,1)}, u32[]{:S(2)}, u32[]{:S(2)}) collective-permute-start(bf16[256,512]{1,0:T(8,128)(2,1)} %get-tuple-element.53), channel_id=1, source_target_pairs={{0,1},{1,2},{2,3},{3,0},{4,5},{5,6},{6,7},{7,4},{8,9},{9,10},{10,1... | collective-permute-start | bytes 786440 | tf_op jit(solution)/shard_map/ppermute | solution.py:501
  61.1 24.1 %collective-permute-start.9 = (bf16[256,512]{1,0:T(8,128)(2,1)}, bf16[256,512]{1,0:T(8,128)(2,1)}, u32[]{:S(2)}, u32[]{:S(2)}) collective-permute-start(bf16[256,512]{1,0:T(8,128)(2,1)} %get-tuple-element.54), channel_id=1, source_target_pairs={{0,2},{1,3},{2,0},{3,1},{4,6},{5,7},{6,4},{7,5},{8,10},{9,11},{10,... | collective-permute-start | bytes 786440 | tf_op jit(solution)/shard_map/ppermute | solution.py:501
  62.8 24.8 %collective-permute-start.2 = (bf16[64,8,256]{2,1,0:T(8,128)(2,1)}, bf16[64,8,256]{2,1,0:T(8,128)(2,1)}, u32[]{:S(2)}, u32[]{:S(2)}) collective-permute-start(bf16[64,8,256]{2,1,0:T(8,128)(2,1)} %bitcast.18), channel_id=1, source_target_pairs={{0,1},{1,2},{2,3},{3,0},{4,5},{5,6},{6,7},{7,4},{8,9},{9,10},{10,1... | collective-permute-start | bytes 786440 | tf_op jit(solution)/shard_map/ppermute | solution.py:496
  64.4 24.0 %collective-permute-start.3 = (bf16[64,8,256]{2,1,0:T(8,128)(2,1)}, bf16[64,8,256]{2,1,0:T(8,128)(2,1)}, u32[]{:S(2)}, u32[]{:S(2)}) collective-permute-start(bf16[64,8,256]{2,1,0:T(8,128)(2,1)} %bitcast.19), channel_id=1, source_target_pairs={{0,2},{1,3},{2,0},{3,1},{4,6},{5,7},{6,4},{7,5},{8,10},{9,11},{10,... | collective-permute-start | bytes 786440 | tf_op jit(solution)/shard_map/ppermute | solution.py:496
  69.2 0.7 copy-start.7
  69.9 18.5 %collective-permute-start.4 = (bf16[64,8,256]{2,1,0:T(8,128)(2,1)}, bf16[64,8,256]{2,1,0:T(8,128)(2,1)}, u32[]{:S(2)}, u32[]{:S(2)}) collective-permute-start(bf16[64,8,256]{2,1,0:T(8,128)(2,1)} %bitcast.20), channel_id=1, source_target_pairs={{0,3},{1,0},{2,1},{3,2},{4,7},{5,4},{6,5},{7,6},{8,11},{9,8},{10,9... | collective-permute-start | bytes 786440 | tf_op jit(solution)/shard_map/ppermute | solution.py:496
  72.3 0.7 copy-start.4
  73.0 32.0 %copy-start.6 = (bf16[16,256]{1,0:T(8,128)(2,1)}, bf16[16,256]{1,0:T(8,128)(2,1)S(1)}, u32[]{:S(2)}) copy-start(bf16[16,256]{1,0:T(8,128)(2,1)S(1)} %get-tuple-element.60.refs_8_) | copy-start | bytes 24580
  73.0 22.9 %all-to-all-start.2 = ((bf16[64,8,128]{2,1,0:T(8,128)(2,1)}), bf16[64,8,128]{2,1,0:T(8,128)(2,1)S(1)}, u32[]{:S(2)}, u32[]{:S(2)}) async-start(bf16[64,8,128]{2,1,0:T(8,128)(2,1)} %copy-done.4), calls=%async_computation.2 | async-start | bytes 262144 | tf_op jit(solution)/shard_map/all_to_all | solution.py:523
  84.8 4.1 %collective-permute-start.5 = (bf16[16,256]{1,0:T(8,128)(2,1)S(1)}, bf16[16,256]{1,0:T(8,128)(2,1)S(1)}, u32[]{:S(2)}, u32[]{:S(2)}) collective-permute-start(bf16[16,256]{1,0:T(8,128)(2,1)S(1)} %get-tuple-element.60.refs_8_), channel_id=1, source_target_pairs={{0,1},{1,2},{2,3},{3,0},{4,5},{5,6},{6,7},{7,4},{8,9},{9,10},{10,1... | collective-permute-start | bytes 24584 | tf_op jit(solution)/shard_map/ppermute | solution.py:496
  85.2 4.3 %collective-permute-start.6 = (bf16[16,256]{1,0:T(8,128)(2,1)S(1)}, bf16[16,256]{1,0:T(8,128)(2,1)S(1)}, u32[]{:S(2)}, u32[]{:S(2)}) collective-permute-start(bf16[16,256]{1,0:T(8,128)(2,1)S(1)} %get-tuple-element.60.refs_8_), channel_id=1, source_target_pairs={{0,2},{1,3},{2,0},{3,1},{4,6},{5,7},{6,4},{7,5},{8,10},{9,11},{10,... | collective-permute-start | bytes 24584 | tf_op jit(solution)/shard_map/ppermute | solution.py:496
  87.6 2.8 %collective-permute-start.7 = (bf16[16,256]{1,0:T(8,128)(2,1)S(1)}, bf16[16,256]{1,0:T(8,128)(2,1)S(1)}, u32[]{:S(2)}, u32[]{:S(2)}) collective-permute-start(bf16[16,256]{1,0:T(8,128)(2,1)S(1)} %get-tuple-element.60.refs_8_), channel_id=1, source_target_pairs={{0,3},{1,0},{2,1},{3,2},{4,7},{5,4},{6,5},{7,6},{8,11},{9,8},{10,9... | collective-permute-start | bytes 24584 | tf_op jit(solution)/shard_map/ppermute | solution.py:496
  88.8 16.1 %copy-start.8 = (bf16[16,256]{1,0:T(8,128)(2,1)}, bf16[16,256]{1,0:T(8,128)(2,1)S(1)}, u32[]{:S(2)}) copy-start(bf16[16,256]{1,0:T(8,128)(2,1)S(1)} %collective-permute-done.5.refs_9_) | copy-start | bytes 24580
  89.5 6.4 %copy-start.9 = (bf16[16,256]{1,0:T(8,128)(2,1)}, bf16[16,256]{1,0:T(8,128)(2,1)S(1)}, u32[]{:S(2)}) copy-start(bf16[16,256]{1,0:T(8,128)(2,1)S(1)} %collective-permute-done.6.refs_10_) | copy-start | bytes 24580
  90.4 5.5 %copy-start.10 = (bf16[16,256]{1,0:T(8,128)(2,1)}, bf16[16,256]{1,0:T(8,128)(2,1)S(1)}, u32[]{:S(2)}) copy-start(bf16[16,256]{1,0:T(8,128)(2,1)S(1)} %collective-permute-done.7.refs_11_) | copy-start | bytes 24580
  95.9 6.4 %collective-permute-start.11 = (bf16[64,8,128]{2,1,0:T(8,128)(2,1)S(1)}, bf16[64,8,128]{2,1,0:T(8,128)(2,1)S(1)}, u32[]{:S(2)}, u32[]{:S(2)}) collective-permute-start(bf16[64,8,128]{2,1,0:T(8,128)(2,1)S(1)} %all-to-all-done.2.refs_0_), channel_id=1, source_target_pairs={{0,1},{1,2},{2,3},{3,0},{4,5},{5,6},{6,7},{7,4},{8,9},{9,10},{10,1... | collective-permute-start | bytes 393224 | tf_op jit(solution)/shard_map/ppermute | solution.py:496
  96.2 8.4 %collective-permute-start.12 = (bf16[64,8,128]{2,1,0:T(8,128)(2,1)S(1)}, bf16[64,8,128]{2,1,0:T(8,128)(2,1)S(1)}, u32[]{:S(2)}, u32[]{:S(2)}) collective-permute-start(bf16[64,8,128]{2,1,0:T(8,128)(2,1)S(1)} %all-to-all-done.2.refs_0_), channel_id=1, source_target_pairs={{0,2},{1,3},{2,0},{3,1},{4,6},{5,7},{6,4},{7,5},{8,10},{9,11},{10,... | collective-permute-start | bytes 393224 | tf_op jit(solution)/shard_map/ppermute | solution.py:496
  98.6 6.3 %collective-permute-start.13 = (bf16[64,8,128]{2,1,0:T(8,128)(2,1)S(1)}, bf16[64,8,128]{2,1,0:T(8,128)(2,1)}, u32[]{:S(2)}, u32[]{:S(2)}) collective-permute-start(bf16[64,8,128]{2,1,0:T(8,128)(2,1)S(1)} %all-to-all-done.2.refs_0_), channel_id=1, source_target_pairs={{0,3},{1,0},{2,1},{3,2},{4,7},{5,4},{6,5},{7,6},{8,11},{9,8},{10,9... | collective-permute-start | bytes 393224 | tf_op jit(solution)/shard_map/ppermute | solution.py:496
  110.2 29.2 %copy-start.5 = (bf16[16,512]{1,0:T(8,128)(2,1)}, bf16[16,512]{1,0:T(8,128)(2,1)S(1)}, u32[]{:S(2)}) copy-start(bf16[16,512]{1,0:T(8,128)(2,1)S(1)} %get-tuple-element.77.refs_1_) | copy-start | bytes 49156
  110.3 6.2 %collective-permute-start.14 = (bf16[256,256]{1,0:T(8,128)(2,1)S(1)}, bf16[256,256]{1,0:T(8,128)(2,1)S(1)}, u32[]{:S(2)}, u32[]{:S(2)}) collective-permute-start(bf16[256,256]{1,0:T(8,128)(2,1)S(1)} %get-tuple-element.68.refs_0_), channel_id=1, source_target_pairs={{0,1},{1,2},{2,3},{3,0},{4,5},{5,6},{6,7},{7,4},{8,9},{9,10},{10,1... | collective-permute-start | bytes 393224 | tf_op jit(solution)/shard_map/ppermute | solution.py:496
  112.2 8.5 %collective-permute-start.15 = (bf16[256,256]{1,0:T(8,128)(2,1)S(1)}, bf16[256,256]{1,0:T(8,128)(2,1)S(1)}, u32[]{:S(2)}, u32[]{:S(2)}) collective-permute-start(bf16[256,256]{1,0:T(8,128)(2,1)S(1)} %get-tuple-element.68.refs_0_), channel_id=1, source_target_pairs={{0,2},{1,3},{2,0},{3,1},{4,6},{5,7},{6,4},{7,5},{8,10},{9,11},{10,... | collective-permute-start | bytes 393224 | tf_op jit(solution)/shard_map/ppermute | solution.py:496
  114.9 5.8 %collective-permute-start.16 = (bf16[256,256]{1,0:T(8,128)(2,1)S(1)}, bf16[256,256]{1,0:T(8,128)(2,1)S(1)}, u32[]{:S(2)}, u32[]{:S(2)}) collective-permute-start(bf16[256,256]{1,0:T(8,128)(2,1)S(1)} %get-tuple-element.68.refs_0_), channel_id=1, source_target_pairs={{0,3},{1,0},{2,1},{3,2},{4,7},{5,4},{6,5},{7,6},{8,11},{9,8},{10,9... | collective-permute-start | bytes 393224 | tf_op jit(solution)/shard_map/ppermute | solution.py:496
  141.4 4.1 %collective-permute-start.17 = (bf16[16,512]{1,0:T(8,128)(2,1)}, bf16[16,512]{1,0:T(8,128)(2,1)S(1)}, u32[]{:S(2)}, u32[]{:S(2)}) collective-permute-start(bf16[16,512]{1,0:T(8,128)(2,1)} %blend.1.refs_4_), channel_id=1, source_target_pairs={{0,1},{1,2},{2,3},{3,0},{4,5},{5,6},{6,7},{7,4},{8,9},{9,10},{10,1... | collective-permute-start | bytes 49160 | tf_op jit(solution)/shard_map/ppermute | solution.py:496
  141.5 4.4 %collective-permute-start.18 = (bf16[16,512]{1,0:T(8,128)(2,1)}, bf16[16,512]{1,0:T(8,128)(2,1)S(1)}, u32[]{:S(2)}, u32[]{:S(2)}) collective-permute-start(bf16[16,512]{1,0:T(8,128)(2,1)} %blend.1.refs_4_), channel_id=1, source_target_pairs={{0,2},{1,3},{2,0},{3,1},{4,6},{5,7},{6,4},{7,5},{8,10},{9,11},{10,... | collective-permute-start | bytes 49160 | tf_op jit(solution)/shard_map/ppermute | solution.py:496
  144.4 2.8 %collective-permute-start.19 = (bf16[16,512]{1,0:T(8,128)(2,1)}, bf16[16,512]{1,0:T(8,128)(2,1)S(1)}, u32[]{:S(2)}, u32[]{:S(2)}) collective-permute-start(bf16[16,512]{1,0:T(8,128)(2,1)} %blend.1.refs_4_), channel_id=1, source_target_pairs={{0,3},{1,0},{2,1},{3,2},{4,7},{5,4},{6,5},{7,6},{8,11},{9,8},{10,9... | collective-permute-start | bytes 49160 | tf_op jit(solution)/shard_map/ppermute | solution.py:496
Sparse Core Ops, SparseCore 0:
  9.8 55.9 all-gather.1

commit v4 on v3

--- a/solution.py
+++ b/solution.py
@@ -30,14 +30,25 @@
         return self.buf
 
 
-def run(body, name, outs, near, far, scratch=(), after=(), moves=()):
-    nn, nf, na, nm = len(near), len(far), len(after), len(moves)
+class Leaving:
+    def __init__(self, buf, copy):
+        self.buf, self.copy, self.sent = buf, copy, False
+
+    def send(self):
+        self.copy.start()
+        self.sent = True
+
+
+def run(body, name, outs, near, far, scratch=(), after=(), moves=(), leaving=()):
+    nn, nf, na, nm, no, nl = len(near), len(far), len(after), len(moves), len(outs), len(leaving)
     parts = 4
 
     def kernel(*refs):
         ins, refs = refs[: nn + nf + na + nm], refs[nn + nf + na + nm :]
-        outputs, moved, rest = refs[: len(outs)], refs[len(outs) : len(outs) + nm], refs[len(outs) + nm :]
-        bufs, sems, move_sems, own = rest[:nf], rest[nf], rest[nf + 1], rest[nf + 2 :]
+        outputs, out_hbm, moved = refs[:no], refs[no : no + nl], refs[no + nl : no + nl + nm]
+        rest = refs[no + nl + nm :]
+        bufs, out_bufs, rest = rest[:nf], rest[nf : nf + nl], rest[nf + nl :]
+        sems, move_sems, out_sems, own = rest[0], rest[1], rest[2], rest[3:]
         copies = [pltpu.make_async_copy(ins[nn + i], bufs[i], sems.at[i]) for i in range(nf)]
         for copy in copies:
             copy.start()
@@ -50,9 +61,16 @@
                 moving.append(pltpu.make_async_copy(src, dst, move_sems.at[parts * i + j]))
         for copy in moving:
             copy.start()
-        body(ins[:nn], pending, outputs, own)
+        going = [
+            Leaving(out_bufs[i], pltpu.make_async_copy(out_bufs[i], out_hbm[i], out_sems.at[i])) for i in range(nl)
+        ]
+        body(ins[:nn], pending, (*outputs, *going), own)
         for p in pending:
             p.get()
+        for g in going:
+            if not g.sent:
+                g.send()
+            g.copy.wait()
         for copy in moving:
             copy.wait()
 
@@ -63,11 +81,13 @@
     return pl.pallas_call(
         kernel,
         name=name,
-        out_shape=list(outs) + [sds(x.shape, x.dtype) for x in moves],
+        out_shape=list(outs)
+        + [pltpu.HBM(x.shape, x.dtype) for x in leaving]
+        + [sds(x.shape, x.dtype) for x in moves],
         in_specs=[VM] * nn + [hbm] * nf + [any_space] * na + [hbm] * nm,
-        out_specs=[VM] * (len(outs) + nm),
-        scratch_shapes=[pltpu.VMEM(x.shape, x.dtype) for x in far]
-        + [pltpu.SemaphoreType.DMA((max(nf, 1),)), pltpu.SemaphoreType.DMA((max(nm * parts, 1),))]
+        out_specs=[VM] * no + [hbm] * nl + [VM] * nm,
+        scratch_shapes=[pltpu.VMEM(x.shape, x.dtype) for x in (*far, *leaving)]
+        + [pltpu.SemaphoreType.DMA((max(n, 1),)) for n in (nf, nm * parts, nl)]
         + list(scratch),
         compiler_params=VLIM,
     )(*near, *pin(far), *after, *pin(moves))
@@ -184,15 +204,19 @@
     )
 
 
-def attn_kernel(pick_ref, count_ref, same_ref, mine_ref, spread_ref, spread16_ref, kv_ref, qa_ref, qb_ref, keep_ref, send_ref, res_ref, n_scr, m_scr, l_scr):
+def attn_body(near, far, outs, own):
+    pick_ref, count_ref, same_ref, mine_ref, spread_ref, spread16_ref, kv_ref, qa_ref, qb_ref = near
+    keep_ref, send_ref, res = outs
+    n_scr, m_scr, l_scr = own
+    core = core_id()
+    res.buf[:, core] = qa_ref[:, 16:24, :]
+    res.buf[:, 1 - core] = qb_ref[:, 24:32, :]
+    res.send()
     slots = kv_ref.shape[0]
     page = kv_ref.shape[2]
     half = qa_ref.shape[0] * 16
     qa, qb = (r[:, 0:16, :].reshape(half, 2 * HD) for r in (qa_ref, qb_ref))
     chosen = dot(pick_ref[:, :half], qa) + dot(pick_ref[:, half:], qb)
-    core = core_id()
-    res_ref[:, core] = qa_ref[:, 16:24, :]
-    res_ref[:, 1 - core] = qb_ref[:, 24:32, :]
     low_lanes = iota((8, 2 * HD), 1) < HD
     rel = iota((16, 8 * page), 1) - (iota((16, 8 * page), 0) % 8) * page
     rel = rel.astype(F32)
@@ -243,23 +267,14 @@
 
 def attend_pages(tables, qa, qb):
     slots, total = tables[0].shape
-    return pl.pallas_call(
-        attn_kernel,
-        name="attend_pages",
-        out_shape=[sds((total // 32, 48, HD), BF16)] * 2 + [sds((total // 32, 2, 8, 2 * HD), BF16)],
-        in_specs=[VM] * 9,
-        out_specs=[VM] * 3,
-        scratch_shapes=[
-            pltpu.VMEM((2, slots, HD), F32),
-            pltpu.VMEM((2, slots, slots), F32),
-            pltpu.VMEM((2, slots, slots), F32),
-        ],
-        compiler_params=VLIM,
-    )(*tables, qa, qb)
+    scratch = [pltpu.VMEM((2, slots, n), F32) for n in (HD, slots, slots)]
+    outs = [sds((total // 32, 48, HD), BF16)] * 2
+    leaving = [sds((total // 32, 2, 8, 2 * HD), BF16)]
+    return run(attn_body, "attend_pages", outs, [*tables, qa, qb], [], scratch, leaving=leaving)
 
 
 def merge_body(near, far, outs, own):
-    (a_ref, b_ref), out_ref = near, outs[0]
+    (a_ref, b_ref), out_ref = near, outs[0].buf
     a, b = a_ref[:, 32:48, :].astype(F32), b_ref[:, 32:48, :].astype(F32)
     lane, row = iota(a.shape, 2), iota(a.shape, 1)
     board = jnp.zeros(a.shape, F32)
@@ -277,36 +292,59 @@
 
 
 def merge(a, b):
-    return run(merge_body, "merge", [sds(a.shape, BF16)], [a, b], [])[0]
+    return run(merge_body, "merge", [], [a, b], [], leaving=[sds(a.shape, BF16)])[0]
 
 
 def fetch(after, *arrays):
     return run(lambda *_: None, "fetch", [], [], [], after=[after], moves=arrays)
 
 
-def split_kernel(w_ref, *refs):
-    outs, sems = refs[:4], refs[4]
-    width = outs[0].shape[1]
-    copies = []
-    for k in range(4):
-        cols = pl.ds(pl.multiple_of(((head_id() + k) % 4) * width, width), width)
-        copies.append(pltpu.make_async_copy(w_ref.at[:, cols], outs[k], sems.at[k]))
-    for copy in copies:
-        copy.start()
-    for copy in copies:
-        copy.wait()
-
-
-def split_columns(w):
+def column_kernel(w_ref, after_ref, out_ref, sem):
+    width = out_ref.shape[1]
+    cols = pl.ds(pl.multiple_of(head_id() * width, width), width)
+    copy = pltpu.make_async_copy(w_ref.at[:, cols], out_ref, sem)
+    copy.start()
+    copy.wait()
+
+
+def fetch_columns(after, w):
     return pl.pallas_call(
-        split_kernel,
-        name="split_columns",
-        out_shape=[sds((w.shape[0], w.shape[1] // 4), w.dtype)] * 4,
-        in_specs=[pl.BlockSpec(memory_space=pltpu.HBM)],
-        out_specs=[VM] * 4,
-        scratch_shapes=[pltpu.SemaphoreType.DMA((4,))],
+        column_kernel,
+        name="fetch_columns",
+        out_shape=sds((w.shape[0], w.shape[1] // 4), w.dtype),
+        in_specs=[pl.BlockSpec(memory_space=pltpu.HBM), pl.BlockSpec(memory_space=pl.ANY)],
+        out_specs=VM,
+        scratch_shapes=[pltpu.SemaphoreType.DMA],
         compiler_params=VLIM,
-    )(pltpu.with_memory_space_constraint(w, pltpu.HBM))
+    )(pltpu.with_memory_space_constraint(w, pltpu.HBM), after)
+
+
+def cells_body(near, far, outs, own):
+    rows = outs[0].shape[0] // 2
+    lane = iota((rows, outs[0].shape[1]), 1)
+    outs[0][...] = cell_map(flip(far[0].get()[...], 1), (lane // 8).astype(F32), lane)
+
+
+def cells_table(routes, experts, after):
+    out = sds((2 * routes.shape[0], experts * 8), BF16)
+    return run(cells_body, "cells_table", [out], [], [routes.T], after=[after])[0]
+
+
+def mix_body(near, far, outs, own):
+    routes, share = flip(far[0].get()[...], 1), flip(far[1].get()[...], 3)
+    rows, cells = outs[0].shape
+    lane = iota((rows, cells), 1)
+    expert = (lane // 4).astype(F32)
+    mix = jnp.zeros((rows, cells), F32)
+    for k in range(routes.shape[1]):
+        mix = mix + jnp.where(routes[:, k : k + 1] == expert, share[:, k : k + 1], 0.0)
+    mix = jnp.where(rank_of(hits(routes, expert)) == (lane % 4).astype(F32), mix, 0.0)
+    outs[0][...], outs[1][...] = hi_lo(mix)
+
+
+def mix_table(routes, route_weights, experts, after):
+    out = sds((routes.shape[0], experts * 4), BF16)
+    return run(mix_body, "mix_table", [out, out], [], [routes.T, route_weights.T], after=[after])
 
 
 def read_stats(board, h):
@@ -335,17 +373,14 @@
         att.append((n + new * v) / (den + new))
     att_ref, disp_ref = outs
     att_ref[...] = jnp.concatenate(att, axis=1).astype(BF16)
-    rows = att_ref.shape[0]
-    lane = iota((rows, disp_ref.shape[0] * 8), 1)
-    pick = cell_map(flip(far[2].get()[...], 1), (lane // 8).astype(F32), lane)
     both = jnp.concatenate(att, axis=0).astype(BF16)
-    out = lax.dot_general(pick, both, (((0,), (0,)), ((), ())), preferred_element_type=F32)
+    out = lax.dot_general(far[2].get()[...], both, (((0,), (0,)), ((), ())), preferred_element_type=F32)
     disp_ref[...] = out.astype(BF16).reshape(disp_ref.shape)
 
 
-def owner_part(parts, queries, new_kv, routes, experts):
+def owner_part(parts, queries, new_kv, cells, experts):
     outs = [sds(queries.shape, BF16), sds((experts, 8, HD), BF16)]
-    return run(owner_body, "owner_part", outs, [parts], [queries, new_kv, routes.T])
+    return run(owner_body, "owner_part", outs, [parts], [queries, new_kv, cells])
 
 
 def flip(x, terms):
@@ -385,93 +420,103 @@
     return a, b
 
 
+def head_blocks(size):
+    return [pl.multiple_of(((head_id() + 4 - k) % 4) * size, size) for k in range(4)]
+
+
+def early_body(near, far, outs, own):
+    tok_ref, wo_ref = near
+    xs = outs[0]
+    eff, w = 2 * HD, xs.shape[2]
+    att = jnp.concatenate(unfold(tok_ref[...].astype(F32)), axis=1).astype(BF16)
+    rows = pl.ds(head_blocks(eff)[0], eff)
+    for k, first in enumerate(head_blocks(2 * w)):
+        pair = unfold(far[k].get()[...].astype(F32))
+        for f in range(2):
+            xs[2 * k + f] = pair[f] + dot(att, wo_ref[rows, pl.ds(first + f * w, w)])
+
+
+def early_rows(tokens, out_weight, res):
+    n = tokens.shape[0]
+    w = res[0].shape[2]
+    return run(early_body, "early_rows", [sds((8, n * 4, w), F32)], [tokens, out_weight], res)[0]
+
+
 def expert_body(near, far, outs, own):
-    inner_ref, hid_ref = outs
-    xs = own[0]
-    att, (wo_ref, wg_ref, wu_ref) = near[:4], near[4:]
-    gain, mine, res, own_res = far[0], far[1:5], far[5:9], far[9]
-    head = head_id()
+    inner_ref, hid = outs
+    hs = own[0]
+    att, (xs, wo_ref, wg_ref, wu_ref) = near[:3], near[3:]
+    gain, mine, own_res = far[0], far[1:5], far[5]
     n = inner_ref.shape[0]
     eff = 2 * HD
     w = xs.shape[2]
     att = [jnp.concatenate(unfold(a[...].astype(F32)), axis=1).astype(BF16) for a in att]
-    block = [pl.multiple_of(((head + 4 - k) % 4) * eff, eff) for k in range(4)]
+    block = head_blocks(eff)
+    firsts = [first + f * w for first in head_blocks(2 * w) for f in range(2)]
+    cols = pl.ds(head_blocks(2 * w)[0], 2 * w)
+    acc = own_res.get()[:, cols].astype(F32)
+    acc = acc + sum(dot(mine[i].get()[...], wo_ref[pl.ds(block[i], eff), cols]) for i in range(4))
+    hid.buf[...] = acc.astype(BF16)
+    hid.send()
     total = jnp.zeros((n, 1), F32)
-    for k in range(4):
-        pair = unfold(res[k].get()[...].astype(F32))
-        for f in range(2):
-            first = pl.multiple_of(((head + 4 - k) % 4) * 2 * w + f * w, w)
-            acc = dot(att[0], wo_ref[pl.ds(block[0], eff), pl.ds(first, w)])
-            for i in range(1, 4):
-                acc = acc + dot(att[i], wo_ref[pl.ds(block[i], eff), pl.ds(first, w)])
-            part = (pair[f] + acc).astype(BF16).astype(F32)
-            xs[2 * k + f] = part
-            total = total + jnp.sum(part * part, axis=1, keepdims=True)
+    for j, first in enumerate(firsts):
+        acc = xs[j]
+        for i in range(3):
+            acc = acc + dot(att[i], wo_ref[pl.ds(block[i + 1], eff), pl.ds(first, w)])
+        part = acc.astype(BF16)
+        hs[j] = part
+        part = part.astype(F32)
+        total = total + jnp.sum(part * part, axis=1, keepdims=True)
     scale = lax.rsqrt(total / (8 * w) + EPS)
     gain_ref = gain.get()
     gate = jnp.zeros((n, wg_ref.shape[1]), F32)
     up = jnp.zeros((n, wg_ref.shape[1]), F32)
-    for k in range(4):
-        for f in range(2):
-            first = pl.multiple_of(((head + 4 - k) % 4) * 2 * w + f * w, w)
-            normed = (xs[2 * k + f] * scale * gain_ref[:, pl.ds(first, w)]).astype(BF16)
-            gate = gate + dot(normed, wg_ref[pl.ds(first, w), :])
-            up = up + dot(normed, wu_ref[pl.ds(first, w), :])
+    for j, first in enumerate(firsts):
+        normed = (hs[j].astype(F32) * scale * gain_ref[:, pl.ds(first, w)]).astype(BF16)
+        gate = gate + dot(normed, wg_ref[pl.ds(first, w), :])
+        up = up + dot(normed, wu_ref[pl.ds(first, w), :])
     inner_ref[...] = (gate / (1.0 + jnp.exp(-gate)) * up).astype(BF16)
-    cols = pl.ds(pl.multiple_of(head * 2 * w, 2 * w), 2 * w)
-    acc = own_res.get()[:, cols].astype(F32)
-    acc = acc + sum(dot(mine[i].get()[...], wo_ref[pl.ds(block[i], eff), cols]) for i in range(4))
-    hid_ref[...] = acc.astype(BF16)
-
-
-def expert_rows(tokens, out_weight, w_gate, w_up, gain, mine, res, residual):
-    n, _, half = tokens[0].shape
-    w = res[0].shape[2]
-    outs = [sds((n * 4, w_gate.shape[1]), BF16), sds((residual.shape[0], 2 * w), BF16)]
-    scratch = [pltpu.VMEM((8, n * 4, w), F32)]
-    near = [*tokens, out_weight, w_gate, w_up]
-    return run(expert_body, "expert_rows", outs, near, [gain.reshape(1, -1), *mine, *res, residual], scratch)
+
+
+def expert_rows(tokens, early, out_weight, w_gate, w_up, gain, mine, residual):
+    _, n, w = early.shape
+    outs, leaving = [sds((n, w_gate.shape[1]), BF16)], [sds((residual.shape[0], 2 * w), BF16)]
+    near = [*tokens, early, out_weight, w_gate, w_up]
+    scratch = [pltpu.VMEM((8, n, w), BF16)]
+    far = [gain.reshape(1, -1), *mine, residual]
+    return run(expert_body, "expert_rows", outs, near, far, scratch, leaving=leaving)
 
 
 def down_body(near, far, outs, own):
-    out_ref = outs[0]
-    acc = sum(dot(near[k][...], near[4 + k][...]) for k in range(4))
+    w_ref, out_ref = near[4], outs[0]
+    block = head_blocks(near[0].shape[1])
+    acc = sum(dot(near[k][...], w_ref[pl.ds(block[k], near[k].shape[1]), :]) for k in range(4))
     width = acc.shape[1]
     a, b = fold(acc[:, : width // 2], acc[:, width // 2 :])
     out_ref[:, 0] = a.astype(BF16)
     out_ref[:, 1] = b.astype(BF16)
 
 
-def down(inners, w_cols):
+def down(inners, w_cols, after):
     rows = inners[0].shape[0]
-    width = w_cols[0].shape[1]
-    out = run(down_body, "down", [sds((rows // 8, 2, 8, width // 2), BF16)], [*inners, *w_cols], [])[0]
+    width = w_cols.shape[1]
+    out = run(down_body, "down", [sds((rows // 8, 2, 8, width // 2), BF16)], [*inners, w_cols], [], after=[after])[0]
     return out.reshape(rows // 4, 8, width // 2)
 
 
 def blend_body(near, far, outs, own):
-    y_ref, out_ref = near[0], outs[0]
-    rows = out_ref.shape[0]
-    routes, share = flip(far[1].get()[...], 1), flip(far[2].get()[...], 3)
-    cells = y_ref.shape[0] * 4
-    lane = iota((rows, cells), 1)
-    expert = (lane // 4).astype(F32)
-    mix = jnp.zeros((rows, cells), F32)
-    for k in range(routes.shape[1]):
-        mix = mix + jnp.where(routes[:, k : k + 1] == expert, share[:, k : k + 1], 0.0)
-    mix = jnp.where(rank_of(hits(routes, expert)) == (lane % 4).astype(F32), mix, 0.0)
-    m_hi, m_lo = hi_lo(mix)
+    y_ref, hi_ref, low_ref = near
     w = y_ref.shape[2]
     hid_ref = far[0].get()
     for f, part in enumerate(unfold(y_ref[...].astype(F32))):
         part = part.astype(BF16)
         hid = hid_ref[:, f * w : f * w + w].astype(F32)
-        out_ref[:, f * w : f * w + w] = (hid + (dot(m_hi, part) + dot(m_lo, part))).astype(BF16)
-
-
-def blend(returned, hidden, routes, route_weights):
-    out = sds(hidden.shape, BF16)
-    return run(blend_body, "blend", [out], [returned], [hidden, routes.T, route_weights.T])[0]
+        moe = dot(hi_ref[...], part) + dot(low_ref[...], part)
+        outs[0][:, f * w : f * w + w] = (hid + moe).astype(BF16)
+
+
+def blend(returned, mix, hidden):
+    return run(blend_body, "blend", [sds(hidden.shape, BF16)], [returned, *mix], [hidden])[0]
 
 
 def norm_body(near, far, outs, own):
@@ -513,21 +558,27 @@
     experts = lax.axis_size(REQ)
     chips = experts // 2
     out_weight = lax.all_gather(out_weight, "head", axis=0, tiled=True)
+    w_down_all = lax.all_gather(w_down[0], "head", axis=0, tiled=True)
     qa = lax.all_to_all(outset(queries, residual, routes, chips), ("z", "y"), 0, 0, tiled=True)
-    w_cols = to_heads(split_columns(w_down[0]))
     tables = slot_tables(slot_request, slot_page, slot_used, lengths, kv_cache, [qa])
     keep, send, res = attend_pages(tables, qa, swap_core(qa))
+    merged = merge(keep, swap_core(send))
+    cells = cells_table(routes, experts, merged)
     res = from_heads(res.reshape(experts, 8, -1))
-    arrived = lax.all_to_all(merge(keep, swap_core(send)), ("z", "y"), 0, 0, tiled=True)
-    attended, disp = owner_part(arrived, queries, new_kv, routes, experts)
+    arrived = lax.all_to_all(merged, ("z", "y"), 0, 0, tiled=True)
+    arrived, res, cells = lax.optimization_barrier((arrived, res, cells))
+    attended, disp = owner_part(arrived, queries, new_kv, cells, experts)
     tokens = lax.all_to_all(disp, REQ, 0, 0, tiled=True)
-    mine = from_heads(attended)
-    tokens, res, mine, w_cols = lax.optimization_barrier((tokens, res, mine, w_cols))
+    tokens, attended = lax.optimization_barrier((tokens, attended))
     out_weight, w_gate, w_up = fetch(tokens, out_weight, w_gate[0], w_up[0])
-    inner, hidden = expert_rows(from_heads(tokens), out_weight, w_gate, w_up, norm_gain, mine, res, residual)
-    expert_out = down(from_heads(inner), fetch(inner, *w_cols))
+    early = early_rows(tokens, out_weight, res)
+    others, mine = from_heads(tokens)[1:], from_heads(attended)
+    inner, hidden = expert_rows(others, early, out_weight, w_gate, w_up, norm_gain, mine, residual)
+    w_cols = fetch_columns(inner, w_down_all)
+    mix = mix_table(routes, route_weights, experts, inner)
+    expert_out = down(from_heads(inner), w_cols, mix[0])
     returned = lax.all_to_all(expert_out, REQ, 0, 0, tiled=True)
-    stream = blend(returned, hidden, routes, route_weights)
+    stream = blend(returned, mix, hidden)
     normed = norm_parts(from_heads(stream), next_gain)
     next_qkv = jnp.einsum("td,dcf->tcf", normed, next_weight, preferred_element_type=F32).astype(BF16)
     return stream, next_qkv

time: 157 us -> 180 us (1.15)
  blocking collectives: 46.4 us -> 76.2 us
  starting transfers between devices: 40.8 us -> 25.2 us
  waiting for transfers between devices: 23.5 us -> 30.9 us
  Pallas kernels: 26.4 us -> 28.6 us
    all_to_all x0 -> x1, blocking collectives: none -> 21.6 us  [local(): tokens = lax.all_to_all(disp, REQ, 0, 0, tiled=True)]
    ppermute x15, waiting for transfers between devices: 11.5 us -> 26.7 us  [from_heads(): lax.ppermute(x, 'head', [(i, (i + k) % n) for i in range(n)])]
    all_to_all x2 -> x1, starting transfers between devices: 16.1 us -> 4.45 us  [local(): arrived = lax.all_to_all(merged, ('z', 'y'), 0, 0, tiled=True)]
    all_to_all x1, blocking collectives: 18.3 us -> 26.5 us  [local(): returned = lax.all_to_all(expert_out, REQ, 0, 0, tiled=True)]
    all_to_all x2 -> x1, waiting for transfers between devices: 5.45 us -> 0.01 us  [local(): arrived = lax.all_to_all(merged, ('z', 'y'), 0, 0, tiled=True)]
    ppermute x3 -> x0, starting transfers between devices: 4.25 us -> none  [to_heads(): lax.ppermute(xs[k], 'head', [(i, (i + k) % n) for i in range(n)])]
    ppermute x3 -> x0, waiting for transfers between devices: 4.18 us -> none  [to_heads(): lax.ppermute(xs[k], 'head', [(i, (i + k) % n) for i in range(n)])]
    pallas_call x12 -> x14, Pallas kernels: 26.4 us -> 28.6 us  [the longest x13 27.4 us: run(): pl.pallas_call(kernel, name=name, out_shape=list(outs) + [pltpu.HBM(x.sha...]
  transfers between devices with their start and end apart: 23 -> 20, of which waited for: 13 -> 9; matrix products, arithmetic and copies ran while one was open for 0% -> 0% of each run, Pallas kernels for 11% -> 14%
where the time goes in v4:
time: 180 us; the launch traced here: 179 us
  blocking collectives  76.2 us (42%)
  waiting for transfers between devices  30.9 us (17%)
  Pallas kernels  28.6 us (16%)
  starting transfers between devices  25.2 us (14%)
  between operations  14.3 us (8%)
  local copies, waits for them, and re-layouts  2.32 us (1%)
    all_to_all x1, blocking collectives, local(): lax.all_to_all(outset(queries, residual, routes, chips), ('z', 'y'), 0, 0...  28.1 us
    pallas_call x13, Pallas kernels, run(): pl.pallas_call(kernel, name=name, out_shape=list(outs) + [pltpu.HBM(x.sha...  27.4 us
    ppermute x15, waiting for transfers between devices, from_heads(): lax.ppermute(x, 'head', [(i, (i + k) % n) for i in range(n)])  26.7 us
    all_to_all x1, blocking collectives, local(): returned = lax.all_to_all(expert_out, REQ, 0, 0, tiled=True)  26.5 us
    all_to_all x1, blocking collectives, local(): tokens = lax.all_to_all(disp, REQ, 0, 0, tiled=True)  21.6 us
    ppermute x15, starting transfers between devices, from_heads(): lax.ppermute(x, 'head', [(i, (i + k) % n) for i in range(n)])  18.2 us
    all_to_all x1, starting transfers between devices, local(): arrived = lax.all_to_all(merged, ('z', 'y'), 0, 0, tiled=True)  4.45 us
  transfers between devices with their start and end apart: 20, of which 9 were waited for; matrix products, arithmetic and copies ran while one was open for 0% of the time, Pallas kernels for 14%

profile of v4, /device:TPU:1, one launch (start us, length us, event | category | flops | bytes accessed | tf_op | source)
XLA Modules:
  0.0 178.8 jit_solution(17159894456039110999)
XLA Ops:
  7.2 0.7 all-gather.4.cloned.1.call-update
  8.0 0.7 all-gather.6.cloned.1.call-update
  8.7 1.4 outset.1
  10.1 28.1 %all_to_all.20.refs_4_.refs_7_ = bf16[32,32,256]{2,1,0:T(8,128)(2,1)S(1)} all-to-all(bf16[32,32,256]{2,1,0:T(8,128)(2,1)S(1)} %outset.1), channel_id=1, replica_groups=mesh['z'=8,'y'=4,'c'=2,'head'=4] {'z','y'}, dimensions={0} | all-to-all | bytes 1048576 | tf_op jit(solution)/shard_map/all_to_all | solution.py:562
  38.2 2.4 %collective-permute-start = (bf16[32,32,256]{2,1,0:T(8,128)(2,1)S(1)}, bf16[32,32,256]{2,1,0:T(8,128)(2,1)S(1)}, u32[]{:S(2)}, u32[]{:S(2)}) collective-permute-start(bf16[32,32,256]{2,1,0:T(8,128)(2,1)S(1)} %all_to_all.20.refs_4_.refs_7_), channel_id=1, source_target_pairs={{0,4},{4,0},{1,5},{5,1},{2,6},{6,2},{3,7},{7,3},{8,12},{12,8},{9,1... | collective-permute-start | bytes 1572872 | tf_op jit(solution)/shard_map/ppermute | solution.py:550
  40.6 2.3 %slot_tables.1 = (bf16[128,1024]{1,0:T(8,128)(2,1)S(1)}, f32[128,128]{1,0:T(8,128)S(1)}, f32[128,128]{1,0:T(8,128)S(1)}, f32[128,128]{1,0:T(8,128)S(1)}, bf16[10...) custom-call(s32[1,128]{1,0:T(1,128)} %bitcast.32, s32[1,128]{1,0:T(1,128)} %bitcast.33, ...), custom_call_target="tpu_custom_call" | custom-call | tf_op jit(solution)/shard_map/slot_tables/pallas_call | solution.py:81
  42.9 5.6 %attend_pages.1 = (bf16[32,48,128]{2,1,0:T(8,128)(2,1)S(1)}, bf16[32,48,128]{2,1,0:T(8,128)(2,1)S(1)}, bf16[32,2,8,256]{3,2,1,0:T(8,128)(2,1)}) custom-call(bf16[128,1024]{1,0:T(8,128)(2,1)S(1)} %get-tuple-element.29.refs_0_, f32[128,128]{1,0:T(8,128)S(1)} %get-tuple-element.30.refs_1_, f32[128,128]{1,0:T(8,128)S(1)} %get-tuple-element.31.refs_2_, ...), custom_call_target="tpu_custom_call" | custom-call | tf_op jit(solution)/shard_map/attend_pages/pallas_call | solution.py:81
  48.6 0.1 collective-permute-start.1
  48.7 1.7 collective-permute-done.1.refs_1_
  50.4 1.7 merge.1.refs_1_
  52.1 4.4 %all-to-all-start.1 = ((bf16[32,48,128]{2,1,0:T(8,128)(2,1)}), bf16[32,48,128]{2,1,0:T(8,128)(2,1)S(1)}, u32[]{:S(2)}, u32[]{:S(2)}) async-start(bf16[32,48,128]{2,1,0:T(8,128)(2,1)} %merge.1.refs_1_), calls=%async_computation.1 | async-start | bytes 786432 | tf_op jit(solution)/shard_map/all_to_all | solution.py:568
  56.6 1.3 collective-permute-start.2
  57.9 2.5 %collective-permute-start.3 = (bf16[64,8,256]{2,1,0:T(8,128)(2,1)}, bf16[64,8,256]{2,1,0:T(8,128)(2,1)S(1)}, u32[]{:S(2)}, u32[]{:S(2)}) collective-permute-start(bf16[64,8,256]{2,1,0:T(8,128)(2,1)} %bitcast.22), channel_id=1, source_target_pairs={{0,2},{1,3},{2,0},{3,1},{4,6},{5,7},{6,4},{7,5},{8,10},{9,11},{10,... | collective-permute-start | bytes 786440 | tf_op jit(solution)/shard_map/ppermute | solution.py:541
  60.3 1.2 collective-permute-start.4
  61.5 1.0 copy-done.1
  62.5 1.1 cells_table.1.refs_3_
  63.5 0.6 copy-done.2
  64.1 5.5 %collective-permute-done.2.refs_3_ = bf16[64,8,256]{2,1,0:T(8,128)(2,1)S(1)} collective-permute-done((bf16[64,8,256]{2,1,0:T(8,128)(2,1)}, bf16[64,8,256]{2,1,0:T(8,128)(2,1)S(1)}, u32[]{:S(2)}, u32[]{:S(2)}) %collective-permute-start.2) | collective-permute-done | bytes 262176 | tf_op jit(solution)/shard_map/ppermute | solution.py:541
  69.7 5.9 %collective-permute-done.3.refs_4_ = bf16[64,8,256]{2,1,0:T(8,128)(2,1)S(1)} collective-permute-done((bf16[64,8,256]{2,1,0:T(8,128)(2,1)}, bf16[64,8,256]{2,1,0:T(8,128)(2,1)S(1)}, u32[]{:S(2)}, u32[]{:S(2)}) %collective-permute-start.3) | collective-permute-done | bytes 262176 | tf_op jit(solution)/shard_map/ppermute | solution.py:541
  75.6 0.7 copy-done.5
  76.3 1.5 owner_part.1
  77.8 21.6 %all_to_all.21.refs_0_ = bf16[64,8,128]{2,1,0:T(8,128)(2,1)S(1)} all-to-all(bf16[64,8,128]{2,1,0:T(8,128)(2,1)S(1)} %get-tuple-element.41), channel_id=1, replica_groups=mesh['z'=8,'y'=4,'c'=2,'head'=4] {'z','y','c'}, dimensions={0} | all-to-all | bytes 262144 | tf_op jit(solution)/shard_map/all_to_all | solution.py:571
  99.4 1.2 collective-permute-start.6
  100.6 1.8 %collective-permute-start.7 = (bf16[64,8,128]{2,1,0:T(8,128)(2,1)S(1)}, bf16[64,8,128]{2,1,0:T(8,128)(2,1)}, u32[]{:S(2)}, u32[]{:S(2)}) collective-permute-start(bf16[64,8,128]{2,1,0:T(8,128)(2,1)S(1)} %all_to_all.21.refs_0_), channel_id=1, source_target_pairs={{0,3},{1,0},{2,1},{3,2},{4,7},{5,4},{6,5},{7,6},{8,11},{9,8},{10,9... | collective-permute-start | bytes 393224 | tf_op jit(solution)/shard_map/ppermute | solution.py:541
  102.4 0.3 collective-permute-start.10
  102.7 1.2 collective-permute-start.8
  103.9 11.3 %collective-permute-done.10.refs_11_ = bf16[16,256]{1,0:T(8,128)(2,1)S(1)} collective-permute-done((bf16[16,256]{1,0:T(8,128)(2,1)S(1)}, bf16[16,256]{1,0:T(8,128)(2,1)S(1)}, u32[]{:S(2)}, u32[]{:S(2)}) %collective-permute-start.10) | collective-permute-done | bytes 8224 | tf_op jit(solution)/shard_map/ppermute | solution.py:541
  115.2 0.9 collective-permute-start.9
  116.1 3.0 %fetch.1 = (bf16[1024,2048]{1,0:T(8,128)(2,1)S(1)}, bf16[2048,256]{1,0:T(8,128)(2,1)S(1)}, bf16[2048,256]{1,0:T(8,128)(2,1)S(1)}) custom-call(bf16[64,8,128]{2,1,0:T(8,128)(2,1)S(1)} %all_to_all.21.refs_0_, bf16[1024,2048]{1,0:T(8,128)(2,1)} %all-gather.4.cloned.1.call-done.refs_1_, bf16[2048,256]{1,0:T(8,128)(2,1)} %bitcast.19, bf16[2048,256]{1,0:T(8,128)(2,1)} %bitcast.20), custom_call_target="tpu_custom_call" | custom-call | tf_op jit(solution)/shard_map/fetch/pallas_call | solution.py:81
  119.1 2.0 %early_rows.1.refs_3_ = f32[8,256,256]{2,1,0:T(8,128)S(1)} custom-call(bf16[64,8,128]{2,1,0:T(8,128)(2,1)S(1)} %all_to_all.21.refs_0_, bf16[1024,2048]{1,0:T(8,128)(2,1)S(1)} %get-tuple-element.44.refs_1_.refs_4_, bf16[64,8,256]{2,1,0:T(8,128)(2,1)} %bitcast.24, bf16[64,8,256]{2,1,0:T(8,128)(2,1)} %copy-done.4, bf16[64,8,256]{2,1,0:T(8,128)(2,1)} %copy-done.5, ...), custom_call_target="tpu_custom_call" | custom-call | tf_op jit(solution)/shard_map/early_rows/pallas_call | solution.py:81
  121.1 4.0 %expert_rows.1 = (bf16[256,256]{1,0:T(8,128)(2,1)S(1)}, bf16[16,512]{1,0:T(8,128)(2,1)}) custom-call(bf16[64,8,128]{2,1,0:T(8,128)(2,1)S(1)} %collective-permute-done.5.refs_0_, bf16[64,8,128]{2,1,0:T(8,128)(2,1)S(1)} %collective-permute-done.6.refs_1_, bf16[64,8,128]{2,1,0:T(8,128)(2,1)} %collective-permute-done.7.refs_2_, ...), custom_call_target="tpu_custom_call" | custom-call | tf_op jit(solution)/shard_map/expert_rows/pallas_call | solution.py:81
  125.2 2.1 %collective-permute-start.12 = (bf16[256,256]{1,0:T(8,128)(2,1)S(1)}, bf16[256,256]{1,0:T(8,128)(2,1)S(1)}, u32[]{:S(2)}, u32[]{:S(2)}) collective-permute-start(bf16[256,256]{1,0:T(8,128)(2,1)S(1)} %get-tuple-element.52.after_ref.refs_2_.refs_0_), channel_id=1, source_target_pairs={{0,2},{1,3},{2,0},{3,1},{4,6},{5,7},{6,4},{7,5},{8,10},{9,11},{10,... | collective-permute-start | bytes 393224 | tf_op jit(solution)/shard_map/ppermute | solution.py:541
  127.3 2.0 %collective-permute-start.13 = (bf16[256,256]{1,0:T(8,128)(2,1)S(1)}, bf16[256,256]{1,0:T(8,128)(2,1)}, u32[]{:S(2)}, u32[]{:S(2)}) collective-permute-start(bf16[256,256]{1,0:T(8,128)(2,1)S(1)} %get-tuple-element.52.after_ref.refs_2_.refs_0_), channel_id=1, source_target_pairs={{0,3},{1,0},{2,1},{3,2},{4,7},{5,4},{6,5},{7,6},{8,11},{9,8},{10,9... | collective-permute-start | bytes 393224 | tf_op jit(solution)/shard_map/ppermute | solution.py:541
  129.3 1.2 all-gather.6.cloned.1.call-done
  130.4 1.2 fetch_columns.1.refs_4_
  131.7 1.1 mix_table.1
  132.8 2.4 %collective-permute-done.12.refs_2_ = bf16[256,256]{1,0:T(8,128)(2,1)S(1)} collective-permute-done((bf16[256,256]{1,0:T(8,128)(2,1)S(1)}, bf16[256,256]{1,0:T(8,128)(2,1)S(1)}, u32[]{:S(2)}, u32[]{:S(2)}) %collective-permute-start.12) | collective-permute-done | bytes 131104 | tf_op jit(solution)/shard_map/ppermute | solution.py:541
  135.2 1.4 down.1
  136.6 26.5 %all_to_all.22.refs_0_ = bf16[64,8,256]{2,1,0:T(8,128)(2,1)S(1)} all-to-all(bf16[64,8,256]{2,1,0:T(8,128)(2,1)S(1)} %bitcast.17), channel_id=1, replica_groups=mesh['z'=8,'y'=4,'c'=2,'head'=4] {'z','y','c'}, dimensions={0} | all-to-all | bytes 524288 | tf_op jit(solution)/shard_map/all_to_all | solution.py:580
  163.1 1.6 blend.1.refs_4_
  164.7 0.6 collective-permute-start.14
  165.3 1.5 collective-permute-start.15
  166.8 1.6 collective-permute-start.16
  168.4 0.4 collective-permute-done.14.refs_0_
  168.8 0.9 collective-permute-done.15.refs_1_
  169.7 0.2 collective-permute-done.16.refs_2_
  169.9 0.9 norm_parts.1
  170.8 1.1 convolution_convert_fusion
  (26 shorter events, 0.2 us)
Async XLA Ops:
  7.2 163.6 %copy-start = (bf16[2048,3,256]{2,0,1:T(8,128)(2,1)S(1)}, bf16[2048,3,256]{2,0,1:T(8,128)(2,1)}, u32[]{:S(2)}) copy-start(bf16[2048,3,256]{2,0,1:T(8,128)(2,1)} %param.33) | copy-start | bytes 9437188
  7.2 108.9 %all-gather.4.cloned.1.call-start = ((), (), s32[]{:S(2)}) async-start(), calls=%async_computation.4 | async-start | bytes 5242880 | tf_op jit(solution)/shard_map/all_gather | solution.py:560
  7.9 122.5 %all-gather.6.cloned.1.call-start = ((), (), s32[]{:S(2)}) async-start(), calls=%async_computation.5 | async-start | bytes 5242880 | tf_op jit(solution)/shard_map/all_gather | solution.py:561
  38.2 4.7 %collective-permute-start = (bf16[32,32,256]{2,1,0:T(8,128)(2,1)S(1)}, bf16[32,32,256]{2,1,0:T(8,128)(2,1)S(1)}, u32[]{:S(2)}, u32[]{:S(2)}) collective-permute-start(bf16[32,32,256]{2,1,0:T(8,128)(2,1)S(1)} %all_to_all.20.refs_4_.refs_7_), channel_id=1, source_target_pairs={{0,4},{4,0},{1,5},{5,1},{2,6},{6,2},{3,7},{7,3},{8,12},{12,8},{9,1... | collective-permute-start | bytes 1572872 | tf_op jit(solution)/shard_map/ppermute | solution.py:550
  48.6 1.8 %collective-permute-start.1 = (bf16[32,48,128]{2,1,0:T(8,128)(2,1)S(1)}, bf16[32,48,128]{2,1,0:T(8,128)(2,1)S(1)}, u32[]{:S(2)}, u32[]{:S(2)}) collective-permute-start(bf16[32,48,128]{2,1,0:T(8,128)(2,1)S(1)} %get-tuple-element.37), channel_id=1, source_target_pairs={{0,4},{4,0},{1,5},{5,1},{2,6},{6,2},{3,7},{7,3},{8,12},{12,8},{9,1... | collective-permute-start | bytes 1179656 | tf_op jit(solution)/shard_map/ppermute | solution.py:550
  52.1 24.2 %all-to-all-start.1 = ((bf16[32,48,128]{2,1,0:T(8,128)(2,1)}), bf16[32,48,128]{2,1,0:T(8,128)(2,1)S(1)}, u32[]{:S(2)}, u32[]{:S(2)}) async-start(bf16[32,48,128]{2,1,0:T(8,128)(2,1)} %merge.1.refs_1_), calls=%async_computation.1 | async-start | bytes 786432 | tf_op jit(solution)/shard_map/all_to_all | solution.py:568
  56.6 13.1 %collective-permute-start.2 = (bf16[64,8,256]{2,1,0:T(8,128)(2,1)}, bf16[64,8,256]{2,1,0:T(8,128)(2,1)S(1)}, u32[]{:S(2)}, u32[]{:S(2)}) collective-permute-start(bf16[64,8,256]{2,1,0:T(8,128)(2,1)} %bitcast.21), channel_id=1, source_target_pairs={{0,1},{1,2},{2,3},{3,0},{4,5},{5,6},{6,7},{7,4},{8,9},{9,10},{10,1... | collective-permute-start | bytes 786440 | tf_op jit(solution)/shard_map/ppermute | solution.py:541
  57.9 17.7 %collective-permute-start.3 = (bf16[64,8,256]{2,1,0:T(8,128)(2,1)}, bf16[64,8,256]{2,1,0:T(8,128)(2,1)S(1)}, u32[]{:S(2)}, u32[]{:S(2)}) collective-permute-start(bf16[64,8,256]{2,1,0:T(8,128)(2,1)} %bitcast.22), channel_id=1, source_target_pairs={{0,2},{1,3},{2,0},{3,1},{4,6},{5,7},{6,4},{7,5},{8,10},{9,11},{10,... | collective-permute-start | bytes 786440 | tf_op jit(solution)/shard_map/ppermute | solution.py:541
  60.3 16.0 %collective-permute-start.4 = (bf16[64,8,256]{2,1,0:T(8,128)(2,1)}, bf16[64,8,256]{2,1,0:T(8,128)(2,1)}, u32[]{:S(2)}, u32[]{:S(2)}) collective-permute-start(bf16[64,8,256]{2,1,0:T(8,128)(2,1)} %bitcast.23), channel_id=1, source_target_pairs={{0,3},{1,0},{2,1},{3,2},{4,7},{5,4},{6,5},{7,6},{8,11},{9,8},{10,9... | collective-permute-start | bytes 786440 | tf_op jit(solution)/shard_map/ppermute | solution.py:541
  61.5 1.0 copy-start.1
  63.5 0.6 copy-start.2
  69.7 5.9 %copy-start.4 = (bf16[64,8,256]{2,1,0:T(8,128)(2,1)}, bf16[64,8,256]{2,1,0:T(8,128)(2,1)S(1)}, u32[]{:S(2)}) copy-start(bf16[64,8,256]{2,1,0:T(8,128)(2,1)S(1)} %collective-permute-done.2.refs_3_) | copy-start | bytes 786436
  75.6 0.7 copy-start.5
  77.8 43.3 %copy-start.3 = (bf16[16,256]{1,0:T(8,128)(2,1)}, bf16[16,256]{1,0:T(8,128)(2,1)S(1)}, u32[]{:S(2)}) copy-start(bf16[16,256]{1,0:T(8,128)(2,1)S(1)} %get-tuple-element.51.refs_8_) | copy-start | bytes 24580
  99.4 21.7 %collective-permute-start.5 = (bf16[64,8,128]{2,1,0:T(8,128)(2,1)S(1)}, bf16[64,8,128]{2,1,0:T(8,128)(2,1)S(1)}, u32[]{:S(2)}, u32[]{:S(2)}) collective-permute-start(bf16[64,8,128]{2,1,0:T(8,128)(2,1)S(1)} %all_to_all.21.refs_0_), channel_id=1, source_target_pairs={{0,1},{1,2},{2,3},{3,0},{4,5},{5,6},{6,7},{7,4},{8,9},{9,10},{10,1... | collective-permute-start | bytes 393224 | tf_op jit(solution)/shard_map/ppermute | solution.py:541
  99.4 21.7 %collective-permute-start.6 = (bf16[64,8,128]{2,1,0:T(8,128)(2,1)S(1)}, bf16[64,8,128]{2,1,0:T(8,128)(2,1)S(1)}, u32[]{:S(2)}, u32[]{:S(2)}) collective-permute-start(bf16[64,8,128]{2,1,0:T(8,128)(2,1)S(1)} %all_to_all.21.refs_0_), channel_id=1, source_target_pairs={{0,2},{1,3},{2,0},{3,1},{4,6},{5,7},{6,4},{7,5},{8,10},{9,11},{10,... | collective-permute-start | bytes 393224 | tf_op jit(solution)/shard_map/ppermute | solution.py:541
  100.6 20.5 %collective-permute-start.7 = (bf16[64,8,128]{2,1,0:T(8,128)(2,1)S(1)}, bf16[64,8,128]{2,1,0:T(8,128)(2,1)}, u32[]{:S(2)}, u32[]{:S(2)}) collective-permute-start(bf16[64,8,128]{2,1,0:T(8,128)(2,1)S(1)} %all_to_all.21.refs_0_), channel_id=1, source_target_pairs={{0,3},{1,0},{2,1},{3,2},{4,7},{5,4},{6,5},{7,6},{8,11},{9,8},{10,9... | collective-permute-start | bytes 393224 | tf_op jit(solution)/shard_map/ppermute | solution.py:541
  102.4 12.8 %collective-permute-start.10 = (bf16[16,256]{1,0:T(8,128)(2,1)S(1)}, bf16[16,256]{1,0:T(8,128)(2,1)S(1)}, u32[]{:S(2)}, u32[]{:S(2)}) collective-permute-start(bf16[16,256]{1,0:T(8,128)(2,1)S(1)} %get-tuple-element.51.refs_8_), channel_id=1, source_target_pairs={{0,3},{1,0},{2,1},{3,2},{4,7},{5,4},{6,5},{7,6},{8,11},{9,8},{10,9... | collective-permute-start | bytes 24584 | tf_op jit(solution)/shard_map/ppermute | solution.py:541
  102.7 18.4 %collective-permute-start.8 = (bf16[16,256]{1,0:T(8,128)(2,1)S(1)}, bf16[16,256]{1,0:T(8,128)(2,1)}, u32[]{:S(2)}, u32[]{:S(2)}) collective-permute-start(bf16[16,256]{1,0:T(8,128)(2,1)S(1)} %get-tuple-element.51.refs_8_), channel_id=1, source_target_pairs={{0,1},{1,2},{2,3},{3,0},{4,5},{5,6},{6,7},{7,4},{8,9},{9,10},{10,1... | collective-permute-start | bytes 24584 | tf_op jit(solution)/shard_map/ppermute | solution.py:541
  115.2 5.8 %copy-start.6 = (bf16[16,256]{1,0:T(8,128)(2,1)}, bf16[16,256]{1,0:T(8,128)(2,1)S(1)}, u32[]{:S(2)}) copy-start(bf16[16,256]{1,0:T(8,128)(2,1)S(1)} %collective-permute-done.10.refs_11_) | copy-start | bytes 24580
  115.2 5.9 %collective-permute-start.9 = (bf16[16,256]{1,0:T(8,128)(2,1)S(1)}, bf16[16,256]{1,0:T(8,128)(2,1)}, u32[]{:S(2)}, u32[]{:S(2)}) collective-permute-start(bf16[16,256]{1,0:T(8,128)(2,1)S(1)} %get-tuple-element.51.refs_8_), channel_id=1, source_target_pairs={{0,2},{1,3},{2,0},{3,1},{4,6},{5,7},{6,4},{7,5},{8,10},{9,11},{10,... | collective-permute-start | bytes 24584 | tf_op jit(solution)/shard_map/ppermute | solution.py:541
  125.1 7.7 %collective-permute-start.11 = (bf16[256,256]{1,0:T(8,128)(2,1)S(1)}, bf16[256,256]{1,0:T(8,128)(2,1)S(1)}, u32[]{:S(2)}, u32[]{:S(2)}) collective-permute-start(bf16[256,256]{1,0:T(8,128)(2,1)S(1)} %get-tuple-element.52.after_ref.refs_2_.refs_0_), channel_id=1, source_target_pairs={{0,1},{1,2},{2,3},{3,0},{4,5},{5,6},{6,7},{7,4},{8,9},{9,10},{10,1... | collective-permute-start | bytes 393224 | tf_op jit(solution)/shard_map/ppermute | solution.py:541
  125.2 10.0 %collective-permute-start.12 = (bf16[256,256]{1,0:T(8,128)(2,1)S(1)}, bf16[256,256]{1,0:T(8,128)(2,1)S(1)}, u32[]{:S(2)}, u32[]{:S(2)}) collective-permute-start(bf16[256,256]{1,0:T(8,128)(2,1)S(1)} %get-tuple-element.52.after_ref.refs_2_.refs_0_), channel_id=1, source_target_pairs={{0,2},{1,3},{2,0},{3,1},{4,6},{5,7},{6,4},{7,5},{8,10},{9,11},{10,... | collective-permute-start | bytes 393224 | tf_op jit(solution)/shard_map/ppermute | solution.py:541
  127.3 7.9 %collective-permute-start.13 = (bf16[256,256]{1,0:T(8,128)(2,1)S(1)}, bf16[256,256]{1,0:T(8,128)(2,1)}, u32[]{:S(2)}, u32[]{:S(2)}) collective-permute-start(bf16[256,256]{1,0:T(8,128)(2,1)S(1)} %get-tuple-element.52.after_ref.refs_2_.refs_0_), channel_id=1, source_target_pairs={{0,3},{1,0},{2,1},{3,2},{4,7},{5,4},{6,5},{7,6},{8,11},{9,8},{10,9... | collective-permute-start | bytes 393224 | tf_op jit(solution)/shard_map/ppermute | solution.py:541
  164.7 4.1 %collective-permute-start.14 = (bf16[16,512]{1,0:T(8,128)(2,1)}, bf16[16,512]{1,0:T(8,128)(2,1)S(1)}, u32[]{:S(2)}, u32[]{:S(2)}) collective-permute-start(bf16[16,512]{1,0:T(8,128)(2,1)} %blend.1.refs_4_), channel_id=1, source_target_pairs={{0,1},{1,2},{2,3},{3,0},{4,5},{5,6},{6,7},{7,4},{8,9},{9,10},{10,1... | collective-permute-start | bytes 49160 | tf_op jit(solution)/shard_map/ppermute | solution.py:541
  165.3 4.3 %collective-permute-start.15 = (bf16[16,512]{1,0:T(8,128)(2,1)}, bf16[16,512]{1,0:T(8,128)(2,1)S(1)}, u32[]{:S(2)}, u32[]{:S(2)}) collective-permute-start(bf16[16,512]{1,0:T(8,128)(2,1)} %blend.1.refs_4_), channel_id=1, source_target_pairs={{0,2},{1,3},{2,0},{3,1},{4,6},{5,7},{6,4},{7,5},{8,10},{9,11},{10,... | collective-permute-start | bytes 49160 | tf_op jit(solution)/shard_map/ppermute | solution.py:541
  166.8 3.1 %collective-permute-start.16 = (bf16[16,512]{1,0:T(8,128)(2,1)}, bf16[16,512]{1,0:T(8,128)(2,1)S(1)}, u32[]{:S(2)}, u32[]{:S(2)}) collective-permute-start(bf16[16,512]{1,0:T(8,128)(2,1)} %blend.1.refs_4_), channel_id=1, source_target_pairs={{0,3},{1,0},{2,1},{3,2},{4,7},{5,4},{6,5},{7,6},{8,11},{9,8},{10,9... | collective-permute-start | bytes 49160 | tf_op jit(solution)/shard_map/ppermute | solution.py:541
Sparse Core Ops, SparseCore 0:
  9.8 57.6 all-gather.3
  69.3 61.0 all-gather.5

commit v5 on v4

--- a/solution.py
+++ b/solution.py
@@ -30,6 +30,10 @@
         return self.buf
 
 
+def pin(xs):
+    return [pltpu.with_memory_space_constraint(x, pltpu.HBM) for x in xs]
+
+
 class Leaving:
     def __init__(self, buf, copy):
         self.buf, self.copy, self.sent = buf, copy, False
@@ -39,8 +43,11 @@
         self.sent = True
 
 
-def run(body, name, outs, near, far, scratch=(), after=(), moves=(), leaving=()):
-    nn, nf, na, nm, no, nl = len(near), len(far), len(after), len(moves), len(outs), len(leaving)
+def run(body, name, outs, near, far, scratch=(), after=(), moves=(), leaving=(), after_hbm=()):
+    nn, nf, nm, no, nl = len(near), len(far), len(moves), len(outs), len(leaving)
+    after = [*after, *pin(after_hbm)]
+    na = len(after)
+    nh = len(after_hbm)
     parts = 4
 
     def kernel(*refs):
@@ -74,9 +81,6 @@
         for copy in moving:
             copy.wait()
 
-    def pin(xs):
-        return [pltpu.with_memory_space_constraint(x, pltpu.HBM) for x in xs]
-
     hbm, any_space = pl.BlockSpec(memory_space=pltpu.HBM), pl.BlockSpec(memory_space=pl.ANY)
     return pl.pallas_call(
         kernel,
@@ -84,7 +88,7 @@
         out_shape=list(outs)
         + [pltpu.HBM(x.shape, x.dtype) for x in leaving]
         + [sds(x.shape, x.dtype) for x in moves],
-        in_specs=[VM] * nn + [hbm] * nf + [any_space] * na + [hbm] * nm,
+        in_specs=[VM] * nn + [hbm] * nf + [any_space] * (na - nh) + [hbm] * (nh + nm),
         out_specs=[VM] * no + [hbm] * nl + [VM] * nm,
         scratch_shapes=[pltpu.VMEM(x.shape, x.dtype) for x in (*far, *leaving)]
         + [pltpu.SemaphoreType.DMA((max(n, 1),)) for n in (nf, nm * parts, nl)]
@@ -299,24 +303,30 @@
     return run(lambda *_: None, "fetch", [], [], [], after=[after], moves=arrays)
 
 
-def column_kernel(w_ref, after_ref, out_ref, sem):
-    width = out_ref.shape[1]
-    cols = pl.ds(pl.multiple_of(head_id() * width, width), width)
-    copy = pltpu.make_async_copy(w_ref.at[:, cols], out_ref, sem)
-    copy.start()
-    copy.wait()
-
-
-def fetch_columns(after, w):
+def split_kernel(w_ref, after_ref, *refs):
+    outs, sems = refs[:4], refs[4]
+    width = outs[0].shape[1]
+    copies = []
+    for k in range(4):
+        cols = pl.ds(pl.multiple_of(((head_id() + k) % 4) * width, width), width)
+        copies.append(pltpu.make_async_copy(w_ref.at[:, cols], outs[k], sems.at[k]))
+    for copy in copies:
+        copy.start()
+    for copy in copies:
+        copy.wait()
+
+
+def split_columns(w, after):
+    hbm = pl.BlockSpec(memory_space=pltpu.HBM)
     return pl.pallas_call(
-        column_kernel,
-        name="fetch_columns",
-        out_shape=sds((w.shape[0], w.shape[1] // 4), w.dtype),
-        in_specs=[pl.BlockSpec(memory_space=pltpu.HBM), pl.BlockSpec(memory_space=pl.ANY)],
-        out_specs=VM,
-        scratch_shapes=[pltpu.SemaphoreType.DMA],
+        split_kernel,
+        name="split_columns",
+        out_shape=[pltpu.HBM((w.shape[0], w.shape[1] // 4), w.dtype)] * 4,
+        in_specs=[hbm] * 2,
+        out_specs=[hbm] * 4,
+        scratch_shapes=[pltpu.SemaphoreType.DMA((4,))],
         compiler_params=VLIM,
-    )(pltpu.with_memory_space_constraint(w, pltpu.HBM), after)
+    )(*pin([w, after]))
 
 
 def cells_body(near, far, outs, own):
@@ -327,7 +337,7 @@
 
 def cells_table(routes, experts, after):
     out = sds((2 * routes.shape[0], experts * 8), BF16)
-    return run(cells_body, "cells_table", [out], [], [routes.T], after=[after])[0]
+    return run(cells_body, "cells_table", [out], [], [routes.T], after_hbm=[after])[0]
 
 
 def mix_body(near, far, outs, own):
@@ -371,7 +381,8 @@
         new = jnp.exp(own - top)
         v = nkv[:, 2 * HD + HD * h : 2 * HD + HD * h + HD]
         att.append((n + new * v) / (den + new))
-    att_ref, disp_ref = outs
+    att_ref, disp = outs
+    disp_ref = disp.buf
     att_ref[...] = jnp.concatenate(att, axis=1).astype(BF16)
     both = jnp.concatenate(att, axis=0).astype(BF16)
     out = lax.dot_general(far[2].get()[...], both, (((0,), (0,)), ((), ())), preferred_element_type=F32)
@@ -379,8 +390,8 @@
 
 
 def owner_part(parts, queries, new_kv, cells, experts):
-    outs = [sds(queries.shape, BF16), sds((experts, 8, HD), BF16)]
-    return run(owner_body, "owner_part", outs, [parts], [queries, new_kv, cells])
+    outs, leaving = [sds(queries.shape, BF16)], [sds((experts, 8, HD), BF16)]
+    return run(owner_body, "owner_part", outs, [parts], [queries, new_kv, cells], leaving=leaving)
 
 
 def flip(x, terms):
@@ -488,9 +499,8 @@
 
 
 def down_body(near, far, outs, own):
-    w_ref, out_ref = near[4], outs[0]
-    block = head_blocks(near[0].shape[1])
-    acc = sum(dot(near[k][...], w_ref[pl.ds(block[k], near[k].shape[1]), :]) for k in range(4))
+    out_ref = outs[0]
+    acc = sum(dot(near[k][...], near[4 + k][...]) for k in range(4))
     width = acc.shape[1]
     a, b = fold(acc[:, : width // 2], acc[:, width // 2 :])
     out_ref[:, 0] = a.astype(BF16)
@@ -499,8 +509,8 @@
 
 def down(inners, w_cols, after):
     rows = inners[0].shape[0]
-    width = w_cols.shape[1]
-    out = run(down_body, "down", [sds((rows // 8, 2, 8, width // 2), BF16)], [*inners, w_cols], [], after=[after])[0]
+    width = w_cols[0].shape[1]
+    out = run(down_body, "down", [sds((rows // 8, 2, 8, width // 2), BF16)], [*inners, *w_cols], [], after=[after])[0]
     return out.reshape(rows // 4, 8, width // 2)
 
 
@@ -558,23 +568,23 @@
     experts = lax.axis_size(REQ)
     chips = experts // 2
     out_weight = lax.all_gather(out_weight, "head", axis=0, tiled=True)
-    w_down_all = lax.all_gather(w_down[0], "head", axis=0, tiled=True)
     qa = lax.all_to_all(outset(queries, residual, routes, chips), ("z", "y"), 0, 0, tiled=True)
     tables = slot_tables(slot_request, slot_page, slot_used, lengths, kv_cache, [qa])
     keep, send, res = attend_pages(tables, qa, swap_core(qa))
     merged = merge(keep, swap_core(send))
+    w_cols = to_heads(split_columns(w_down[0], merged))
     cells = cells_table(routes, experts, merged)
     res = from_heads(res.reshape(experts, 8, -1))
     arrived = lax.all_to_all(merged, ("z", "y"), 0, 0, tiled=True)
-    arrived, res, cells = lax.optimization_barrier((arrived, res, cells))
+    arrived, cells = lax.optimization_barrier((arrived, cells))
     attended, disp = owner_part(arrived, queries, new_kv, cells, experts)
     tokens = lax.all_to_all(disp, REQ, 0, 0, tiled=True)
-    tokens, attended = lax.optimization_barrier((tokens, attended))
+    tokens, attended, res, w_cols = lax.optimization_barrier((tokens, attended, res, w_cols))
     out_weight, w_gate, w_up = fetch(tokens, out_weight, w_gate[0], w_up[0])
     early = early_rows(tokens, out_weight, res)
     others, mine = from_heads(tokens)[1:], from_heads(attended)
     inner, hidden = expert_rows(others, early, out_weight, w_gate, w_up, norm_gain, mine, residual)
-    w_cols = fetch_columns(inner, w_down_all)
+    w_cols = fetch(inner, *w_cols)
     mix = mix_table(routes, route_weights, experts, inner)
     expert_out = down(from_heads(inner), w_cols, mix[0])
     returned = lax.all_to_all(expert_out, REQ, 0, 0, tiled=True)

time: 180 us -> 188 us (1.044)
  Pallas kernels: 28.6 us -> 61.6 us
  blocking collectives: 76.2 us -> 47.6 us
  starting transfers between devices: 25.2 us -> 40.2 us
  waiting for transfers between devices: 30.9 us -> 21.3 us
    pallas_call x1, Pallas kernels: 1.23 us -> 32.9 us  [split_columns(): pl.pallas_call(split_kernel, name='split_columns', out_shape=[pltpu.HBM((...]
    all_to_all x1 -> x0, blocking collectives: 21.6 us -> none  [local(): tokens = lax.all_to_all(disp, REQ, 0, 0, tiled=True)]
    ppermute x15, waiting for transfers between devices: 26.7 us -> 7.82 us  [from_heads(): lax.ppermute(x, 'head', [(i, (i + k) % n) for i in range(n)])]
    all_to_all x0 -> x1, starting transfers between devices: none -> 11.8 us  [local(): tokens = lax.all_to_all(disp, REQ, 0, 0, tiled=True)]
    all_to_all x0 -> x1, waiting for transfers between devices: none -> 11.1 us  [local(): tokens = lax.all_to_all(disp, REQ, 0, 0, tiled=True)]
    all_to_all x1, blocking collectives: 26.5 us -> 19.5 us  [local(): returned = lax.all_to_all(expert_out, REQ, 0, 0, tiled=True)]
    ppermute x0 -> x3, starting transfers between devices: none -> 2.91 us  [to_heads(): lax.ppermute(xs[k], 'head', [(i, (i + k) % n) for i in range(n)])]
    pallas_call x13 -> x14, Pallas kernels: 27.4 us -> 28.7 us  [run(): pl.pallas_call(kernel, name=name, out_shape=list(outs) + [pltpu.HBM(x.sha...]
  transfers between devices with their start and end apart: 20 -> 23, of which waited for: 9 -> 8; matrix products, arithmetic and copies ran while one was open for 0% -> 0% of each run, Pallas kernels for 14% -> 29%
where the time goes in v5:
time: 188 us; the launch traced here: 187 us
  Pallas kernels  61.6 us (33%)
  blocking collectives  47.6 us (25%)
  starting transfers between devices  40.2 us (21%)
  waiting for transfers between devices  21.3 us (11%)
  between operations  14.3 us (8%)
    pallas_call x1, Pallas kernels, split_columns(): pl.pallas_call(split_kernel, name='split_columns', out_shape=[pltpu.HBM((...  32.9 us
    pallas_call x14, Pallas kernels, run(): pl.pallas_call(kernel, name=name, out_shape=list(outs) + [pltpu.HBM(x.sha...  28.7 us
    all_to_all x1, blocking collectives, local(): lax.all_to_all(outset(queries, residual, routes, chips), ('z', 'y'), 0, 0...  28.1 us
    all_to_all x1, blocking collectives, local(): returned = lax.all_to_all(expert_out, REQ, 0, 0, tiled=True)  19.5 us
    ppermute x15, starting transfers between devices, from_heads(): lax.ppermute(x, 'head', [(i, (i + k) % n) for i in range(n)])  18.6 us
    all_to_all x1, starting transfers between devices, local(): tokens = lax.all_to_all(disp, REQ, 0, 0, tiled=True)  11.8 us
    all_to_all x1, waiting for transfers between devices, local(): tokens = lax.all_to_all(disp, REQ, 0, 0, tiled=True)  11.1 us
    ppermute x15, waiting for transfers between devices, from_heads(): lax.ppermute(x, 'head', [(i, (i + k) % n) for i in range(n)])  7.82 us
  transfers between devices with their start and end apart: 23, of which 8 were waited for; matrix products, arithmetic and copies ran while one was open for 0% of the time, Pallas kernels for 29%

profile of v5, /device:TPU:1, one launch (start us, length us, event | category | flops | bytes accessed | tf_op | source)
XLA Modules:
  0.0 187.5 jit_solution(14880027512302318934)
XLA Ops:
  7.2 0.7 all-gather.2.cloned.1.call-update
  7.9 1.6 outset.1
  9.5 28.1 %all_to_all.20.refs_4_.refs_7_ = bf16[32,32,256]{2,1,0:T(8,128)(2,1)S(1)} all-to-all(bf16[32,32,256]{2,1,0:T(8,128)(2,1)S(1)} %outset.1), channel_id=1, replica_groups=mesh['z'=8,'y'=4,'c'=2,'head'=4] {'z','y'}, dimensions={0} | all-to-all | bytes 1048576 | tf_op jit(solution)/shard_map/all_to_all | solution.py:571
  37.6 2.4 %collective-permute-start = (bf16[32,32,256]{2,1,0:T(8,128)(2,1)S(1)}, bf16[32,32,256]{2,1,0:T(8,128)(2,1)S(1)}, u32[]{:S(2)}, u32[]{:S(2)}) collective-permute-start(bf16[32,32,256]{2,1,0:T(8,128)(2,1)S(1)} %all_to_all.20.refs_4_.refs_7_), channel_id=1, source_target_pairs={{0,4},{4,0},{1,5},{5,1},{2,6},{6,2},{3,7},{7,3},{8,12},{12,8},{9,1... | collective-permute-start | bytes 1572872 | tf_op jit(solution)/shard_map/ppermute | solution.py:560
  40.0 2.3 %slot_tables.1 = (bf16[128,1024]{1,0:T(8,128)(2,1)S(1)}, f32[128,128]{1,0:T(8,128)S(1)}, f32[128,128]{1,0:T(8,128)S(1)}, f32[128,128]{1,0:T(8,128)S(1)}, bf16[10...) custom-call(s32[1,128]{1,0:T(1,128)} %bitcast.32, s32[1,128]{1,0:T(1,128)} %bitcast.33, ...), custom_call_target="tpu_custom_call" | custom-call | tf_op jit(solution)/shard_map/slot_tables/pallas_call | solution.py:85
  42.4 5.6 %attend_pages.1 = (bf16[32,48,128]{2,1,0:T(8,128)(2,1)S(1)}, bf16[32,48,128]{2,1,0:T(8,128)(2,1)S(1)}, bf16[32,2,8,256]{3,2,1,0:T(8,128)(2,1)}) custom-call(bf16[128,1024]{1,0:T(8,128)(2,1)S(1)} %get-tuple-element.41.refs_0_, f32[128,128]{1,0:T(8,128)S(1)} %get-tuple-element.42.refs_1_, f32[128,128]{1,0:T(8,128)S(1)} %get-tuple-element.43.refs_2_, ...), custom_call_target="tpu_custom_call" | custom-call | tf_op jit(solution)/shard_map/attend_pages/pallas_call | solution.py:85
  48.0 0.1 collective-permute-start.1
  48.2 1.7 collective-permute-done.1.refs_1_
  49.8 1.7 merge.1.refs_1_.after_ref
  51.6 4.4 %all-to-all-start.1 = ((bf16[32,48,128]{2,1,0:T(8,128)(2,1)}), bf16[32,48,128]{2,1,0:T(8,128)(2,1)S(1)}, u32[]{:S(2)}, u32[]{:S(2)}) async-start(bf16[32,48,128]{2,1,0:T(8,128)(2,1)} %merge.1.refs_1_.after_ref), calls=%async_computation.1 | async-start | bytes 786432 | tf_op jit(solution)/shard_map/all_to_all | solution.py:578
  56.0 1.3 collective-permute-start.2
  57.3 2.5 %collective-permute-start.3 = (bf16[64,8,256]{2,1,0:T(8,128)(2,1)}, bf16[64,8,256]{2,1,0:T(8,128)(2,1)}, u32[]{:S(2)}, u32[]{:S(2)}) collective-permute-start(bf16[64,8,256]{2,1,0:T(8,128)(2,1)} %bitcast.22), channel_id=1, source_target_pairs={{0,2},{1,3},{2,0},{3,1},{4,6},{5,7},{6,4},{7,5},{8,10},{9,11},{10,... | collective-permute-start | bytes 786440 | tf_op jit(solution)/shard_map/ppermute | solution.py:551
  59.8 1.1 collective-permute-start.4
  60.9 32.9 %split_columns.1 = (bf16[256,512]{1,0:T(8,128)(2,1)}, bf16[256,512]{1,0:T(8,128)(2,1)}, bf16[256,512]{1,0:T(8,128)(2,1)}, bf16[256,512]{1,0:T(8,128)(2,1)}) custom-call(bf16[256,2048]{1,0:T(8,128)(2,1)} %bitcast.20, bf16[32,48,128]{2,1,0:T(8,128)(2,1)} %merge.1.refs_1_.after_ref), custom_call_target="tpu_custom_call" | custom-call | tf_op jit(solution)/shard_map/split_columns/pallas_call | solution.py:321
  93.8 0.4 collective-permute-start.5
  94.2 0.9 collective-permute-start.6
  95.1 0.7 copy-done.3
  95.8 1.6 collective-permute-start.7
  97.4 1.1 cells_table.1.refs_3_
  98.5 0.6 copy-done.1
  99.1 2.1 %owner_part.1 = (bf16[16,256]{1,0:T(8,128)(2,1)S(1)}, bf16[64,8,128]{2,1,0:T(8,128)(2,1)}) custom-call(bf16[32,48,128]{2,1,0:T(8,128)(2,1)S(1)} %all-to-all-done.1.refs_0_, bf16[16,256]{1,0:T(8,128)(2,1)} %refs_1_.3, bf16[16,2,256]{2,1,0:T(2,128)(2,1)} %refs_2_.1, bf16[32,512]{1,0:T(8,128)(2,1)} %copy-done.1), custom_call_target="tpu_custom_call" | custom-call | tf_op jit(solution)/shard_map/owner_part/pallas_call | solution.py:85
  101.3 11.8 %all-to-all-start.2 = ((bf16[64,8,128]{2,1,0:T(8,128)(2,1)}), bf16[64,8,128]{2,1,0:T(8,128)(2,1)S(1)}, u32[]{:S(2)}, u32[]{:S(2)}) async-start(bf16[64,8,128]{2,1,0:T(8,128)(2,1)} %get-tuple-element.52), calls=%async_computation.2 | async-start | bytes 262144 | tf_op jit(solution)/shard_map/all_to_all | solution.py:581
  113.1 11.1 %all-to-all-done.2.refs_0_ = bf16[64,8,128]{2,1,0:T(8,128)(2,1)S(1)} async-done(((bf16[64,8,128]{2,1,0:T(8,128)(2,1)}), bf16[64,8,128]{2,1,0:T(8,128)(2,1)S(1)}, u32[]{:S(2)}, u32[]{:S(2)}) %all-to-all-start.2) | async-done | bytes 131104 | tf_op jit(solution)/shard_map/all_to_all | solution.py:581
  124.2 1.0 collective-permute-start.10
  125.2 0.4 collective-permute-start.8
  125.6 2.5 %collective-permute-start.9 = (bf16[64,8,128]{2,1,0:T(8,128)(2,1)S(1)}, bf16[64,8,128]{2,1,0:T(8,128)(2,1)}, u32[]{:S(2)}, u32[]{:S(2)}) collective-permute-start(bf16[64,8,128]{2,1,0:T(8,128)(2,1)S(1)} %all-to-all-done.2.refs_0_), channel_id=1, source_target_pairs={{0,2},{1,3},{2,0},{3,1},{4,6},{5,7},{6,4},{7,5},{8,10},{9,11},{10,... | collective-permute-start | bytes 393224 | tf_op jit(solution)/shard_map/ppermute | solution.py:551
  128.1 0.3 collective-permute-start.11
  128.5 1.5 collective-permute-start.12
  129.9 2.6 %collective-permute-done.11.refs_9_ = bf16[16,256]{1,0:T(8,128)(2,1)S(1)} collective-permute-done((bf16[16,256]{1,0:T(8,128)(2,1)S(1)}, bf16[16,256]{1,0:T(8,128)(2,1)S(1)}, u32[]{:S(2)}, u32[]{:S(2)}) %collective-permute-start.11) | collective-permute-done | bytes 8224 | tf_op jit(solution)/shard_map/ppermute | solution.py:551
  132.5 1.9 %collective-permute-start.13 = (bf16[16,256]{1,0:T(8,128)(2,1)S(1)}, bf16[16,256]{1,0:T(8,128)(2,1)}, u32[]{:S(2)}, u32[]{:S(2)}) collective-permute-start(bf16[16,256]{1,0:T(8,128)(2,1)S(1)} %get-tuple-element.67.refs_8_), channel_id=1, source_target_pairs={{0,3},{1,0},{2,1},{3,2},{4,7},{5,4},{6,5},{7,6},{8,11},{9,8},{10,9... | collective-permute-start | bytes 24584 | tf_op jit(solution)/shard_map/ppermute | solution.py:551
  134.4 2.9 %fetch.2 = (bf16[1024,2048]{1,0:T(8,128)(2,1)S(1)}, bf16[2048,256]{1,0:T(8,128)(2,1)S(1)}, bf16[2048,256]{1,0:T(8,128)(2,1)S(1)}) custom-call(bf16[64,8,128]{2,1,0:T(8,128)(2,1)S(1)} %all-to-all-done.2.refs_0_, bf16[1024,2048]{1,0:T(8,128)(2,1)} %all-gather.2.cloned.1.call-done.refs_1_, bf16[2048,256]{1,0:T(8,128)(2,1)} %bitcast.18, bf16[2048,256]{1,0:T(8,128)(2,1)} %bitcast.19), custom_call_target="tpu_custom_call" | custom-call | tf_op jit(solution)/shard_map/fetch/pallas_call | solution.py:85
  137.3 1.9 %early_rows.1.refs_3_ = f32[8,256,256]{2,1,0:T(8,128)S(1)} custom-call(bf16[64,8,128]{2,1,0:T(8,128)(2,1)S(1)} %all-to-all-done.2.refs_0_, bf16[1024,2048]{1,0:T(8,128)(2,1)S(1)} %get-tuple-element.60.refs_1_.refs_4_, bf16[64,8,256]{2,1,0:T(8,128)(2,1)} %bitcast.24, bf16[64,8,256]{2,1,0:T(8,128)(2,1)} %copy-done.3, ...), custom_call_target="tpu_custom_call" | custom-call | tf_op jit(solution)/shard_map/early_rows/pallas_call | solution.py:85
  139.3 4.0 %expert_rows.1 = (bf16[256,256]{1,0:T(8,128)(2,1)S(1)}, bf16[16,512]{1,0:T(8,128)(2,1)}) custom-call(bf16[64,8,128]{2,1,0:T(8,128)(2,1)S(1)} %collective-permute-done.8.refs_0_, bf16[64,8,128]{2,1,0:T(8,128)(2,1)} %collective-permute-done.9.refs_1_, bf16[64,8,128]{2,1,0:T(8,128)(2,1)S(1)} %collective-permute-done.10.refs_2_, ...), custom_call_target="tpu_custom_call" | custom-call | tf_op jit(solution)/shard_map/expert_rows/pallas_call | solution.py:85
  143.4 1.2 collective-permute-start.15
  144.6 1.5 collective-permute-start.16
  146.0 1.1 mix_table.1
  147.1 1.4 fetch.3
  148.5 1.5 collective-permute-done.14.refs_1_
  150.1 0.9 collective-permute-done.16.refs_3_
  150.9 0.5 down.1
  151.4 19.5 %all_to_all.21.refs_0_ = bf16[64,8,256]{2,1,0:T(8,128)(2,1)S(1)} all-to-all(bf16[64,8,256]{2,1,0:T(8,128)(2,1)S(1)} %bitcast.17), channel_id=1, replica_groups=mesh['z'=8,'y'=4,'c'=2,'head'=4] {'z','y','c'}, dimensions={0} | all-to-all | bytes 524288 | tf_op jit(solution)/shard_map/all_to_all | solution.py:590
  170.9 1.6 blend.1.refs_4_
  172.6 3.2 %collective-permute-start.18 = (bf16[16,512]{1,0:T(8,128)(2,1)}, bf16[16,512]{1,0:T(8,128)(2,1)S(1)}, u32[]{:S(2)}, u32[]{:S(2)}) collective-permute-start(bf16[16,512]{1,0:T(8,128)(2,1)} %blend.1.refs_4_), channel_id=1, source_target_pairs={{0,2},{1,3},{2,0},{3,1},{4,6},{5,7},{6,4},{7,5},{8,10},{9,11},{10,... | collective-permute-start | bytes 49160 | tf_op jit(solution)/shard_map/ppermute | solution.py:551
  175.8 0.8 collective-permute-done.17.refs_0_
  176.6 0.7 collective-permute-done.18.refs_1_
  177.3 1.3 collective-permute-done.19.refs_2_
  178.6 0.9 norm_parts.1
  179.5 1.1 convolution_convert_fusion
  (27 shorter events, 0.3 us)
Async XLA Ops:
  7.2 172.3 %copy-start = (bf16[2048,3,256]{2,0,1:T(8,128)(2,1)S(1)}, bf16[2048,3,256]{2,0,1:T(8,128)(2,1)}, u32[]{:S(2)}) copy-start(bf16[2048,3,256]{2,0,1:T(8,128)(2,1)} %param.33) | copy-start | bytes 9437188
  7.2 127.2 %all-gather.2.cloned.1.call-start = ((), (), s32[]{:S(2)}) async-start(), calls=%async_computation.4 | async-start | bytes 5242880 | tf_op jit(solution)/shard_map/all_gather | solution.py:570
  37.6 4.8 %collective-permute-start = (bf16[32,32,256]{2,1,0:T(8,128)(2,1)S(1)}, bf16[32,32,256]{2,1,0:T(8,128)(2,1)S(1)}, u32[]{:S(2)}, u32[]{:S(2)}) collective-permute-start(bf16[32,32,256]{2,1,0:T(8,128)(2,1)S(1)} %all_to_all.20.refs_4_.refs_7_), channel_id=1, source_target_pairs={{0,4},{4,0},{1,5},{5,1},{2,6},{6,2},{3,7},{7,3},{8,12},{12,8},{9,1... | collective-permute-start | bytes 1572872 | tf_op jit(solution)/shard_map/ppermute | solution.py:560
  48.0 1.8 collective-permute-start.1
  51.6 47.5 %all-to-all-start.1 = ((bf16[32,48,128]{2,1,0:T(8,128)(2,1)}), bf16[32,48,128]{2,1,0:T(8,128)(2,1)S(1)}, u32[]{:S(2)}, u32[]{:S(2)}) async-start(bf16[32,48,128]{2,1,0:T(8,128)(2,1)} %merge.1.refs_1_.after_ref), calls=%async_computation.1 | async-start | bytes 786432 | tf_op jit(solution)/shard_map/all_to_all | solution.py:578
  56.0 39.1 %collective-permute-start.2 = (bf16[64,8,256]{2,1,0:T(8,128)(2,1)}, bf16[64,8,256]{2,1,0:T(8,128)(2,1)S(1)}, u32[]{:S(2)}, u32[]{:S(2)}) collective-permute-start(bf16[64,8,256]{2,1,0:T(8,128)(2,1)} %bitcast.21), channel_id=1, source_target_pairs={{0,1},{1,2},{2,3},{3,0},{4,5},{5,6},{6,7},{7,4},{8,9},{9,10},{10,1... | collective-permute-start | bytes 786440 | tf_op jit(solution)/shard_map/ppermute | solution.py:551
  57.3 55.8 %collective-permute-start.3 = (bf16[64,8,256]{2,1,0:T(8,128)(2,1)}, bf16[64,8,256]{2,1,0:T(8,128)(2,1)}, u32[]{:S(2)}, u32[]{:S(2)}) collective-permute-start(bf16[64,8,256]{2,1,0:T(8,128)(2,1)} %bitcast.22), channel_id=1, source_target_pairs={{0,2},{1,3},{2,0},{3,1},{4,6},{5,7},{6,4},{7,5},{8,10},{9,11},{10,... | collective-permute-start | bytes 786440 | tf_op jit(solution)/shard_map/ppermute | solution.py:551
  59.8 53.3 %collective-permute-start.4 = (bf16[64,8,256]{2,1,0:T(8,128)(2,1)}, bf16[64,8,256]{2,1,0:T(8,128)(2,1)}, u32[]{:S(2)}, u32[]{:S(2)}) collective-permute-start(bf16[64,8,256]{2,1,0:T(8,128)(2,1)} %bitcast.23), channel_id=1, source_target_pairs={{0,3},{1,0},{2,1},{3,2},{4,7},{5,4},{6,5},{7,6},{8,11},{9,8},{10,9... | collective-permute-start | bytes 786440 | tf_op jit(solution)/shard_map/ppermute | solution.py:551
  93.8 19.3 %collective-permute-start.5 = (bf16[256,512]{1,0:T(8,128)(2,1)}, bf16[256,512]{1,0:T(8,128)(2,1)}, u32[]{:S(2)}, u32[]{:S(2)}) collective-permute-start(bf16[256,512]{1,0:T(8,128)(2,1)} %get-tuple-element.56), channel_id=1, source_target_pairs={{0,1},{1,2},{2,3},{3,0},{4,5},{5,6},{6,7},{7,4},{8,9},{9,10},{10,1... | collective-permute-start | bytes 786440 | tf_op jit(solution)/shard_map/ppermute | solution.py:556
  94.2 18.9 %collective-permute-start.6 = (bf16[256,512]{1,0:T(8,128)(2,1)}, bf16[256,512]{1,0:T(8,128)(2,1)}, u32[]{:S(2)}, u32[]{:S(2)}) collective-permute-start(bf16[256,512]{1,0:T(8,128)(2,1)} %get-tuple-element.57), channel_id=1, source_target_pairs={{0,2},{1,3},{2,0},{3,1},{4,6},{5,7},{6,4},{7,5},{8,10},{9,11},{10,... | collective-permute-start | bytes 786440 | tf_op jit(solution)/shard_map/ppermute | solution.py:556
  95.1 0.7 copy-start.3
  95.8 17.3 %collective-permute-start.7 = (bf16[256,512]{1,0:T(8,128)(2,1)}, bf16[256,512]{1,0:T(8,128)(2,1)}, u32[]{:S(2)}, u32[]{:S(2)}) collective-permute-start(bf16[256,512]{1,0:T(8,128)(2,1)} %get-tuple-element.58), channel_id=1, source_target_pairs={{0,3},{1,0},{2,1},{3,2},{4,7},{5,4},{6,5},{7,6},{8,11},{9,8},{10,9... | collective-permute-start | bytes 786440 | tf_op jit(solution)/shard_map/ppermute | solution.py:556
  98.5 0.6 copy-start.1
  101.2 36.0 %copy-start.2 = (bf16[16,256]{1,0:T(8,128)(2,1)}, bf16[16,256]{1,0:T(8,128)(2,1)S(1)}, u32[]{:S(2)}) copy-start(bf16[16,256]{1,0:T(8,128)(2,1)S(1)} %get-tuple-element.67.refs_8_) | copy-start | bytes 24580
  101.3 22.9 %all-to-all-start.2 = ((bf16[64,8,128]{2,1,0:T(8,128)(2,1)}), bf16[64,8,128]{2,1,0:T(8,128)(2,1)S(1)}, u32[]{:S(2)}, u32[]{:S(2)}) async-start(bf16[64,8,128]{2,1,0:T(8,128)(2,1)} %get-tuple-element.52), calls=%async_computation.2 | async-start | bytes 262144 | tf_op jit(solution)/shard_map/all_to_all | solution.py:581
  124.2 15.1 %collective-permute-start.10 = (bf16[64,8,128]{2,1,0:T(8,128)(2,1)S(1)}, bf16[64,8,128]{2,1,0:T(8,128)(2,1)S(1)}, u32[]{:S(2)}, u32[]{:S(2)}) collective-permute-start(bf16[64,8,128]{2,1,0:T(8,128)(2,1)S(1)} %all-to-all-done.2.refs_0_), channel_id=1, source_target_pairs={{0,3},{1,0},{2,1},{3,2},{4,7},{5,4},{6,5},{7,6},{8,11},{9,8},{10,9... | collective-permute-start | bytes 393224 | tf_op jit(solution)/shard_map/ppermute | solution.py:551
  125.2 14.1 %collective-permute-start.8 = (bf16[64,8,128]{2,1,0:T(8,128)(2,1)S(1)}, bf16[64,8,128]{2,1,0:T(8,128)(2,1)S(1)}, u32[]{:S(2)}, u32[]{:S(2)}) collective-permute-start(bf16[64,8,128]{2,1,0:T(8,128)(2,1)S(1)} %all-to-all-done.2.refs_0_), channel_id=1, source_target_pairs={{0,1},{1,2},{2,3},{3,0},{4,5},{5,6},{6,7},{7,4},{8,9},{9,10},{10,1... | collective-permute-start | bytes 393224 | tf_op jit(solution)/shard_map/ppermute | solution.py:551
  125.6 13.7 %collective-permute-start.9 = (bf16[64,8,128]{2,1,0:T(8,128)(2,1)S(1)}, bf16[64,8,128]{2,1,0:T(8,128)(2,1)}, u32[]{:S(2)}, u32[]{:S(2)}) collective-permute-start(bf16[64,8,128]{2,1,0:T(8,128)(2,1)S(1)} %all-to-all-done.2.refs_0_), channel_id=1, source_target_pairs={{0,2},{1,3},{2,0},{3,1},{4,6},{5,7},{6,4},{7,5},{8,10},{9,11},{10,... | collective-permute-start | bytes 393224 | tf_op jit(solution)/shard_map/ppermute | solution.py:551
  128.1 4.4 %collective-permute-start.11 = (bf16[16,256]{1,0:T(8,128)(2,1)S(1)}, bf16[16,256]{1,0:T(8,128)(2,1)S(1)}, u32[]{:S(2)}, u32[]{:S(2)}) collective-permute-start(bf16[16,256]{1,0:T(8,128)(2,1)S(1)} %get-tuple-element.67.refs_8_), channel_id=1, source_target_pairs={{0,1},{1,2},{2,3},{3,0},{4,5},{5,6},{6,7},{7,4},{8,9},{9,10},{10,1... | collective-permute-start | bytes 24584 | tf_op jit(solution)/shard_map/ppermute | solution.py:551
  128.5 10.8 %collective-permute-start.12 = (bf16[16,256]{1,0:T(8,128)(2,1)S(1)}, bf16[16,256]{1,0:T(8,128)(2,1)}, u32[]{:S(2)}, u32[]{:S(2)}) collective-permute-start(bf16[16,256]{1,0:T(8,128)(2,1)S(1)} %get-tuple-element.67.refs_8_), channel_id=1, source_target_pairs={{0,2},{1,3},{2,0},{3,1},{4,6},{5,7},{6,4},{7,5},{8,10},{9,11},{10,... | collective-permute-start | bytes 24584 | tf_op jit(solution)/shard_map/ppermute | solution.py:551
  132.5 4.8 %copy-start.4 = (bf16[16,256]{1,0:T(8,128)(2,1)}, bf16[16,256]{1,0:T(8,128)(2,1)S(1)}, u32[]{:S(2)}) copy-start(bf16[16,256]{1,0:T(8,128)(2,1)S(1)} %collective-permute-done.11.refs_9_) | copy-start | bytes 24580
  132.5 6.8 %collective-permute-start.13 = (bf16[16,256]{1,0:T(8,128)(2,1)S(1)}, bf16[16,256]{1,0:T(8,128)(2,1)}, u32[]{:S(2)}, u32[]{:S(2)}) collective-permute-start(bf16[16,256]{1,0:T(8,128)(2,1)S(1)} %get-tuple-element.67.refs_8_), channel_id=1, source_target_pairs={{0,3},{1,0},{2,1},{3,2},{4,7},{5,4},{6,5},{7,6},{8,11},{9,8},{10,9... | collective-permute-start | bytes 24584 | tf_op jit(solution)/shard_map/ppermute | solution.py:551
  143.3 6.8 %collective-permute-start.14 = (bf16[256,256]{1,0:T(8,128)(2,1)S(1)}, bf16[256,256]{1,0:T(8,128)(2,1)S(1)}, u32[]{:S(2)}, u32[]{:S(2)}) collective-permute-start(bf16[256,256]{1,0:T(8,128)(2,1)S(1)} %get-tuple-element.68.refs_0_.refs_2_), channel_id=1, source_target_pairs={{0,1},{1,2},{2,3},{3,0},{4,5},{5,6},{6,7},{7,4},{8,9},{9,10},{10,1... | collective-permute-start | bytes 393224 | tf_op jit(solution)/shard_map/ppermute | solution.py:551
  143.4 6.7 %collective-permute-start.15 = (bf16[256,256]{1,0:T(8,128)(2,1)S(1)}, bf16[256,256]{1,0:T(8,128)(2,1)S(1)}, u32[]{:S(2)}, u32[]{:S(2)}) collective-permute-start(bf16[256,256]{1,0:T(8,128)(2,1)S(1)} %get-tuple-element.68.refs_0_.refs_2_), channel_id=1, source_target_pairs={{0,2},{1,3},{2,0},{3,1},{4,6},{5,7},{6,4},{7,5},{8,10},{9,11},{10,... | collective-permute-start | bytes 393224 | tf_op jit(solution)/shard_map/ppermute | solution.py:551
  144.6 6.4 %collective-permute-start.16 = (bf16[256,256]{1,0:T(8,128)(2,1)S(1)}, bf16[256,256]{1,0:T(8,128)(2,1)S(1)}, u32[]{:S(2)}, u32[]{:S(2)}) collective-permute-start(bf16[256,256]{1,0:T(8,128)(2,1)S(1)} %get-tuple-element.68.refs_0_.refs_2_), channel_id=1, source_target_pairs={{0,3},{1,0},{2,1},{3,2},{4,7},{5,4},{6,5},{7,6},{8,11},{9,8},{10,9... | collective-permute-start | bytes 393224 | tf_op jit(solution)/shard_map/ppermute | solution.py:551
  172.5 4.1 %collective-permute-start.17 = (bf16[16,512]{1,0:T(8,128)(2,1)}, bf16[16,512]{1,0:T(8,128)(2,1)S(1)}, u32[]{:S(2)}, u32[]{:S(2)}) collective-permute-start(bf16[16,512]{1,0:T(8,128)(2,1)} %blend.1.refs_4_), channel_id=1, source_target_pairs={{0,1},{1,2},{2,3},{3,0},{4,5},{5,6},{6,7},{7,4},{8,9},{9,10},{10,1... | collective-permute-start | bytes 49160 | tf_op jit(solution)/shard_map/ppermute | solution.py:551
  172.6 4.7 %collective-permute-start.18 = (bf16[16,512]{1,0:T(8,128)(2,1)}, bf16[16,512]{1,0:T(8,128)(2,1)S(1)}, u32[]{:S(2)}, u32[]{:S(2)}) collective-permute-start(bf16[16,512]{1,0:T(8,128)(2,1)} %blend.1.refs_4_), channel_id=1, source_target_pairs={{0,2},{1,3},{2,0},{3,1},{4,6},{5,7},{6,4},{7,5},{8,10},{9,11},{10,... | collective-permute-start | bytes 49160 | tf_op jit(solution)/shard_map/ppermute | solution.py:551
  175.8 2.8 %collective-permute-start.19 = (bf16[16,512]{1,0:T(8,128)(2,1)}, bf16[16,512]{1,0:T(8,128)(2,1)S(1)}, u32[]{:S(2)}, u32[]{:S(2)}) collective-permute-start(bf16[16,512]{1,0:T(8,128)(2,1)} %blend.1.refs_4_), channel_id=1, source_target_pairs={{0,3},{1,0},{2,1},{3,2},{4,7},{5,4},{6,5},{7,6},{8,11},{9,8},{10,9... | collective-permute-start | bytes 49160 | tf_op jit(solution)/shard_map/ppermute | solution.py:551
Sparse Core Ops, SparseCore 0:
  9.8 58.2 all-gather.1

commit v6 on v5

--- a/solution.py
+++ b/solution.py
@@ -295,8 +295,8 @@
     out_ref[:, 32:48, :] = board.astype(BF16)
 
 
-def merge(a, b):
-    return run(merge_body, "merge", [], [a, b], [], leaving=[sds(a.shape, BF16)])[0]
+def merge(a, b, after):
+    return run(merge_body, "merge", [], [a, b], [], after_hbm=[after], leaving=[sds(a.shape, BF16)])[0]
 
 
 def fetch(after, *arrays):
@@ -304,40 +304,34 @@
 
 
 def split_kernel(w_ref, after_ref, *refs):
-    outs, sems = refs[:4], refs[4]
+    outs, bufs, sems = refs[:4], refs[4:8], refs[8]
     width = outs[0].shape[1]
-    copies = []
+    cuts, writes = [], []
     for k in range(4):
         cols = pl.ds(pl.multiple_of(((head_id() + k) % 4) * width, width), width)
-        copies.append(pltpu.make_async_copy(w_ref.at[:, cols], outs[k], sems.at[k]))
-    for copy in copies:
-        copy.start()
-    for copy in copies:
-        copy.wait()
+        cuts.append(pltpu.make_async_copy(w_ref.at[:, cols], bufs[k], sems.at[k]))
+        writes.append(pltpu.make_async_copy(bufs[k], outs[k], sems.at[4 + k]))
+    for cut in cuts:
+        cut.start()
+    for cut, write in zip(cuts, writes):
+        cut.wait()
+        write.start()
+    for write in writes:
+        write.wait()
 
 
 def split_columns(w, after):
     hbm = pl.BlockSpec(memory_space=pltpu.HBM)
+    shape = (w.shape[0], w.shape[1] // 4)
     return pl.pallas_call(
         split_kernel,
         name="split_columns",
-        out_shape=[pltpu.HBM((w.shape[0], w.shape[1] // 4), w.dtype)] * 4,
-        in_specs=[hbm] * 2,
+        out_shape=[pltpu.HBM(shape, w.dtype)] * 4,
+        in_specs=[hbm, pl.BlockSpec(memory_space=pl.ANY)],
         out_specs=[hbm] * 4,
-        scratch_shapes=[pltpu.SemaphoreType.DMA((4,))],
+        scratch_shapes=[pltpu.VMEM(shape, w.dtype)] * 4 + [pltpu.SemaphoreType.DMA((8,))],
         compiler_params=VLIM,
-    )(*pin([w, after]))
-
-
-def cells_body(near, far, outs, own):
-    rows = outs[0].shape[0] // 2
-    lane = iota((rows, outs[0].shape[1]), 1)
-    outs[0][...] = cell_map(flip(far[0].get()[...], 1), (lane // 8).astype(F32), lane)
-
-
-def cells_table(routes, experts, after):
-    out = sds((2 * routes.shape[0], experts * 8), BF16)
-    return run(cells_body, "cells_table", [out], [], [routes.T], after_hbm=[after])[0]
+    )(*pin([w]), after)
 
 
 def mix_body(near, far, outs, own):
@@ -384,14 +378,17 @@
     att_ref, disp = outs
     disp_ref = disp.buf
     att_ref[...] = jnp.concatenate(att, axis=1).astype(BF16)
+    rows = att_ref.shape[0]
+    lane = iota((rows, disp_ref.shape[0] * 8), 1)
+    pick = cell_map(flip(far[2].get()[...], 1), (lane // 8).astype(F32), lane)
     both = jnp.concatenate(att, axis=0).astype(BF16)
-    out = lax.dot_general(far[2].get()[...], both, (((0,), (0,)), ((), ())), preferred_element_type=F32)
+    out = lax.dot_general(pick, both, (((0,), (0,)), ((), ())), preferred_element_type=F32)
     disp_ref[...] = out.astype(BF16).reshape(disp_ref.shape)
 
 
-def owner_part(parts, queries, new_kv, cells, experts):
+def owner_part(parts, queries, new_kv, routes, experts):
     outs, leaving = [sds(queries.shape, BF16)], [sds((experts, 8, HD), BF16)]
-    return run(owner_body, "owner_part", outs, [parts], [queries, new_kv, cells], leaving=leaving)
+    return run(owner_body, "owner_part", outs, [parts], [queries, new_kv, routes.T], leaving=leaving)
 
 
 def flip(x, terms):
@@ -571,18 +568,18 @@
     qa = lax.all_to_all(outset(queries, residual, routes, chips), ("z", "y"), 0, 0, tiled=True)
     tables = slot_tables(slot_request, slot_page, slot_used, lengths, kv_cache, [qa])
     keep, send, res = attend_pages(tables, qa, swap_core(qa))
-    merged = merge(keep, swap_core(send))
-    w_cols = to_heads(split_columns(w_down[0], merged))
-    cells = cells_table(routes, experts, merged)
+    blocks = split_columns(w_down[0], send)
+    merged = merge(keep, swap_core(send), blocks[0])
+    w_cols = to_heads(blocks)
     res = from_heads(res.reshape(experts, 8, -1))
     arrived = lax.all_to_all(merged, ("z", "y"), 0, 0, tiled=True)
-    arrived, cells = lax.optimization_barrier((arrived, cells))
-    attended, disp = owner_part(arrived, queries, new_kv, cells, experts)
+    attended, disp = owner_part(arrived, queries, new_kv, routes, experts)
     tokens = lax.all_to_all(disp, REQ, 0, 0, tiled=True)
-    tokens, attended, res, w_cols = lax.optimization_barrier((tokens, attended, res, w_cols))
+    mine = from_heads(attended)
+    tokens, mine, res, w_cols = lax.optimization_barrier((tokens, mine, res, w_cols))
     out_weight, w_gate, w_up = fetch(tokens, out_weight, w_gate[0], w_up[0])
     early = early_rows(tokens, out_weight, res)
-    others, mine = from_heads(tokens)[1:], from_heads(attended)
+    others = from_heads(tokens)[1:]
     inner, hidden = expert_rows(others, early, out_weight, w_gate, w_up, norm_gain, mine, residual)
     w_cols = fetch(inner, *w_cols)
     mix = mix_table(routes, route_weights, experts, inner)

time: 188 us -> 156 us (0.83)
  Pallas kernels: 61.6 us -> 30 us
    pallas_call x1, Pallas kernels: 32.9 us -> 2.02 us  [split_columns(): pl.pallas_call(split_kernel, name='split_columns', out_shape=[pltpu.HBM(s...]
    all_to_all x1, waiting for transfers between devices: 11.1 us -> 4.75 us  [local(): tokens = lax.all_to_all(disp, REQ, 0, 0, tiled=True)]
    ppermute x3, waiting for transfers between devices: 0.01 us -> 6.27 us  [to_heads(): lax.ppermute(xs[k], 'head', [(i, (i + k) % n) for i in range(n)])]
    pallas_call x14 -> x13, Pallas kernels: 28.7 us -> 28 us  [run(): pl.pallas_call(kernel, name=name, out_shape=list(outs) + [pltpu.HBM(x.sha...]
  transfers between devices with their start and end apart: 23 -> 23, of which waited for: 8 -> 11; matrix products, arithmetic and copies ran while one was open for 0% -> 0% of each run, Pallas kernels for 29% -> 15%
where the time goes in v6:
time: 156 us; the launch traced here: 155 us
  blocking collectives  46.7 us (30%)
  starting transfers between devices  41.4 us (27%)
  Pallas kernels  30 us (19%)
  waiting for transfers between devices  20.6 us (13%)
  between operations  14.3 us (9%)
    all_to_all x1, blocking collectives, local(): lax.all_to_all(outset(queries, residual, routes, chips), ('z', 'y'), 0, 0...  28.1 us
    pallas_call x13, Pallas kernels, run(): pl.pallas_call(kernel, name=name, out_shape=list(outs) + [pltpu.HBM(x.sha...  28 us
    ppermute x15, starting transfers between devices, from_heads(): lax.ppermute(x, 'head', [(i, (i + k) % n) for i in range(n)])  18.8 us
    all_to_all x1, blocking collectives, local(): returned = lax.all_to_all(expert_out, REQ, 0, 0, tiled=True)  18.6 us
    all_to_all x1, starting transfers between devices, local(): tokens = lax.all_to_all(disp, REQ, 0, 0, tiled=True)  11.3 us
    ppermute x15, waiting for transfers between devices, from_heads(): lax.ppermute(x, 'head', [(i, (i + k) % n) for i in range(n)])  8.86 us
    ppermute x3, waiting for transfers between devices, to_heads(): lax.ppermute(xs[k], 'head', [(i, (i + k) % n) for i in range(n)])  6.27 us
    all_to_all x1, waiting for transfers between devices, local(): tokens = lax.all_to_all(disp, REQ, 0, 0, tiled=True)  4.75 us
  transfers between devices with their start and end apart: 23, of which 11 were waited for; matrix products, arithmetic and copies ran while one was open for 0% of the time, Pallas kernels for 15%

profile of v6, /device:TPU:1, one launch (start us, length us, event | category | flops | bytes accessed | tf_op | source)
XLA Modules:
  0.0 155.3 jit_solution(18421711966513758991)
XLA Ops:
  7.2 0.7 all-gather.2.cloned.1.call-update
  7.9 1.6 %outset.1 = bf16[32,32,256]{2,1,0:T(8,128)(2,1)S(1)} custom-call(bf16[16,256]{1,0:T(8,128)(2,1)} %refs_1_.3, bf16[16,2048]{1,0:T(8,128)(2,1)} %refs_12_.1, s32[8,16]{1,0:T(8,128)} %bitcast.25), custom_call_target="tpu_custom_call" | custom-call | tf_op jit(solution)/shard_map/outset/pallas_call | solution.py:85
  9.5 28.1 %all_to_all.20.refs_4_.refs_7_ = bf16[32,32,256]{2,1,0:T(8,128)(2,1)S(1)} all-to-all(bf16[32,32,256]{2,1,0:T(8,128)(2,1)S(1)} %outset.1), channel_id=1, replica_groups=mesh['z'=8,'y'=4,'c'=2,'head'=4] {'z','y'}, dimensions={0} | all-to-all | bytes 1048576 | tf_op jit(solution)/shard_map/all_to_all | solution.py:568
  37.6 2.4 %collective-permute-start = (bf16[32,32,256]{2,1,0:T(8,128)(2,1)S(1)}, bf16[32,32,256]{2,1,0:T(8,128)(2,1)S(1)}, u32[]{:S(2)}, u32[]{:S(2)}) collective-permute-start(bf16[32,32,256]{2,1,0:T(8,128)(2,1)S(1)} %all_to_all.20.refs_4_.refs_7_), channel_id=1, source_target_pairs={{0,4},{4,0},{1,5},{5,1},{2,6},{6,2},{3,7},{7,3},{8,12},{12,8},{9,1... | collective-permute-start | bytes 1572872 | tf_op jit(solution)/shard_map/ppermute | solution.py:557
  40.0 2.3 %slot_tables.1 = (bf16[128,1024]{1,0:T(8,128)(2,1)S(1)}, f32[128,128]{1,0:T(8,128)S(1)}, f32[128,128]{1,0:T(8,128)S(1)}, f32[128,128]{1,0:T(8,128)S(1)}, bf16[10...) custom-call(s32[1,128]{1,0:T(1,128)} %bitcast.32, s32[1,128]{1,0:T(1,128)} %bitcast.33, ...), custom_call_target="tpu_custom_call" | custom-call | tf_op jit(solution)/shard_map/slot_tables/pallas_call | solution.py:85
  42.4 5.6 %attend_pages.1 = (bf16[32,48,128]{2,1,0:T(8,128)(2,1)S(1)}, bf16[32,48,128]{2,1,0:T(8,128)(2,1)S(1)}, bf16[32,2,8,256]{3,2,1,0:T(8,128)(2,1)}) custom-call(bf16[128,1024]{1,0:T(8,128)(2,1)S(1)} %get-tuple-element.42.refs_0_, f32[128,128]{1,0:T(8,128)S(1)} %get-tuple-element.43.refs_1_, f32[128,128]{1,0:T(8,128)S(1)} %get-tuple-element.44.refs_2_, ...), custom_call_target="tpu_custom_call" | custom-call | tf_op jit(solution)/shard_map/attend_pages/pallas_call | solution.py:85
  48.2 2.0 %split_columns.1 = (bf16[256,512]{1,0:T(8,128)(2,1)}, bf16[256,512]{1,0:T(8,128)(2,1)}, bf16[256,512]{1,0:T(8,128)(2,1)}, bf16[256,512]{1,0:T(8,128)(2,1)}) custom-call(bf16[256,2048]{1,0:T(8,128)(2,1)} %bitcast.20, bf16[32,48,128]{2,1,0:T(8,128)(2,1)S(1)} %get-tuple-element.50.after_ref), custom_call_target="tpu_custom_call" | custom-call | tf_op jit(solution)/shard_map/split_columns/pallas_call | solution.py:326
  50.2 1.7 %merge.1 = bf16[32,48,128]{2,1,0:T(8,128)(2,1)} custom-call(bf16[32,48,128]{2,1,0:T(8,128)(2,1)S(1)} %get-tuple-element.49.refs_0_, bf16[32,48,128]{2,1,0:T(8,128)(2,1)S(1)} %collective-permute-done.1.refs_1_, bf16[256,512]{1,0:T(8,128)(2,1)} %get-tuple-element.71.refs_2_.refs_1_), custom_call_target="tpu_custom_call" | custom-call | tf_op jit(solution)/shard_map/merge/pallas_call | solution.py:85
  51.9 4.4 %all-to-all-start.1 = ((bf16[32,48,128]{2,1,0:T(8,128)(2,1)}), bf16[32,48,128]{2,1,0:T(8,128)(2,1)S(1)}, u32[]{:S(2)}, u32[]{:S(2)}) async-start(bf16[32,48,128]{2,1,0:T(8,128)(2,1)} %merge.1), calls=%async_computation.1 | async-start | bytes 786432 | tf_op jit(solution)/shard_map/all_to_all | solution.py:575
  56.3 2.6 %collective-permute-start.10 = (bf16[256,512]{1,0:T(8,128)(2,1)}, bf16[256,512]{1,0:T(8,128)(2,1)S(1)}, u32[]{:S(2)}, u32[]{:S(2)}) collective-permute-start(bf16[256,512]{1,0:T(8,128)(2,1)} %get-tuple-element.57), channel_id=1, source_target_pairs={{0,3},{1,0},{2,1},{3,2},{4,7},{5,4},{6,5},{7,6},{8,11},{9,8},{10,9... | collective-permute-start | bytes 786440 | tf_op jit(solution)/shard_map/ppermute | solution.py:553
  58.9 1.7 %collective-permute-start.9 = (bf16[256,512]{1,0:T(8,128)(2,1)}, bf16[256,512]{1,0:T(8,128)(2,1)}, u32[]{:S(2)}, u32[]{:S(2)}) collective-permute-start(bf16[256,512]{1,0:T(8,128)(2,1)} %get-tuple-element.56), channel_id=1, source_target_pairs={{0,2},{1,3},{2,0},{3,1},{4,6},{5,7},{6,4},{7,5},{8,10},{9,11},{10,... | collective-permute-start | bytes 786440 | tf_op jit(solution)/shard_map/ppermute | solution.py:553
  60.6 1.5 collective-permute-start.5
  62.2 0.6 collective-permute-start.6
  62.8 6.3 %collective-permute-done.10.refs_4_ = bf16[256,512]{1,0:T(8,128)(2,1)S(1)} collective-permute-done((bf16[256,512]{1,0:T(8,128)(2,1)}, bf16[256,512]{1,0:T(8,128)(2,1)S(1)}, u32[]{:S(2)}, u32[]{:S(2)}) %collective-permute-start.10) | collective-permute-done | bytes 262176 | tf_op jit(solution)/shard_map/ppermute | solution.py:553
  69.1 0.7 copy-done.2
  69.8 1.1 collective-permute-start.7
  70.9 2.5 %owner_part.1 = (bf16[16,256]{1,0:T(8,128)(2,1)S(1)}, bf16[64,8,128]{2,1,0:T(8,128)(2,1)}) custom-call(bf16[32,48,128]{2,1,0:T(8,128)(2,1)S(1)} %all-to-all-done.1.refs_0_, bf16[16,256]{1,0:T(8,128)(2,1)} %refs_1_.3, bf16[16,2,256]{2,1,0:T(2,128)(2,1)} %refs_2_.1, s32[8,16]{1,0:T(8,128)} %bitcast.26), custom_call_target="tpu_custom_call" | custom-call | tf_op jit(solution)/shard_map/owner_part/pallas_call | solution.py:85
  73.4 11.3 %all-to-all-start.2 = ((bf16[64,8,128]{2,1,0:T(8,128)(2,1)}), bf16[64,8,128]{2,1,0:T(8,128)(2,1)S(1)}, u32[]{:S(2)}, u32[]{:S(2)}) async-start(bf16[64,8,128]{2,1,0:T(8,128)(2,1)} %get-tuple-element.52), calls=%async_computation.2 | async-start | bytes 262144 | tf_op jit(solution)/shard_map/all_to_all | solution.py:577
  84.8 0.5 collective-permute-start.2
  85.3 2.4 %collective-permute-start.3 = (bf16[16,256]{1,0:T(8,128)(2,1)S(1)}, bf16[16,256]{1,0:T(8,128)(2,1)S(1)}, u32[]{:S(2)}, u32[]{:S(2)}) collective-permute-start(bf16[16,256]{1,0:T(8,128)(2,1)S(1)} %get-tuple-element.66.refs_8_), channel_id=1, source_target_pairs={{0,2},{1,3},{2,0},{3,1},{4,6},{5,7},{6,4},{7,5},{8,10},{9,11},{10,... | collective-permute-start | bytes 24584 | tf_op jit(solution)/shard_map/ppermute | solution.py:548
  87.7 0.7 collective-permute-start.4
  88.4 0.4 collective-permute-done.2.refs_9_
  88.9 0.8 collective-permute-done.3.refs_10_
  89.6 0.9 collective-permute-done.4.refs_11_
  90.5 0.6 copy-done.5
  91.1 4.7 %all-to-all-done.2.refs_0_ = bf16[64,8,128]{2,1,0:T(8,128)(2,1)S(1)} async-done(((bf16[64,8,128]{2,1,0:T(8,128)(2,1)}), bf16[64,8,128]{2,1,0:T(8,128)(2,1)S(1)}, u32[]{:S(2)}, u32[]{:S(2)}) %all-to-all-start.2) | async-done | bytes 131104 | tf_op jit(solution)/shard_map/all_to_all | solution.py:577
  95.9 0.5 collective-permute-start.11
  96.3 2.4 %collective-permute-start.12 = (bf16[64,8,128]{2,1,0:T(8,128)(2,1)S(1)}, bf16[64,8,128]{2,1,0:T(8,128)(2,1)S(1)}, u32[]{:S(2)}, u32[]{:S(2)}) collective-permute-start(bf16[64,8,128]{2,1,0:T(8,128)(2,1)S(1)} %all-to-all-done.2.refs_0_), channel_id=1, source_target_pairs={{0,2},{1,3},{2,0},{3,1},{4,6},{5,7},{6,4},{7,5},{8,10},{9,11},{10,... | collective-permute-start | bytes 393224 | tf_op jit(solution)/shard_map/ppermute | solution.py:548
  98.8 0.7 collective-permute-start.13
  99.4 2.9 %fetch.2 = (bf16[1024,2048]{1,0:T(8,128)(2,1)S(1)}, bf16[2048,256]{1,0:T(8,128)(2,1)S(1)}, bf16[2048,256]{1,0:T(8,128)(2,1)S(1)}) custom-call(bf16[64,8,128]{2,1,0:T(8,128)(2,1)S(1)} %all-to-all-done.2.refs_0_, bf16[1024,2048]{1,0:T(8,128)(2,1)} %all-gather.2.cloned.1.call-done.refs_1_, bf16[2048,256]{1,0:T(8,128)(2,1)} %bitcast.18, bf16[2048,256]{1,0:T(8,128)(2,1)} %bitcast.19), custom_call_target="tpu_custom_call" | custom-call | tf_op jit(solution)/shard_map/fetch/pallas_call | solution.py:85
  102.4 1.9 %early_rows.1.refs_3_ = f32[8,256,256]{2,1,0:T(8,128)S(1)} custom-call(bf16[64,8,128]{2,1,0:T(8,128)(2,1)S(1)} %all-to-all-done.2.refs_0_, bf16[1024,2048]{1,0:T(8,128)(2,1)S(1)} %get-tuple-element.59.refs_1_.refs_4_, bf16[64,8,256]{2,1,0:T(8,128)(2,1)} %bitcast.24, bf16[64,8,256]{2,1,0:T(8,128)(2,1)} %collective-permute-done.5.refs_3_, ...), custom_call_target="tpu_custom_call" | custom-call | tf_op jit(solution)/shard_map/early_rows/pallas_call | solution.py:85
  104.3 0.5 collective-permute-done.12.refs_1_
  105.0 4.0 %expert_rows.1 = (bf16[256,256]{1,0:T(8,128)(2,1)S(1)}, bf16[16,512]{1,0:T(8,128)(2,1)}) custom-call(bf16[64,8,128]{2,1,0:T(8,128)(2,1)S(1)} %collective-permute-done.11.refs_0_, bf16[64,8,128]{2,1,0:T(8,128)(2,1)S(1)} %collective-permute-done.12.refs_1_, bf16[64,8,128]{2,1,0:T(8,128)(2,1)} %collective-permute-done.13.refs_2_, ...), custom_call_target="tpu_custom_call" | custom-call | tf_op jit(solution)/shard_map/expert_rows/pallas_call | solution.py:85
  108.9 1.9 %collective-permute-start.14 = (bf16[256,256]{1,0:T(8,128)(2,1)S(1)}, bf16[256,256]{1,0:T(8,128)(2,1)S(1)}, u32[]{:S(2)}, u32[]{:S(2)}) collective-permute-start(bf16[256,256]{1,0:T(8,128)(2,1)S(1)} %get-tuple-element.70.refs_0_.refs_2_), channel_id=1, source_target_pairs={{0,1},{1,2},{2,3},{3,0},{4,5},{5,6},{6,7},{7,4},{8,9},{9,10},{10,1... | collective-permute-start | bytes 393224 | tf_op jit(solution)/shard_map/ppermute | solution.py:548
  110.9 2.7 %collective-permute-start.15 = (bf16[256,256]{1,0:T(8,128)(2,1)S(1)}, bf16[256,256]{1,0:T(8,128)(2,1)S(1)}, u32[]{:S(2)}, u32[]{:S(2)}) collective-permute-start(bf16[256,256]{1,0:T(8,128)(2,1)S(1)} %get-tuple-element.70.refs_0_.refs_2_), channel_id=1, source_target_pairs={{0,2},{1,3},{2,0},{3,1},{4,6},{5,7},{6,4},{7,5},{8,10},{9,11},{10,... | collective-permute-start | bytes 393224 | tf_op jit(solution)/shard_map/ppermute | solution.py:548
  113.6 1.1 mix_table.1
  114.7 1.4 fetch.3
  116.1 3.3 %collective-permute-done.15.refs_2_ = bf16[256,256]{1,0:T(8,128)(2,1)S(1)} collective-permute-done((bf16[256,256]{1,0:T(8,128)(2,1)S(1)}, bf16[256,256]{1,0:T(8,128)(2,1)S(1)}, u32[]{:S(2)}, u32[]{:S(2)}) %collective-permute-start.15) | collective-permute-done | bytes 131104 | tf_op jit(solution)/shard_map/ppermute | solution.py:548
  119.4 0.5 down.1
  119.9 18.6 %all_to_all.21.refs_0_ = bf16[64,8,256]{2,1,0:T(8,128)(2,1)S(1)} all-to-all(bf16[64,8,256]{2,1,0:T(8,128)(2,1)S(1)} %bitcast.17), channel_id=1, replica_groups=mesh['z'=8,'y'=4,'c'=2,'head'=4] {'z','y','c'}, dimensions={0} | all-to-all | bytes 524288 | tf_op jit(solution)/shard_map/all_to_all | solution.py:587
  138.4 1.6 %blend.1.refs_4_ = bf16[16,512]{1,0:T(8,128)(2,1)} custom-call(bf16[64,8,256]{2,1,0:T(8,128)(2,1)S(1)} %all_to_all.21.refs_0_, bf16[16,256]{1,0:T(8,128)(2,1)S(1)} %get-tuple-element.79.refs_8_.refs_1_, bf16[16,256]{1,0:T(8,128)(2,1)S(1)} %get-tuple-element.80.refs_2_, bf16[16,512]{1,0:T(8,128)(2,1)} %get-tuple-element.81.refs_3_), custom_call_target="tpu_custom_call" | custom-call | tf_op jit(solution)/shard_map/blend/pallas_call | solution.py:85
  140.0 0.6 collective-permute-start.17
  140.6 3.0 %collective-permute-start.18 = (bf16[16,512]{1,0:T(8,128)(2,1)}, bf16[16,512]{1,0:T(8,128)(2,1)S(1)}, u32[]{:S(2)}, u32[]{:S(2)}) collective-permute-start(bf16[16,512]{1,0:T(8,128)(2,1)} %blend.1.refs_4_), channel_id=1, source_target_pairs={{0,2},{1,3},{2,0},{3,1},{4,6},{5,7},{6,4},{7,5},{8,10},{9,11},{10,... | collective-permute-start | bytes 49160 | tf_op jit(solution)/shard_map/ppermute | solution.py:548
  143.6 0.4 collective-permute-done.17.refs_0_
  144.1 1.1 collective-permute-done.18.refs_1_
  145.1 1.3 collective-permute-done.19.refs_2_
  146.4 0.9 norm_parts.1
  147.3 1.1 convolution_convert_fusion
  (28 shorter events, 0.4 us)
Async XLA Ops:
  7.2 140.2 %copy-start = (bf16[2048,3,256]{2,0,1:T(8,128)(2,1)S(1)}, bf16[2048,3,256]{2,0,1:T(8,128)(2,1)}, u32[]{:S(2)}) copy-start(bf16[2048,3,256]{2,0,1:T(8,128)(2,1)} %param.33) | copy-start | bytes 9437188
  7.2 92.3 %all-gather.2.cloned.1.call-start = ((), (), s32[]{:S(2)}) async-start(), calls=%async_computation.4 | async-start | bytes 5242880 | tf_op jit(solution)/shard_map/all_gather | solution.py:567
  37.6 4.8 %collective-permute-start = (bf16[32,32,256]{2,1,0:T(8,128)(2,1)S(1)}, bf16[32,32,256]{2,1,0:T(8,128)(2,1)S(1)}, u32[]{:S(2)}, u32[]{:S(2)}) collective-permute-start(bf16[32,32,256]{2,1,0:T(8,128)(2,1)S(1)} %all_to_all.20.refs_4_.refs_7_), channel_id=1, source_target_pairs={{0,4},{4,0},{1,5},{5,1},{2,6},{6,2},{3,7},{7,3},{8,12},{12,8},{9,1... | collective-permute-start | bytes 1572872 | tf_op jit(solution)/shard_map/ppermute | solution.py:557
  48.0 2.2 %collective-permute-start.1 = (bf16[32,48,128]{2,1,0:T(8,128)(2,1)S(1)}, bf16[32,48,128]{2,1,0:T(8,128)(2,1)S(1)}, u32[]{:S(2)}, u32[]{:S(2)}) collective-permute-start(bf16[32,48,128]{2,1,0:T(8,128)(2,1)S(1)} %get-tuple-element.50.after_ref), channel_id=1, source_target_pairs={{0,4},{4,0},{1,5},{5,1},{2,6},{6,2},{3,7},{7,3},{8,12},{12,8},{9,1... | collective-permute-start | bytes 1179656 | tf_op jit(solution)/shard_map/ppermute | solution.py:557
  51.9 19.0 %all-to-all-start.1 = ((bf16[32,48,128]{2,1,0:T(8,128)(2,1)}), bf16[32,48,128]{2,1,0:T(8,128)(2,1)S(1)}, u32[]{:S(2)}, u32[]{:S(2)}) async-start(bf16[32,48,128]{2,1,0:T(8,128)(2,1)} %merge.1), calls=%async_computation.1 | async-start | bytes 786432 | tf_op jit(solution)/shard_map/all_to_all | solution.py:575
  56.3 12.7 %collective-permute-start.10 = (bf16[256,512]{1,0:T(8,128)(2,1)}, bf16[256,512]{1,0:T(8,128)(2,1)S(1)}, u32[]{:S(2)}, u32[]{:S(2)}) collective-permute-start(bf16[256,512]{1,0:T(8,128)(2,1)} %get-tuple-element.57), channel_id=1, source_target_pairs={{0,3},{1,0},{2,1},{3,2},{4,7},{5,4},{6,5},{7,6},{8,11},{9,8},{10,9... | collective-permute-start | bytes 786440 | tf_op jit(solution)/shard_map/ppermute | solution.py:553
  58.9 25.8 %collective-permute-start.8 = (bf16[256,512]{1,0:T(8,128)(2,1)}, bf16[256,512]{1,0:T(8,128)(2,1)}, u32[]{:S(2)}, u32[]{:S(2)}) collective-permute-start(bf16[256,512]{1,0:T(8,128)(2,1)} %get-tuple-element.55), channel_id=1, source_target_pairs={{0,1},{1,2},{2,3},{3,0},{4,5},{5,6},{6,7},{7,4},{8,9},{9,10},{10,1... | collective-permute-start | bytes 786440 | tf_op jit(solution)/shard_map/ppermute | solution.py:553
  58.9 26.4 %collective-permute-start.9 = (bf16[256,512]{1,0:T(8,128)(2,1)}, bf16[256,512]{1,0:T(8,128)(2,1)}, u32[]{:S(2)}, u32[]{:S(2)}) collective-permute-start(bf16[256,512]{1,0:T(8,128)(2,1)} %get-tuple-element.56), channel_id=1, source_target_pairs={{0,2},{1,3},{2,0},{3,1},{4,6},{5,7},{6,4},{7,5},{8,10},{9,11},{10,... | collective-permute-start | bytes 786440 | tf_op jit(solution)/shard_map/ppermute | solution.py:553
  60.6 27.1 %collective-permute-start.5 = (bf16[64,8,256]{2,1,0:T(8,128)(2,1)}, bf16[64,8,256]{2,1,0:T(8,128)(2,1)}, u32[]{:S(2)}, u32[]{:S(2)}) collective-permute-start(bf16[64,8,256]{2,1,0:T(8,128)(2,1)} %bitcast.21), channel_id=1, source_target_pairs={{0,1},{1,2},{2,3},{3,0},{4,5},{5,6},{6,7},{7,4},{8,9},{9,10},{10,1... | collective-permute-start | bytes 786440 | tf_op jit(solution)/shard_map/ppermute | solution.py:548
  62.2 26.2 %collective-permute-start.6 = (bf16[64,8,256]{2,1,0:T(8,128)(2,1)}, bf16[64,8,256]{2,1,0:T(8,128)(2,1)}, u32[]{:S(2)}, u32[]{:S(2)}) collective-permute-start(bf16[64,8,256]{2,1,0:T(8,128)(2,1)} %bitcast.22), channel_id=1, source_target_pairs={{0,2},{1,3},{2,0},{3,1},{4,6},{5,7},{6,4},{7,5},{8,10},{9,11},{10,... | collective-permute-start | bytes 786440 | tf_op jit(solution)/shard_map/ppermute | solution.py:548
  69.1 0.7 copy-start.2
  69.8 18.7 %collective-permute-start.7 = (bf16[64,8,256]{2,1,0:T(8,128)(2,1)}, bf16[64,8,256]{2,1,0:T(8,128)(2,1)}, u32[]{:S(2)}, u32[]{:S(2)}) collective-permute-start(bf16[64,8,256]{2,1,0:T(8,128)(2,1)} %bitcast.23), channel_id=1, source_target_pairs={{0,3},{1,0},{2,1},{3,2},{4,7},{5,4},{6,5},{7,6},{8,11},{9,8},{10,9... | collective-permute-start | bytes 786440 | tf_op jit(solution)/shard_map/ppermute | solution.py:548
  73.4 28.9 %copy-start.1 = (bf16[16,256]{1,0:T(8,128)(2,1)}, bf16[16,256]{1,0:T(8,128)(2,1)S(1)}, u32[]{:S(2)}) copy-start(bf16[16,256]{1,0:T(8,128)(2,1)S(1)} %get-tuple-element.66.refs_8_) | copy-start | bytes 24580
  73.4 22.5 %all-to-all-start.2 = ((bf16[64,8,128]{2,1,0:T(8,128)(2,1)}), bf16[64,8,128]{2,1,0:T(8,128)(2,1)S(1)}, u32[]{:S(2)}, u32[]{:S(2)}) async-start(bf16[64,8,128]{2,1,0:T(8,128)(2,1)} %get-tuple-element.52), calls=%async_computation.2 | async-start | bytes 262144 | tf_op jit(solution)/shard_map/all_to_all | solution.py:577
  84.8 4.1 %collective-permute-start.2 = (bf16[16,256]{1,0:T(8,128)(2,1)S(1)}, bf16[16,256]{1,0:T(8,128)(2,1)S(1)}, u32[]{:S(2)}, u32[]{:S(2)}) collective-permute-start(bf16[16,256]{1,0:T(8,128)(2,1)S(1)} %get-tuple-element.66.refs_8_), channel_id=1, source_target_pairs={{0,1},{1,2},{2,3},{3,0},{4,5},{5,6},{6,7},{7,4},{8,9},{9,10},{10,1... | collective-permute-start | bytes 24584 | tf_op jit(solution)/shard_map/ppermute | solution.py:548
  85.3 4.3 %collective-permute-start.3 = (bf16[16,256]{1,0:T(8,128)(2,1)S(1)}, bf16[16,256]{1,0:T(8,128)(2,1)S(1)}, u32[]{:S(2)}, u32[]{:S(2)}) collective-permute-start(bf16[16,256]{1,0:T(8,128)(2,1)S(1)} %get-tuple-element.66.refs_8_), channel_id=1, source_target_pairs={{0,2},{1,3},{2,0},{3,1},{4,6},{5,7},{6,4},{7,5},{8,10},{9,11},{10,... | collective-permute-start | bytes 24584 | tf_op jit(solution)/shard_map/ppermute | solution.py:548
  87.7 2.8 %collective-permute-start.4 = (bf16[16,256]{1,0:T(8,128)(2,1)S(1)}, bf16[16,256]{1,0:T(8,128)(2,1)S(1)}, u32[]{:S(2)}, u32[]{:S(2)}) collective-permute-start(bf16[16,256]{1,0:T(8,128)(2,1)S(1)} %get-tuple-element.66.refs_8_), channel_id=1, source_target_pairs={{0,3},{1,0},{2,1},{3,2},{4,7},{5,4},{6,5},{7,6},{8,11},{9,8},{10,9... | collective-permute-start | bytes 24584 | tf_op jit(solution)/shard_map/ppermute | solution.py:548
  88.9 13.5 %copy-start.3 = (bf16[16,256]{1,0:T(8,128)(2,1)}, bf16[16,256]{1,0:T(8,128)(2,1)S(1)}, u32[]{:S(2)}) copy-start(bf16[16,256]{1,0:T(8,128)(2,1)S(1)} %collective-permute-done.2.refs_9_) | copy-start | bytes 24580
  89.6 0.9 copy-start.4
  90.5 0.6 copy-start.5
  95.9 8.4 %collective-permute-start.11 = (bf16[64,8,128]{2,1,0:T(8,128)(2,1)S(1)}, bf16[64,8,128]{2,1,0:T(8,128)(2,1)S(1)}, u32[]{:S(2)}, u32[]{:S(2)}) collective-permute-start(bf16[64,8,128]{2,1,0:T(8,128)(2,1)S(1)} %all-to-all-done.2.refs_0_), channel_id=1, source_target_pairs={{0,1},{1,2},{2,3},{3,0},{4,5},{5,6},{6,7},{7,4},{8,9},{9,10},{10,1... | collective-permute-start | bytes 393224 | tf_op jit(solution)/shard_map/ppermute | solution.py:548
  96.3 8.4 %collective-permute-start.12 = (bf16[64,8,128]{2,1,0:T(8,128)(2,1)S(1)}, bf16[64,8,128]{2,1,0:T(8,128)(2,1)S(1)}, u32[]{:S(2)}, u32[]{:S(2)}) collective-permute-start(bf16[64,8,128]{2,1,0:T(8,128)(2,1)S(1)} %all-to-all-done.2.refs_0_), channel_id=1, source_target_pairs={{0,2},{1,3},{2,0},{3,1},{4,6},{5,7},{6,4},{7,5},{8,10},{9,11},{10,... | collective-permute-start | bytes 393224 | tf_op jit(solution)/shard_map/ppermute | solution.py:548
  98.8 6.2 %collective-permute-start.13 = (bf16[64,8,128]{2,1,0:T(8,128)(2,1)S(1)}, bf16[64,8,128]{2,1,0:T(8,128)(2,1)}, u32[]{:S(2)}, u32[]{:S(2)}) collective-permute-start(bf16[64,8,128]{2,1,0:T(8,128)(2,1)S(1)} %all-to-all-done.2.refs_0_), channel_id=1, source_target_pairs={{0,3},{1,0},{2,1},{3,2},{4,7},{5,4},{6,5},{7,6},{8,11},{9,8},{10,9... | collective-permute-start | bytes 393224 | tf_op jit(solution)/shard_map/ppermute | solution.py:548
  108.9 7.1 %collective-permute-start.14 = (bf16[256,256]{1,0:T(8,128)(2,1)S(1)}, bf16[256,256]{1,0:T(8,128)(2,1)S(1)}, u32[]{:S(2)}, u32[]{:S(2)}) collective-permute-start(bf16[256,256]{1,0:T(8,128)(2,1)S(1)} %get-tuple-element.70.refs_0_.refs_2_), channel_id=1, source_target_pairs={{0,1},{1,2},{2,3},{3,0},{4,5},{5,6},{6,7},{7,4},{8,9},{9,10},{10,1... | collective-permute-start | bytes 393224 | tf_op jit(solution)/shard_map/ppermute | solution.py:548
  110.9 8.5 %collective-permute-start.15 = (bf16[256,256]{1,0:T(8,128)(2,1)S(1)}, bf16[256,256]{1,0:T(8,128)(2,1)S(1)}, u32[]{:S(2)}, u32[]{:S(2)}) collective-permute-start(bf16[256,256]{1,0:T(8,128)(2,1)S(1)} %get-tuple-element.70.refs_0_.refs_2_), channel_id=1, source_target_pairs={{0,2},{1,3},{2,0},{3,1},{4,6},{5,7},{6,4},{7,5},{8,10},{9,11},{10,... | collective-permute-start | bytes 393224 | tf_op jit(solution)/shard_map/ppermute | solution.py:548
  113.6 5.8 %collective-permute-start.16 = (bf16[256,256]{1,0:T(8,128)(2,1)S(1)}, bf16[256,256]{1,0:T(8,128)(2,1)S(1)}, u32[]{:S(2)}, u32[]{:S(2)}) collective-permute-start(bf16[256,256]{1,0:T(8,128)(2,1)S(1)} %get-tuple-element.70.refs_0_.refs_2_), channel_id=1, source_target_pairs={{0,3},{1,0},{2,1},{3,2},{4,7},{5,4},{6,5},{7,6},{8,11},{9,8},{10,9... | collective-permute-start | bytes 393224 | tf_op jit(solution)/shard_map/ppermute | solution.py:548
  140.0 4.1 %collective-permute-start.17 = (bf16[16,512]{1,0:T(8,128)(2,1)}, bf16[16,512]{1,0:T(8,128)(2,1)S(1)}, u32[]{:S(2)}, u32[]{:S(2)}) collective-permute-start(bf16[16,512]{1,0:T(8,128)(2,1)} %blend.1.refs_4_), channel_id=1, source_target_pairs={{0,1},{1,2},{2,3},{3,0},{4,5},{5,6},{6,7},{7,4},{8,9},{9,10},{10,1... | collective-permute-start | bytes 49160 | tf_op jit(solution)/shard_map/ppermute | solution.py:548
  140.6 4.5 %collective-permute-start.18 = (bf16[16,512]{1,0:T(8,128)(2,1)}, bf16[16,512]{1,0:T(8,128)(2,1)S(1)}, u32[]{:S(2)}, u32[]{:S(2)}) collective-permute-start(bf16[16,512]{1,0:T(8,128)(2,1)} %blend.1.refs_4_), channel_id=1, source_target_pairs={{0,2},{1,3},{2,0},{3,1},{4,6},{5,7},{6,4},{7,5},{8,10},{9,11},{10,... | collective-permute-start | bytes 49160 | tf_op jit(solution)/shard_map/ppermute | solution.py:548
  143.6 2.8 %collective-permute-start.19 = (bf16[16,512]{1,0:T(8,128)(2,1)}, bf16[16,512]{1,0:T(8,128)(2,1)S(1)}, u32[]{:S(2)}, u32[]{:S(2)}) collective-permute-start(bf16[16,512]{1,0:T(8,128)(2,1)} %blend.1.refs_4_), channel_id=1, source_target_pairs={{0,3},{1,0},{2,1},{3,2},{4,7},{5,4},{6,5},{7,6},{8,11},{9,8},{10,9... | collective-permute-start | bytes 49160 | tf_op jit(solution)/shard_map/ppermute | solution.py:548
Sparse Core Ops, SparseCore 0:
  9.8 57.7 all-gather.1

commit v7 on v5

--- a/solution.py
+++ b/solution.py
@@ -34,21 +34,36 @@
     return [pltpu.with_memory_space_constraint(x, pltpu.HBM) for x in xs]
 
 
+PIECES = 4
+
+
 class Leaving:
-    def __init__(self, buf, copy):
-        self.buf, self.copy, self.sent = buf, copy, False
+    def __init__(self, buf, out, sems, base):
+        rows = buf.shape[0] // PIECES
+        parts = [pl.ds(j * rows, rows) for j in range(PIECES)]
+        self.buf, self.sent = buf, 0
+        self.copies = [pltpu.make_async_copy(buf.at[p], out.at[p], sems.at[base + j]) for j, p in enumerate(parts)]
 
     def send(self):
-        self.copy.start()
-        self.sent = True
+        self.copies[self.sent].start()
+        self.sent += 1
+
+    def finish(self):
+        while self.sent < PIECES:
+            self.send()
+        for copy in self.copies:
+            copy.wait()
+
+
+def part_of(x):
+    return x if isinstance(x, tuple) else (x, 0, x.shape[0])
 
 
 def run(body, name, outs, near, far, scratch=(), after=(), moves=(), leaving=(), after_hbm=()):
-    nn, nf, nm, no, nl = len(near), len(far), len(moves), len(outs), len(leaving)
     after = [*after, *pin(after_hbm)]
-    na = len(after)
-    nh = len(after_hbm)
-    parts = 4
+    far, moves = [part_of(x) for x in far], [part_of(x) for x in moves]
+    na, nh, nn, nf, nm = len(after), len(after_hbm), len(near), len(far), len(moves)
+    no, nl = len(outs), len(leaving)
 
     def kernel(*refs):
         ins, refs = refs[: nn + nf + na + nm], refs[nn + nf + na + nm :]
@@ -56,45 +71,46 @@
         rest = refs[no + nl + nm :]
         bufs, out_bufs, rest = rest[:nf], rest[nf : nf + nl], rest[nf + nl :]
         sems, move_sems, out_sems, own = rest[0], rest[1], rest[2], rest[3:]
-        copies = [pltpu.make_async_copy(ins[nn + i], bufs[i], sems.at[i]) for i in range(nf)]
-        for copy in copies:
+        pending = []
+        for i, (x, first, rows) in enumerate(far):
+            src = ins[nn + i] if rows == x.shape[0] else ins[nn + i].at[pl.ds(first, rows)]
+            copy = pltpu.make_async_copy(src, bufs[i], sems.at[i])
             copy.start()
-        pending = [Pending(b, c) for b, c in zip(bufs, copies)]
+            pending.append(Pending(bufs[i], copy))
         moving = []
-        for i in range(nm):
-            rows = moved[i].shape[0] // parts
-            for j in range(parts):
-                src, dst = ins[nn + nf + na + i].at[pl.ds(j * rows, rows)], moved[i].at[pl.ds(j * rows, rows)]
-                moving.append(pltpu.make_async_copy(src, dst, move_sems.at[parts * i + j]))
+        for i, (x, first, rows) in enumerate(moves):
+            rows = rows // PIECES
+            for j in range(PIECES):
+                src = ins[nn + nf + na + i].at[pl.ds(first + j * rows, rows)]
+                dst = moved[i].at[pl.ds(j * rows, rows)]
+                moving.append(pltpu.make_async_copy(src, dst, move_sems.at[PIECES * i + j]))
         for copy in moving:
             copy.start()
-        going = [
-            Leaving(out_bufs[i], pltpu.make_async_copy(out_bufs[i], out_hbm[i], out_sems.at[i])) for i in range(nl)
-        ]
+        going = [Leaving(out_bufs[i], out_hbm[i], out_sems, PIECES * i) for i in range(nl)]
         body(ins[:nn], pending, (*outputs, *going), own)
         for p in pending:
             p.get()
         for g in going:
-            if not g.sent:
-                g.send()
-            g.copy.wait()
+            g.finish()
         for copy in moving:
             copy.wait()
 
     hbm, any_space = pl.BlockSpec(memory_space=pltpu.HBM), pl.BlockSpec(memory_space=pl.ANY)
+    far_shapes = [((r,) + x.shape[1:], x.dtype) for x, _, r in far]
     return pl.pallas_call(
         kernel,
         name=name,
         out_shape=list(outs)
         + [pltpu.HBM(x.shape, x.dtype) for x in leaving]
-        + [sds(x.shape, x.dtype) for x in moves],
+        + [sds((r,) + x.shape[1:], x.dtype) for x, _, r in moves],
         in_specs=[VM] * nn + [hbm] * nf + [any_space] * (na - nh) + [hbm] * (nh + nm),
         out_specs=[VM] * no + [hbm] * nl + [VM] * nm,
-        scratch_shapes=[pltpu.VMEM(x.shape, x.dtype) for x in (*far, *leaving)]
-        + [pltpu.SemaphoreType.DMA((max(n, 1),)) for n in (nf, nm * parts, nl)]
+        scratch_shapes=[pltpu.VMEM(*f) for f in far_shapes]
+        + [pltpu.VMEM(x.shape, x.dtype) for x in leaving]
+        + [pltpu.SemaphoreType.DMA((max(n, 1),)) for n in (nf, nm * PIECES, nl * PIECES)]
         + list(scratch),
         compiler_params=VLIM,
-    )(*near, *pin(far), *after, *pin(moves))
+    )(*near, *pin([x for x, _, _ in far]), *after, *pin([x for x, _, _ in moves]))
 
 
 def sds(shape, dtype):
@@ -210,12 +226,8 @@
 
 def attn_body(near, far, outs, own):
     pick_ref, count_ref, same_ref, mine_ref, spread_ref, spread16_ref, kv_ref, qa_ref, qb_ref = near
-    keep_ref, send_ref, res = outs
+    keep_ref, send_ref = outs
     n_scr, m_scr, l_scr = own
-    core = core_id()
-    res.buf[:, core] = qa_ref[:, 16:24, :]
-    res.buf[:, 1 - core] = qb_ref[:, 24:32, :]
-    res.send()
     slots = kv_ref.shape[0]
     page = kv_ref.shape[2]
     half = qa_ref.shape[0] * 16
@@ -273,71 +285,93 @@
     slots, total = tables[0].shape
     scratch = [pltpu.VMEM((2, slots, n), F32) for n in (HD, slots, slots)]
     outs = [sds((total // 32, 48, HD), BF16)] * 2
-    leaving = [sds((total // 32, 2, 8, 2 * HD), BF16)]
-    return run(attn_body, "attend_pages", outs, [*tables, qa, qb], [], scratch, leaving=leaving)
+    return run(attn_body, "attend_pages", outs, [*tables, qa, qb], [], scratch)
 
 
 def merge_body(near, far, outs, own):
-    (a_ref, b_ref), out_ref = near, outs[0].buf
-    a, b = a_ref[:, 32:48, :].astype(F32), b_ref[:, 32:48, :].astype(F32)
-    lane, row = iota(a.shape, 2), iota(a.shape, 1)
-    board = jnp.zeros(a.shape, F32)
-    for h in range(2):
-        (ma, la), (mb, lb) = read_stats(a, h), read_stats(b, h)
-        m = jnp.maximum(ma, mb)
-        fa, fb = jnp.exp(ma - m), jnp.exp(mb - m)
-        rows = slice(16 * h, 16 * h + 16)
-        out_ref[:, rows, :] = (a_ref[:, rows, :].astype(F32) * fa + b_ref[:, rows, :].astype(F32) * fb).astype(BF16)
-        l = la * fa + lb * fb
-        l_hi = l.astype(BF16).astype(F32)
-        for i, stat in enumerate((m, l_hi, l - l_hi)):
-            board = jnp.where(lane == row + 32 * i + 16 * h, stat, board)
-    out_ref[:, 32:48, :] = board.astype(BF16)
-
-
-def merge(a, b):
-    return run(merge_body, "merge", [], [a, b], [], leaving=[sds(a.shape, BF16)])[0]
+    chips = near[0].shape[0] // PIECES
+    for piece in range(PIECES):
+        part = slice(piece * chips, piece * chips + chips)
+        a_ref, b_ref, out_ref = near[0].at[part], near[1].at[part], outs[0].buf.at[part]
+        a, b = a_ref[:, 32:48, :].astype(F32), b_ref[:, 32:48, :].astype(F32)
+        lane, row = iota(a.shape, 2), iota(a.shape, 1)
+        board = jnp.zeros(a.shape, F32)
+        for h in range(2):
+            (ma, la), (mb, lb) = read_stats(a, h), read_stats(b, h)
+            m = jnp.maximum(ma, mb)
+            fa, fb = jnp.exp(ma - m), jnp.exp(mb - m)
+            rows = slice(16 * h, 16 * h + 16)
+            out_ref[:, rows, :] = (a_ref[:, rows, :].astype(F32) * fa + b_ref[:, rows, :].astype(F32) * fb).astype(BF16)
+            l = la * fa + lb * fb
+            l_hi = l.astype(BF16).astype(F32)
+            for i, stat in enumerate((m, l_hi, l - l_hi)):
+                board = jnp.where(lane == row + 32 * i + 16 * h, stat, board)
+        out_ref[:, 32:48, :] = board.astype(BF16)
+        outs[0].send()
+
+
+def merge(a, b, after):
+    return run(merge_body, "merge", [], [a, b], [], after_hbm=[after], leaving=[sds(a.shape, BF16)])[0]
 
 
 def fetch(after, *arrays):
     return run(lambda *_: None, "fetch", [], [], [], after=[after], moves=arrays)
 
 
-def split_kernel(w_ref, after_ref, *refs):
-    outs, sems = refs[:4], refs[4]
-    width = outs[0].shape[1]
-    copies = []
+def pack_kernel(w_ref, qa_ref, qb_ref, after_ref, *refs):
+    outs, res_buf, bufs, sems = refs[:4], refs[4], refs[5:9], refs[9]
+    rows, width = bufs[0].shape[0] // 2, bufs[0].shape[1]
+    held = res_buf.shape[0]
+    cuts, writes = [], []
     for k in range(4):
-        cols = pl.ds(pl.multiple_of(((head_id() + k) % 4) * width, width), width)
-        copies.append(pltpu.make_async_copy(w_ref.at[:, cols], outs[k], sems.at[k]))
-    for copy in copies:
-        copy.start()
-    for copy in copies:
-        copy.wait()
-
-
-def split_columns(w, after):
+        first = pl.multiple_of(((head_id() + k) % 4) * 2 * width, 2 * width)
+        for f in range(2):
+            src = w_ref.at[:, pl.ds(first + f * width, width)]
+            cuts.append(pltpu.make_async_copy(src, bufs[k].at[pl.ds(f * rows, rows)], sems.at[2 * k + f]))
+        writes.append(pltpu.make_async_copy(bufs[k], outs[k].at[pl.ds(held, 2 * rows)], sems.at[8 + k]))
+    for cut in cuts:
+        cut.start()
+    mine, other = qa_ref[:, 16:24, :].astype(F32), qb_ref[:, 24:32, :].astype(F32)
+    first = core_id() == 0
+    both = [jnp.where(first, mine, other), jnp.where(first, other, mine)]
+    res_buf[...] = jnp.stack(both, axis=1).reshape(res_buf.shape).astype(BF16)
+    for k in range(4):
+        writes.append(pltpu.make_async_copy(res_buf, outs[k].at[pl.ds(0, held)], sems.at[12 + k]))
+        writes[-1].start()
+    for k in range(4):
+        cuts[2 * k].wait()
+        cuts[2 * k + 1].wait()
+        writes[k].start()
+    for write in writes:
+        write.wait()
+
+
+def pack(w_down, qa, qb, after):
     hbm = pl.BlockSpec(memory_space=pltpu.HBM)
+    rows, width = w_down.shape[0], w_down.shape[1] // 8
+    held = qa.shape[0] * 16
     return pl.pallas_call(
-        split_kernel,
-        name="split_columns",
-        out_shape=[pltpu.HBM((w.shape[0], w.shape[1] // 4), w.dtype)] * 4,
-        in_specs=[hbm] * 2,
+        pack_kernel,
+        name="pack",
+        out_shape=[pltpu.HBM((held + 2 * rows, width), BF16)] * 4,
+        in_specs=[hbm, VM, VM, pl.BlockSpec(memory_space=pl.ANY)],
         out_specs=[hbm] * 4,
-        scratch_shapes=[pltpu.SemaphoreType.DMA((4,))],
+        scratch_shapes=[pltpu.VMEM((held, width), BF16)]
+        + [pltpu.VMEM((2 * rows, width), BF16)] * 4
+        + [pltpu.SemaphoreType.DMA((16,))],
         compiler_params=VLIM,
-    )(*pin([w, after]))
+    )(*pin([w_down]), qa, qb, after)
 
 
 def cells_body(near, far, outs, own):
-    rows = outs[0].shape[0] // 2
-    lane = iota((rows, outs[0].shape[1]), 1)
-    outs[0][...] = cell_map(flip(far[0].get()[...], 1), (lane // 8).astype(F32), lane)
+    buf = outs[0].buf
+    lane = iota((buf.shape[0] // 2, buf.shape[1]), 1)
+    buf[...] = cell_map(flip(far[0].get()[...], 1), (lane // 8).astype(F32), lane)
 
 
 def cells_table(routes, experts, after):
     out = sds((2 * routes.shape[0], experts * 8), BF16)
-    return run(cells_body, "cells_table", [out], [], [routes.T], after_hbm=[after])[0]
+    return run(cells_body, "cells_table", [], [], [routes.T], after_hbm=[after], leaving=[out])[0]
 
 
 def mix_body(near, far, outs, own):
@@ -442,14 +476,15 @@
     att = jnp.concatenate(unfold(tok_ref[...].astype(F32)), axis=1).astype(BF16)
     rows = pl.ds(head_blocks(eff)[0], eff)
     for k, first in enumerate(head_blocks(2 * w)):
-        pair = unfold(far[k].get()[...].astype(F32))
+        res = far[k].get()[...].astype(F32)
+        pair = unfold(res.reshape(res.shape[0] // 8, 8, w))
         for f in range(2):
             xs[2 * k + f] = pair[f] + dot(att, wo_ref[rows, pl.ds(first + f * w, w)])
 
 
 def early_rows(tokens, out_weight, res):
     n = tokens.shape[0]
-    w = res[0].shape[2]
+    w = res[0][0].shape[1]
     return run(early_body, "early_rows", [sds((8, n * 4, w), F32)], [tokens, out_weight], res)[0]
 
 
@@ -468,7 +503,8 @@
     acc = own_res.get()[:, cols].astype(F32)
     acc = acc + sum(dot(mine[i].get()[...], wo_ref[pl.ds(block[i], eff), cols]) for i in range(4))
     hid.buf[...] = acc.astype(BF16)
-    hid.send()
+    for _ in range(PIECES):
+        hid.send()
     total = jnp.zeros((n, 1), F32)
     for j, first in enumerate(firsts):
         acc = xs[j]
@@ -500,9 +536,10 @@
 
 def down_body(near, far, outs, own):
     out_ref = outs[0]
-    acc = sum(dot(near[k][...], near[4 + k][...]) for k in range(4))
-    width = acc.shape[1]
-    a, b = fold(acc[:, : width // 2], acc[:, width // 2 :])
+    k_rows = near[0].shape[1]
+    left = sum(dot(near[k][...], near[4 + k][0:k_rows]) for k in range(4))
+    right = sum(dot(near[k][...], near[4 + k][k_rows : 2 * k_rows]) for k in range(4))
+    a, b = fold(left, right)
     out_ref[:, 0] = a.astype(BF16)
     out_ref[:, 1] = b.astype(BF16)
 
@@ -510,8 +547,8 @@
 def down(inners, w_cols, after):
     rows = inners[0].shape[0]
     width = w_cols[0].shape[1]
-    out = run(down_body, "down", [sds((rows // 8, 2, 8, width // 2), BF16)], [*inners, *w_cols], [], after=[after])[0]
-    return out.reshape(rows // 4, 8, width // 2)
+    out = run(down_body, "down", [sds((rows // 8, 2, 8, width), BF16)], [*inners, *w_cols], [], after=[after])[0]
+    return out.reshape(rows // 4, 8, width)
 
 
 def blend_body(near, far, outs, own):
@@ -529,21 +566,24 @@
     return run(blend_body, "blend", [sds(hidden.shape, BF16)], [returned, *mix], [hidden])[0]
 
 
-def norm_body(near, far, outs, own):
-    head = head_id()
+def qkv_body(near, far, outs, own):
+    w_ref = near[3]
     w = near[0].shape[1]
-    parts = [s[...].astype(F32) for s in (far[1].get(), *near)]
+    parts = [s[...].astype(F32) for s in (far[1].get(), *near[:3])]
     total = sum(jnp.sum(p * p, axis=1, keepdims=True) for p in parts)
     scale = lax.rsqrt(total / (4 * w) + EPS)
     gain_ref = far[0].get()
-    for k, p in enumerate(parts):
-        cols = pl.ds(pl.multiple_of(((head + 4 - k) % 4) * w, w), w)
-        outs[0][:, cols] = (p * scale * gain_ref[:, cols]).astype(BF16)
-
-
-def norm_parts(parts, gain):
-    rows, w = parts[0].shape
-    return run(norm_body, "norm_parts", [sds((rows, 4 * w), BF16)], parts[1:], [gain.reshape(1, -1), parts[0]])[0]
+    cols = [pl.ds(first, w) for first in head_blocks(w)]
+    normed = [(p * scale * gain_ref[:, c]).astype(BF16) for p, c in zip(parts, cols)]
+    for i in range(outs[0].shape[0]):
+        acc = sum(dot(n, w_ref[i, c, :]) for n, c in zip(normed, cols))
+        outs[0][i] = acc.astype(BF16)
+
+
+def next_proj(parts, gain, weight):
+    kinds, _, width = weight.shape
+    out = sds((kinds, parts[0].shape[0], width), BF16)
+    return run(qkv_body, "next_proj", [out], [*parts[1:], weight], [gain.reshape(1, -1), parts[0]])[0]
 
 
 def from_heads(x):
@@ -570,27 +610,30 @@
     out_weight = lax.all_gather(out_weight, "head", axis=0, tiled=True)
     qa = lax.all_to_all(outset(queries, residual, routes, chips), ("z", "y"), 0, 0, tiled=True)
     tables = slot_tables(slot_request, slot_page, slot_used, lengths, kv_cache, [qa])
-    keep, send, res = attend_pages(tables, qa, swap_core(qa))
-    merged = merge(keep, swap_core(send))
-    w_cols = to_heads(split_columns(w_down[0], merged))
+    qb = swap_core(qa)
+    keep, send = attend_pages(tables, qa, qb)
+    packs = pack(w_down[0], qa, qb, send)
+    merged = merge(keep, swap_core(send), packs[0])
+    packs = to_heads(packs)
     cells = cells_table(routes, experts, merged)
-    res = from_heads(res.reshape(experts, 8, -1))
     arrived = lax.all_to_all(merged, ("z", "y"), 0, 0, tiled=True)
     arrived, cells = lax.optimization_barrier((arrived, cells))
     attended, disp = owner_part(arrived, queries, new_kv, cells, experts)
     tokens = lax.all_to_all(disp, REQ, 0, 0, tiled=True)
-    tokens, attended, res, w_cols = lax.optimization_barrier((tokens, attended, res, w_cols))
+    mine = from_heads(attended)
+    tokens, mine, packs = lax.optimization_barrier((tokens, mine, packs))
+    held = experts * 8
+    res = [(p, 0, held) for p in packs]
     out_weight, w_gate, w_up = fetch(tokens, out_weight, w_gate[0], w_up[0])
     early = early_rows(tokens, out_weight, res)
-    others, mine = from_heads(tokens)[1:], from_heads(attended)
+    others = from_heads(tokens)[1:]
     inner, hidden = expert_rows(others, early, out_weight, w_gate, w_up, norm_gain, mine, residual)
-    w_cols = fetch(inner, *w_cols)
+    w_cols = fetch(inner, *[(p, held, p.shape[0] - held) for p in packs])
     mix = mix_table(routes, route_weights, experts, inner)
     expert_out = down(from_heads(inner), w_cols, mix[0])
     returned = lax.all_to_all(expert_out, REQ, 0, 0, tiled=True)
     stream = blend(returned, mix, hidden)
-    normed = norm_parts(from_heads(stream), next_gain)
-    next_qkv = jnp.einsum("td,dcf->tcf", normed, next_weight, preferred_element_type=F32).astype(BF16)
+    next_qkv = next_proj(from_heads(stream), next_gain, next_weight.transpose(1, 0, 2)).transpose(1, 0, 2)
     return stream, next_qkv
 
 

time: 188 us -> 151 us (0.80)
  Pallas kernels: 61.6 us -> 31 us
  starting transfers between devices: 40.2 us -> 35.2 us
  blocking collectives: 47.6 us -> 50.5 us
  waiting for transfers between devices: 21.3 us -> 18.9 us
    pallas_call x1, Pallas kernels: 32.9 us -> 2.57 us  [pack(): pl.pallas_call(pack_kernel, name='pack', out_shape=[pltpu.HBM((held + 2 *...]
    all_to_all x1, waiting for transfers between devices: 11.1 us -> 2.73 us  [local(): tokens = lax.all_to_all(disp, REQ, 0, 0, tiled=True)]
    all_to_all x1, waiting for transfers between devices: 0.01 us -> 7.29 us  [local(): arrived = lax.all_to_all(merged, ('z', 'y'), 0, 0, tiled=True)]
    all_to_all x1, starting transfers between devices: 11.8 us -> 6.87 us  [local(): tokens = lax.all_to_all(disp, REQ, 0, 0, tiled=True)]
    ppermute x3, waiting for transfers between devices: 0.01 us -> 3.16 us  [to_heads(): lax.ppermute(xs[k], 'head', [(i, (i + k) % n) for i in range(n)])]
    all_to_all x1, blocking collectives: 19.5 us -> 22.4 us  [local(): returned = lax.all_to_all(expert_out, REQ, 0, 0, tiled=True)]
    ppermute x15 -> x12, waiting for transfers between devices: 7.82 us -> 5.06 us  [from_heads(): lax.ppermute(x, 'head', [(i, (i + k) % n) for i in range(n)])]
    ppermute x15 -> x12, starting transfers between devices: 18.6 us -> 16.5 us  [from_heads(): lax.ppermute(x, 'head', [(i, (i + k) % n) for i in range(n)])]
  transfers between devices with their start and end apart: 23 -> 20, of which waited for: 8 -> 11; matrix products, arithmetic and copies ran while one was open for 0% -> 0% of each run, Pallas kernels for 29% -> 16%
where the time goes in v7:
time: 151 us; the launch traced here: 150 us
  blocking collectives  50.5 us (33%)
  starting transfers between devices  35.2 us (23%)
  Pallas kernels  31 us (21%)
  waiting for transfers between devices  18.9 us (13%)
  between operations  14.3 us (9%)
    pallas_call x14, Pallas kernels, run(): pl.pallas_call(kernel, name=name, out_shape=list(outs) + [pltpu.HBM(x.sha...  28.4 us
    all_to_all x1, blocking collectives, local(): lax.all_to_all(outset(queries, residual, routes, chips), ('z', 'y'), 0, 0...  28.1 us
    all_to_all x1, blocking collectives, local(): returned = lax.all_to_all(expert_out, REQ, 0, 0, tiled=True)  22.4 us
    ppermute x12, starting transfers between devices, from_heads(): lax.ppermute(x, 'head', [(i, (i + k) % n) for i in range(n)])  16.5 us
    all_to_all x1, waiting for transfers between devices, local(): arrived = lax.all_to_all(merged, ('z', 'y'), 0, 0, tiled=True)  7.29 us
    all_to_all x1, starting transfers between devices, local(): tokens = lax.all_to_all(disp, REQ, 0, 0, tiled=True)  6.87 us
    ppermute x12, waiting for transfers between devices, from_heads(): lax.ppermute(x, 'head', [(i, (i + k) % n) for i in range(n)])  5.06 us
    ppermute x3, starting transfers between devices, to_heads(): lax.ppermute(xs[k], 'head', [(i, (i + k) % n) for i in range(n)])  4.87 us
  transfers between devices with their start and end apart: 20, of which 11 were waited for; matrix products, arithmetic and copies ran while one was open for 0% of the time, Pallas kernels for 16%

profile of v7, /device:TPU:1, one launch (start us, length us, event | category | flops | bytes accessed | tf_op | source)
XLA Modules:
  0.0 149.9 jit_solution(2091007593970055737)
XLA Ops:
  7.2 0.0 all-gather.2.cloned.1.call-start
  7.2 0.7 all-gather.2.cloned.1.call-update
  7.9 1.4 outset.1
  9.3 28.1 %all_to_all.20.refs_4_.refs_7_.qa_ref = bf16[32,32,256]{2,1,0:T(8,128)(2,1)S(1)} all-to-all(bf16[32,32,256]{2,1,0:T(8,128)(2,1)S(1)} %outset.1), channel_id=1, replica_groups=mesh['z'=8,'y'=4,'c'=2,'head'=4] {'z','y'}, dimensions={0} | all-to-all | bytes 1048576 | tf_op jit(solution)/shard_map/all_to_all | solution.py:611
  37.4 2.4 %collective-permute-start = (bf16[32,32,256]{2,1,0:T(8,128)(2,1)S(1)}, bf16[32,32,256]{2,1,0:T(8,128)(2,1)S(1)}, u32[]{:S(2)}, u32[]{:S(2)}) collective-permute-start(bf16[32,32,256]{2,1,0:T(8,128)(2,1)S(1)} %all_to_all.20.refs_4_.refs_7_.qa_ref), channel_id=1, source_target_pairs={{0,4},{4,0},{1,5},{5,1},{2,6},{6,2},{3,7},{7,3},{8,12},{12,8},{9,1... | collective-permute-start | bytes 1572872 | tf_op jit(solution)/shard_map/ppermute | solution.py:600
  39.8 2.4 %slot_tables.1 = (bf16[128,1024]{1,0:T(8,128)(2,1)S(1)}, f32[128,128]{1,0:T(8,128)S(1)}, f32[128,128]{1,0:T(8,128)S(1)}, f32[128,128]{1,0:T(8,128)S(1)}, bf16[10...) custom-call(s32[1,128]{1,0:T(1,128)} %bitcast.27, s32[1,128]{1,0:T(1,128)} %bitcast.28, ...), custom_call_target="tpu_custom_call" | custom-call | tf_op jit(solution)/shard_map/slot_tables/pallas_call | solution.py:100
  42.2 5.0 %attend_pages.1 = (bf16[32,48,128]{2,1,0:T(8,128)(2,1)S(1)}, bf16[32,48,128]{2,1,0:T(8,128)(2,1)S(1)}) custom-call(bf16[128,1024]{1,0:T(8,128)(2,1)S(1)} %get-tuple-element.39.refs_0_, f32[128,128]{1,0:T(8,128)S(1)} %get-tuple-element.40.refs_1_, f32[128,128]{1,0:T(8,128)S(1)} %get-tuple-element.41.refs_2_, f32[128,128]{1,0:T(8,128)S(1)} %get-tuple-element.42.refs_3_, ...), custom_call_target="tpu_custom_call" | custom-call | tf_op jit(solution)/shard_map/attend_pages/pallas_call | solution.py:100
  47.2 0.1 collective-permute-start.1
  47.3 2.6 %pack.1 = (bf16[1024,256]{1,0:T(8,128)(2,1)}, bf16[1024,256]{1,0:T(8,128)(2,1)}, bf16[1024,256]{1,0:T(8,128)(2,1)}, bf16[1024,256]{1,0:T(8,128)(2,1)}) custom-call(bf16[256,2048]{1,0:T(8,128)(2,1)} %bitcast.18, bf16[32,32,256]{2,1,0:T(8,128)(2,1)S(1)} %all_to_all.20.refs_4_.refs_7_.qa_ref, bf16[32,32,256]{2,1,0:T(8,128)(2,1)S(1)} %collective-permute-done.refs_8_.qb_ref, ...), custom_call_target="tpu_custom_call" | custom-call | tf_op jit(solution)/shard_map/pack/pallas_call | solution.py:353
  49.9 1.4 merge.1.refs_1_
  51.3 4.4 %all-to-all-start.1 = ((bf16[32,48,128]{2,1,0:T(8,128)(2,1)}), bf16[32,48,128]{2,1,0:T(8,128)(2,1)S(1)}, u32[]{:S(2)}, u32[]{:S(2)}) async-start(bf16[32,48,128]{2,1,0:T(8,128)(2,1)} %merge.1.refs_1_), calls=%async_computation.1 | async-start | bytes 786432 | tf_op jit(solution)/shard_map/all_to_all | solution.py:619
  55.8 1.3 collective-permute-start.5
  57.0 2.5 %collective-permute-start.6 = (bf16[1024,256]{1,0:T(8,128)(2,1)}, bf16[1024,256]{1,0:T(8,128)(2,1)S(1)}, u32[]{:S(2)}, u32[]{:S(2)}) collective-permute-start(bf16[1024,256]{1,0:T(8,128)(2,1)} %get-tuple-element.54), channel_id=1, source_target_pairs={{0,2},{1,3},{2,0},{3,1},{4,6},{5,7},{6,4},{7,5},{8,10},{9,11},{10,... | collective-permute-start | bytes 1572872 | tf_op jit(solution)/shard_map/ppermute | solution.py:596
  59.5 1.1 collective-permute-start.7
  60.6 1.7 %cells_table.1.refs_3_ = bf16[32,512]{1,0:T(8,128)(2,1)} custom-call(s32[8,16]{1,0:T(8,128)} %bitcast.20, bf16[32,48,128]{2,1,0:T(8,128)(2,1)} %merge.1.refs_1_), custom_call_target="tpu_custom_call" | custom-call | tf_op jit(solution)/shard_map/cells_table/pallas_call | solution.py:100
  62.3 7.3 %all-to-all-done.1.refs_0_ = bf16[32,48,128]{2,1,0:T(8,128)(2,1)S(1)} async-done(((bf16[32,48,128]{2,1,0:T(8,128)(2,1)}), bf16[32,48,128]{2,1,0:T(8,128)(2,1)S(1)}, u32[]{:S(2)}, u32[]{:S(2)}) %all-to-all-start.1) | async-done | bytes 393248 | tf_op jit(solution)/shard_map/all_to_all | solution.py:619
  69.6 2.2 %owner_part.1 = (bf16[16,256]{1,0:T(8,128)(2,1)S(1)}, bf16[64,8,128]{2,1,0:T(8,128)(2,1)}) custom-call(bf16[32,48,128]{2,1,0:T(8,128)(2,1)S(1)} %all-to-all-done.1.refs_0_, bf16[16,256]{1,0:T(8,128)(2,1)} %refs_1_.3, bf16[16,2,256]{2,1,0:T(2,128)(2,1)} %refs_2_.1, bf16[32,512]{1,0:T(8,128)(2,1)} %cells_table.1.refs_3_), custom_call_target="tpu_custom_call" | custom-call | tf_op jit(solution)/shard_map/owner_part/pallas_call | solution.py:100
  71.8 6.9 %all-to-all-start.2 = ((bf16[64,8,128]{2,1,0:T(8,128)(2,1)}), bf16[64,8,128]{2,1,0:T(8,128)(2,1)S(1)}, u32[]{:S(2)}, u32[]{:S(2)}) async-start(bf16[64,8,128]{2,1,0:T(8,128)(2,1)} %get-tuple-element.51), calls=%async_computation.2 | async-start | bytes 262144 | tf_op jit(solution)/shard_map/all_to_all | solution.py:622
  78.7 1.3 collective-permute-start.2
  79.9 2.5 %collective-permute-start.3 = (bf16[16,256]{1,0:T(8,128)(2,1)S(1)}, bf16[16,256]{1,0:T(8,128)(2,1)S(1)}, u32[]{:S(2)}, u32[]{:S(2)}) collective-permute-start(bf16[16,256]{1,0:T(8,128)(2,1)S(1)} %get-tuple-element.64.refs_8_), channel_id=1, source_target_pairs={{0,2},{1,3},{2,0},{3,1},{4,6},{5,7},{6,4},{7,5},{8,10},{9,11},{10,... | collective-permute-start | bytes 24584 | tf_op jit(solution)/shard_map/ppermute | solution.py:591
  82.4 1.1 collective-permute-start.4
  83.6 3.2 %collective-permute-done.6.refs_4_.refs_3_ = bf16[1024,256]{1,0:T(8,128)(2,1)S(1)} collective-permute-done((bf16[1024,256]{1,0:T(8,128)(2,1)}, bf16[1024,256]{1,0:T(8,128)(2,1)S(1)}, u32[]{:S(2)}, u32[]{:S(2)}) %collective-permute-start.6) | collective-permute-done | bytes 524320 | tf_op jit(solution)/shard_map/ppermute | solution.py:596
  86.7 0.3 collective-permute-done.3.refs_10_
  87.1 2.7 %all-to-all-done.2.refs_0_ = bf16[64,8,128]{2,1,0:T(8,128)(2,1)S(1)} async-done(((bf16[64,8,128]{2,1,0:T(8,128)(2,1)}), bf16[64,8,128]{2,1,0:T(8,128)(2,1)S(1)}, u32[]{:S(2)}, u32[]{:S(2)}) %all-to-all-start.2) | async-done | bytes 131104 | tf_op jit(solution)/shard_map/all_to_all | solution.py:622
  89.8 2.5 %collective-permute-start.10 = (bf16[64,8,128]{2,1,0:T(8,128)(2,1)S(1)}, bf16[64,8,128]{2,1,0:T(8,128)(2,1)S(1)}, u32[]{:S(2)}, u32[]{:S(2)}) collective-permute-start(bf16[64,8,128]{2,1,0:T(8,128)(2,1)S(1)} %all-to-all-done.2.refs_0_), channel_id=1, source_target_pairs={{0,3},{1,0},{2,1},{3,2},{4,7},{5,4},{6,5},{7,6},{8,11},{9,8},{10,9... | collective-permute-start | bytes 393224 | tf_op jit(solution)/shard_map/ppermute | solution.py:591
  92.3 1.7 %collective-permute-start.9 = (bf16[64,8,128]{2,1,0:T(8,128)(2,1)S(1)}, bf16[64,8,128]{2,1,0:T(8,128)(2,1)S(1)}, u32[]{:S(2)}, u32[]{:S(2)}) collective-permute-start(bf16[64,8,128]{2,1,0:T(8,128)(2,1)S(1)} %all-to-all-done.2.refs_0_), channel_id=1, source_target_pairs={{0,2},{1,3},{2,0},{3,1},{4,6},{5,7},{6,4},{7,5},{8,10},{9,11},{10,... | collective-permute-start | bytes 393224 | tf_op jit(solution)/shard_map/ppermute | solution.py:591
  94.0 2.9 %fetch.2 = (bf16[1024,2048]{1,0:T(8,128)(2,1)S(1)}, bf16[2048,256]{1,0:T(8,128)(2,1)S(1)}, bf16[2048,256]{1,0:T(8,128)(2,1)S(1)}) custom-call(bf16[64,8,128]{2,1,0:T(8,128)(2,1)S(1)} %all-to-all-done.2.refs_0_, bf16[1024,2048]{1,0:T(8,128)(2,1)} %all-gather.2.cloned.1.call-done.refs_1_, bf16[2048,256]{1,0:T(8,128)(2,1)} %bitcast.16, bf16[2048,256]{1,0:T(8,128)(2,1)} %bitcast.17), custom_call_target="tpu_custom_call" | custom-call | tf_op jit(solution)/shard_map/fetch/pallas_call | solution.py:100
  96.9 1.9 %early_rows.1.refs_3_ = f32[8,256,256]{2,1,0:T(8,128)S(1)} custom-call(bf16[64,8,128]{2,1,0:T(8,128)(2,1)S(1)} %all-to-all-done.2.refs_0_, bf16[1024,2048]{1,0:T(8,128)(2,1)S(1)} %get-tuple-element.57.refs_1_.refs_4_, bf16[1024,256]{1,0:T(8,128)(2,1)} %get-tuple-element.58.refs_2_.refs_1_, bf16[1024,256]{1,0:T(8,128)(2,1)} %copy-done.2, ...), custom_call_target="tpu_custom_call" | custom-call | tf_op jit(solution)/shard_map/early_rows/pallas_call | solution.py:100
  98.9 0.3 collective-permute-done.8.refs_0_
  99.2 0.5 collective-permute-done.9.refs_1_
  99.7 3.1 %expert_rows.1 = (bf16[256,256]{1,0:T(8,128)(2,1)S(1)}, bf16[16,512]{1,0:T(8,128)(2,1)}) custom-call(bf16[64,8,128]{2,1,0:T(8,128)(2,1)S(1)} %collective-permute-done.8.refs_0_, bf16[64,8,128]{2,1,0:T(8,128)(2,1)S(1)} %collective-permute-done.9.refs_1_, bf16[64,8,128]{2,1,0:T(8,128)(2,1)S(1)} %collective-permute-done.10.refs_2_, ...), custom_call_target="tpu_custom_call" | custom-call | tf_op jit(solution)/shard_map/expert_rows/pallas_call | solution.py:100
  102.8 0.0 copy-start
  102.8 0.9 collective-permute-start.11
  103.7 1.0 collective-permute-start.12
  104.6 1.9 %collective-permute-start.13 = (bf16[256,256]{1,0:T(8,128)(2,1)S(1)}, bf16[256,256]{1,0:T(8,128)(2,1)S(1)}, u32[]{:S(2)}, u32[]{:S(2)}) collective-permute-start(bf16[256,256]{1,0:T(8,128)(2,1)S(1)} %get-tuple-element.68.refs_0_.refs_2_), channel_id=1, source_target_pairs={{0,3},{1,0},{2,1},{3,2},{4,7},{5,4},{6,5},{7,6},{8,11},{9,8},{10,9... | collective-permute-start | bytes 393224 | tf_op jit(solution)/shard_map/ppermute | solution.py:591
  106.5 1.4 fetch.3
  107.9 1.1 mix_table.1
  109.0 0.9 collective-permute-done.12.refs_2_
  109.9 0.3 collective-permute-done.13.refs_3_
  110.2 0.5 down.1
  110.6 22.4 %all_to_all.21.refs_0_ = bf16[64,8,256]{2,1,0:T(8,128)(2,1)S(1)} all-to-all(bf16[64,8,256]{2,1,0:T(8,128)(2,1)S(1)} %bitcast.15), channel_id=1, replica_groups=mesh['z'=8,'y'=4,'c'=2,'head'=4] {'z','y','c'}, dimensions={0} | all-to-all | bytes 524288 | tf_op jit(solution)/shard_map/all_to_all | solution.py:634
  133.0 1.6 %blend.1.refs_5_ = bf16[16,512]{1,0:T(8,128)(2,1)} custom-call(bf16[64,8,256]{2,1,0:T(8,128)(2,1)S(1)} %all_to_all.21.refs_0_, bf16[16,256]{1,0:T(8,128)(2,1)S(1)} %get-tuple-element.73.refs_8_.refs_1_, bf16[16,256]{1,0:T(8,128)(2,1)S(1)} %get-tuple-element.74.refs_2_, bf16[16,512]{1,0:T(8,128)(2,1)} %get-tuple-element.75.refs_3_), custom_call_target="tpu_custom_call" | custom-call | tf_op jit(solution)/shard_map/blend/pallas_call | solution.py:100
  134.6 0.4 collective-permute-start.14
  135.0 3.2 %collective-permute-start.15 = (bf16[16,512]{1,0:T(8,128)(2,1)}, bf16[16,512]{1,0:T(8,128)(2,1)S(1)}, u32[]{:S(2)}, u32[]{:S(2)}) collective-permute-start(bf16[16,512]{1,0:T(8,128)(2,1)} %blend.1.refs_5_), channel_id=1, source_target_pairs={{0,2},{1,3},{2,0},{3,1},{4,6},{5,7},{6,4},{7,5},{8,10},{9,11},{10,... | collective-permute-start | bytes 49160 | tf_op jit(solution)/shard_map/ppermute | solution.py:591
  138.2 0.4 collective-permute-done.14.refs_0_
  138.7 1.1 collective-permute-done.15.refs_1_
  139.7 1.3 collective-permute-done.16.refs_2_
  141.0 2.0 %next_proj.1 = bf16[3,16,256]{2,1,0:T(8,128)(2,1)} custom-call(bf16[16,512]{1,0:T(8,128)(2,1)S(1)} %collective-permute-done.14.refs_0_, bf16[16,512]{1,0:T(8,128)(2,1)S(1)} %collective-permute-done.15.refs_1_, bf16[16,512]{1,0:T(8,128)(2,1)S(1)} %collective-permute-done.16.refs_2_, bf16[3,2048,256]{2,1,0:T(8,128)(2,1)S(1)} %bitcast.14, f32[1,2048]{1,0:T(1,128)} %bitcast.24, ...), custom_call_target="tpu_custom_call" | custom-call | tf_op jit(solution)/shard_map/next_proj/pallas_call | solution.py:100
  (26 shorter events, 0.1 us)
Async XLA Ops:
  7.2 86.8 %all-gather.2.cloned.1.call-start = ((), (), s32[]{:S(2)}) async-start(), calls=%async_computation.4 | async-start | bytes 5242880 | tf_op jit(solution)/shard_map/all_gather | solution.py:610
  37.4 4.8 %collective-permute-start = (bf16[32,32,256]{2,1,0:T(8,128)(2,1)S(1)}, bf16[32,32,256]{2,1,0:T(8,128)(2,1)S(1)}, u32[]{:S(2)}, u32[]{:S(2)}) collective-permute-start(bf16[32,32,256]{2,1,0:T(8,128)(2,1)S(1)} %all_to_all.20.refs_4_.refs_7_.qa_ref), channel_id=1, source_target_pairs={{0,4},{4,0},{1,5},{5,1},{2,6},{6,2},{3,7},{7,3},{8,12},{12,8},{9,1... | collective-permute-start | bytes 1572872 | tf_op jit(solution)/shard_map/ppermute | solution.py:600
  47.2 2.7 %collective-permute-start.1 = (bf16[32,48,128]{2,1,0:T(8,128)(2,1)S(1)}, bf16[32,48,128]{2,1,0:T(8,128)(2,1)S(1)}, u32[]{:S(2)}, u32[]{:S(2)}) collective-permute-start(bf16[32,48,128]{2,1,0:T(8,128)(2,1)S(1)} %get-tuple-element.47.after_ref), channel_id=1, source_target_pairs={{0,4},{4,0},{1,5},{5,1},{2,6},{6,2},{3,7},{7,3},{8,12},{12,8},{9,1... | collective-permute-start | bytes 1179656 | tf_op jit(solution)/shard_map/ppermute | solution.py:600
  51.3 18.3 %all-to-all-start.1 = ((bf16[32,48,128]{2,1,0:T(8,128)(2,1)}), bf16[32,48,128]{2,1,0:T(8,128)(2,1)S(1)}, u32[]{:S(2)}, u32[]{:S(2)}) async-start(bf16[32,48,128]{2,1,0:T(8,128)(2,1)} %merge.1.refs_1_), calls=%async_computation.1 | async-start | bytes 786432 | tf_op jit(solution)/shard_map/all_to_all | solution.py:619
  55.8 26.7 %collective-permute-start.5 = (bf16[1024,256]{1,0:T(8,128)(2,1)}, bf16[1024,256]{1,0:T(8,128)(2,1)S(1)}, u32[]{:S(2)}, u32[]{:S(2)}) collective-permute-start(bf16[1024,256]{1,0:T(8,128)(2,1)} %get-tuple-element.53), channel_id=1, source_target_pairs={{0,1},{1,2},{2,3},{3,0},{4,5},{5,6},{6,7},{7,4},{8,9},{9,10},{10,1... | collective-permute-start | bytes 1572872 | tf_op jit(solution)/shard_map/ppermute | solution.py:596
  57.0 29.7 %collective-permute-start.6 = (bf16[1024,256]{1,0:T(8,128)(2,1)}, bf16[1024,256]{1,0:T(8,128)(2,1)S(1)}, u32[]{:S(2)}, u32[]{:S(2)}) collective-permute-start(bf16[1024,256]{1,0:T(8,128)(2,1)} %get-tuple-element.54), channel_id=1, source_target_pairs={{0,2},{1,3},{2,0},{3,1},{4,6},{5,7},{6,4},{7,5},{8,10},{9,11},{10,... | collective-permute-start | bytes 1572872 | tf_op jit(solution)/shard_map/ppermute | solution.py:596
  59.5 27.2 %collective-permute-start.7 = (bf16[1024,256]{1,0:T(8,128)(2,1)}, bf16[1024,256]{1,0:T(8,128)(2,1)S(1)}, u32[]{:S(2)}, u32[]{:S(2)}) collective-permute-start(bf16[1024,256]{1,0:T(8,128)(2,1)} %get-tuple-element.55), channel_id=1, source_target_pairs={{0,3},{1,0},{2,1},{3,2},{4,7},{5,4},{6,5},{7,6},{8,11},{9,8},{10,9... | collective-permute-start | bytes 1572872 | tf_op jit(solution)/shard_map/ppermute | solution.py:596
  71.8 27.1 %copy-start.1 = (bf16[16,256]{1,0:T(8,128)(2,1)}, bf16[16,256]{1,0:T(8,128)(2,1)S(1)}, u32[]{:S(2)}) copy-start(bf16[16,256]{1,0:T(8,128)(2,1)S(1)} %get-tuple-element.64.refs_8_) | copy-start | bytes 24580
  71.8 18.0 %all-to-all-start.2 = ((bf16[64,8,128]{2,1,0:T(8,128)(2,1)}), bf16[64,8,128]{2,1,0:T(8,128)(2,1)S(1)}, u32[]{:S(2)}, u32[]{:S(2)}) async-start(bf16[64,8,128]{2,1,0:T(8,128)(2,1)} %get-tuple-element.51), calls=%async_computation.2 | async-start | bytes 262144 | tf_op jit(solution)/shard_map/all_to_all | solution.py:622
  78.7 8.0 %collective-permute-start.2 = (bf16[16,256]{1,0:T(8,128)(2,1)S(1)}, bf16[16,256]{1,0:T(8,128)(2,1)S(1)}, u32[]{:S(2)}, u32[]{:S(2)}) collective-permute-start(bf16[16,256]{1,0:T(8,128)(2,1)S(1)} %get-tuple-element.64.refs_8_), channel_id=1, source_target_pairs={{0,1},{1,2},{2,3},{3,0},{4,5},{5,6},{6,7},{7,4},{8,9},{9,10},{10,1... | collective-permute-start | bytes 24584 | tf_op jit(solution)/shard_map/ppermute | solution.py:591
  79.9 7.1 %collective-permute-start.3 = (bf16[16,256]{1,0:T(8,128)(2,1)S(1)}, bf16[16,256]{1,0:T(8,128)(2,1)S(1)}, u32[]{:S(2)}, u32[]{:S(2)}) collective-permute-start(bf16[16,256]{1,0:T(8,128)(2,1)S(1)} %get-tuple-element.64.refs_8_), channel_id=1, source_target_pairs={{0,2},{1,3},{2,0},{3,1},{4,6},{5,7},{6,4},{7,5},{8,10},{9,11},{10,... | collective-permute-start | bytes 24584 | tf_op jit(solution)/shard_map/ppermute | solution.py:591
  82.4 14.4 %copy-start.2 = (bf16[1024,256]{1,0:T(8,128)(2,1)}, bf16[1024,256]{1,0:T(8,128)(2,1)S(1)}, u32[]{:S(2)}) copy-start(bf16[1024,256]{1,0:T(8,128)(2,1)S(1)} %collective-permute-done.5.refs_3_.refs_2_) | copy-start | bytes 1572868
  82.4 4.6 %collective-permute-start.4 = (bf16[16,256]{1,0:T(8,128)(2,1)S(1)}, bf16[16,256]{1,0:T(8,128)(2,1)S(1)}, u32[]{:S(2)}, u32[]{:S(2)}) collective-permute-start(bf16[16,256]{1,0:T(8,128)(2,1)S(1)} %get-tuple-element.64.refs_8_), channel_id=1, source_target_pairs={{0,3},{1,0},{2,1},{3,2},{4,7},{5,4},{6,5},{7,6},{8,11},{9,8},{10,9... | collective-permute-start | bytes 24584 | tf_op jit(solution)/shard_map/ppermute | solution.py:591
  86.7 10.2 %copy-start.3 = (bf16[1024,256]{1,0:T(8,128)(2,1)}, bf16[1024,256]{1,0:T(8,128)(2,1)S(1)}, u32[]{:S(2)}) copy-start(bf16[1024,256]{1,0:T(8,128)(2,1)S(1)} %collective-permute-done.6.refs_4_.refs_3_) | copy-start | bytes 1572868
  86.7 10.2 %copy-start.4 = (bf16[1024,256]{1,0:T(8,128)(2,1)}, bf16[1024,256]{1,0:T(8,128)(2,1)S(1)}, u32[]{:S(2)}) copy-start(bf16[1024,256]{1,0:T(8,128)(2,1)S(1)} %collective-permute-done.7.refs_5_.refs_4_) | copy-start | bytes 1572868
  86.7 12.1 %copy-start.5 = (bf16[16,256]{1,0:T(8,128)(2,1)}, bf16[16,256]{1,0:T(8,128)(2,1)S(1)}, u32[]{:S(2)}) copy-start(bf16[16,256]{1,0:T(8,128)(2,1)S(1)} %collective-permute-done.2.refs_9_) | copy-start | bytes 24580
  87.1 11.8 %copy-start.6 = (bf16[16,256]{1,0:T(8,128)(2,1)}, bf16[16,256]{1,0:T(8,128)(2,1)S(1)}, u32[]{:S(2)}) copy-start(bf16[16,256]{1,0:T(8,128)(2,1)S(1)} %collective-permute-done.3.refs_10_) | copy-start | bytes 24580
  87.1 11.8 %copy-start.7 = (bf16[16,256]{1,0:T(8,128)(2,1)}, bf16[16,256]{1,0:T(8,128)(2,1)S(1)}, u32[]{:S(2)}) copy-start(bf16[16,256]{1,0:T(8,128)(2,1)S(1)} %collective-permute-done.4.refs_11_) | copy-start | bytes 24580
  89.8 9.1 %collective-permute-start.10 = (bf16[64,8,128]{2,1,0:T(8,128)(2,1)S(1)}, bf16[64,8,128]{2,1,0:T(8,128)(2,1)S(1)}, u32[]{:S(2)}, u32[]{:S(2)}) collective-permute-start(bf16[64,8,128]{2,1,0:T(8,128)(2,1)S(1)} %all-to-all-done.2.refs_0_), channel_id=1, source_target_pairs={{0,3},{1,0},{2,1},{3,2},{4,7},{5,4},{6,5},{7,6},{8,11},{9,8},{10,9... | collective-permute-start | bytes 393224 | tf_op jit(solution)/shard_map/ppermute | solution.py:591
  92.3 7.0 %collective-permute-start.8 = (bf16[64,8,128]{2,1,0:T(8,128)(2,1)S(1)}, bf16[64,8,128]{2,1,0:T(8,128)(2,1)S(1)}, u32[]{:S(2)}, u32[]{:S(2)}) collective-permute-start(bf16[64,8,128]{2,1,0:T(8,128)(2,1)S(1)} %all-to-all-done.2.refs_0_), channel_id=1, source_target_pairs={{0,1},{1,2},{2,3},{3,0},{4,5},{5,6},{6,7},{7,4},{8,9},{9,10},{10,1... | collective-permute-start | bytes 393224 | tf_op jit(solution)/shard_map/ppermute | solution.py:591
  92.3 7.4 %collective-permute-start.9 = (bf16[64,8,128]{2,1,0:T(8,128)(2,1)S(1)}, bf16[64,8,128]{2,1,0:T(8,128)(2,1)S(1)}, u32[]{:S(2)}, u32[]{:S(2)}) collective-permute-start(bf16[64,8,128]{2,1,0:T(8,128)(2,1)S(1)} %all-to-all-done.2.refs_0_), channel_id=1, source_target_pairs={{0,2},{1,3},{2,0},{3,1},{4,6},{5,7},{6,4},{7,5},{8,10},{9,11},{10,... | collective-permute-start | bytes 393224 | tf_op jit(solution)/shard_map/ppermute | solution.py:591
  102.8 38.3 %copy-start = (bf16[2048,3,256]{2,0,1:T(8,128)(2,1)S(1)}, bf16[2048,3,256]{2,0,1:T(8,128)(2,1)}, u32[]{:S(2)}) copy-start(bf16[2048,3,256]{2,0,1:T(8,128)(2,1)} %param.33) | copy-start | bytes 9437188
  102.8 6.2 %collective-permute-start.11 = (bf16[256,256]{1,0:T(8,128)(2,1)S(1)}, bf16[256,256]{1,0:T(8,128)(2,1)S(1)}, u32[]{:S(2)}, u32[]{:S(2)}) collective-permute-start(bf16[256,256]{1,0:T(8,128)(2,1)S(1)} %get-tuple-element.68.refs_0_.refs_2_), channel_id=1, source_target_pairs={{0,1},{1,2},{2,3},{3,0},{4,5},{5,6},{6,7},{7,4},{8,9},{9,10},{10,1... | collective-permute-start | bytes 393224 | tf_op jit(solution)/shard_map/ppermute | solution.py:591
  103.7 6.2 %collective-permute-start.12 = (bf16[256,256]{1,0:T(8,128)(2,1)S(1)}, bf16[256,256]{1,0:T(8,128)(2,1)S(1)}, u32[]{:S(2)}, u32[]{:S(2)}) collective-permute-start(bf16[256,256]{1,0:T(8,128)(2,1)S(1)} %get-tuple-element.68.refs_0_.refs_2_), channel_id=1, source_target_pairs={{0,2},{1,3},{2,0},{3,1},{4,6},{5,7},{6,4},{7,5},{8,10},{9,11},{10,... | collective-permute-start | bytes 393224 | tf_op jit(solution)/shard_map/ppermute | solution.py:591
  104.6 5.5 %collective-permute-start.13 = (bf16[256,256]{1,0:T(8,128)(2,1)S(1)}, bf16[256,256]{1,0:T(8,128)(2,1)S(1)}, u32[]{:S(2)}, u32[]{:S(2)}) collective-permute-start(bf16[256,256]{1,0:T(8,128)(2,1)S(1)} %get-tuple-element.68.refs_0_.refs_2_), channel_id=1, source_target_pairs={{0,3},{1,0},{2,1},{3,2},{4,7},{5,4},{6,5},{7,6},{8,11},{9,8},{10,9... | collective-permute-start | bytes 393224 | tf_op jit(solution)/shard_map/ppermute | solution.py:591
  134.6 4.1 %collective-permute-start.14 = (bf16[16,512]{1,0:T(8,128)(2,1)}, bf16[16,512]{1,0:T(8,128)(2,1)S(1)}, u32[]{:S(2)}, u32[]{:S(2)}) collective-permute-start(bf16[16,512]{1,0:T(8,128)(2,1)} %blend.1.refs_5_), channel_id=1, source_target_pairs={{0,1},{1,2},{2,3},{3,0},{4,5},{5,6},{6,7},{7,4},{8,9},{9,10},{10,1... | collective-permute-start | bytes 49160 | tf_op jit(solution)/shard_map/ppermute | solution.py:591
  135.0 4.7 %collective-permute-start.15 = (bf16[16,512]{1,0:T(8,128)(2,1)}, bf16[16,512]{1,0:T(8,128)(2,1)S(1)}, u32[]{:S(2)}, u32[]{:S(2)}) collective-permute-start(bf16[16,512]{1,0:T(8,128)(2,1)} %blend.1.refs_5_), channel_id=1, source_target_pairs={{0,2},{1,3},{2,0},{3,1},{4,6},{5,7},{6,4},{7,5},{8,10},{9,11},{10,... | collective-permute-start | bytes 49160 | tf_op jit(solution)/shard_map/ppermute | solution.py:591
  138.2 2.8 %collective-permute-start.16 = (bf16[16,512]{1,0:T(8,128)(2,1)}, bf16[16,512]{1,0:T(8,128)(2,1)S(1)}, u32[]{:S(2)}, u32[]{:S(2)}) collective-permute-start(bf16[16,512]{1,0:T(8,128)(2,1)} %blend.1.refs_5_), channel_id=1, source_target_pairs={{0,3},{1,0},{2,1},{3,2},{4,7},{5,4},{6,5},{7,6},{8,11},{9,8},{10,9... | collective-permute-start | bytes 49160 | tf_op jit(solution)/shard_map/ppermute | solution.py:591
Sparse Core Ops, SparseCore 0:
  9.8 58.3 all-gather.1

commit v8 on v7

--- a/solution.py
+++ b/solution.py
@@ -53,6 +53,18 @@
             self.send()
         for copy in self.copies:
             copy.wait()
+
+
+class Moved:
+    def __init__(self, buf, copies):
+        self.buf, self.copies, self.done = buf, copies, False
+
+    def get(self):
+        if not self.done:
+            for copy in self.copies:
+                copy.wait()
+            self.done = True
+        return self.buf
 
 
 def part_of(x):
@@ -79,21 +91,21 @@
             pending.append(Pending(bufs[i], copy))
         moving = []
         for i, (x, first, rows) in enumerate(moves):
-            rows = rows // PIECES
+            rows, copies = rows // PIECES, []
             for j in range(PIECES):
                 src = ins[nn + nf + na + i].at[pl.ds(first + j * rows, rows)]
                 dst = moved[i].at[pl.ds(j * rows, rows)]
-                moving.append(pltpu.make_async_copy(src, dst, move_sems.at[PIECES * i + j]))
-        for copy in moving:
-            copy.start()
+                copies.append(pltpu.make_async_copy(src, dst, move_sems.at[PIECES * i + j]))
+                copies[-1].start()
+            moving.append(Moved(moved[i], copies))
         going = [Leaving(out_bufs[i], out_hbm[i], out_sems, PIECES * i) for i in range(nl)]
-        body(ins[:nn], pending, (*outputs, *going), own)
+        body(ins[:nn], pending, (*outputs, *going, *moving), own)
         for p in pending:
             p.get()
         for g in going:
             g.finish()
-        for copy in moving:
-            copy.wait()
+        for m in moving:
+            m.get()
 
     hbm, any_space = pl.BlockSpec(memory_space=pltpu.HBM), pl.BlockSpec(memory_space=pl.ANY)
     far_shapes = [((r,) + x.shape[1:], x.dtype) for x, _, r in far]
@@ -174,7 +186,7 @@
 
 
 def tables_body(near, far, outs, own, page):
-    pick_ref, count_ref, same_ref, mine_ref, spread_ref, spread16_ref = outs
+    pick_ref, count_ref, same_ref, mine_ref, spread_ref, spread16_ref = outs[:6]
     req = far[0].get()[...]
     slots, total = pick_ref.shape
     half = total // 2
@@ -310,8 +322,8 @@
         outs[0].send()
 
 
-def merge(a, b, after):
-    return run(merge_body, "merge", [], [a, b], [], after_hbm=[after], leaving=[sds(a.shape, BF16)])[0]
+def merge(a, b):
+    return run(merge_body, "merge", [], [a, b], [], leaving=[sds(a.shape, BF16)])[0]
 
 
 def fetch(after, *arrays):
@@ -319,9 +331,15 @@
 
 
 def pack_kernel(w_ref, qa_ref, qb_ref, after_ref, *refs):
-    outs, res_buf, bufs, sems = refs[:4], refs[4], refs[5:9], refs[9]
+    outs, res_buf, in_a, in_b, bufs, sems = refs[:4], refs[4], refs[5], refs[6], refs[7:11], refs[11]
     rows, width = bufs[0].shape[0] // 2, bufs[0].shape[1]
     held = res_buf.shape[0]
+    reads = [
+        pltpu.make_async_copy(qa_ref.at[:, pl.ds(16, 8), :], in_a, sems.at[16]),
+        pltpu.make_async_copy(qb_ref.at[:, pl.ds(24, 8), :], in_b, sems.at[17]),
+    ]
+    for read in reads:
+        read.start()
     cuts, writes = [], []
     for k in range(4):
         first = pl.multiple_of(((head_id() + k) % 4) * 2 * width, 2 * width)
@@ -331,7 +349,9 @@
         writes.append(pltpu.make_async_copy(bufs[k], outs[k].at[pl.ds(held, 2 * rows)], sems.at[8 + k]))
     for cut in cuts:
         cut.start()
-    mine, other = qa_ref[:, 16:24, :].astype(F32), qb_ref[:, 24:32, :].astype(F32)
+    for read in reads:
+        read.wait()
+    mine, other = in_a[...].astype(F32), in_b[...].astype(F32)
     first = core_id() == 0
     both = [jnp.where(first, mine, other), jnp.where(first, other, mine)]
     res_buf[...] = jnp.stack(both, axis=1).reshape(res_buf.shape).astype(BF16)
@@ -349,18 +369,20 @@
 def pack(w_down, qa, qb, after):
     hbm = pl.BlockSpec(memory_space=pltpu.HBM)
     rows, width = w_down.shape[0], w_down.shape[1] // 8
-    held = qa.shape[0] * 16
+    chips = qa.shape[0]
+    held = chips * 16
     return pl.pallas_call(
         pack_kernel,
         name="pack",
         out_shape=[pltpu.HBM((held + 2 * rows, width), BF16)] * 4,
-        in_specs=[hbm, VM, VM, pl.BlockSpec(memory_space=pl.ANY)],
+        in_specs=[hbm] * 4,
         out_specs=[hbm] * 4,
         scratch_shapes=[pltpu.VMEM((held, width), BF16)]
+        + [pltpu.VMEM((chips, 8, width), BF16)] * 2
         + [pltpu.VMEM((2 * rows, width), BF16)] * 4
-        + [pltpu.SemaphoreType.DMA((16,))],
+        + [pltpu.SemaphoreType.DMA((18,))],
         compiler_params=VLIM,
-    )(*pin([w_down]), qa, qb, after)
+    )(*pin([w_down, qa, qb, after]))
 
 
 def cells_body(near, far, outs, own):
@@ -470,29 +492,31 @@
 
 
 def early_body(near, far, outs, own):
-    tok_ref, wo_ref = near
-    xs = outs[0]
+    tok_ref = near[0]
+    xs, wo = outs
     eff, w = 2 * HD, xs.shape[2]
     att = jnp.concatenate(unfold(tok_ref[...].astype(F32)), axis=1).astype(BF16)
+    for k in range(4):
+        res = far[k].get()[...].astype(F32)
+        xs[2 * k], xs[2 * k + 1] = unfold(res.reshape(res.shape[0] // 8, 8, w))
+    wo_ref = wo.get()
     rows = pl.ds(head_blocks(eff)[0], eff)
     for k, first in enumerate(head_blocks(2 * w)):
-        res = far[k].get()[...].astype(F32)
-        pair = unfold(res.reshape(res.shape[0] // 8, 8, w))
         for f in range(2):
-            xs[2 * k + f] = pair[f] + dot(att, wo_ref[rows, pl.ds(first + f * w, w)])
+            xs[2 * k + f] = xs[2 * k + f] + dot(att, wo_ref[rows, pl.ds(first + f * w, w)])
 
 
 def early_rows(tokens, out_weight, res):
     n = tokens.shape[0]
     w = res[0][0].shape[1]
-    return run(early_body, "early_rows", [sds((8, n * 4, w), F32)], [tokens, out_weight], res)[0]
+    return run(early_body, "early_rows", [sds((8, n * 4, w), F32)], [tokens], res, moves=[out_weight])
 
 
 def expert_body(near, far, outs, own):
     inner_ref, hid = outs
     hs = own[0]
-    att, (xs, wo_ref, wg_ref, wu_ref) = near[:3], near[3:]
-    gain, mine, own_res = far[0], far[1:5], far[5]
+    att, (xs, wo_ref) = near[:3], near[3:]
+    gain, mine, own_res, w_gate, w_up = far[0], far[1:5], *far[5:]
     n = inner_ref.shape[0]
     eff = 2 * HD
     w = xs.shape[2]
@@ -516,6 +540,7 @@
         total = total + jnp.sum(part * part, axis=1, keepdims=True)
     scale = lax.rsqrt(total / (8 * w) + EPS)
     gain_ref = gain.get()
+    wg_ref, wu_ref = w_gate.get(), w_up.get()
     gate = jnp.zeros((n, wg_ref.shape[1]), F32)
     up = jnp.zeros((n, wg_ref.shape[1]), F32)
     for j, first in enumerate(firsts):
@@ -528,9 +553,9 @@
 def expert_rows(tokens, early, out_weight, w_gate, w_up, gain, mine, residual):
     _, n, w = early.shape
     outs, leaving = [sds((n, w_gate.shape[1]), BF16)], [sds((residual.shape[0], 2 * w), BF16)]
-    near = [*tokens, early, out_weight, w_gate, w_up]
+    near = [*tokens, early, out_weight]
     scratch = [pltpu.VMEM((8, n, w), BF16)]
-    far = [gain.reshape(1, -1), *mine, residual]
+    far = [gain.reshape(1, -1), *mine, residual, w_gate, w_up]
     return run(expert_body, "expert_rows", outs, near, far, scratch, leaving=leaving)
 
 
@@ -566,24 +591,39 @@
     return run(blend_body, "blend", [sds(hidden.shape, BF16)], [returned, *mix], [hidden])[0]
 
 
-def qkv_body(near, far, outs, own):
-    w_ref = near[3]
-    w = near[0].shape[1]
-    parts = [s[...].astype(F32) for s in (far[1].get(), *near[:3])]
-    total = sum(jnp.sum(p * p, axis=1, keepdims=True) for p in parts)
-    scale = lax.rsqrt(total / (4 * w) + EPS)
-    gain_ref = far[0].get()
-    cols = [pl.ds(first, w) for first in head_blocks(w)]
-    normed = [(p * scale * gain_ref[:, c]).astype(BF16) for p, c in zip(parts, cols)]
-    for i in range(outs[0].shape[0]):
-        acc = sum(dot(n, w_ref[i, c, :]) for n, c in zip(normed, cols))
-        outs[0][i] = acc.astype(BF16)
+def proj_share(x, k, gain_ref, w_ref):
+    w = x.shape[1]
+    cols = pl.ds(head_blocks(w)[k], w)
+    part = (x * gain_ref[:, cols]).astype(BF16)
+    return [dot(part, w_ref[i, cols, :]) for i in range(w_ref.shape[0])], jnp.sum(x * x, axis=1, keepdims=True)
+
+
+def own_proj_body(near, far, outs, own):
+    shares, total = proj_share(far[1].get()[...].astype(F32), 0, far[0].get(), near[0])
+    for i, share in enumerate(shares):
+        outs[0][i] = share
+    outs[1][...] = jnp.broadcast_to(total, outs[1].shape)
+
+
+def proj_body(near, far, outs, own):
+    others, w_ref, first_ref, total_ref = near[:3], near[3], near[4], near[5]
+    total = total_ref[:, 0:1]
+    accs = [first_ref[i] for i in range(w_ref.shape[0])]
+    for k, s in enumerate(others):
+        shares, add = proj_share(s[...].astype(F32), k + 1, far[0].get(), w_ref)
+        accs, total = [a + b for a, b in zip(accs, shares)], total + add
+    scale = lax.rsqrt(total / w_ref.shape[1] + EPS)
+    for i, acc in enumerate(accs):
+        outs[0][i] = (acc * scale).astype(BF16)
 
 
 def next_proj(parts, gain, weight):
     kinds, _, width = weight.shape
-    out = sds((kinds, parts[0].shape[0], width), BF16)
-    return run(qkv_body, "next_proj", [out], [*parts[1:], weight], [gain.reshape(1, -1), parts[0]])[0]
+    rows = parts[0].shape[0]
+    shape = (kinds, rows, width)
+    gain = gain.reshape(1, -1)
+    first = run(own_proj_body, "own_proj", [sds(shape, F32), sds((rows, HD), F32)], [weight], [gain, parts[0]])
+    return run(proj_body, "next_proj", [sds(shape, BF16)], [*parts[1:], weight, *first], [gain])[0]
 
 
 def from_heads(x):
@@ -612,9 +652,8 @@
     tables = slot_tables(slot_request, slot_page, slot_used, lengths, kv_cache, [qa])
     qb = swap_core(qa)
     keep, send = attend_pages(tables, qa, qb)
-    packs = pack(w_down[0], qa, qb, send)
-    merged = merge(keep, swap_core(send), packs[0])
-    packs = to_heads(packs)
+    merged = merge(keep, swap_core(send))
+    packs = to_heads(pack(w_down[0], qa, qb, merged))
     cells = cells_table(routes, experts, merged)
     arrived = lax.all_to_all(merged, ("z", "y"), 0, 0, tiled=True)
     arrived, cells = lax.optimization_barrier((arrived, cells))
@@ -624,10 +663,9 @@
     tokens, mine, packs = lax.optimization_barrier((tokens, mine, packs))
     held = experts * 8
     res = [(p, 0, held) for p in packs]
-    out_weight, w_gate, w_up = fetch(tokens, out_weight, w_gate[0], w_up[0])
-    early = early_rows(tokens, out_weight, res)
+    early, out_weight = early_rows(tokens, out_weight, res)
     others = from_heads(tokens)[1:]
-    inner, hidden = expert_rows(others, early, out_weight, w_gate, w_up, norm_gain, mine, residual)
+    inner, hidden = expert_rows(others, early, out_weight, w_gate[0], w_up[0], norm_gain, mine, residual)
     w_cols = fetch(inner, *[(p, held, p.shape[0] - held) for p in packs])
     mix = mix_table(routes, route_weights, experts, inner)
     expert_out = down(from_heads(inner), w_cols, mix[0])

time: 151 us -> 151 us (level)
    all_to_all x1, waiting for transfers between devices: 7.29 us -> 5.04 us  [local(): arrived = lax.all_to_all(merged, ('z', 'y'), 0, 0, tiled=True)]
  transfers between devices with their start and end apart: 20 -> 20, of which waited for: 11 -> 11; matrix products, arithmetic and copies ran while one was open for 0% -> 0% of each run, Pallas kernels for 16% -> 15%
where the time goes in v8:
time: 151 us; the launch traced here: 150 us
  blocking collectives  51.4 us (34%)
  starting transfers between devices  35.1 us (23%)
  Pallas kernels  30 us (20%)
  waiting for transfers between devices  18.9 us (13%)
  between operations  14.3 us (9%)
    all_to_all x1, blocking collectives, local(): lax.all_to_all(outset(queries, residual, routes, chips), ('z', 'y'), 0, 0...  28.1 us
    pallas_call x14, Pallas kernels, run(): pl.pallas_call(kernel, name=name, out_shape=list(outs) + [pltpu.HBM(x.sha...  27.5 us
    all_to_all x1, blocking collectives, local(): returned = lax.all_to_all(expert_out, REQ, 0, 0, tiled=True)  23.3 us
    ppermute x12, starting transfers between devices, from_heads(): lax.ppermute(x, 'head', [(i, (i + k) % n) for i in range(n)])  16.6 us
    all_to_all x1, starting transfers between devices, local(): tokens = lax.all_to_all(disp, REQ, 0, 0, tiled=True)  6.51 us
    ppermute x12, waiting for transfers between devices, from_heads(): lax.ppermute(x, 'head', [(i, (i + k) % n) for i in range(n)])  5.84 us
    all_to_all x1, waiting for transfers between devices, local(): arrived = lax.all_to_all(merged, ('z', 'y'), 0, 0, tiled=True)  5.04 us
    ppermute x3, starting transfers between devices, to_heads(): lax.ppermute(xs[k], 'head', [(i, (i + k) % n) for i in range(n)])  4.92 us
  transfers between devices with their start and end apart: 20, of which 11 were waited for; matrix products, arithmetic and copies ran while one was open for 0% of the time, Pallas kernels for 15%

profile of v8, /device:TPU:1, one launch (start us, length us, event | category | flops | bytes accessed | tf_op | source)
XLA Modules:
  0.0 149.8 jit_solution(15985286208749541685)
XLA Ops:
  7.2 0.0 all-gather.2.cloned.1.call-start
  7.2 0.7 all-gather.2.cloned.1.call-update
  7.9 1.4 outset.1
  9.3 28.1 %all_to_all.20.refs_4_.refs_7_.qa_ref = bf16[32,32,256]{2,1,0:T(8,128)(2,1)S(1)} all-to-all(bf16[32,32,256]{2,1,0:T(8,128)(2,1)S(1)} %outset.1), channel_id=1, replica_groups=mesh['z'=8,'y'=4,'c'=2,'head'=4] {'z','y'}, dimensions={0} | all-to-all | bytes 1048576 | tf_op jit(solution)/shard_map/all_to_all | solution.py:651
  37.4 2.4 %collective-permute-start = (bf16[32,32,256]{2,1,0:T(8,128)(2,1)S(1)}, bf16[32,32,256]{2,1,0:T(8,128)(2,1)S(1)}, u32[]{:S(2)}, u32[]{:S(2)}) collective-permute-start(bf16[32,32,256]{2,1,0:T(8,128)(2,1)S(1)} %all_to_all.20.refs_4_.refs_7_.qa_ref), channel_id=1, source_target_pairs={{0,4},{4,0},{1,5},{5,1},{2,6},{6,2},{3,7},{7,3},{8,12},{12,8},{9,1... | collective-permute-start | bytes 1572872 | tf_op jit(solution)/shard_map/ppermute | solution.py:640
  39.8 2.4 %slot_tables.1 = (bf16[128,1024]{1,0:T(8,128)(2,1)S(1)}, f32[128,128]{1,0:T(8,128)S(1)}, f32[128,128]{1,0:T(8,128)S(1)}, f32[128,128]{1,0:T(8,128)S(1)}, bf16[10...) custom-call(s32[1,128]{1,0:T(1,128)} %bitcast.29, s32[1,128]{1,0:T(1,128)} %bitcast.30, ...), custom_call_target="tpu_custom_call" | custom-call | tf_op jit(solution)/shard_map/slot_tables/pallas_call | solution.py:112
  42.2 5.0 %attend_pages.1 = (bf16[32,48,128]{2,1,0:T(8,128)(2,1)S(1)}, bf16[32,48,128]{2,1,0:T(8,128)(2,1)S(1)}) custom-call(bf16[128,1024]{1,0:T(8,128)(2,1)S(1)} %get-tuple-element.40.refs_0_, f32[128,128]{1,0:T(8,128)S(1)} %get-tuple-element.41.refs_1_, f32[128,128]{1,0:T(8,128)S(1)} %get-tuple-element.42.refs_2_, f32[128,128]{1,0:T(8,128)S(1)} %get-tuple-element.43.refs_3_, ...), custom_call_target="tpu_custom_call" | custom-call | tf_op jit(solution)/shard_map/attend_pages/pallas_call | solution.py:112
  47.2 0.3 collective-permute-start.1
  47.5 1.5 collective-permute-done.1.refs_1_
  49.0 1.4 merge.1.refs_1_.after_ref
  50.5 4.4 %all-to-all-start.1 = ((bf16[32,48,128]{2,1,0:T(8,128)(2,1)}), bf16[32,48,128]{2,1,0:T(8,128)(2,1)S(1)}, u32[]{:S(2)}, u32[]{:S(2)}) async-start(bf16[32,48,128]{2,1,0:T(8,128)(2,1)} %merge.1.refs_1_.after_ref), calls=%async_computation.1 | async-start | bytes 786432 | tf_op jit(solution)/shard_map/all_to_all | solution.py:658
  54.9 2.5 %pack.1 = (bf16[1024,256]{1,0:T(8,128)(2,1)}, bf16[1024,256]{1,0:T(8,128)(2,1)}, bf16[1024,256]{1,0:T(8,128)(2,1)}, bf16[1024,256]{1,0:T(8,128)(2,1)}) custom-call(bf16[256,2048]{1,0:T(8,128)(2,1)} %bitcast.19, bf16[32,32,256]{2,1,0:T(8,128)(2,1)} %copy-done.1, bf16[32,32,256]{2,1,0:T(8,128)(2,1)} %copy-done.2, bf16[32,48,128]{2,1,0:T(8,128)(2,1)} %merge.1.refs_1_.after_ref), custom_call_target="tpu_custom_call" | custom-call | tf_op jit(solution)/shard_map/pack/pallas_call | solution.py:374
  57.4 1.3 collective-permute-start.5
  58.7 2.5 %collective-permute-start.6 = (bf16[1024,256]{1,0:T(8,128)(2,1)}, bf16[1024,256]{1,0:T(8,128)(2,1)S(1)}, u32[]{:S(2)}, u32[]{:S(2)}) collective-permute-start(bf16[1024,256]{1,0:T(8,128)(2,1)} %get-tuple-element.55), channel_id=1, source_target_pairs={{0,2},{1,3},{2,0},{3,1},{4,6},{5,7},{6,4},{7,5},{8,10},{9,11},{10,... | collective-permute-start | bytes 1572872 | tf_op jit(solution)/shard_map/ppermute | solution.py:636
  61.2 1.1 collective-permute-start.7
  62.3 1.7 %cells_table.1.refs_3_ = bf16[32,512]{1,0:T(8,128)(2,1)} custom-call(s32[8,16]{1,0:T(8,128)} %bitcast.21, bf16[32,48,128]{2,1,0:T(8,128)(2,1)} %merge.1.refs_1_.after_ref), custom_call_target="tpu_custom_call" | custom-call | tf_op jit(solution)/shard_map/cells_table/pallas_call | solution.py:112
  64.0 5.0 %all-to-all-done.1.refs_0_ = bf16[32,48,128]{2,1,0:T(8,128)(2,1)S(1)} async-done(((bf16[32,48,128]{2,1,0:T(8,128)(2,1)}), bf16[32,48,128]{2,1,0:T(8,128)(2,1)S(1)}, u32[]{:S(2)}, u32[]{:S(2)}) %all-to-all-start.1) | async-done | bytes 393248 | tf_op jit(solution)/shard_map/all_to_all | solution.py:658
  69.1 2.2 %owner_part.1 = (bf16[16,256]{1,0:T(8,128)(2,1)S(1)}, bf16[64,8,128]{2,1,0:T(8,128)(2,1)}) custom-call(bf16[32,48,128]{2,1,0:T(8,128)(2,1)S(1)} %all-to-all-done.1.refs_0_, bf16[16,256]{1,0:T(8,128)(2,1)} %refs_1_.3, bf16[16,2,256]{2,1,0:T(2,128)(2,1)} %refs_2_.1, bf16[32,512]{1,0:T(8,128)(2,1)} %cells_table.1.refs_3_), custom_call_target="tpu_custom_call" | custom-call | tf_op jit(solution)/shard_map/owner_part/pallas_call | solution.py:112
  71.3 6.5 %all-to-all-start.2 = ((bf16[64,8,128]{2,1,0:T(8,128)(2,1)}), bf16[64,8,128]{2,1,0:T(8,128)(2,1)S(1)}, u32[]{:S(2)}, u32[]{:S(2)}) async-start(bf16[64,8,128]{2,1,0:T(8,128)(2,1)} %get-tuple-element.51), calls=%async_computation.2 | async-start | bytes 262144 | tf_op jit(solution)/shard_map/all_to_all | solution.py:661
  77.8 1.3 collective-permute-start.2
  79.1 2.5 %collective-permute-start.3 = (bf16[16,256]{1,0:T(8,128)(2,1)S(1)}, bf16[16,256]{1,0:T(8,128)(2,1)S(1)}, u32[]{:S(2)}, u32[]{:S(2)}) collective-permute-start(bf16[16,256]{1,0:T(8,128)(2,1)S(1)} %get-tuple-element.64.refs_6_), channel_id=1, source_target_pairs={{0,2},{1,3},{2,0},{3,1},{4,6},{5,7},{6,4},{7,5},{8,10},{9,11},{10,... | collective-permute-start | bytes 24584 | tf_op jit(solution)/shard_map/ppermute | solution.py:631
  81.6 1.1 collective-permute-start.4
  82.7 4.1 %collective-permute-done.6.refs_3_ = bf16[1024,256]{1,0:T(8,128)(2,1)S(1)} collective-permute-done((bf16[1024,256]{1,0:T(8,128)(2,1)}, bf16[1024,256]{1,0:T(8,128)(2,1)S(1)}, u32[]{:S(2)}, u32[]{:S(2)}) %collective-permute-start.6) | collective-permute-done | bytes 524320 | tf_op jit(solution)/shard_map/ppermute | solution.py:636
  86.8 0.3 collective-permute-done.3.refs_8_
  87.2 1.7 %all-to-all-done.2.refs_0_ = bf16[64,8,128]{2,1,0:T(8,128)(2,1)S(1)} async-done(((bf16[64,8,128]{2,1,0:T(8,128)(2,1)}), bf16[64,8,128]{2,1,0:T(8,128)(2,1)S(1)}, u32[]{:S(2)}, u32[]{:S(2)}) %all-to-all-start.2) | async-done | bytes 131104 | tf_op jit(solution)/shard_map/all_to_all | solution.py:661
  88.9 2.5 %collective-permute-start.10 = (bf16[64,8,128]{2,1,0:T(8,128)(2,1)S(1)}, bf16[64,8,128]{2,1,0:T(8,128)(2,1)S(1)}, u32[]{:S(2)}, u32[]{:S(2)}) collective-permute-start(bf16[64,8,128]{2,1,0:T(8,128)(2,1)S(1)} %all-to-all-done.2.refs_0_), channel_id=1, source_target_pairs={{0,3},{1,0},{2,1},{3,2},{4,7},{5,4},{6,5},{7,6},{8,11},{9,8},{10,9... | collective-permute-start | bytes 393224 | tf_op jit(solution)/shard_map/ppermute | solution.py:631
  91.4 1.7 %collective-permute-start.9 = (bf16[64,8,128]{2,1,0:T(8,128)(2,1)S(1)}, bf16[64,8,128]{2,1,0:T(8,128)(2,1)S(1)}, u32[]{:S(2)}, u32[]{:S(2)}) collective-permute-start(bf16[64,8,128]{2,1,0:T(8,128)(2,1)S(1)} %all-to-all-done.2.refs_0_), channel_id=1, source_target_pairs={{0,2},{1,3},{2,0},{3,1},{4,6},{5,7},{6,4},{7,5},{8,10},{9,11},{10,... | collective-permute-start | bytes 393224 | tf_op jit(solution)/shard_map/ppermute | solution.py:631
  93.1 0.0 all-gather.2.cloned.1.call-done.refs_5_
  93.2 3.0 %early_rows.1 = (f32[8,256,256]{2,1,0:T(8,128)S(1)}, bf16[1024,2048]{1,0:T(8,128)(2,1)S(1)}) custom-call(bf16[64,8,128]{2,1,0:T(8,128)(2,1)S(1)} %all-to-all-done.2.refs_0_, bf16[1024,256]{1,0:T(8,128)(2,1)} %get-tuple-element.58.refs_1_, bf16[1024,256]{1,0:T(8,128)(2,1)} %copy-done.4, bf16[1024,256]{1,0:T(8,128)(2,1)} %copy-done.5, ...), custom_call_target="tpu_custom_call" | custom-call | tf_op jit(solution)/shard_map/early_rows/pallas_call | solution.py:112
  96.2 2.2 %collective-permute-done.8.refs_0_ = bf16[64,8,128]{2,1,0:T(8,128)(2,1)S(1)} collective-permute-done((bf16[64,8,128]{2,1,0:T(8,128)(2,1)S(1)}, bf16[64,8,128]{2,1,0:T(8,128)(2,1)S(1)}, u32[]{:S(2)}, u32[]{:S(2)}) %collective-permute-start.8) | collective-permute-done | bytes 131104 | tf_op jit(solution)/shard_map/ppermute | solution.py:631
  98.4 0.5 collective-permute-done.9.refs_1_
  98.9 3.1 %expert_rows.1 = (bf16[256,256]{1,0:T(8,128)(2,1)S(1)}, bf16[16,512]{1,0:T(8,128)(2,1)}) custom-call(bf16[64,8,128]{2,1,0:T(8,128)(2,1)S(1)} %collective-permute-done.8.refs_0_, bf16[64,8,128]{2,1,0:T(8,128)(2,1)S(1)} %collective-permute-done.9.refs_1_, bf16[64,8,128]{2,1,0:T(8,128)(2,1)S(1)} %collective-permute-done.10.refs_2_, ...), custom_call_target="tpu_custom_call" | custom-call | tf_op jit(solution)/shard_map/expert_rows/pallas_call | solution.py:112
  102.0 0.1 collective-permute-start.11
  102.1 1.8 %collective-permute-start.12 = (bf16[256,256]{1,0:T(8,128)(2,1)S(1)}, bf16[256,256]{1,0:T(8,128)(2,1)S(1)}, u32[]{:S(2)}, u32[]{:S(2)}) collective-permute-start(bf16[256,256]{1,0:T(8,128)(2,1)S(1)} %get-tuple-element.68.refs_0_.refs_2_), channel_id=1, source_target_pairs={{0,2},{1,3},{2,0},{3,1},{4,6},{5,7},{6,4},{7,5},{8,10},{9,11},{10,... | collective-permute-start | bytes 393224 | tf_op jit(solution)/shard_map/ppermute | solution.py:631
  103.9 1.9 %collective-permute-start.13 = (bf16[256,256]{1,0:T(8,128)(2,1)S(1)}, bf16[256,256]{1,0:T(8,128)(2,1)S(1)}, u32[]{:S(2)}, u32[]{:S(2)}) collective-permute-start(bf16[256,256]{1,0:T(8,128)(2,1)S(1)} %get-tuple-element.68.refs_0_.refs_2_), channel_id=1, source_target_pairs={{0,3},{1,0},{2,1},{3,2},{4,7},{5,4},{6,5},{7,6},{8,11},{9,8},{10,9... | collective-permute-start | bytes 393224 | tf_op jit(solution)/shard_map/ppermute | solution.py:631
  105.7 1.4 fetch.1
  107.1 1.1 mix_table.1
  108.2 0.3 collective-permute-done.11.refs_1_
  108.5 0.9 collective-permute-done.13.refs_3_
  109.4 0.5 down.1
  109.9 23.3 %all_to_all.21.refs_0_ = bf16[64,8,256]{2,1,0:T(8,128)(2,1)S(1)} all-to-all(bf16[64,8,256]{2,1,0:T(8,128)(2,1)S(1)} %bitcast.16), channel_id=1, replica_groups=mesh['z'=8,'y'=4,'c'=2,'head'=4] {'z','y','c'}, dimensions={0} | all-to-all | bytes 524288 | tf_op jit(solution)/shard_map/all_to_all | solution.py:672
  133.2 1.6 %blend.1.refs_2_ = bf16[16,512]{1,0:T(8,128)(2,1)} custom-call(bf16[64,8,256]{2,1,0:T(8,128)(2,1)S(1)} %all_to_all.21.refs_0_, bf16[16,256]{1,0:T(8,128)(2,1)S(1)} %get-tuple-element.73.refs_8_.refs_1_, bf16[16,256]{1,0:T(8,128)(2,1)S(1)} %get-tuple-element.74.refs_2_, bf16[16,512]{1,0:T(8,128)(2,1)} %get-tuple-element.75.refs_3_), custom_call_target="tpu_custom_call" | custom-call | tf_op jit(solution)/shard_map/blend/pallas_call | solution.py:112
  134.7 0.4 collective-permute-start.14
  135.2 3.2 %collective-permute-start.15 = (bf16[16,512]{1,0:T(8,128)(2,1)}, bf16[16,512]{1,0:T(8,128)(2,1)S(1)}, u32[]{:S(2)}, u32[]{:S(2)}) collective-permute-start(bf16[16,512]{1,0:T(8,128)(2,1)} %blend.1.refs_2_), channel_id=1, source_target_pairs={{0,2},{1,3},{2,0},{3,1},{4,6},{5,7},{6,4},{7,5},{8,10},{9,11},{10,... | collective-permute-start | bytes 49160 | tf_op jit(solution)/shard_map/ppermute | solution.py:631
  138.4 1.0 own_proj.1
  139.5 0.4 collective-permute-done.15.refs_1_
  139.9 1.3 collective-permute-done.16.refs_2_
  141.2 1.8 %next_proj.1 = bf16[3,16,256]{2,1,0:T(8,128)(2,1)} custom-call(bf16[16,512]{1,0:T(8,128)(2,1)S(1)} %collective-permute-done.14.refs_0_, bf16[16,512]{1,0:T(8,128)(2,1)S(1)} %collective-permute-done.15.refs_1_, bf16[16,512]{1,0:T(8,128)(2,1)S(1)} %collective-permute-done.16.refs_2_, bf16[3,2048,256]{2,1,0:T(8,128)(2,1)S(1)} %bitcast.15, ...), custom_call_target="tpu_custom_call" | custom-call | tf_op jit(solution)/shard_map/next_proj/pallas_call | solution.py:112
  (30 shorter events, 0.1 us)
Async XLA Ops:
  7.2 86.0 %all-gather.2.cloned.1.call-start = ((), (), s32[]{:S(2)}) async-start(), calls=%async_computation.4 | async-start | bytes 5242880 | tf_op jit(solution)/shard_map/all_gather | solution.py:650
  37.4 9.8 %copy-start.1 = (bf16[32,32,256]{2,1,0:T(8,128)(2,1)}, bf16[32,32,256]{2,1,0:T(8,128)(2,1)S(1)}, u32[]{:S(2)}) copy-start(bf16[32,32,256]{2,1,0:T(8,128)(2,1)S(1)} %all_to_all.20.refs_4_.refs_7_.qa_ref) | copy-start | bytes 1572868
  37.4 4.8 %collective-permute-start = (bf16[32,32,256]{2,1,0:T(8,128)(2,1)S(1)}, bf16[32,32,256]{2,1,0:T(8,128)(2,1)S(1)}, u32[]{:S(2)}, u32[]{:S(2)}) collective-permute-start(bf16[32,32,256]{2,1,0:T(8,128)(2,1)S(1)} %all_to_all.20.refs_4_.refs_7_.qa_ref), channel_id=1, source_target_pairs={{0,4},{4,0},{1,5},{5,1},{2,6},{6,2},{3,7},{7,3},{8,12},{12,8},{9,1... | collective-permute-start | bytes 1572872 | tf_op jit(solution)/shard_map/ppermute | solution.py:640
  42.2 12.7 %copy-start.2 = (bf16[32,32,256]{2,1,0:T(8,128)(2,1)}, bf16[32,32,256]{2,1,0:T(8,128)(2,1)S(1)}, u32[]{:S(2)}) copy-start(bf16[32,32,256]{2,1,0:T(8,128)(2,1)S(1)} %collective-permute-done.refs_8_.qb_ref) | copy-start | bytes 1572868
  47.2 1.8 %collective-permute-start.1 = (bf16[32,48,128]{2,1,0:T(8,128)(2,1)S(1)}, bf16[32,48,128]{2,1,0:T(8,128)(2,1)S(1)}, u32[]{:S(2)}, u32[]{:S(2)}) collective-permute-start(bf16[32,48,128]{2,1,0:T(8,128)(2,1)S(1)} %get-tuple-element.48), channel_id=1, source_target_pairs={{0,4},{4,0},{1,5},{5,1},{2,6},{6,2},{3,7},{7,3},{8,12},{12,8},{9,1... | collective-permute-start | bytes 1179656 | tf_op jit(solution)/shard_map/ppermute | solution.py:640
  50.5 18.6 %all-to-all-start.1 = ((bf16[32,48,128]{2,1,0:T(8,128)(2,1)}), bf16[32,48,128]{2,1,0:T(8,128)(2,1)S(1)}, u32[]{:S(2)}, u32[]{:S(2)}) async-start(bf16[32,48,128]{2,1,0:T(8,128)(2,1)} %merge.1.refs_1_.after_ref), calls=%async_computation.1 | async-start | bytes 786432 | tf_op jit(solution)/shard_map/all_to_all | solution.py:658
  57.4 24.2 %collective-permute-start.5 = (bf16[1024,256]{1,0:T(8,128)(2,1)}, bf16[1024,256]{1,0:T(8,128)(2,1)S(1)}, u32[]{:S(2)}, u32[]{:S(2)}) collective-permute-start(bf16[1024,256]{1,0:T(8,128)(2,1)} %get-tuple-element.54), channel_id=1, source_target_pairs={{0,1},{1,2},{2,3},{3,0},{4,5},{5,6},{6,7},{7,4},{8,9},{9,10},{10,1... | collective-permute-start | bytes 1572872 | tf_op jit(solution)/shard_map/ppermute | solution.py:636
  58.7 28.1 %collective-permute-start.6 = (bf16[1024,256]{1,0:T(8,128)(2,1)}, bf16[1024,256]{1,0:T(8,128)(2,1)S(1)}, u32[]{:S(2)}, u32[]{:S(2)}) collective-permute-start(bf16[1024,256]{1,0:T(8,128)(2,1)} %get-tuple-element.55), channel_id=1, source_target_pairs={{0,2},{1,3},{2,0},{3,1},{4,6},{5,7},{6,4},{7,5},{8,10},{9,11},{10,... | collective-permute-start | bytes 1572872 | tf_op jit(solution)/shard_map/ppermute | solution.py:636
  61.2 25.6 %collective-permute-start.7 = (bf16[1024,256]{1,0:T(8,128)(2,1)}, bf16[1024,256]{1,0:T(8,128)(2,1)S(1)}, u32[]{:S(2)}, u32[]{:S(2)}) collective-permute-start(bf16[1024,256]{1,0:T(8,128)(2,1)} %get-tuple-element.56), channel_id=1, source_target_pairs={{0,3},{1,0},{2,1},{3,2},{4,7},{5,4},{6,5},{7,6},{8,11},{9,8},{10,9... | collective-permute-start | bytes 1572872 | tf_op jit(solution)/shard_map/ppermute | solution.py:636
  71.2 27.6 %copy-start.3 = (bf16[16,256]{1,0:T(8,128)(2,1)}, bf16[16,256]{1,0:T(8,128)(2,1)S(1)}, u32[]{:S(2)}) copy-start(bf16[16,256]{1,0:T(8,128)(2,1)S(1)} %get-tuple-element.64.refs_6_) | copy-start | bytes 24580
  71.3 17.6 %all-to-all-start.2 = ((bf16[64,8,128]{2,1,0:T(8,128)(2,1)}), bf16[64,8,128]{2,1,0:T(8,128)(2,1)S(1)}, u32[]{:S(2)}, u32[]{:S(2)}) async-start(bf16[64,8,128]{2,1,0:T(8,128)(2,1)} %get-tuple-element.51), calls=%async_computation.2 | async-start | bytes 262144 | tf_op jit(solution)/shard_map/all_to_all | solution.py:661
  77.8 9.1 %collective-permute-start.2 = (bf16[16,256]{1,0:T(8,128)(2,1)S(1)}, bf16[16,256]{1,0:T(8,128)(2,1)S(1)}, u32[]{:S(2)}, u32[]{:S(2)}) collective-permute-start(bf16[16,256]{1,0:T(8,128)(2,1)S(1)} %get-tuple-element.64.refs_6_), channel_id=1, source_target_pairs={{0,1},{1,2},{2,3},{3,0},{4,5},{5,6},{6,7},{7,4},{8,9},{9,10},{10,1... | collective-permute-start | bytes 24584 | tf_op jit(solution)/shard_map/ppermute | solution.py:631
  79.1 8.1 %collective-permute-start.3 = (bf16[16,256]{1,0:T(8,128)(2,1)S(1)}, bf16[16,256]{1,0:T(8,128)(2,1)S(1)}, u32[]{:S(2)}, u32[]{:S(2)}) collective-permute-start(bf16[16,256]{1,0:T(8,128)(2,1)S(1)} %get-tuple-element.64.refs_6_), channel_id=1, source_target_pairs={{0,2},{1,3},{2,0},{3,1},{4,6},{5,7},{6,4},{7,5},{8,10},{9,11},{10,... | collective-permute-start | bytes 24584 | tf_op jit(solution)/shard_map/ppermute | solution.py:631
  81.6 11.6 %copy-start.4 = (bf16[1024,256]{1,0:T(8,128)(2,1)}, bf16[1024,256]{1,0:T(8,128)(2,1)S(1)}, u32[]{:S(2)}) copy-start(bf16[1024,256]{1,0:T(8,128)(2,1)S(1)} %collective-permute-done.5.refs_2_) | copy-start | bytes 1572868
  81.6 5.6 %collective-permute-start.4 = (bf16[16,256]{1,0:T(8,128)(2,1)S(1)}, bf16[16,256]{1,0:T(8,128)(2,1)S(1)}, u32[]{:S(2)}, u32[]{:S(2)}) collective-permute-start(bf16[16,256]{1,0:T(8,128)(2,1)S(1)} %get-tuple-element.64.refs_6_), channel_id=1, source_target_pairs={{0,3},{1,0},{2,1},{3,2},{4,7},{5,4},{6,5},{7,6},{8,11},{9,8},{10,9... | collective-permute-start | bytes 24584 | tf_op jit(solution)/shard_map/ppermute | solution.py:631
  86.8 6.3 %copy-start.5 = (bf16[1024,256]{1,0:T(8,128)(2,1)}, bf16[1024,256]{1,0:T(8,128)(2,1)S(1)}, u32[]{:S(2)}) copy-start(bf16[1024,256]{1,0:T(8,128)(2,1)S(1)} %collective-permute-done.6.refs_3_) | copy-start | bytes 1572868
  86.8 6.3 %copy-start.6 = (bf16[1024,256]{1,0:T(8,128)(2,1)}, bf16[1024,256]{1,0:T(8,128)(2,1)S(1)}, u32[]{:S(2)}) copy-start(bf16[1024,256]{1,0:T(8,128)(2,1)S(1)} %collective-permute-done.7.refs_4_) | copy-start | bytes 1572868
  86.8 12.0 %copy-start.7 = (bf16[16,256]{1,0:T(8,128)(2,1)}, bf16[16,256]{1,0:T(8,128)(2,1)S(1)}, u32[]{:S(2)}) copy-start(bf16[16,256]{1,0:T(8,128)(2,1)S(1)} %collective-permute-done.2.refs_7_) | copy-start | bytes 24580
  87.2 11.7 %copy-start.8 = (bf16[16,256]{1,0:T(8,128)(2,1)}, bf16[16,256]{1,0:T(8,128)(2,1)S(1)}, u32[]{:S(2)}) copy-start(bf16[16,256]{1,0:T(8,128)(2,1)S(1)} %collective-permute-done.3.refs_8_) | copy-start | bytes 24580
  87.2 11.7 %copy-start.9 = (bf16[16,256]{1,0:T(8,128)(2,1)}, bf16[16,256]{1,0:T(8,128)(2,1)S(1)}, u32[]{:S(2)}) copy-start(bf16[16,256]{1,0:T(8,128)(2,1)S(1)} %collective-permute-done.4.refs_9_) | copy-start | bytes 24580
  88.9 7.3 %collective-permute-start.10 = (bf16[64,8,128]{2,1,0:T(8,128)(2,1)S(1)}, bf16[64,8,128]{2,1,0:T(8,128)(2,1)S(1)}, u32[]{:S(2)}, u32[]{:S(2)}) collective-permute-start(bf16[64,8,128]{2,1,0:T(8,128)(2,1)S(1)} %all-to-all-done.2.refs_0_), channel_id=1, source_target_pairs={{0,3},{1,0},{2,1},{3,2},{4,7},{5,4},{6,5},{7,6},{8,11},{9,8},{10,9... | collective-permute-start | bytes 393224 | tf_op jit(solution)/shard_map/ppermute | solution.py:631
  91.4 7.0 %collective-permute-start.8 = (bf16[64,8,128]{2,1,0:T(8,128)(2,1)S(1)}, bf16[64,8,128]{2,1,0:T(8,128)(2,1)S(1)}, u32[]{:S(2)}, u32[]{:S(2)}) collective-permute-start(bf16[64,8,128]{2,1,0:T(8,128)(2,1)S(1)} %all-to-all-done.2.refs_0_), channel_id=1, source_target_pairs={{0,1},{1,2},{2,3},{3,0},{4,5},{5,6},{6,7},{7,4},{8,9},{9,10},{10,1... | collective-permute-start | bytes 393224 | tf_op jit(solution)/shard_map/ppermute | solution.py:631
  91.4 7.4 %collective-permute-start.9 = (bf16[64,8,128]{2,1,0:T(8,128)(2,1)S(1)}, bf16[64,8,128]{2,1,0:T(8,128)(2,1)S(1)}, u32[]{:S(2)}, u32[]{:S(2)}) collective-permute-start(bf16[64,8,128]{2,1,0:T(8,128)(2,1)S(1)} %all-to-all-done.2.refs_0_), channel_id=1, source_target_pairs={{0,2},{1,3},{2,0},{3,1},{4,6},{5,7},{6,4},{7,5},{8,10},{9,11},{10,... | collective-permute-start | bytes 393224 | tf_op jit(solution)/shard_map/ppermute | solution.py:631
  102.0 36.4 %copy-start = (bf16[2048,3,256]{2,0,1:T(8,128)(2,1)S(1)}, bf16[2048,3,256]{2,0,1:T(8,128)(2,1)}, u32[]{:S(2)}) copy-start(bf16[2048,3,256]{2,0,1:T(8,128)(2,1)} %param.33) | copy-start | bytes 9437188
  102.0 6.5 %collective-permute-start.11 = (bf16[256,256]{1,0:T(8,128)(2,1)S(1)}, bf16[256,256]{1,0:T(8,128)(2,1)S(1)}, u32[]{:S(2)}, u32[]{:S(2)}) collective-permute-start(bf16[256,256]{1,0:T(8,128)(2,1)S(1)} %get-tuple-element.68.refs_0_.refs_2_), channel_id=1, source_target_pairs={{0,1},{1,2},{2,3},{3,0},{4,5},{5,6},{6,7},{7,4},{8,9},{9,10},{10,1... | collective-permute-start | bytes 393224 | tf_op jit(solution)/shard_map/ppermute | solution.py:631
  102.1 6.4 %collective-permute-start.12 = (bf16[256,256]{1,0:T(8,128)(2,1)S(1)}, bf16[256,256]{1,0:T(8,128)(2,1)S(1)}, u32[]{:S(2)}, u32[]{:S(2)}) collective-permute-start(bf16[256,256]{1,0:T(8,128)(2,1)S(1)} %get-tuple-element.68.refs_0_.refs_2_), channel_id=1, source_target_pairs={{0,2},{1,3},{2,0},{3,1},{4,6},{5,7},{6,4},{7,5},{8,10},{9,11},{10,... | collective-permute-start | bytes 393224 | tf_op jit(solution)/shard_map/ppermute | solution.py:631
  103.9 5.5 %collective-permute-start.13 = (bf16[256,256]{1,0:T(8,128)(2,1)S(1)}, bf16[256,256]{1,0:T(8,128)(2,1)S(1)}, u32[]{:S(2)}, u32[]{:S(2)}) collective-permute-start(bf16[256,256]{1,0:T(8,128)(2,1)S(1)} %get-tuple-element.68.refs_0_.refs_2_), channel_id=1, source_target_pairs={{0,3},{1,0},{2,1},{3,2},{4,7},{5,4},{6,5},{7,6},{8,11},{9,8},{10,9... | collective-permute-start | bytes 393224 | tf_op jit(solution)/shard_map/ppermute | solution.py:631
  134.7 4.7 %collective-permute-start.14 = (bf16[16,512]{1,0:T(8,128)(2,1)}, bf16[16,512]{1,0:T(8,128)(2,1)S(1)}, u32[]{:S(2)}, u32[]{:S(2)}) collective-permute-start(bf16[16,512]{1,0:T(8,128)(2,1)} %blend.1.refs_2_), channel_id=1, source_target_pairs={{0,1},{1,2},{2,3},{3,0},{4,5},{5,6},{6,7},{7,4},{8,9},{9,10},{10,1... | collective-permute-start | bytes 49160 | tf_op jit(solution)/shard_map/ppermute | solution.py:631
  135.2 4.7 %collective-permute-start.15 = (bf16[16,512]{1,0:T(8,128)(2,1)}, bf16[16,512]{1,0:T(8,128)(2,1)S(1)}, u32[]{:S(2)}, u32[]{:S(2)}) collective-permute-start(bf16[16,512]{1,0:T(8,128)(2,1)} %blend.1.refs_2_), channel_id=1, source_target_pairs={{0,2},{1,3},{2,0},{3,1},{4,6},{5,7},{6,4},{7,5},{8,10},{9,11},{10,... | collective-permute-start | bytes 49160 | tf_op jit(solution)/shard_map/ppermute | solution.py:631
  138.4 2.8 %collective-permute-start.16 = (bf16[16,512]{1,0:T(8,128)(2,1)}, bf16[16,512]{1,0:T(8,128)(2,1)S(1)}, u32[]{:S(2)}, u32[]{:S(2)}) collective-permute-start(bf16[16,512]{1,0:T(8,128)(2,1)} %blend.1.refs_2_), channel_id=1, source_target_pairs={{0,3},{1,0},{2,1},{3,2},{4,7},{5,4},{6,5},{7,6},{8,11},{9,8},{10,9... | collective-permute-start | bytes 49160 | tf_op jit(solution)/shard_map/ppermute | solution.py:631
Sparse Core Ops, SparseCore 0:
  9.8 56.7 all-gather.1

commit v9 on v8

--- a/solution.py
+++ b/solution.py
@@ -186,13 +186,14 @@
 
 
 def tables_body(near, far, outs, own, page):
-    pick_ref, count_ref, same_ref, mine_ref, spread_ref, spread16_ref = outs[:6]
+    pick_ref, count_ref, same_ref, mine_ref, spread_ref, spread8_ref = outs[:6]
     req = far[0].get()[...]
     slots, total = pick_ref.shape
     half = total // 2
     place = jnp.where((req // 16) % 2 == core_id(), 0, half) + (req // 32) * 16 + req % 16
     spread_ref[...] = jnp.where(iota((total, slots), 0) == place, 1.0, 0.0).astype(BF16)
-    spread16_ref[...] = jnp.where(iota((total, slots), 0) // 16 == place // 16, 1.0, 0.0).astype(BF16)
+    owners = jnp.where(iota((half, slots), 0) // 8 == place // 16, 1.0, 0.0)
+    spread8_ref[...] = owners.astype(BF16)
     eye = iota((slots, slots), 0) == iota((slots, slots), 1)
 
     def to_col(row):
@@ -227,7 +228,7 @@
             sds((slots, slots), F32),
             sds((slots, HD), F32),
             sds((total, slots), BF16),
-            sds((total, slots), BF16),
+            sds((total // 2, slots), BF16),
         ],
         [],
         [slot_request.reshape(1, slots), slot_page.reshape(1, slots), slot_used.reshape(1, slots), lengths.reshape(1, total)],
@@ -237,7 +238,7 @@
 
 
 def attn_body(near, far, outs, own):
-    pick_ref, count_ref, same_ref, mine_ref, spread_ref, spread16_ref, kv_ref, qa_ref, qb_ref = near
+    pick_ref, count_ref, same_ref, mine_ref, spread_ref, spread8_ref, kv_ref, qa_ref, qb_ref = near
     keep_ref, send_ref = outs
     n_scr, m_scr, l_scr = own
     slots = kv_ref.shape[0]
@@ -288,15 +289,15 @@
         for i, stat in enumerate((m_ref, l_hi, l_sum - l_hi)):
             board = jnp.where(group == 2 * i + h, stat, board)
     board = jnp.where(mine_ref[...] > 0.0, board, 0.0).astype(BF16)
-    out = dot(spread16_ref[...], board).astype(BF16)
-    keep_ref[:, 32:48, :] = out[:half].reshape(half // 16, 16, HD)
-    send_ref[:, 32:48, :] = out[half:].reshape(half // 16, 16, HD)
+    out = dot(spread8_ref[...], board).astype(BF16)
+    keep_ref[:, 32:40, :] = out[: half // 2].reshape(half // 16, 8, HD)
+    send_ref[:, 32:40, :] = out[half // 2 :].reshape(half // 16, 8, HD)
 
 
 def attend_pages(tables, qa, qb):
     slots, total = tables[0].shape
     scratch = [pltpu.VMEM((2, slots, n), F32) for n in (HD, slots, slots)]
-    outs = [sds((total // 32, 48, HD), BF16)] * 2
+    outs = [sds((total // 32, 40, HD), BF16)] * 2
     return run(attn_body, "attend_pages", outs, [*tables, qa, qb], [], scratch)
 
 
@@ -305,7 +306,7 @@
     for piece in range(PIECES):
         part = slice(piece * chips, piece * chips + chips)
         a_ref, b_ref, out_ref = near[0].at[part], near[1].at[part], outs[0].buf.at[part]
-        a, b = a_ref[:, 32:48, :].astype(F32), b_ref[:, 32:48, :].astype(F32)
+        a, b = a_ref[:, 32:40, :].astype(F32), b_ref[:, 32:40, :].astype(F32)
         lane, row = iota(a.shape, 2), iota(a.shape, 1)
         board = jnp.zeros(a.shape, F32)
         for h in range(2):
@@ -317,8 +318,10 @@
             l = la * fa + lb * fb
             l_hi = l.astype(BF16).astype(F32)
             for i, stat in enumerate((m, l_hi, l - l_hi)):
-                board = jnp.where(lane == row + 32 * i + 16 * h, stat, board)
-        out_ref[:, 32:48, :] = board.astype(BF16)
+                for u in range(2):
+                    at = row + 8 * u + 32 * i + 16 * h
+                    board = jnp.where(lane == at, stat[:, 8 * u : 8 * u + 8], board)
+        out_ref[:, 32:40, :] = board.astype(BF16)
         outs[0].send()
 
 
@@ -414,35 +417,44 @@
 
 
 def read_stats(board, h):
-    lane, row = iota(board.shape, 2), iota(board.shape, 1) + 16 * h
-    m = jnp.sum(jnp.where(lane == row, board, 0.0), axis=2, keepdims=True)
-    l = jnp.sum(jnp.where((lane == row + 32) | (lane == row + 64), board, 0.0), axis=2, keepdims=True)
+    lane, row = iota(board.shape, 2), iota(board.shape, 1)
+    ms, ls = [], []
+    for u in range(2):
+        at = row + 8 * u + 16 * h
+        ms.append(jnp.sum(jnp.where(lane == at, board, 0.0), axis=2, keepdims=True))
+        ls.append(jnp.sum(jnp.where((lane == at + 32) | (lane == at + 64), board, 0.0), axis=2, keepdims=True))
+    m, l = jnp.concatenate(ms, axis=1), jnp.concatenate(ls, axis=1)
     return jnp.where(l > 0.0, m, FLOOR), l
 
 
 def owner_body(near, far, outs, own_scratch):
     part_ref = near[0]
-    board = part_ref[:, 32:48, :].astype(F32)
+    att_ref, disp = outs
+    board = part_ref[:, 32:40, :].astype(F32)
+    stats = [read_stats(board, h) for h in range(2)]
+    tops = [jnp.max(m, axis=0) for m, _ in stats]
     q = far[0].get()[...].astype(F32)
     nkv = far[1].get()[...].astype(F32)
     nkv = jnp.concatenate([nkv[:, 0, :], nkv[:, 1, :]], axis=1)
     att = []
-    for h in range(2):
-        m, l = read_stats(board, h)
+    for h, (m, l) in enumerate(stats):
         own = jnp.sum(q[:, HD * h : HD * h + HD] * nkv[:, HD * h : HD * h + HD], axis=1, keepdims=True) * SCALE
-        top = jnp.maximum(jnp.max(m, axis=0), own)
+        top = jnp.maximum(tops[h], own)
         lift = jnp.exp(m - top[None])
         n = jnp.sum(part_ref[:, 16 * h : 16 * h + 16, :].astype(F32) * lift, axis=0)
         den = jnp.sum(l * lift, axis=0)
         new = jnp.exp(own - top)
         v = nkv[:, 2 * HD + HD * h : 2 * HD + HD * h + HD]
         att.append((n + new * v) / (den + new))
-    att_ref, disp = outs
-    disp_ref = disp.buf
+    both = jnp.concatenate(att, axis=0).astype(BF16)
+    pick = far[2].get()
+    cells = pick.shape[1] // PIECES
+    for j in range(PIECES):
+        part = pick[:, j * cells : j * cells + cells]
+        out = lax.dot_general(part, both, (((0,), (0,)), ((), ())), preferred_element_type=F32)
+        disp.buf[j * cells // 8 : (j + 1) * cells // 8] = out.astype(BF16).reshape(cells // 8, 8, HD)
+        disp.send()
     att_ref[...] = jnp.concatenate(att, axis=1).astype(BF16)
-    both = jnp.concatenate(att, axis=0).astype(BF16)
-    out = lax.dot_general(far[2].get()[...], both, (((0,), (0,)), ((), ())), preferred_element_type=F32)
-    disp_ref[...] = out.astype(BF16).reshape(disp_ref.shape)
 
 
 def owner_part(parts, queries, new_kv, cells, experts):
@@ -523,12 +535,6 @@
     att = [jnp.concatenate(unfold(a[...].astype(F32)), axis=1).astype(BF16) for a in att]
     block = head_blocks(eff)
     firsts = [first + f * w for first in head_blocks(2 * w) for f in range(2)]
-    cols = pl.ds(head_blocks(2 * w)[0], 2 * w)
-    acc = own_res.get()[:, cols].astype(F32)
-    acc = acc + sum(dot(mine[i].get()[...], wo_ref[pl.ds(block[i], eff), cols]) for i in range(4))
-    hid.buf[...] = acc.astype(BF16)
-    for _ in range(PIECES):
-        hid.send()
     total = jnp.zeros((n, 1), F32)
     for j, first in enumerate(firsts):
         acc = xs[j]
@@ -538,6 +544,12 @@
         hs[j] = part
         part = part.astype(F32)
         total = total + jnp.sum(part * part, axis=1, keepdims=True)
+    cols = pl.ds(head_blocks(2 * w)[0], 2 * w)
+    acc = own_res.get()[:, cols].astype(F32)
+    acc = acc + sum(dot(mine[i].get()[...], wo_ref[pl.ds(block[i], eff), cols]) for i in range(4))
+    hid.buf[...] = acc.astype(BF16)
+    for _ in range(PIECES):
+        hid.send()
     scale = lax.rsqrt(total / (8 * w) + EPS)
     gain_ref = gain.get()
     wg_ref, wu_ref = w_gate.get(), w_up.get()
@@ -579,12 +591,14 @@
 def blend_body(near, far, outs, own):
     y_ref, hi_ref, low_ref = near
     w = y_ref.shape[2]
+    moe = []
+    for part in unfold(y_ref[...].astype(F32)):
+        part = part.astype(BF16)
+        moe.append(dot(hi_ref[...], part) + dot(low_ref[...], part))
     hid_ref = far[0].get()
-    for f, part in enumerate(unfold(y_ref[...].astype(F32))):
-        part = part.astype(BF16)
-        hid = hid_ref[:, f * w : f * w + w].astype(F32)
-        moe = dot(hi_ref[...], part) + dot(low_ref[...], part)
-        outs[0][:, f * w : f * w + w] = (hid + moe).astype(BF16)
+    for f in range(2):
+        cols = slice(f * w, f * w + w)
+        outs[0][:, cols] = (hid_ref[:, cols].astype(F32) + moe[f]).astype(BF16)
 
 
 def blend(returned, mix, hidden):
@@ -603,14 +617,15 @@
     for i, share in enumerate(shares):
         outs[0][i] = share
     outs[1][...] = jnp.broadcast_to(total, outs[1].shape)
+    outs[2][...] = far[0].get()[...]
 
 
 def proj_body(near, far, outs, own):
-    others, w_ref, first_ref, total_ref = near[:3], near[3], near[4], near[5]
+    others, (w_ref, first_ref, total_ref, gain_ref) = near[:3], near[3:]
     total = total_ref[:, 0:1]
     accs = [first_ref[i] for i in range(w_ref.shape[0])]
     for k, s in enumerate(others):
-        shares, add = proj_share(s[...].astype(F32), k + 1, far[0].get(), w_ref)
+        shares, add = proj_share(s[...].astype(F32), k + 1, gain_ref, w_ref)
         accs, total = [a + b for a, b in zip(accs, shares)], total + add
     scale = lax.rsqrt(total / w_ref.shape[1] + EPS)
     for i, acc in enumerate(accs):
@@ -622,8 +637,9 @@
     rows = parts[0].shape[0]
     shape = (kinds, rows, width)
     gain = gain.reshape(1, -1)
-    first = run(own_proj_body, "own_proj", [sds(shape, F32), sds((rows, HD), F32)], [weight], [gain, parts[0]])
-    return run(proj_body, "next_proj", [sds(shape, BF16)], [*parts[1:], weight, *first], [gain])[0]
+    outs = [sds(shape, F32), sds((rows, HD), F32), sds(gain.shape, F32)]
+    first = run(own_proj_body, "own_proj", outs, [weight], [gain, parts[0]])
+    return run(proj_body, "next_proj", [sds(shape, BF16)], [*parts[1:], weight, *first], [])[0]
 
 
 def from_heads(x):

time: 151 us -> 150 us (level)
  waiting for transfers between devices: 18.9 us -> 22.3 us
  starting transfers between devices: 35.1 us -> 33.2 us
  blocking collectives: 51.4 us -> 49.8 us
    ppermute x12, waiting for transfers between devices: 5.84 us -> 9.58 us  [from_heads(): lax.ppermute(x, 'head', [(i, (i + k) % n) for i in range(n)])]
    ppermute x12, starting transfers between devices: 16.6 us -> 13.5 us  [from_heads(): lax.ppermute(x, 'head', [(i, (i + k) % n) for i in range(n)])]
    all_to_all x1, blocking collectives: 23.3 us -> 21.7 us  [local(): returned = lax.all_to_all(expert_out, REQ, 0, 0, tiled=True)]
  transfers between devices with their start and end apart: 20 -> 20, of which waited for: 11 -> 9; matrix products, arithmetic and copies ran while one was open for 0% -> 0% of each run, Pallas kernels for 15% -> 16%
where the time goes in v9:
time: 150 us
  blocking collectives  49.8 us (33%)
  starting transfers between devices  33.2 us (22%)
  Pallas kernels  30 us (20%)
  waiting for transfers between devices  22.3 us (15%)
  between operations  14.3 us (10%)
    all_to_all x1, blocking collectives, local(): lax.all_to_all(outset(queries, residual, routes, chips), ('z', 'y'), 0, 0...  28.1 us
    pallas_call x14, Pallas kernels, run(): pl.pallas_call(kernel, name=name, out_shape=list(outs) + [pltpu.HBM(x.sha...  27.4 us
    all_to_all x1, blocking collectives, local(): returned = lax.all_to_all(expert_out, REQ, 0, 0, tiled=True)  21.7 us
    ppermute x12, starting transfers between devices, from_heads(): lax.ppermute(x, 'head', [(i, (i + k) % n) for i in range(n)])  13.5 us
    ppermute x12, waiting for transfers between devices, from_heads(): lax.ppermute(x, 'head', [(i, (i + k) % n) for i in range(n)])  9.58 us
    all_to_all x1, starting transfers between devices, local(): tokens = lax.all_to_all(disp, REQ, 0, 0, tiled=True)  7.57 us
    ppermute x3, waiting for transfers between devices, to_heads(): lax.ppermute(xs[k], 'head', [(i, (i + k) % n) for i in range(n)])  5.27 us
    ppermute x3, starting transfers between devices, to_heads(): lax.ppermute(xs[k], 'head', [(i, (i + k) % n) for i in range(n)])  4.92 us
  transfers between devices with their start and end apart: 20, of which 9 were waited for; matrix products, arithmetic and copies ran while one was open for 0% of the time, Pallas kernels for 16%

profile of v9, /device:TPU:1, one launch (start us, length us, event | category | flops | bytes accessed | tf_op | source)
XLA Modules:
  0.0 149.6 jit_solution(3890930692339374788)
XLA Ops:
  7.2 0.0 all-gather.2.cloned.1.call-start
  7.2 0.7 all-gather.2.cloned.1.call-update
  7.9 1.4 outset.1
  9.3 28.1 %all_to_all.20.refs_4_.refs_7_.qa_ref = bf16[32,32,256]{2,1,0:T(8,128)(2,1)S(1)} all-to-all(bf16[32,32,256]{2,1,0:T(8,128)(2,1)S(1)} %outset.1), channel_id=1, replica_groups=mesh['z'=8,'y'=4,'c'=2,'head'=4] {'z','y'}, dimensions={0} | all-to-all | bytes 1048576 | tf_op jit(solution)/shard_map/all_to_all | solution.py:667
  37.4 2.4 %collective-permute-start = (bf16[32,32,256]{2,1,0:T(8,128)(2,1)S(1)}, bf16[32,32,256]{2,1,0:T(8,128)(2,1)S(1)}, u32[]{:S(2)}, u32[]{:S(2)}) collective-permute-start(bf16[32,32,256]{2,1,0:T(8,128)(2,1)S(1)} %all_to_all.20.refs_4_.refs_7_.qa_ref), channel_id=1, source_target_pairs={{0,4},{4,0},{1,5},{5,1},{2,6},{6,2},{3,7},{7,3},{8,12},{12,8},{9,1... | collective-permute-start | bytes 1572872 | tf_op jit(solution)/shard_map/ppermute | solution.py:656
  39.8 2.4 %slot_tables.1 = (bf16[128,1024]{1,0:T(8,128)(2,1)S(1)}, f32[128,128]{1,0:T(8,128)S(1)}, f32[128,128]{1,0:T(8,128)S(1)}, f32[128,128]{1,0:T(8,128)S(1)}, bf16[10...) custom-call(s32[1,128]{1,0:T(1,128)} %bitcast.28, s32[1,128]{1,0:T(1,128)} %bitcast.29, ...), custom_call_target="tpu_custom_call" | custom-call | tf_op jit(solution)/shard_map/slot_tables/pallas_call | solution.py:112
  42.2 5.1 %attend_pages.1 = (bf16[32,40,128]{2,1,0:T(8,128)(2,1)S(1)}, bf16[32,40,128]{2,1,0:T(8,128)(2,1)S(1)}) custom-call(bf16[128,1024]{1,0:T(8,128)(2,1)S(1)} %get-tuple-element.41.refs_0_, f32[128,128]{1,0:T(8,128)S(1)} %get-tuple-element.42.refs_1_, f32[128,128]{1,0:T(8,128)S(1)} %get-tuple-element.43.refs_2_, f32[128,128]{1,0:T(8,128)S(1)} %get-tuple-element.44.refs_3_, ...), custom_call_target="tpu_custom_call" | custom-call | tf_op jit(solution)/shard_map/attend_pages/pallas_call | solution.py:112
  47.3 0.3 collective-permute-start.1
  47.6 1.4 collective-permute-done.1.refs_1_
  49.0 1.8 %merge.1.refs_1_.after_ref = bf16[32,40,128]{2,1,0:T(8,128)(2,1)} custom-call(bf16[32,40,128]{2,1,0:T(8,128)(2,1)S(1)} %get-tuple-element.48.refs_0_, bf16[32,40,128]{2,1,0:T(8,128)(2,1)S(1)} %collective-permute-done.1.refs_1_), custom_call_target="tpu_custom_call" | custom-call | tf_op jit(solution)/shard_map/merge/pallas_call | solution.py:112
  50.9 4.4 %all-to-all-start.1 = ((bf16[32,40,128]{2,1,0:T(8,128)(2,1)}), bf16[32,40,128]{2,1,0:T(8,128)(2,1)S(1)}, u32[]{:S(2)}, u32[]{:S(2)}) async-start(bf16[32,40,128]{2,1,0:T(8,128)(2,1)} %merge.1.refs_1_.after_ref), calls=%async_computation.1 | async-start | bytes 655360 | tf_op jit(solution)/shard_map/all_to_all | solution.py:674
  55.3 2.5 %pack.1 = (bf16[1024,256]{1,0:T(8,128)(2,1)}, bf16[1024,256]{1,0:T(8,128)(2,1)}, bf16[1024,256]{1,0:T(8,128)(2,1)}, bf16[1024,256]{1,0:T(8,128)(2,1)}) custom-call(bf16[256,2048]{1,0:T(8,128)(2,1)} %bitcast.19, bf16[32,32,256]{2,1,0:T(8,128)(2,1)} %copy-done.1, bf16[32,32,256]{2,1,0:T(8,128)(2,1)} %copy-done.2, bf16[32,40,128]{2,1,0:T(8,128)(2,1)} %merge.1.refs_1_.after_ref), custom_call_target="tpu_custom_call" | custom-call | tf_op jit(solution)/shard_map/pack/pallas_call | solution.py:377
  57.8 1.3 collective-permute-start.5
  59.1 2.5 %collective-permute-start.6 = (bf16[1024,256]{1,0:T(8,128)(2,1)}, bf16[1024,256]{1,0:T(8,128)(2,1)S(1)}, u32[]{:S(2)}, u32[]{:S(2)}) collective-permute-start(bf16[1024,256]{1,0:T(8,128)(2,1)} %get-tuple-element.56), channel_id=1, source_target_pairs={{0,2},{1,3},{2,0},{3,1},{4,6},{5,7},{6,4},{7,5},{8,10},{9,11},{10,... | collective-permute-start | bytes 1572872 | tf_op jit(solution)/shard_map/ppermute | solution.py:652
  61.6 1.1 collective-permute-start.7
  62.8 1.7 %cells_table.1.refs_3_ = bf16[32,512]{1,0:T(8,128)(2,1)} custom-call(s32[8,16]{1,0:T(8,128)} %bitcast.21, bf16[32,40,128]{2,1,0:T(8,128)(2,1)} %merge.1.refs_1_.after_ref), custom_call_target="tpu_custom_call" | custom-call | tf_op jit(solution)/shard_map/cells_table/pallas_call | solution.py:112
  64.5 3.7 %all-to-all-done.1.refs_0_ = bf16[32,40,128]{2,1,0:T(8,128)(2,1)S(1)} async-done(((bf16[32,40,128]{2,1,0:T(8,128)(2,1)}), bf16[32,40,128]{2,1,0:T(8,128)(2,1)S(1)}, u32[]{:S(2)}, u32[]{:S(2)}) %all-to-all-start.1) | async-done | bytes 327712 | tf_op jit(solution)/shard_map/all_to_all | solution.py:674
  68.1 2.0 %owner_part.1 = (bf16[16,256]{1,0:T(8,128)(2,1)S(1)}, bf16[64,8,128]{2,1,0:T(8,128)(2,1)}) custom-call(bf16[32,40,128]{2,1,0:T(8,128)(2,1)S(1)} %all-to-all-done.1.refs_0_, bf16[16,256]{1,0:T(8,128)(2,1)} %refs_1_.3, bf16[16,2,256]{2,1,0:T(2,128)(2,1)} %refs_2_.1, bf16[32,512]{1,0:T(8,128)(2,1)} %cells_table.1.refs_3_), custom_call_target="tpu_custom_call" | custom-call | tf_op jit(solution)/shard_map/owner_part/pallas_call | solution.py:112
  70.1 0.0 copy-start.3
  70.2 7.6 %all-to-all-start.2 = ((bf16[64,8,128]{2,1,0:T(8,128)(2,1)}), bf16[64,8,128]{2,1,0:T(8,128)(2,1)S(1)}, u32[]{:S(2)}, u32[]{:S(2)}) async-start(bf16[64,8,128]{2,1,0:T(8,128)(2,1)} %get-tuple-element.52), calls=%async_computation.2 | async-start | bytes 262144 | tf_op jit(solution)/shard_map/all_to_all | solution.py:677
  77.7 0.4 collective-permute-start.2
  78.1 2.3 %collective-permute-start.3 = (bf16[16,256]{1,0:T(8,128)(2,1)S(1)}, bf16[16,256]{1,0:T(8,128)(2,1)S(1)}, u32[]{:S(2)}, u32[]{:S(2)}) collective-permute-start(bf16[16,256]{1,0:T(8,128)(2,1)S(1)} %get-tuple-element.65.refs_6_), channel_id=1, source_target_pairs={{0,2},{1,3},{2,0},{3,1},{4,6},{5,7},{6,4},{7,5},{8,10},{9,11},{10,... | collective-permute-start | bytes 24584 | tf_op jit(solution)/shard_map/ppermute | solution.py:647
  80.4 0.0 collective-permute-done.5.refs_2_
  80.4 1.1 collective-permute-start.4
  81.6 5.3 %collective-permute-done.6.refs_3_ = bf16[1024,256]{1,0:T(8,128)(2,1)S(1)} collective-permute-done((bf16[1024,256]{1,0:T(8,128)(2,1)}, bf16[1024,256]{1,0:T(8,128)(2,1)S(1)}, u32[]{:S(2)}, u32[]{:S(2)}) %collective-permute-start.6) | collective-permute-done | bytes 524320 | tf_op jit(solution)/shard_map/ppermute | solution.py:652
  86.8 0.3 collective-permute-done.3.refs_8_
  87.2 1.7 %all-to-all-done.2.refs_0_ = bf16[64,8,128]{2,1,0:T(8,128)(2,1)S(1)} async-done(((bf16[64,8,128]{2,1,0:T(8,128)(2,1)}), bf16[64,8,128]{2,1,0:T(8,128)(2,1)S(1)}, u32[]{:S(2)}, u32[]{:S(2)}) %all-to-all-start.2) | async-done | bytes 131104 | tf_op jit(solution)/shard_map/all_to_all | solution.py:677
  88.9 1.6 %collective-permute-start.10 = (bf16[64,8,128]{2,1,0:T(8,128)(2,1)S(1)}, bf16[64,8,128]{2,1,0:T(8,128)(2,1)S(1)}, u32[]{:S(2)}, u32[]{:S(2)}) collective-permute-start(bf16[64,8,128]{2,1,0:T(8,128)(2,1)S(1)} %all-to-all-done.2.refs_0_), channel_id=1, source_target_pairs={{0,3},{1,0},{2,1},{3,2},{4,7},{5,4},{6,5},{7,6},{8,11},{9,8},{10,9... | collective-permute-start | bytes 393224 | tf_op jit(solution)/shard_map/ppermute | solution.py:647
  90.5 1.7 %collective-permute-start.9 = (bf16[64,8,128]{2,1,0:T(8,128)(2,1)S(1)}, bf16[64,8,128]{2,1,0:T(8,128)(2,1)S(1)}, u32[]{:S(2)}, u32[]{:S(2)}) collective-permute-start(bf16[64,8,128]{2,1,0:T(8,128)(2,1)S(1)} %all-to-all-done.2.refs_0_), channel_id=1, source_target_pairs={{0,2},{1,3},{2,0},{3,1},{4,6},{5,7},{6,4},{7,5},{8,10},{9,11},{10,... | collective-permute-start | bytes 393224 | tf_op jit(solution)/shard_map/ppermute | solution.py:647
  92.2 3.1 %early_rows.1 = (f32[8,256,256]{2,1,0:T(8,128)S(1)}, bf16[1024,2048]{1,0:T(8,128)(2,1)S(1)}) custom-call(bf16[64,8,128]{2,1,0:T(8,128)(2,1)S(1)} %all-to-all-done.2.refs_0_, bf16[1024,256]{1,0:T(8,128)(2,1)} %get-tuple-element.59.refs_1_, bf16[1024,256]{1,0:T(8,128)(2,1)} %copy-done.4, bf16[1024,256]{1,0:T(8,128)(2,1)} %copy-done.5, ...), custom_call_target="tpu_custom_call" | custom-call | tf_op jit(solution)/shard_map/early_rows/pallas_call | solution.py:112
  95.3 4.1 %collective-permute-done.8.refs_0_ = bf16[64,8,128]{2,1,0:T(8,128)(2,1)S(1)} collective-permute-done((bf16[64,8,128]{2,1,0:T(8,128)(2,1)S(1)}, bf16[64,8,128]{2,1,0:T(8,128)(2,1)S(1)}, u32[]{:S(2)}, u32[]{:S(2)}) %collective-permute-start.8) | collective-permute-done | bytes 131104 | tf_op jit(solution)/shard_map/ppermute | solution.py:647
  99.4 3.6 %expert_rows.1 = (bf16[256,256]{1,0:T(8,128)(2,1)S(1)}, bf16[16,512]{1,0:T(8,128)(2,1)}) custom-call(bf16[64,8,128]{2,1,0:T(8,128)(2,1)S(1)} %collective-permute-done.8.refs_0_, bf16[64,8,128]{2,1,0:T(8,128)(2,1)S(1)} %collective-permute-done.9.refs_1_, bf16[64,8,128]{2,1,0:T(8,128)(2,1)S(1)} %collective-permute-done.10.refs_2_, ...), custom_call_target="tpu_custom_call" | custom-call | tf_op jit(solution)/shard_map/expert_rows/pallas_call | solution.py:112
  103.0 0.0 copy-start
  103.0 0.1 collective-permute-start.11
  103.1 0.2 collective-permute-start.12
  103.4 2.4 %collective-permute-start.13 = (bf16[256,256]{1,0:T(8,128)(2,1)S(1)}, bf16[256,256]{1,0:T(8,128)(2,1)S(1)}, u32[]{:S(2)}, u32[]{:S(2)}) collective-permute-start(bf16[256,256]{1,0:T(8,128)(2,1)S(1)} %get-tuple-element.69.refs_0_.refs_2_), channel_id=1, source_target_pairs={{0,3},{1,0},{2,1},{3,2},{4,7},{5,4},{6,5},{7,6},{8,11},{9,8},{10,9... | collective-permute-start | bytes 393224 | tf_op jit(solution)/shard_map/ppermute | solution.py:647
  105.8 1.4 fetch.1
  107.2 1.1 mix_table.1
  108.3 3.4 %collective-permute-done.11.refs_1_ = bf16[256,256]{1,0:T(8,128)(2,1)S(1)} collective-permute-done((bf16[256,256]{1,0:T(8,128)(2,1)S(1)}, bf16[256,256]{1,0:T(8,128)(2,1)S(1)}, u32[]{:S(2)}, u32[]{:S(2)}) %collective-permute-start.11) | collective-permute-done | bytes 131104 | tf_op jit(solution)/shard_map/ppermute | solution.py:647
  111.7 0.5 down.1
  112.1 21.7 %all_to_all.21.refs_0_ = bf16[64,8,256]{2,1,0:T(8,128)(2,1)S(1)} all-to-all(bf16[64,8,256]{2,1,0:T(8,128)(2,1)S(1)} %bitcast.16), channel_id=1, replica_groups=mesh['z'=8,'y'=4,'c'=2,'head'=4] {'z','y','c'}, dimensions={0} | all-to-all | bytes 524288 | tf_op jit(solution)/shard_map/all_to_all | solution.py:688
  133.9 1.4 blend.1.refs_2_
  135.2 0.4 collective-permute-start.14
  135.6 3.2 %collective-permute-start.15 = (bf16[16,512]{1,0:T(8,128)(2,1)}, bf16[16,512]{1,0:T(8,128)(2,1)S(1)}, u32[]{:S(2)}, u32[]{:S(2)}) collective-permute-start(bf16[16,512]{1,0:T(8,128)(2,1)} %blend.1.refs_2_), channel_id=1, source_target_pairs={{0,2},{1,3},{2,0},{3,1},{4,6},{5,7},{6,4},{7,5},{8,10},{9,11},{10,... | collective-permute-start | bytes 49160 | tf_op jit(solution)/shard_map/ppermute | solution.py:647
  138.9 1.0 own_proj.1
  139.9 0.4 collective-permute-done.15.refs_1_
  140.4 1.3 collective-permute-done.16.refs_2_
  141.7 1.1 next_proj.1
  (30 shorter events, 0.1 us)
Async XLA Ops:
  7.2 85.0 %all-gather.2.cloned.1.call-start = ((), (), s32[]{:S(2)}) async-start(), calls=%async_computation.4 | async-start | bytes 5242880 | tf_op jit(solution)/shard_map/all_gather | solution.py:666
  37.4 9.9 %copy-start.1 = (bf16[32,32,256]{2,1,0:T(8,128)(2,1)}, bf16[32,32,256]{2,1,0:T(8,128)(2,1)S(1)}, u32[]{:S(2)}) copy-start(bf16[32,32,256]{2,1,0:T(8,128)(2,1)S(1)} %all_to_all.20.refs_4_.refs_7_.qa_ref) | copy-start | bytes 1572868
  37.4 4.8 %collective-permute-start = (bf16[32,32,256]{2,1,0:T(8,128)(2,1)S(1)}, bf16[32,32,256]{2,1,0:T(8,128)(2,1)S(1)}, u32[]{:S(2)}, u32[]{:S(2)}) collective-permute-start(bf16[32,32,256]{2,1,0:T(8,128)(2,1)S(1)} %all_to_all.20.refs_4_.refs_7_.qa_ref), channel_id=1, source_target_pairs={{0,4},{4,0},{1,5},{5,1},{2,6},{6,2},{3,7},{7,3},{8,12},{12,8},{9,1... | collective-permute-start | bytes 1572872 | tf_op jit(solution)/shard_map/ppermute | solution.py:656
  42.2 13.1 %copy-start.2 = (bf16[32,32,256]{2,1,0:T(8,128)(2,1)}, bf16[32,32,256]{2,1,0:T(8,128)(2,1)S(1)}, u32[]{:S(2)}) copy-start(bf16[32,32,256]{2,1,0:T(8,128)(2,1)S(1)} %collective-permute-done.refs_8_.qb_ref) | copy-start | bytes 1572868
  47.3 1.7 %collective-permute-start.1 = (bf16[32,40,128]{2,1,0:T(8,128)(2,1)S(1)}, bf16[32,40,128]{2,1,0:T(8,128)(2,1)S(1)}, u32[]{:S(2)}, u32[]{:S(2)}) collective-permute-start(bf16[32,40,128]{2,1,0:T(8,128)(2,1)S(1)} %get-tuple-element.49), channel_id=1, source_target_pairs={{0,4},{4,0},{1,5},{5,1},{2,6},{6,2},{3,7},{7,3},{8,12},{12,8},{9,1... | collective-permute-start | bytes 983048 | tf_op jit(solution)/shard_map/ppermute | solution.py:656
  50.9 17.3 %all-to-all-start.1 = ((bf16[32,40,128]{2,1,0:T(8,128)(2,1)}), bf16[32,40,128]{2,1,0:T(8,128)(2,1)S(1)}, u32[]{:S(2)}, u32[]{:S(2)}) async-start(bf16[32,40,128]{2,1,0:T(8,128)(2,1)} %merge.1.refs_1_.after_ref), calls=%async_computation.1 | async-start | bytes 655360 | tf_op jit(solution)/shard_map/all_to_all | solution.py:674
  57.8 22.6 %collective-permute-start.5 = (bf16[1024,256]{1,0:T(8,128)(2,1)}, bf16[1024,256]{1,0:T(8,128)(2,1)S(1)}, u32[]{:S(2)}, u32[]{:S(2)}) collective-permute-start(bf16[1024,256]{1,0:T(8,128)(2,1)} %get-tuple-element.55), channel_id=1, source_target_pairs={{0,1},{1,2},{2,3},{3,0},{4,5},{5,6},{6,7},{7,4},{8,9},{9,10},{10,1... | collective-permute-start | bytes 1572872 | tf_op jit(solution)/shard_map/ppermute | solution.py:652
  59.1 27.7 %collective-permute-start.6 = (bf16[1024,256]{1,0:T(8,128)(2,1)}, bf16[1024,256]{1,0:T(8,128)(2,1)S(1)}, u32[]{:S(2)}, u32[]{:S(2)}) collective-permute-start(bf16[1024,256]{1,0:T(8,128)(2,1)} %get-tuple-element.56), channel_id=1, source_target_pairs={{0,2},{1,3},{2,0},{3,1},{4,6},{5,7},{6,4},{7,5},{8,10},{9,11},{10,... | collective-permute-start | bytes 1572872 | tf_op jit(solution)/shard_map/ppermute | solution.py:652
  61.6 25.2 %collective-permute-start.7 = (bf16[1024,256]{1,0:T(8,128)(2,1)}, bf16[1024,256]{1,0:T(8,128)(2,1)S(1)}, u32[]{:S(2)}, u32[]{:S(2)}) collective-permute-start(bf16[1024,256]{1,0:T(8,128)(2,1)} %get-tuple-element.57), channel_id=1, source_target_pairs={{0,3},{1,0},{2,1},{3,2},{4,7},{5,4},{6,5},{7,6},{8,11},{9,8},{10,9... | collective-permute-start | bytes 1572872 | tf_op jit(solution)/shard_map/ppermute | solution.py:652
  70.1 29.2 %copy-start.3 = (bf16[16,256]{1,0:T(8,128)(2,1)}, bf16[16,256]{1,0:T(8,128)(2,1)S(1)}, u32[]{:S(2)}) copy-start(bf16[16,256]{1,0:T(8,128)(2,1)S(1)} %get-tuple-element.65.refs_6_) | copy-start | bytes 24580
  70.2 18.7 %all-to-all-start.2 = ((bf16[64,8,128]{2,1,0:T(8,128)(2,1)}), bf16[64,8,128]{2,1,0:T(8,128)(2,1)S(1)}, u32[]{:S(2)}, u32[]{:S(2)}) async-start(bf16[64,8,128]{2,1,0:T(8,128)(2,1)} %get-tuple-element.52), calls=%async_computation.2 | async-start | bytes 262144 | tf_op jit(solution)/shard_map/all_to_all | solution.py:677
  77.7 9.1 %collective-permute-start.2 = (bf16[16,256]{1,0:T(8,128)(2,1)S(1)}, bf16[16,256]{1,0:T(8,128)(2,1)S(1)}, u32[]{:S(2)}, u32[]{:S(2)}) collective-permute-start(bf16[16,256]{1,0:T(8,128)(2,1)S(1)} %get-tuple-element.65.refs_6_), channel_id=1, source_target_pairs={{0,1},{1,2},{2,3},{3,0},{4,5},{5,6},{6,7},{7,4},{8,9},{9,10},{10,1... | collective-permute-start | bytes 24584 | tf_op jit(solution)/shard_map/ppermute | solution.py:647
  78.1 9.0 %collective-permute-start.3 = (bf16[16,256]{1,0:T(8,128)(2,1)S(1)}, bf16[16,256]{1,0:T(8,128)(2,1)S(1)}, u32[]{:S(2)}, u32[]{:S(2)}) collective-permute-start(bf16[16,256]{1,0:T(8,128)(2,1)S(1)} %get-tuple-element.65.refs_6_), channel_id=1, source_target_pairs={{0,2},{1,3},{2,0},{3,1},{4,6},{5,7},{6,4},{7,5},{8,10},{9,11},{10,... | collective-permute-start | bytes 24584 | tf_op jit(solution)/shard_map/ppermute | solution.py:647
  80.4 11.8 %copy-start.4 = (bf16[1024,256]{1,0:T(8,128)(2,1)}, bf16[1024,256]{1,0:T(8,128)(2,1)S(1)}, u32[]{:S(2)}) copy-start(bf16[1024,256]{1,0:T(8,128)(2,1)S(1)} %collective-permute-done.5.refs_2_) | copy-start | bytes 1572868
  80.4 6.7 %collective-permute-start.4 = (bf16[16,256]{1,0:T(8,128)(2,1)S(1)}, bf16[16,256]{1,0:T(8,128)(2,1)S(1)}, u32[]{:S(2)}, u32[]{:S(2)}) collective-permute-start(bf16[16,256]{1,0:T(8,128)(2,1)S(1)} %get-tuple-element.65.refs_6_), channel_id=1, source_target_pairs={{0,3},{1,0},{2,1},{3,2},{4,7},{5,4},{6,5},{7,6},{8,11},{9,8},{10,9... | collective-permute-start | bytes 24584 | tf_op jit(solution)/shard_map/ppermute | solution.py:647
  86.8 5.4 %copy-start.5 = (bf16[1024,256]{1,0:T(8,128)(2,1)}, bf16[1024,256]{1,0:T(8,128)(2,1)S(1)}, u32[]{:S(2)}) copy-start(bf16[1024,256]{1,0:T(8,128)(2,1)S(1)} %collective-permute-done.6.refs_3_) | copy-start | bytes 1572868
  86.8 5.4 %copy-start.6 = (bf16[1024,256]{1,0:T(8,128)(2,1)}, bf16[1024,256]{1,0:T(8,128)(2,1)S(1)}, u32[]{:S(2)}) copy-start(bf16[1024,256]{1,0:T(8,128)(2,1)S(1)} %collective-permute-done.7.refs_4_) | copy-start | bytes 1572868
  86.8 12.6 %copy-start.7 = (bf16[16,256]{1,0:T(8,128)(2,1)}, bf16[16,256]{1,0:T(8,128)(2,1)S(1)}, u32[]{:S(2)}) copy-start(bf16[16,256]{1,0:T(8,128)(2,1)S(1)} %collective-permute-done.2.refs_7_) | copy-start | bytes 24580
  87.2 12.2 %copy-start.8 = (bf16[16,256]{1,0:T(8,128)(2,1)}, bf16[16,256]{1,0:T(8,128)(2,1)S(1)}, u32[]{:S(2)}) copy-start(bf16[16,256]{1,0:T(8,128)(2,1)S(1)} %collective-permute-done.3.refs_8_) | copy-start | bytes 24580
  87.2 12.2 %copy-start.9 = (bf16[16,256]{1,0:T(8,128)(2,1)}, bf16[16,256]{1,0:T(8,128)(2,1)S(1)}, u32[]{:S(2)}) copy-start(bf16[16,256]{1,0:T(8,128)(2,1)S(1)} %collective-permute-done.4.refs_9_) | copy-start | bytes 24580
  88.9 6.4 %collective-permute-start.10 = (bf16[64,8,128]{2,1,0:T(8,128)(2,1)S(1)}, bf16[64,8,128]{2,1,0:T(8,128)(2,1)S(1)}, u32[]{:S(2)}, u32[]{:S(2)}) collective-permute-start(bf16[64,8,128]{2,1,0:T(8,128)(2,1)S(1)} %all-to-all-done.2.refs_0_), channel_id=1, source_target_pairs={{0,3},{1,0},{2,1},{3,2},{4,7},{5,4},{6,5},{7,6},{8,11},{9,8},{10,9... | collective-permute-start | bytes 393224 | tf_op jit(solution)/shard_map/ppermute | solution.py:647
  90.5 8.9 %collective-permute-start.8 = (bf16[64,8,128]{2,1,0:T(8,128)(2,1)S(1)}, bf16[64,8,128]{2,1,0:T(8,128)(2,1)S(1)}, u32[]{:S(2)}, u32[]{:S(2)}) collective-permute-start(bf16[64,8,128]{2,1,0:T(8,128)(2,1)S(1)} %all-to-all-done.2.refs_0_), channel_id=1, source_target_pairs={{0,1},{1,2},{2,3},{3,0},{4,5},{5,6},{6,7},{7,4},{8,9},{9,10},{10,1... | collective-permute-start | bytes 393224 | tf_op jit(solution)/shard_map/ppermute | solution.py:647
  90.5 8.9 %collective-permute-start.9 = (bf16[64,8,128]{2,1,0:T(8,128)(2,1)S(1)}, bf16[64,8,128]{2,1,0:T(8,128)(2,1)S(1)}, u32[]{:S(2)}, u32[]{:S(2)}) collective-permute-start(bf16[64,8,128]{2,1,0:T(8,128)(2,1)S(1)} %all-to-all-done.2.refs_0_), channel_id=1, source_target_pairs={{0,2},{1,3},{2,0},{3,1},{4,6},{5,7},{6,4},{7,5},{8,10},{9,11},{10,... | collective-permute-start | bytes 393224 | tf_op jit(solution)/shard_map/ppermute | solution.py:647
  103.0 35.9 %copy-start = (bf16[2048,3,256]{2,0,1:T(8,128)(2,1)S(1)}, bf16[2048,3,256]{2,0,1:T(8,128)(2,1)}, u32[]{:S(2)}) copy-start(bf16[2048,3,256]{2,0,1:T(8,128)(2,1)} %param.33) | copy-start | bytes 9437188
  103.0 8.6 %collective-permute-start.11 = (bf16[256,256]{1,0:T(8,128)(2,1)S(1)}, bf16[256,256]{1,0:T(8,128)(2,1)S(1)}, u32[]{:S(2)}, u32[]{:S(2)}) collective-permute-start(bf16[256,256]{1,0:T(8,128)(2,1)S(1)} %get-tuple-element.69.refs_0_.refs_2_), channel_id=1, source_target_pairs={{0,1},{1,2},{2,3},{3,0},{4,5},{5,6},{6,7},{7,4},{8,9},{9,10},{10,1... | collective-permute-start | bytes 393224 | tf_op jit(solution)/shard_map/ppermute | solution.py:647
  103.1 8.5 %collective-permute-start.12 = (bf16[256,256]{1,0:T(8,128)(2,1)S(1)}, bf16[256,256]{1,0:T(8,128)(2,1)S(1)}, u32[]{:S(2)}, u32[]{:S(2)}) collective-permute-start(bf16[256,256]{1,0:T(8,128)(2,1)S(1)} %get-tuple-element.69.refs_0_.refs_2_), channel_id=1, source_target_pairs={{0,2},{1,3},{2,0},{3,1},{4,6},{5,7},{6,4},{7,5},{8,10},{9,11},{10,... | collective-permute-start | bytes 393224 | tf_op jit(solution)/shard_map/ppermute | solution.py:647
  103.4 8.3 %collective-permute-start.13 = (bf16[256,256]{1,0:T(8,128)(2,1)S(1)}, bf16[256,256]{1,0:T(8,128)(2,1)S(1)}, u32[]{:S(2)}, u32[]{:S(2)}) collective-permute-start(bf16[256,256]{1,0:T(8,128)(2,1)S(1)} %get-tuple-element.69.refs_0_.refs_2_), channel_id=1, source_target_pairs={{0,3},{1,0},{2,1},{3,2},{4,7},{5,4},{6,5},{7,6},{8,11},{9,8},{10,9... | collective-permute-start | bytes 393224 | tf_op jit(solution)/shard_map/ppermute | solution.py:647
  135.2 4.7 %collective-permute-start.14 = (bf16[16,512]{1,0:T(8,128)(2,1)}, bf16[16,512]{1,0:T(8,128)(2,1)S(1)}, u32[]{:S(2)}, u32[]{:S(2)}) collective-permute-start(bf16[16,512]{1,0:T(8,128)(2,1)} %blend.1.refs_2_), channel_id=1, source_target_pairs={{0,1},{1,2},{2,3},{3,0},{4,5},{5,6},{6,7},{7,4},{8,9},{9,10},{10,1... | collective-permute-start | bytes 49160 | tf_op jit(solution)/shard_map/ppermute | solution.py:647
  135.6 4.7 %collective-permute-start.15 = (bf16[16,512]{1,0:T(8,128)(2,1)}, bf16[16,512]{1,0:T(8,128)(2,1)S(1)}, u32[]{:S(2)}, u32[]{:S(2)}) collective-permute-start(bf16[16,512]{1,0:T(8,128)(2,1)} %blend.1.refs_2_), channel_id=1, source_target_pairs={{0,2},{1,3},{2,0},{3,1},{4,6},{5,7},{6,4},{7,5},{8,10},{9,11},{10,... | collective-permute-start | bytes 49160 | tf_op jit(solution)/shard_map/ppermute | solution.py:647
  138.9 2.8 %collective-permute-start.16 = (bf16[16,512]{1,0:T(8,128)(2,1)}, bf16[16,512]{1,0:T(8,128)(2,1)S(1)}, u32[]{:S(2)}, u32[]{:S(2)}) collective-permute-start(bf16[16,512]{1,0:T(8,128)(2,1)} %blend.1.refs_2_), channel_id=1, source_target_pairs={{0,3},{1,0},{2,1},{3,2},{4,7},{5,4},{6,5},{7,6},{8,11},{9,8},{10,9... | collective-permute-start | bytes 49160 | tf_op jit(solution)/shard_map/ppermute | solution.py:647
Sparse Core Ops, SparseCore 0:
  9.8 56.3 all-gather.1

commit v10 on v9

--- a/solution.py
+++ b/solution.py
@@ -334,7 +334,8 @@
 
 
 def pack_kernel(w_ref, qa_ref, qb_ref, after_ref, *refs):
-    outs, res_buf, in_a, in_b, bufs, sems = refs[:4], refs[4], refs[5], refs[6], refs[7:11], refs[11]
+    outs, far_block, refs = refs[:4], refs[4], refs[5:]
+    res_buf, in_a, in_b, bufs, sems = refs[0], refs[1], refs[2], refs[3:7], refs[7]
     rows, width = bufs[0].shape[0] // 2, bufs[0].shape[1]
     held = res_buf.shape[0]
     reads = [
@@ -349,7 +350,8 @@
         for f in range(2):
             src = w_ref.at[:, pl.ds(first + f * width, width)]
             cuts.append(pltpu.make_async_copy(src, bufs[k].at[pl.ds(f * rows, rows)], sems.at[2 * k + f]))
-        writes.append(pltpu.make_async_copy(bufs[k], outs[k].at[pl.ds(held, 2 * rows)], sems.at[8 + k]))
+        block = far_block if k == 2 else outs[k].at[pl.ds(held, 2 * rows)]
+        writes.append(pltpu.make_async_copy(bufs[k], block, sems.at[8 + k]))
     for cut in cuts:
         cut.start()
     for read in reads:
@@ -377,9 +379,10 @@
     return pl.pallas_call(
         pack_kernel,
         name="pack",
-        out_shape=[pltpu.HBM((held + 2 * rows, width), BF16)] * 4,
+        out_shape=[pltpu.HBM((held + (0 if k == 2 else 2 * rows), width), BF16) for k in range(4)]
+        + [pltpu.HBM((2 * rows, width), BF16)],
         in_specs=[hbm] * 4,
-        out_specs=[hbm] * 4,
+        out_specs=[hbm] * 5,
         scratch_shapes=[pltpu.VMEM((held, width), BF16)]
         + [pltpu.VMEM((chips, 8, width), BF16)] * 2
         + [pltpu.VMEM((2 * rows, width), BF16)] * 4
@@ -535,6 +538,12 @@
     att = [jnp.concatenate(unfold(a[...].astype(F32)), axis=1).astype(BF16) for a in att]
     block = head_blocks(eff)
     firsts = [first + f * w for first in head_blocks(2 * w) for f in range(2)]
+    cols = pl.ds(head_blocks(2 * w)[0], 2 * w)
+    acc = own_res.get()[:, cols].astype(F32)
+    acc = acc + sum(dot(mine[i].get()[...], wo_ref[pl.ds(block[i], eff), cols]) for i in range(4))
+    hid.buf[...] = acc.astype(BF16)
+    for _ in range(PIECES):
+        hid.send()
     total = jnp.zeros((n, 1), F32)
     for j, first in enumerate(firsts):
         acc = xs[j]
@@ -544,12 +553,6 @@
         hs[j] = part
         part = part.astype(F32)
         total = total + jnp.sum(part * part, axis=1, keepdims=True)
-    cols = pl.ds(head_blocks(2 * w)[0], 2 * w)
-    acc = own_res.get()[:, cols].astype(F32)
-    acc = acc + sum(dot(mine[i].get()[...], wo_ref[pl.ds(block[i], eff), cols]) for i in range(4))
-    hid.buf[...] = acc.astype(BF16)
-    for _ in range(PIECES):
-        hid.send()
     scale = lax.rsqrt(total / (8 * w) + EPS)
     gain_ref = gain.get()
     wg_ref, wu_ref = w_gate.get(), w_up.get()
@@ -669,20 +672,24 @@
     qb = swap_core(qa)
     keep, send = attend_pages(tables, qa, qb)
     merged = merge(keep, swap_core(send))
-    packs = to_heads(pack(w_down[0], qa, qb, merged))
+    *packs, block = pack(w_down[0], qa, qb, merged)
+    packs = to_heads(packs)
+    for _ in range(2):
+        block = lax.ppermute(block, "head", [(i, (i + 3) % 4) for i in range(4)])
     cells = cells_table(routes, experts, merged)
     arrived = lax.all_to_all(merged, ("z", "y"), 0, 0, tiled=True)
     arrived, cells = lax.optimization_barrier((arrived, cells))
     attended, disp = owner_part(arrived, queries, new_kv, cells, experts)
     tokens = lax.all_to_all(disp, REQ, 0, 0, tiled=True)
     mine = from_heads(attended)
-    tokens, mine, packs = lax.optimization_barrier((tokens, mine, packs))
+    tokens, mine, packs, block = lax.optimization_barrier((tokens, mine, packs, block))
     held = experts * 8
     res = [(p, 0, held) for p in packs]
     early, out_weight = early_rows(tokens, out_weight, res)
     others = from_heads(tokens)[1:]
     inner, hidden = expert_rows(others, early, out_weight, w_gate[0], w_up[0], norm_gain, mine, residual)
-    w_cols = fetch(inner, *[(p, held, p.shape[0] - held) for p in packs])
+    blocks = [block if k == 2 else (p, held, p.shape[0] - held) for k, p in enumerate(packs)]
+    w_cols = fetch(inner, *blocks)
     mix = mix_table(routes, route_weights, experts, inner)
     expert_out = down(from_heads(inner), w_cols, mix[0])
     returned = lax.all_to_all(expert_out, REQ, 0, 0, tiled=True)

time: 150 us -> 157 us (1.047)
  starting transfers between devices: 33.2 us -> 40.4 us
    ppermute x0 -> x2, waiting for transfers between devices: none -> 9.3 us  [local(): block = lax.ppermute(block, 'head', [(i, (i + 3) % 4) for i in range(4)])]
    ppermute x3, waiting for transfers between devices: 5.27 us -> 0.01 us  [to_heads(): lax.ppermute(xs[k], 'head', [(i, (i + k) % n) for i in range(n)])]
    all_to_all x1, starting transfers between devices: 7.57 us -> 11.8 us  [local(): tokens = lax.all_to_all(disp, REQ, 0, 0, tiled=True)]
    ppermute x0 -> x2, starting transfers between devices: none -> 3.7 us  [local(): block = lax.ppermute(block, 'head', [(i, (i + 3) % 4) for i in range(4)])]
    all_to_all x1, waiting for transfers between devices: 3.7 us -> 0.01 us  [local(): arrived = lax.all_to_all(merged, ('z', 'y'), 0, 0, tiled=True)]
    ppermute x3, starting transfers between devices: 4.92 us -> 2.68 us  [to_heads(): lax.ppermute(xs[k], 'head', [(i, (i + k) % n) for i in range(n)])]
  transfers between devices with their start and end apart: 20 -> 22, of which waited for: 9 -> 10; matrix products, arithmetic and copies ran while one was open for 0% -> 0% of each run, Pallas kernels for 16% -> 15%
where the time goes in v10:
time: 157 us; the launch traced here: 156 us
  blocking collectives  49.2 us (31%)
  starting transfers between devices  40.4 us (26%)
  Pallas kernels  29.5 us (19%)
  waiting for transfers between devices  23 us (15%)
  between operations  14.4 us (9%)
    all_to_all x1, blocking collectives, local(): lax.all_to_all(outset(queries, residual, routes, chips), ('z', 'y'), 0, 0...  28.1 us
    pallas_call x14, Pallas kernels, run(): pl.pallas_call(kernel, name=name, out_shape=list(outs) + [pltpu.HBM(x.sha...  26.9 us
    all_to_all x1, blocking collectives, local(): returned = lax.all_to_all(expert_out, REQ, 0, 0, tiled=True)  21.1 us
    ppermute x12, starting transfers between devices, from_heads(): lax.ppermute(x, 'head', [(i, (i + k) % n) for i in range(n)])  15.1 us
    all_to_all x1, starting transfers between devices, local(): tokens = lax.all_to_all(disp, REQ, 0, 0, tiled=True)  11.8 us
    ppermute x2, waiting for transfers between devices, local(): block = lax.ppermute(block, 'head', [(i, (i + 3) % 4) for i in range(4)])  9.3 us
    ppermute x12, waiting for transfers between devices, from_heads(): lax.ppermute(x, 'head', [(i, (i + k) % n) for i in range(n)])  9.17 us
    all_to_all x1, starting transfers between devices, local(): arrived = lax.all_to_all(merged, ('z', 'y'), 0, 0, tiled=True)  4.39 us
  transfers between devices with their start and end apart: 22, of which 10 were waited for; matrix products, arithmetic and copies ran while one was open for 0% of the time, Pallas kernels for 15%

profile of v10, /device:TPU:1, one launch (start us, length us, event | category | flops | bytes accessed | tf_op | source)
XLA Modules:
  0.0 156.4 jit_solution(9073915530735766532)
XLA Ops:
  7.2 0.0 all-gather.2.cloned.1.call-start
  7.2 0.7 all-gather.2.cloned.1.call-update
  7.9 1.4 outset.1
  9.3 28.1 %all_to_all.20.refs_4_.refs_7_.qa_ref = bf16[32,32,256]{2,1,0:T(8,128)(2,1)S(1)} all-to-all(bf16[32,32,256]{2,1,0:T(8,128)(2,1)S(1)} %outset.1), channel_id=1, replica_groups=mesh['z'=8,'y'=4,'c'=2,'head'=4] {'z','y'}, dimensions={0} | all-to-all | bytes 1048576 | tf_op jit(solution)/shard_map/all_to_all | solution.py:670
  37.4 2.4 %collective-permute-start = (bf16[32,32,256]{2,1,0:T(8,128)(2,1)S(1)}, bf16[32,32,256]{2,1,0:T(8,128)(2,1)S(1)}, u32[]{:S(2)}, u32[]{:S(2)}) collective-permute-start(bf16[32,32,256]{2,1,0:T(8,128)(2,1)S(1)} %all_to_all.20.refs_4_.refs_7_.qa_ref), channel_id=1, source_target_pairs={{0,4},{4,0},{1,5},{5,1},{2,6},{6,2},{3,7},{7,3},{8,12},{12,8},{9,1... | collective-permute-start | bytes 1572872 | tf_op jit(solution)/shard_map/ppermute | solution.py:659
  39.8 2.4 %slot_tables.1 = (bf16[128,1024]{1,0:T(8,128)(2,1)S(1)}, f32[128,128]{1,0:T(8,128)S(1)}, f32[128,128]{1,0:T(8,128)S(1)}, f32[128,128]{1,0:T(8,128)S(1)}, bf16[10...) custom-call(s32[1,128]{1,0:T(1,128)} %bitcast.28, s32[1,128]{1,0:T(1,128)} %bitcast.29, ...), custom_call_target="tpu_custom_call" | custom-call | tf_op jit(solution)/shard_map/slot_tables/pallas_call | solution.py:112
  42.2 5.1 %attend_pages.1 = (bf16[32,40,128]{2,1,0:T(8,128)(2,1)S(1)}, bf16[32,40,128]{2,1,0:T(8,128)(2,1)S(1)}) custom-call(bf16[128,1024]{1,0:T(8,128)(2,1)S(1)} %get-tuple-element.43.refs_0_, f32[128,128]{1,0:T(8,128)S(1)} %get-tuple-element.44.refs_1_, f32[128,128]{1,0:T(8,128)S(1)} %get-tuple-element.45.refs_2_, f32[128,128]{1,0:T(8,128)S(1)} %get-tuple-element.46.refs_3_, ...), custom_call_target="tpu_custom_call" | custom-call | tf_op jit(solution)/shard_map/attend_pages/pallas_call | solution.py:112
  47.3 0.3 collective-permute-start.1
  47.6 1.4 collective-permute-done.1.refs_1_
  49.0 1.8 %merge.1.refs_1_.after_ref = bf16[32,40,128]{2,1,0:T(8,128)(2,1)} custom-call(bf16[32,40,128]{2,1,0:T(8,128)(2,1)S(1)} %get-tuple-element.50.refs_0_, bf16[32,40,128]{2,1,0:T(8,128)(2,1)S(1)} %collective-permute-done.1.refs_1_), custom_call_target="tpu_custom_call" | custom-call | tf_op jit(solution)/shard_map/merge/pallas_call | solution.py:112
  50.9 4.4 %all-to-all-start.1 = ((bf16[32,40,128]{2,1,0:T(8,128)(2,1)}), bf16[32,40,128]{2,1,0:T(8,128)(2,1)S(1)}, u32[]{:S(2)}, u32[]{:S(2)}) async-start(bf16[32,40,128]{2,1,0:T(8,128)(2,1)} %merge.1.refs_1_.after_ref), calls=%async_computation.1 | async-start | bytes 655360 | tf_op jit(solution)/shard_map/all_to_all | solution.py:680
  55.3 2.5 %pack.1 = (bf16[1024,256]{1,0:T(8,128)(2,1)}, bf16[1024,256]{1,0:T(8,128)(2,1)}, bf16[512,256]{1,0:T(8,128)(2,1)}, bf16[1024,256]{1,0:T(8,128)(2,1)}, bf16[512,256]{1,0:T(8,128)(2,1)}) custom-call(bf16[256,2048]{1,0:T(8,128)(2,1)} %bitcast.19, bf16[32,32,256]{2,1,0:T(8,128)(2,1)} %copy-done.1, bf16[32,32,256]{2,1,0:T(8,128)(2,1)} %copy-done.2, ...), custom_call_target="tpu_custom_call" | custom-call | tf_op jit(solution)/shard_map/pack/pallas_call | solution.py:379
  57.8 2.6 %collective-permute-start.8 = (bf16[512,256]{1,0:T(8,128)(2,1)}, bf16[512,256]{1,0:T(8,128)(2,1)S(1)}, u32[]{:S(2)}, u32[]{:S(2)}) collective-permute-start(bf16[512,256]{1,0:T(8,128)(2,1)} %get-tuple-element.60), channel_id=1, source_target_pairs={{0,3},{1,0},{2,1},{3,2},{4,7},{5,4},{6,5},{7,6},{8,11},{9,8},{10,9... | collective-permute-start | bytes 786440 | tf_op jit(solution)/shard_map/ppermute | solution.py:678
  60.4 2.7 %collective-permute-start.7 = (bf16[1024,256]{1,0:T(8,128)(2,1)}, bf16[1024,256]{1,0:T(8,128)(2,1)S(1)}, u32[]{:S(2)}, u32[]{:S(2)}) collective-permute-start(bf16[1024,256]{1,0:T(8,128)(2,1)} %get-tuple-element.59), channel_id=1, source_target_pairs={{0,3},{1,0},{2,1},{3,2},{4,7},{5,4},{6,5},{7,6},{8,11},{9,8},{10,9... | collective-permute-start | bytes 1572872 | tf_op jit(solution)/shard_map/ppermute | solution.py:655
  63.1 5.9 %collective-permute-done.8 = bf16[512,256]{1,0:T(8,128)(2,1)S(1)} collective-permute-done((bf16[512,256]{1,0:T(8,128)(2,1)}, bf16[512,256]{1,0:T(8,128)(2,1)S(1)}, u32[]{:S(2)}, u32[]{:S(2)}) %collective-permute-start.8) | collective-permute-done | bytes 262176 | tf_op jit(solution)/shard_map/ppermute | solution.py:678
  69.0 1.1 collective-permute-start.9
  70.1 1.7 %cells_table.1.refs_3_ = bf16[32,512]{1,0:T(8,128)(2,1)} custom-call(s32[8,16]{1,0:T(8,128)} %bitcast.21, bf16[32,40,128]{2,1,0:T(8,128)(2,1)} %merge.1.refs_1_.after_ref), custom_call_target="tpu_custom_call" | custom-call | tf_op jit(solution)/shard_map/cells_table/pallas_call | solution.py:112
  71.8 2.0 %owner_part.1 = (bf16[16,256]{1,0:T(8,128)(2,1)S(1)}, bf16[64,8,128]{2,1,0:T(8,128)(2,1)}) custom-call(bf16[32,40,128]{2,1,0:T(8,128)(2,1)S(1)} %all-to-all-done.1.refs_0_, bf16[16,256]{1,0:T(8,128)(2,1)} %refs_1_.3, bf16[16,2,256]{2,1,0:T(2,128)(2,1)} %refs_2_.1, bf16[32,512]{1,0:T(8,128)(2,1)} %cells_table.1.refs_3_), custom_call_target="tpu_custom_call" | custom-call | tf_op jit(solution)/shard_map/owner_part/pallas_call | solution.py:112
  73.8 0.0 copy-start.3
  73.8 11.8 %all-to-all-start.2 = ((bf16[64,8,128]{2,1,0:T(8,128)(2,1)}), bf16[64,8,128]{2,1,0:T(8,128)(2,1)S(1)}, u32[]{:S(2)}, u32[]{:S(2)}) async-start(bf16[64,8,128]{2,1,0:T(8,128)(2,1)} %get-tuple-element.54), calls=%async_computation.2 | async-start | bytes 262144 | tf_op jit(solution)/shard_map/all_to_all | solution.py:683
  85.6 0.1 collective-permute-start.2
  85.8 2.4 %collective-permute-start.3 = (bf16[16,256]{1,0:T(8,128)(2,1)S(1)}, bf16[16,256]{1,0:T(8,128)(2,1)S(1)}, u32[]{:S(2)}, u32[]{:S(2)}) collective-permute-start(bf16[16,256]{1,0:T(8,128)(2,1)S(1)} %get-tuple-element.68.refs_6_), channel_id=1, source_target_pairs={{0,2},{1,3},{2,0},{3,1},{4,6},{5,7},{6,4},{7,5},{8,10},{9,11},{10,... | collective-permute-start | bytes 24584 | tf_op jit(solution)/shard_map/ppermute | solution.py:650
  88.1 3.4 %collective-permute-done.9.refs_3_ = bf16[512,256]{1,0:T(8,128)(2,1)S(1)} collective-permute-done((bf16[512,256]{1,0:T(8,128)(2,1)S(1)}, bf16[512,256]{1,0:T(8,128)(2,1)S(1)}, u32[]{:S(2)}, u32[]{:S(2)}) %collective-permute-start.9) | collective-permute-done | bytes 262176 | tf_op jit(solution)/shard_map/ppermute | solution.py:678
  91.5 1.0 collective-permute-start.4
  92.6 1.7 %collective-permute-done.4.refs_9_ = bf16[16,256]{1,0:T(8,128)(2,1)S(1)} collective-permute-done((bf16[16,256]{1,0:T(8,128)(2,1)S(1)}, bf16[16,256]{1,0:T(8,128)(2,1)S(1)}, u32[]{:S(2)}, u32[]{:S(2)}) %collective-permute-start.4) | collective-permute-done | bytes 8224 | tf_op jit(solution)/shard_map/ppermute | solution.py:650
  94.3 2.4 %all-to-all-done.2.refs_0_ = bf16[64,8,128]{2,1,0:T(8,128)(2,1)S(1)} async-done(((bf16[64,8,128]{2,1,0:T(8,128)(2,1)}), bf16[64,8,128]{2,1,0:T(8,128)(2,1)S(1)}, u32[]{:S(2)}, u32[]{:S(2)}) %all-to-all-start.2) | async-done | bytes 131104 | tf_op jit(solution)/shard_map/all_to_all | solution.py:683
  96.8 2.4 %collective-permute-start.11 = (bf16[64,8,128]{2,1,0:T(8,128)(2,1)S(1)}, bf16[64,8,128]{2,1,0:T(8,128)(2,1)S(1)}, u32[]{:S(2)}, u32[]{:S(2)}) collective-permute-start(bf16[64,8,128]{2,1,0:T(8,128)(2,1)S(1)} %all-to-all-done.2.refs_0_), channel_id=1, source_target_pairs={{0,2},{1,3},{2,0},{3,1},{4,6},{5,7},{6,4},{7,5},{8,10},{9,11},{10,... | collective-permute-start | bytes 393224 | tf_op jit(solution)/shard_map/ppermute | solution.py:650
  99.1 1.2 collective-permute-start.12
  100.3 3.1 %early_rows.1 = (f32[8,256,256]{2,1,0:T(8,128)S(1)}, bf16[1024,2048]{1,0:T(8,128)(2,1)S(1)}) custom-call(bf16[64,8,128]{2,1,0:T(8,128)(2,1)S(1)} %all-to-all-done.2.refs_0_, bf16[1024,256]{1,0:T(8,128)(2,1)} %get-tuple-element.62.refs_1_, bf16[1024,256]{1,0:T(8,128)(2,1)} %copy-done.4, bf16[512,256]{1,0:T(8,128)(2,1)} %copy-done.7, ...), custom_call_target="tpu_custom_call" | custom-call | tf_op jit(solution)/shard_map/early_rows/pallas_call | solution.py:112
  103.4 1.8 %collective-permute-done.11.refs_1_ = bf16[64,8,128]{2,1,0:T(8,128)(2,1)S(1)} collective-permute-done((bf16[64,8,128]{2,1,0:T(8,128)(2,1)S(1)}, bf16[64,8,128]{2,1,0:T(8,128)(2,1)S(1)}, u32[]{:S(2)}, u32[]{:S(2)}) %collective-permute-start.11) | collective-permute-done | bytes 131104 | tf_op jit(solution)/shard_map/ppermute | solution.py:650
  105.2 0.5 collective-permute-done.12.refs_2_
  105.7 3.1 %expert_rows.1 = (bf16[256,256]{1,0:T(8,128)(2,1)S(1)}, bf16[16,512]{1,0:T(8,128)(2,1)}) custom-call(bf16[64,8,128]{2,1,0:T(8,128)(2,1)S(1)} %collective-permute-done.10.refs_0_, bf16[64,8,128]{2,1,0:T(8,128)(2,1)S(1)} %collective-permute-done.11.refs_1_, bf16[64,8,128]{2,1,0:T(8,128)(2,1)S(1)} %collective-permute-done.12.refs_2_, ...), custom_call_target="tpu_custom_call" | custom-call | tf_op jit(solution)/shard_map/expert_rows/pallas_call | solution.py:112
  108.9 0.0 copy-start
  108.9 2.0 %collective-permute-start.13 = (bf16[256,256]{1,0:T(8,128)(2,1)S(1)}, bf16[256,256]{1,0:T(8,128)(2,1)S(1)}, u32[]{:S(2)}, u32[]{:S(2)}) collective-permute-start(bf16[256,256]{1,0:T(8,128)(2,1)S(1)} %get-tuple-element.72.refs_0_.refs_2_), channel_id=1, source_target_pairs={{0,1},{1,2},{2,3},{3,0},{4,5},{5,6},{6,7},{7,4},{8,9},{9,10},{10,1... | collective-permute-start | bytes 393224 | tf_op jit(solution)/shard_map/ppermute | solution.py:650
  110.8 2.7 %collective-permute-start.14 = (bf16[256,256]{1,0:T(8,128)(2,1)S(1)}, bf16[256,256]{1,0:T(8,128)(2,1)S(1)}, u32[]{:S(2)}, u32[]{:S(2)}) collective-permute-start(bf16[256,256]{1,0:T(8,128)(2,1)S(1)} %get-tuple-element.72.refs_0_.refs_2_), channel_id=1, source_target_pairs={{0,2},{1,3},{2,0},{3,1},{4,6},{5,7},{6,4},{7,5},{8,10},{9,11},{10,... | collective-permute-start | bytes 393224 | tf_op jit(solution)/shard_map/ppermute | solution.py:650
  113.5 1.4 fetch.1
  114.9 1.1 mix_table.1
  116.0 3.3 %collective-permute-done.14.refs_2_ = bf16[256,256]{1,0:T(8,128)(2,1)S(1)} collective-permute-done((bf16[256,256]{1,0:T(8,128)(2,1)S(1)}, bf16[256,256]{1,0:T(8,128)(2,1)S(1)}, u32[]{:S(2)}, u32[]{:S(2)}) %collective-permute-start.14) | collective-permute-done | bytes 131104 | tf_op jit(solution)/shard_map/ppermute | solution.py:650
  119.4 0.5 down.1
  119.8 21.1 %all_to_all.21.refs_0_ = bf16[64,8,256]{2,1,0:T(8,128)(2,1)S(1)} all-to-all(bf16[64,8,256]{2,1,0:T(8,128)(2,1)S(1)} %bitcast.16), channel_id=1, replica_groups=mesh['z'=8,'y'=4,'c'=2,'head'=4] {'z','y','c'}, dimensions={0} | all-to-all | bytes 524288 | tf_op jit(solution)/shard_map/all_to_all | solution.py:695
  140.9 1.4 blend.1.refs_2_
  142.3 0.6 collective-permute-start.16
  142.9 2.5 %collective-permute-start.17 = (bf16[16,512]{1,0:T(8,128)(2,1)}, bf16[16,512]{1,0:T(8,128)(2,1)S(1)}, u32[]{:S(2)}, u32[]{:S(2)}) collective-permute-start(bf16[16,512]{1,0:T(8,128)(2,1)} %blend.1.refs_2_), channel_id=1, source_target_pairs={{0,2},{1,3},{2,0},{3,1},{4,6},{5,7},{6,4},{7,5},{8,10},{9,11},{10,... | collective-permute-start | bytes 49160 | tf_op jit(solution)/shard_map/ppermute | solution.py:650
  145.4 0.2 collective-permute-start.18
  145.7 1.0 own_proj.1
  146.7 0.6 collective-permute-done.17.refs_1_
  147.3 1.2 collective-permute-done.18.refs_2_
  148.5 1.1 next_proj.1
  (36 shorter events, 0.1 us)
Async XLA Ops:
  7.2 93.2 %all-gather.2.cloned.1.call-start = ((), (), s32[]{:S(2)}) async-start(), calls=%async_computation.4 | async-start | bytes 5242880 | tf_op jit(solution)/shard_map/all_gather | solution.py:669
  37.4 9.9 %copy-start.1 = (bf16[32,32,256]{2,1,0:T(8,128)(2,1)}, bf16[32,32,256]{2,1,0:T(8,128)(2,1)S(1)}, u32[]{:S(2)}) copy-start(bf16[32,32,256]{2,1,0:T(8,128)(2,1)S(1)} %all_to_all.20.refs_4_.refs_7_.qa_ref) | copy-start | bytes 1572868
  37.4 4.8 %collective-permute-start = (bf16[32,32,256]{2,1,0:T(8,128)(2,1)S(1)}, bf16[32,32,256]{2,1,0:T(8,128)(2,1)S(1)}, u32[]{:S(2)}, u32[]{:S(2)}) collective-permute-start(bf16[32,32,256]{2,1,0:T(8,128)(2,1)S(1)} %all_to_all.20.refs_4_.refs_7_.qa_ref), channel_id=1, source_target_pairs={{0,4},{4,0},{1,5},{5,1},{2,6},{6,2},{3,7},{7,3},{8,12},{12,8},{9,1... | collective-permute-start | bytes 1572872 | tf_op jit(solution)/shard_map/ppermute | solution.py:659
  42.2 13.1 %copy-start.2 = (bf16[32,32,256]{2,1,0:T(8,128)(2,1)}, bf16[32,32,256]{2,1,0:T(8,128)(2,1)S(1)}, u32[]{:S(2)}) copy-start(bf16[32,32,256]{2,1,0:T(8,128)(2,1)S(1)} %collective-permute-done.refs_8_.qb_ref) | copy-start | bytes 1572868
  47.3 1.7 %collective-permute-start.1 = (bf16[32,40,128]{2,1,0:T(8,128)(2,1)S(1)}, bf16[32,40,128]{2,1,0:T(8,128)(2,1)S(1)}, u32[]{:S(2)}, u32[]{:S(2)}) collective-permute-start(bf16[32,40,128]{2,1,0:T(8,128)(2,1)S(1)} %get-tuple-element.51), channel_id=1, source_target_pairs={{0,4},{4,0},{1,5},{5,1},{2,6},{6,2},{3,7},{7,3},{8,12},{12,8},{9,1... | collective-permute-start | bytes 983048 | tf_op jit(solution)/shard_map/ppermute | solution.py:659
  50.9 20.9 %all-to-all-start.1 = ((bf16[32,40,128]{2,1,0:T(8,128)(2,1)}), bf16[32,40,128]{2,1,0:T(8,128)(2,1)S(1)}, u32[]{:S(2)}, u32[]{:S(2)}) async-start(bf16[32,40,128]{2,1,0:T(8,128)(2,1)} %merge.1.refs_1_.after_ref), calls=%async_computation.1 | async-start | bytes 655360 | tf_op jit(solution)/shard_map/all_to_all | solution.py:680
  57.8 11.2 %collective-permute-start.8 = (bf16[512,256]{1,0:T(8,128)(2,1)}, bf16[512,256]{1,0:T(8,128)(2,1)S(1)}, u32[]{:S(2)}, u32[]{:S(2)}) collective-permute-start(bf16[512,256]{1,0:T(8,128)(2,1)} %get-tuple-element.60), channel_id=1, source_target_pairs={{0,3},{1,0},{2,1},{3,2},{4,7},{5,4},{6,5},{7,6},{8,11},{9,8},{10,9... | collective-permute-start | bytes 786440 | tf_op jit(solution)/shard_map/ppermute | solution.py:678
  60.4 32.1 %collective-permute-start.5 = (bf16[1024,256]{1,0:T(8,128)(2,1)}, bf16[1024,256]{1,0:T(8,128)(2,1)S(1)}, u32[]{:S(2)}, u32[]{:S(2)}) collective-permute-start(bf16[1024,256]{1,0:T(8,128)(2,1)} %get-tuple-element.57), channel_id=1, source_target_pairs={{0,1},{1,2},{2,3},{3,0},{4,5},{5,6},{6,7},{7,4},{8,9},{9,10},{10,1... | collective-permute-start | bytes 1572872 | tf_op jit(solution)/shard_map/ppermute | solution.py:655
  60.4 32.1 %collective-permute-start.7 = (bf16[1024,256]{1,0:T(8,128)(2,1)}, bf16[1024,256]{1,0:T(8,128)(2,1)S(1)}, u32[]{:S(2)}, u32[]{:S(2)}) collective-permute-start(bf16[1024,256]{1,0:T(8,128)(2,1)} %get-tuple-element.59), channel_id=1, source_target_pairs={{0,3},{1,0},{2,1},{3,2},{4,7},{5,4},{6,5},{7,6},{8,11},{9,8},{10,9... | collective-permute-start | bytes 1572872 | tf_op jit(solution)/shard_map/ppermute | solution.py:655
  63.1 22.6 %collective-permute-start.6 = (bf16[512,256]{1,0:T(8,128)(2,1)}, bf16[512,256]{1,0:T(8,128)(2,1)S(1)}, u32[]{:S(2)}, u32[]{:S(2)}) collective-permute-start(bf16[512,256]{1,0:T(8,128)(2,1)} %get-tuple-element.58), channel_id=1, source_target_pairs={{0,2},{1,3},{2,0},{3,1},{4,6},{5,7},{6,4},{7,5},{8,10},{9,11},{10,... | collective-permute-start | bytes 786440 | tf_op jit(solution)/shard_map/ppermute | solution.py:655
  69.0 22.5 %collective-permute-start.9 = (bf16[512,256]{1,0:T(8,128)(2,1)S(1)}, bf16[512,256]{1,0:T(8,128)(2,1)S(1)}, u32[]{:S(2)}, u32[]{:S(2)}) collective-permute-start(bf16[512,256]{1,0:T(8,128)(2,1)S(1)} %collective-permute-done.8), channel_id=1, source_target_pairs={{0,3},{1,0},{2,1},{3,2},{4,7},{5,4},{6,5},{7,6},{8,11},{9,8},{10,9... | collective-permute-start | bytes 786440 | tf_op jit(solution)/shard_map/ppermute | solution.py:678
  73.8 31.9 %copy-start.3 = (bf16[16,256]{1,0:T(8,128)(2,1)}, bf16[16,256]{1,0:T(8,128)(2,1)S(1)}, u32[]{:S(2)}) copy-start(bf16[16,256]{1,0:T(8,128)(2,1)S(1)} %get-tuple-element.68.refs_6_) | copy-start | bytes 24580
  73.8 23.0 %all-to-all-start.2 = ((bf16[64,8,128]{2,1,0:T(8,128)(2,1)}), bf16[64,8,128]{2,1,0:T(8,128)(2,1)S(1)}, u32[]{:S(2)}, u32[]{:S(2)}) async-start(bf16[64,8,128]{2,1,0:T(8,128)(2,1)} %get-tuple-element.54), calls=%async_computation.2 | async-start | bytes 262144 | tf_op jit(solution)/shard_map/all_to_all | solution.py:683
  85.6 6.9 %collective-permute-start.2 = (bf16[16,256]{1,0:T(8,128)(2,1)S(1)}, bf16[16,256]{1,0:T(8,128)(2,1)S(1)}, u32[]{:S(2)}, u32[]{:S(2)}) collective-permute-start(bf16[16,256]{1,0:T(8,128)(2,1)S(1)} %get-tuple-element.68.refs_6_), channel_id=1, source_target_pairs={{0,1},{1,2},{2,3},{3,0},{4,5},{5,6},{6,7},{7,4},{8,9},{9,10},{10,1... | collective-permute-start | bytes 24584 | tf_op jit(solution)/shard_map/ppermute | solution.py:650
  85.7 14.6 %copy-start.7 = (bf16[512,256]{1,0:T(8,128)(2,1)}, bf16[512,256]{1,0:T(8,128)(2,1)S(1)}, u32[]{:S(2)}) copy-start(bf16[512,256]{1,0:T(8,128)(2,1)S(1)} %collective-permute-done.6.refs_3_) | copy-start | bytes 786436
  85.8 6.9 %collective-permute-start.3 = (bf16[16,256]{1,0:T(8,128)(2,1)S(1)}, bf16[16,256]{1,0:T(8,128)(2,1)S(1)}, u32[]{:S(2)}, u32[]{:S(2)}) collective-permute-start(bf16[16,256]{1,0:T(8,128)(2,1)S(1)} %get-tuple-element.68.refs_6_), channel_id=1, source_target_pairs={{0,2},{1,3},{2,0},{3,1},{4,6},{5,7},{6,4},{7,5},{8,10},{9,11},{10,... | collective-permute-start | bytes 24584 | tf_op jit(solution)/shard_map/ppermute | solution.py:650
  91.5 22.0 %copy-start.6 = (bf16[512,256]{1,0:T(8,128)(2,1)}, bf16[512,256]{1,0:T(8,128)(2,1)S(1)}, u32[]{:S(2)}) copy-start(bf16[512,256]{1,0:T(8,128)(2,1)S(1)} %collective-permute-done.9.refs_3_) | copy-start | bytes 786436
  91.5 2.8 %collective-permute-start.4 = (bf16[16,256]{1,0:T(8,128)(2,1)S(1)}, bf16[16,256]{1,0:T(8,128)(2,1)S(1)}, u32[]{:S(2)}, u32[]{:S(2)}) collective-permute-start(bf16[16,256]{1,0:T(8,128)(2,1)S(1)} %get-tuple-element.68.refs_6_), channel_id=1, source_target_pairs={{0,3},{1,0},{2,1},{3,2},{4,7},{5,4},{6,5},{7,6},{8,11},{9,8},{10,9... | collective-permute-start | bytes 24584 | tf_op jit(solution)/shard_map/ppermute | solution.py:650
  92.6 7.8 %copy-start.4 = (bf16[1024,256]{1,0:T(8,128)(2,1)}, bf16[1024,256]{1,0:T(8,128)(2,1)S(1)}, u32[]{:S(2)}) copy-start(bf16[1024,256]{1,0:T(8,128)(2,1)S(1)} %collective-permute-done.5.refs_2_) | copy-start | bytes 1572868
  92.6 7.8 %copy-start.5 = (bf16[1024,256]{1,0:T(8,128)(2,1)}, bf16[1024,256]{1,0:T(8,128)(2,1)S(1)}, u32[]{:S(2)}) copy-start(bf16[1024,256]{1,0:T(8,128)(2,1)S(1)} %collective-permute-done.7.refs_4_) | copy-start | bytes 1572868
  92.6 13.1 %copy-start.8 = (bf16[16,256]{1,0:T(8,128)(2,1)}, bf16[16,256]{1,0:T(8,128)(2,1)S(1)}, u32[]{:S(2)}) copy-start(bf16[16,256]{1,0:T(8,128)(2,1)S(1)} %collective-permute-done.2.refs_7_) | copy-start | bytes 24580
  92.6 13.1 %copy-start.9 = (bf16[16,256]{1,0:T(8,128)(2,1)}, bf16[16,256]{1,0:T(8,128)(2,1)S(1)}, u32[]{:S(2)}) copy-start(bf16[16,256]{1,0:T(8,128)(2,1)S(1)} %collective-permute-done.3.refs_8_) | copy-start | bytes 24580
  94.3 11.4 %copy-start.10 = (bf16[16,256]{1,0:T(8,128)(2,1)}, bf16[16,256]{1,0:T(8,128)(2,1)S(1)}, u32[]{:S(2)}) copy-start(bf16[16,256]{1,0:T(8,128)(2,1)S(1)} %collective-permute-done.4.refs_9_) | copy-start | bytes 24580
  96.8 6.6 %collective-permute-start.10 = (bf16[64,8,128]{2,1,0:T(8,128)(2,1)S(1)}, bf16[64,8,128]{2,1,0:T(8,128)(2,1)S(1)}, u32[]{:S(2)}, u32[]{:S(2)}) collective-permute-start(bf16[64,8,128]{2,1,0:T(8,128)(2,1)S(1)} %all-to-all-done.2.refs_0_), channel_id=1, source_target_pairs={{0,1},{1,2},{2,3},{3,0},{4,5},{5,6},{6,7},{7,4},{8,9},{9,10},{10,1... | collective-permute-start | bytes 393224 | tf_op jit(solution)/shard_map/ppermute | solution.py:650
  96.8 8.5 %collective-permute-start.11 = (bf16[64,8,128]{2,1,0:T(8,128)(2,1)S(1)}, bf16[64,8,128]{2,1,0:T(8,128)(2,1)S(1)}, u32[]{:S(2)}, u32[]{:S(2)}) collective-permute-start(bf16[64,8,128]{2,1,0:T(8,128)(2,1)S(1)} %all-to-all-done.2.refs_0_), channel_id=1, source_target_pairs={{0,2},{1,3},{2,0},{3,1},{4,6},{5,7},{6,4},{7,5},{8,10},{9,11},{10,... | collective-permute-start | bytes 393224 | tf_op jit(solution)/shard_map/ppermute | solution.py:650
  99.1 6.6 %collective-permute-start.12 = (bf16[64,8,128]{2,1,0:T(8,128)(2,1)S(1)}, bf16[64,8,128]{2,1,0:T(8,128)(2,1)S(1)}, u32[]{:S(2)}, u32[]{:S(2)}) collective-permute-start(bf16[64,8,128]{2,1,0:T(8,128)(2,1)S(1)} %all-to-all-done.2.refs_0_), channel_id=1, source_target_pairs={{0,3},{1,0},{2,1},{3,2},{4,7},{5,4},{6,5},{7,6},{8,11},{9,8},{10,9... | collective-permute-start | bytes 393224 | tf_op jit(solution)/shard_map/ppermute | solution.py:650
  108.9 36.8 %copy-start = (bf16[2048,3,256]{2,0,1:T(8,128)(2,1)S(1)}, bf16[2048,3,256]{2,0,1:T(8,128)(2,1)}, u32[]{:S(2)}) copy-start(bf16[2048,3,256]{2,0,1:T(8,128)(2,1)} %param.33) | copy-start | bytes 9437188
  108.9 7.1 %collective-permute-start.13 = (bf16[256,256]{1,0:T(8,128)(2,1)S(1)}, bf16[256,256]{1,0:T(8,128)(2,1)S(1)}, u32[]{:S(2)}, u32[]{:S(2)}) collective-permute-start(bf16[256,256]{1,0:T(8,128)(2,1)S(1)} %get-tuple-element.72.refs_0_.refs_2_), channel_id=1, source_target_pairs={{0,1},{1,2},{2,3},{3,0},{4,5},{5,6},{6,7},{7,4},{8,9},{9,10},{10,1... | collective-permute-start | bytes 393224 | tf_op jit(solution)/shard_map/ppermute | solution.py:650
  110.8 8.5 %collective-permute-start.14 = (bf16[256,256]{1,0:T(8,128)(2,1)S(1)}, bf16[256,256]{1,0:T(8,128)(2,1)S(1)}, u32[]{:S(2)}, u32[]{:S(2)}) collective-permute-start(bf16[256,256]{1,0:T(8,128)(2,1)S(1)} %get-tuple-element.72.refs_0_.refs_2_), channel_id=1, source_target_pairs={{0,2},{1,3},{2,0},{3,1},{4,6},{5,7},{6,4},{7,5},{8,10},{9,11},{10,... | collective-permute-start | bytes 393224 | tf_op jit(solution)/shard_map/ppermute | solution.py:650
  113.5 5.8 %collective-permute-start.15 = (bf16[256,256]{1,0:T(8,128)(2,1)S(1)}, bf16[256,256]{1,0:T(8,128)(2,1)S(1)}, u32[]{:S(2)}, u32[]{:S(2)}) collective-permute-start(bf16[256,256]{1,0:T(8,128)(2,1)S(1)} %get-tuple-element.72.refs_0_.refs_2_), channel_id=1, source_target_pairs={{0,3},{1,0},{2,1},{3,2},{4,7},{5,4},{6,5},{7,6},{8,11},{9,8},{10,9... | collective-permute-start | bytes 393224 | tf_op jit(solution)/shard_map/ppermute | solution.py:650
  142.3 4.4 %collective-permute-start.16 = (bf16[16,512]{1,0:T(8,128)(2,1)}, bf16[16,512]{1,0:T(8,128)(2,1)S(1)}, u32[]{:S(2)}, u32[]{:S(2)}) collective-permute-start(bf16[16,512]{1,0:T(8,128)(2,1)} %blend.1.refs_2_), channel_id=1, source_target_pairs={{0,1},{1,2},{2,3},{3,0},{4,5},{5,6},{6,7},{7,4},{8,9},{9,10},{10,1... | collective-permute-start | bytes 49160 | tf_op jit(solution)/shard_map/ppermute | solution.py:650
  142.9 4.3 %collective-permute-start.17 = (bf16[16,512]{1,0:T(8,128)(2,1)}, bf16[16,512]{1,0:T(8,128)(2,1)S(1)}, u32[]{:S(2)}, u32[]{:S(2)}) collective-permute-start(bf16[16,512]{1,0:T(8,128)(2,1)} %blend.1.refs_2_), channel_id=1, source_target_pairs={{0,2},{1,3},{2,0},{3,1},{4,6},{5,7},{6,4},{7,5},{8,10},{9,11},{10,... | collective-permute-start | bytes 49160 | tf_op jit(solution)/shard_map/ppermute | solution.py:650
  145.4 3.1 %collective-permute-start.18 = (bf16[16,512]{1,0:T(8,128)(2,1)}, bf16[16,512]{1,0:T(8,128)(2,1)S(1)}, u32[]{:S(2)}, u32[]{:S(2)}) collective-permute-start(bf16[16,512]{1,0:T(8,128)(2,1)} %blend.1.refs_2_), channel_id=1, source_target_pairs={{0,3},{1,0},{2,1},{3,2},{4,7},{5,4},{6,5},{7,6},{8,11},{9,8},{10,9... | collective-permute-start | bytes 49160 | tf_op jit(solution)/shard_map/ppermute | solution.py:650
Sparse Core Ops, SparseCore 0:
  9.8 56.3 all-gather.1

commit v11 on v9

--- a/solution.py
+++ b/solution.py
@@ -535,6 +535,12 @@
     att = [jnp.concatenate(unfold(a[...].astype(F32)), axis=1).astype(BF16) for a in att]
     block = head_blocks(eff)
     firsts = [first + f * w for first in head_blocks(2 * w) for f in range(2)]
+    cols = pl.ds(head_blocks(2 * w)[0], 2 * w)
+    acc = own_res.get()[:, cols].astype(F32)
+    acc = acc + sum(dot(mine[i].get()[...], wo_ref[pl.ds(block[i], eff), cols]) for i in range(4))
+    hid.buf[...] = acc.astype(BF16)
+    for _ in range(PIECES):
+        hid.send()
     total = jnp.zeros((n, 1), F32)
     for j, first in enumerate(firsts):
         acc = xs[j]
@@ -544,12 +550,6 @@
         hs[j] = part
         part = part.astype(F32)
         total = total + jnp.sum(part * part, axis=1, keepdims=True)
-    cols = pl.ds(head_blocks(2 * w)[0], 2 * w)
-    acc = own_res.get()[:, cols].astype(F32)
-    acc = acc + sum(dot(mine[i].get()[...], wo_ref[pl.ds(block[i], eff), cols]) for i in range(4))
-    hid.buf[...] = acc.astype(BF16)
-    for _ in range(PIECES):
-        hid.send()
     scale = lax.rsqrt(total / (8 * w) + EPS)
     gain_ref = gain.get()
     wg_ref, wu_ref = w_gate.get(), w_up.get()

time: 150 us -> 150 us (level)
  no operation moved by 1% of the time
where the time goes in v11:
time: 150 us; the launch traced here: 149 us
  blocking collectives  49.8 us (33%)
  starting transfers between devices  33.2 us (22%)
  Pallas kernels  29.5 us (20%)
  waiting for transfers between devices  22.3 us (15%)
  between operations  14.3 us (10%)
    all_to_all x1, blocking collectives, local(): lax.all_to_all(outset(queries, residual, routes, chips), ('z', 'y'), 0, 0...  28.1 us
    pallas_call x14, Pallas kernels, run(): pl.pallas_call(kernel, name=name, out_shape=list(outs) + [pltpu.HBM(x.sha...  27 us
    all_to_all x1, blocking collectives, local(): returned = lax.all_to_all(expert_out, REQ, 0, 0, tiled=True)  21.7 us
    ppermute x12, starting transfers between devices, from_heads(): lax.ppermute(x, 'head', [(i, (i + k) % n) for i in range(n)])  13.5 us
    ppermute x12, waiting for transfers between devices, from_heads(): lax.ppermute(x, 'head', [(i, (i + k) % n) for i in range(n)])  9.58 us
    all_to_all x1, starting transfers between devices, local(): tokens = lax.all_to_all(disp, REQ, 0, 0, tiled=True)  7.57 us
    ppermute x3, waiting for transfers between devices, to_heads(): lax.ppermute(xs[k], 'head', [(i, (i + k) % n) for i in range(n)])  5.27 us
    ppermute x3, starting transfers between devices, to_heads(): lax.ppermute(xs[k], 'head', [(i, (i + k) % n) for i in range(n)])  4.92 us
  transfers between devices with their start and end apart: 20, of which 9 were waited for; matrix products, arithmetic and copies ran while one was open for 0% of the time, Pallas kernels for 16%

profile of v11, /device:TPU:1, one launch (start us, length us, event | category | flops | bytes accessed | tf_op | source)
XLA Modules:
  0.0 149.1 jit_solution(10339793258984515204)
XLA Ops:
  7.2 0.0 all-gather.2.cloned.1.call-start
  7.2 0.7 all-gather.2.cloned.1.call-update
  7.9 1.4 outset.1
  9.3 28.1 %all_to_all.20.refs_4_.refs_7_.qa_ref = bf16[32,32,256]{2,1,0:T(8,128)(2,1)S(1)} all-to-all(bf16[32,32,256]{2,1,0:T(8,128)(2,1)S(1)} %outset.1), channel_id=1, replica_groups=mesh['z'=8,'y'=4,'c'=2,'head'=4] {'z','y'}, dimensions={0} | all-to-all | bytes 1048576 | tf_op jit(solution)/shard_map/all_to_all | solution.py:667
  37.4 2.4 %collective-permute-start = (bf16[32,32,256]{2,1,0:T(8,128)(2,1)S(1)}, bf16[32,32,256]{2,1,0:T(8,128)(2,1)S(1)}, u32[]{:S(2)}, u32[]{:S(2)}) collective-permute-start(bf16[32,32,256]{2,1,0:T(8,128)(2,1)S(1)} %all_to_all.20.refs_4_.refs_7_.qa_ref), channel_id=1, source_target_pairs={{0,4},{4,0},{1,5},{5,1},{2,6},{6,2},{3,7},{7,3},{8,12},{12,8},{9,1... | collective-permute-start | bytes 1572872 | tf_op jit(solution)/shard_map/ppermute | solution.py:656
  39.8 2.4 %slot_tables.1 = (bf16[128,1024]{1,0:T(8,128)(2,1)S(1)}, f32[128,128]{1,0:T(8,128)S(1)}, f32[128,128]{1,0:T(8,128)S(1)}, f32[128,128]{1,0:T(8,128)S(1)}, bf16[10...) custom-call(s32[1,128]{1,0:T(1,128)} %bitcast.28, s32[1,128]{1,0:T(1,128)} %bitcast.29, ...), custom_call_target="tpu_custom_call" | custom-call | tf_op jit(solution)/shard_map/slot_tables/pallas_call | solution.py:112
  42.2 5.1 %attend_pages.1 = (bf16[32,40,128]{2,1,0:T(8,128)(2,1)S(1)}, bf16[32,40,128]{2,1,0:T(8,128)(2,1)S(1)}) custom-call(bf16[128,1024]{1,0:T(8,128)(2,1)S(1)} %get-tuple-element.41.refs_0_, f32[128,128]{1,0:T(8,128)S(1)} %get-tuple-element.42.refs_1_, f32[128,128]{1,0:T(8,128)S(1)} %get-tuple-element.43.refs_2_, f32[128,128]{1,0:T(8,128)S(1)} %get-tuple-element.44.refs_3_, ...), custom_call_target="tpu_custom_call" | custom-call | tf_op jit(solution)/shard_map/attend_pages/pallas_call | solution.py:112
  47.3 0.3 collective-permute-start.1
  47.6 1.4 collective-permute-done.1.refs_1_
  49.0 1.8 %merge.1.refs_1_.after_ref = bf16[32,40,128]{2,1,0:T(8,128)(2,1)} custom-call(bf16[32,40,128]{2,1,0:T(8,128)(2,1)S(1)} %get-tuple-element.48.refs_0_, bf16[32,40,128]{2,1,0:T(8,128)(2,1)S(1)} %collective-permute-done.1.refs_1_), custom_call_target="tpu_custom_call" | custom-call | tf_op jit(solution)/shard_map/merge/pallas_call | solution.py:112
  50.9 4.4 %all-to-all-start.1 = ((bf16[32,40,128]{2,1,0:T(8,128)(2,1)}), bf16[32,40,128]{2,1,0:T(8,128)(2,1)S(1)}, u32[]{:S(2)}, u32[]{:S(2)}) async-start(bf16[32,40,128]{2,1,0:T(8,128)(2,1)} %merge.1.refs_1_.after_ref), calls=%async_computation.1 | async-start | bytes 655360 | tf_op jit(solution)/shard_map/all_to_all | solution.py:674
  55.3 2.5 %pack.1 = (bf16[1024,256]{1,0:T(8,128)(2,1)}, bf16[1024,256]{1,0:T(8,128)(2,1)}, bf16[1024,256]{1,0:T(8,128)(2,1)}, bf16[1024,256]{1,0:T(8,128)(2,1)}) custom-call(bf16[256,2048]{1,0:T(8,128)(2,1)} %bitcast.19, bf16[32,32,256]{2,1,0:T(8,128)(2,1)} %copy-done.1, bf16[32,32,256]{2,1,0:T(8,128)(2,1)} %copy-done.2, bf16[32,40,128]{2,1,0:T(8,128)(2,1)} %merge.1.refs_1_.after_ref), custom_call_target="tpu_custom_call" | custom-call | tf_op jit(solution)/shard_map/pack/pallas_call | solution.py:377
  57.8 1.3 collective-permute-start.5
  59.1 2.5 %collective-permute-start.6 = (bf16[1024,256]{1,0:T(8,128)(2,1)}, bf16[1024,256]{1,0:T(8,128)(2,1)S(1)}, u32[]{:S(2)}, u32[]{:S(2)}) collective-permute-start(bf16[1024,256]{1,0:T(8,128)(2,1)} %get-tuple-element.56), channel_id=1, source_target_pairs={{0,2},{1,3},{2,0},{3,1},{4,6},{5,7},{6,4},{7,5},{8,10},{9,11},{10,... | collective-permute-start | bytes 1572872 | tf_op jit(solution)/shard_map/ppermute | solution.py:652
  61.6 1.1 collective-permute-start.7
  62.8 1.7 %cells_table.1.refs_3_ = bf16[32,512]{1,0:T(8,128)(2,1)} custom-call(s32[8,16]{1,0:T(8,128)} %bitcast.21, bf16[32,40,128]{2,1,0:T(8,128)(2,1)} %merge.1.refs_1_.after_ref), custom_call_target="tpu_custom_call" | custom-call | tf_op jit(solution)/shard_map/cells_table/pallas_call | solution.py:112
  64.5 3.7 %all-to-all-done.1.refs_0_ = bf16[32,40,128]{2,1,0:T(8,128)(2,1)S(1)} async-done(((bf16[32,40,128]{2,1,0:T(8,128)(2,1)}), bf16[32,40,128]{2,1,0:T(8,128)(2,1)S(1)}, u32[]{:S(2)}, u32[]{:S(2)}) %all-to-all-start.1) | async-done | bytes 327712 | tf_op jit(solution)/shard_map/all_to_all | solution.py:674
  68.1 2.0 %owner_part.1 = (bf16[16,256]{1,0:T(8,128)(2,1)S(1)}, bf16[64,8,128]{2,1,0:T(8,128)(2,1)}) custom-call(bf16[32,40,128]{2,1,0:T(8,128)(2,1)S(1)} %all-to-all-done.1.refs_0_, bf16[16,256]{1,0:T(8,128)(2,1)} %refs_1_.3, bf16[16,2,256]{2,1,0:T(2,128)(2,1)} %refs_2_.1, bf16[32,512]{1,0:T(8,128)(2,1)} %cells_table.1.refs_3_), custom_call_target="tpu_custom_call" | custom-call | tf_op jit(solution)/shard_map/owner_part/pallas_call | solution.py:112
  70.1 0.0 copy-start.3
  70.2 7.6 %all-to-all-start.2 = ((bf16[64,8,128]{2,1,0:T(8,128)(2,1)}), bf16[64,8,128]{2,1,0:T(8,128)(2,1)S(1)}, u32[]{:S(2)}, u32[]{:S(2)}) async-start(bf16[64,8,128]{2,1,0:T(8,128)(2,1)} %get-tuple-element.52), calls=%async_computation.2 | async-start | bytes 262144 | tf_op jit(solution)/shard_map/all_to_all | solution.py:677
  77.7 0.4 collective-permute-start.2
  78.1 2.3 %collective-permute-start.3 = (bf16[16,256]{1,0:T(8,128)(2,1)S(1)}, bf16[16,256]{1,0:T(8,128)(2,1)S(1)}, u32[]{:S(2)}, u32[]{:S(2)}) collective-permute-start(bf16[16,256]{1,0:T(8,128)(2,1)S(1)} %get-tuple-element.65.refs_6_), channel_id=1, source_target_pairs={{0,2},{1,3},{2,0},{3,1},{4,6},{5,7},{6,4},{7,5},{8,10},{9,11},{10,... | collective-permute-start | bytes 24584 | tf_op jit(solution)/shard_map/ppermute | solution.py:647
  80.4 0.0 collective-permute-done.5.refs_2_
  80.4 1.1 collective-permute-start.4
  81.6 5.3 %collective-permute-done.6.refs_3_ = bf16[1024,256]{1,0:T(8,128)(2,1)S(1)} collective-permute-done((bf16[1024,256]{1,0:T(8,128)(2,1)}, bf16[1024,256]{1,0:T(8,128)(2,1)S(1)}, u32[]{:S(2)}, u32[]{:S(2)}) %collective-permute-start.6) | collective-permute-done | bytes 524320 | tf_op jit(solution)/shard_map/ppermute | solution.py:652
  86.8 0.3 collective-permute-done.3.refs_8_
  87.2 1.7 %all-to-all-done.2.refs_0_ = bf16[64,8,128]{2,1,0:T(8,128)(2,1)S(1)} async-done(((bf16[64,8,128]{2,1,0:T(8,128)(2,1)}), bf16[64,8,128]{2,1,0:T(8,128)(2,1)S(1)}, u32[]{:S(2)}, u32[]{:S(2)}) %all-to-all-start.2) | async-done | bytes 131104 | tf_op jit(solution)/shard_map/all_to_all | solution.py:677
  88.9 1.6 %collective-permute-start.10 = (bf16[64,8,128]{2,1,0:T(8,128)(2,1)S(1)}, bf16[64,8,128]{2,1,0:T(8,128)(2,1)S(1)}, u32[]{:S(2)}, u32[]{:S(2)}) collective-permute-start(bf16[64,8,128]{2,1,0:T(8,128)(2,1)S(1)} %all-to-all-done.2.refs_0_), channel_id=1, source_target_pairs={{0,3},{1,0},{2,1},{3,2},{4,7},{5,4},{6,5},{7,6},{8,11},{9,8},{10,9... | collective-permute-start | bytes 393224 | tf_op jit(solution)/shard_map/ppermute | solution.py:647
  90.5 1.7 %collective-permute-start.9 = (bf16[64,8,128]{2,1,0:T(8,128)(2,1)S(1)}, bf16[64,8,128]{2,1,0:T(8,128)(2,1)S(1)}, u32[]{:S(2)}, u32[]{:S(2)}) collective-permute-start(bf16[64,8,128]{2,1,0:T(8,128)(2,1)S(1)} %all-to-all-done.2.refs_0_), channel_id=1, source_target_pairs={{0,2},{1,3},{2,0},{3,1},{4,6},{5,7},{6,4},{7,5},{8,10},{9,11},{10,... | collective-permute-start | bytes 393224 | tf_op jit(solution)/shard_map/ppermute | solution.py:647
  92.2 3.1 %early_rows.1 = (f32[8,256,256]{2,1,0:T(8,128)S(1)}, bf16[1024,2048]{1,0:T(8,128)(2,1)S(1)}) custom-call(bf16[64,8,128]{2,1,0:T(8,128)(2,1)S(1)} %all-to-all-done.2.refs_0_, bf16[1024,256]{1,0:T(8,128)(2,1)} %get-tuple-element.59.refs_1_, bf16[1024,256]{1,0:T(8,128)(2,1)} %copy-done.4, bf16[1024,256]{1,0:T(8,128)(2,1)} %copy-done.5, ...), custom_call_target="tpu_custom_call" | custom-call | tf_op jit(solution)/shard_map/early_rows/pallas_call | solution.py:112
  95.3 4.1 %collective-permute-done.8.refs_0_ = bf16[64,8,128]{2,1,0:T(8,128)(2,1)S(1)} collective-permute-done((bf16[64,8,128]{2,1,0:T(8,128)(2,1)S(1)}, bf16[64,8,128]{2,1,0:T(8,128)(2,1)S(1)}, u32[]{:S(2)}, u32[]{:S(2)}) %collective-permute-start.8) | collective-permute-done | bytes 131104 | tf_op jit(solution)/shard_map/ppermute | solution.py:647
  99.4 3.1 %expert_rows.1 = (bf16[256,256]{1,0:T(8,128)(2,1)S(1)}, bf16[16,512]{1,0:T(8,128)(2,1)}) custom-call(bf16[64,8,128]{2,1,0:T(8,128)(2,1)S(1)} %collective-permute-done.8.refs_0_, bf16[64,8,128]{2,1,0:T(8,128)(2,1)S(1)} %collective-permute-done.9.refs_1_, bf16[64,8,128]{2,1,0:T(8,128)(2,1)S(1)} %collective-permute-done.10.refs_2_, ...), custom_call_target="tpu_custom_call" | custom-call | tf_op jit(solution)/shard_map/expert_rows/pallas_call | solution.py:112
  102.5 0.0 copy-start
  102.6 0.1 collective-permute-start.11
  102.6 0.3 collective-permute-start.12
  102.9 2.4 %collective-permute-start.13 = (bf16[256,256]{1,0:T(8,128)(2,1)S(1)}, bf16[256,256]{1,0:T(8,128)(2,1)S(1)}, u32[]{:S(2)}, u32[]{:S(2)}) collective-permute-start(bf16[256,256]{1,0:T(8,128)(2,1)S(1)} %get-tuple-element.69.refs_0_.refs_2_), channel_id=1, source_target_pairs={{0,3},{1,0},{2,1},{3,2},{4,7},{5,4},{6,5},{7,6},{8,11},{9,8},{10,9... | collective-permute-start | bytes 393224 | tf_op jit(solution)/shard_map/ppermute | solution.py:647
  105.3 1.4 fetch.1
  106.7 1.1 mix_table.1
  107.8 3.4 %collective-permute-done.11.refs_1_ = bf16[256,256]{1,0:T(8,128)(2,1)S(1)} collective-permute-done((bf16[256,256]{1,0:T(8,128)(2,1)S(1)}, bf16[256,256]{1,0:T(8,128)(2,1)S(1)}, u32[]{:S(2)}, u32[]{:S(2)}) %collective-permute-start.11) | collective-permute-done | bytes 131104 | tf_op jit(solution)/shard_map/ppermute | solution.py:647
  111.2 0.5 down.1
  111.7 21.7 %all_to_all.21.refs_0_ = bf16[64,8,256]{2,1,0:T(8,128)(2,1)S(1)} all-to-all(bf16[64,8,256]{2,1,0:T(8,128)(2,1)S(1)} %bitcast.16), channel_id=1, replica_groups=mesh['z'=8,'y'=4,'c'=2,'head'=4] {'z','y','c'}, dimensions={0} | all-to-all | bytes 524288 | tf_op jit(solution)/shard_map/all_to_all | solution.py:688
  133.4 1.4 blend.1.refs_2_
  134.7 0.4 collective-permute-start.14
  135.2 3.2 %collective-permute-start.15 = (bf16[16,512]{1,0:T(8,128)(2,1)}, bf16[16,512]{1,0:T(8,128)(2,1)S(1)}, u32[]{:S(2)}, u32[]{:S(2)}) collective-permute-start(bf16[16,512]{1,0:T(8,128)(2,1)} %blend.1.refs_2_), channel_id=1, source_target_pairs={{0,2},{1,3},{2,0},{3,1},{4,6},{5,7},{6,4},{7,5},{8,10},{9,11},{10,... | collective-permute-start | bytes 49160 | tf_op jit(solution)/shard_map/ppermute | solution.py:647
  138.4 1.0 own_proj.1
  139.5 0.4 collective-permute-done.15.refs_1_
  139.9 1.3 collective-permute-done.16.refs_2_
  141.2 1.1 next_proj.1
  (30 shorter events, 0.1 us)
Async XLA Ops:
  7.2 85.0 %all-gather.2.cloned.1.call-start = ((), (), s32[]{:S(2)}) async-start(), calls=%async_computation.4 | async-start | bytes 5242880 | tf_op jit(solution)/shard_map/all_gather | solution.py:666
  37.4 9.9 %copy-start.1 = (bf16[32,32,256]{2,1,0:T(8,128)(2,1)}, bf16[32,32,256]{2,1,0:T(8,128)(2,1)S(1)}, u32[]{:S(2)}) copy-start(bf16[32,32,256]{2,1,0:T(8,128)(2,1)S(1)} %all_to_all.20.refs_4_.refs_7_.qa_ref) | copy-start | bytes 1572868
  37.4 4.8 %collective-permute-start = (bf16[32,32,256]{2,1,0:T(8,128)(2,1)S(1)}, bf16[32,32,256]{2,1,0:T(8,128)(2,1)S(1)}, u32[]{:S(2)}, u32[]{:S(2)}) collective-permute-start(bf16[32,32,256]{2,1,0:T(8,128)(2,1)S(1)} %all_to_all.20.refs_4_.refs_7_.qa_ref), channel_id=1, source_target_pairs={{0,4},{4,0},{1,5},{5,1},{2,6},{6,2},{3,7},{7,3},{8,12},{12,8},{9,1... | collective-permute-start | bytes 1572872 | tf_op jit(solution)/shard_map/ppermute | solution.py:656
  42.2 13.1 %copy-start.2 = (bf16[32,32,256]{2,1,0:T(8,128)(2,1)}, bf16[32,32,256]{2,1,0:T(8,128)(2,1)S(1)}, u32[]{:S(2)}) copy-start(bf16[32,32,256]{2,1,0:T(8,128)(2,1)S(1)} %collective-permute-done.refs_8_.qb_ref) | copy-start | bytes 1572868
  47.3 1.7 %collective-permute-start.1 = (bf16[32,40,128]{2,1,0:T(8,128)(2,1)S(1)}, bf16[32,40,128]{2,1,0:T(8,128)(2,1)S(1)}, u32[]{:S(2)}, u32[]{:S(2)}) collective-permute-start(bf16[32,40,128]{2,1,0:T(8,128)(2,1)S(1)} %get-tuple-element.49), channel_id=1, source_target_pairs={{0,4},{4,0},{1,5},{5,1},{2,6},{6,2},{3,7},{7,3},{8,12},{12,8},{9,1... | collective-permute-start | bytes 983048 | tf_op jit(solution)/shard_map/ppermute | solution.py:656
  50.9 17.3 %all-to-all-start.1 = ((bf16[32,40,128]{2,1,0:T(8,128)(2,1)}), bf16[32,40,128]{2,1,0:T(8,128)(2,1)S(1)}, u32[]{:S(2)}, u32[]{:S(2)}) async-start(bf16[32,40,128]{2,1,0:T(8,128)(2,1)} %merge.1.refs_1_.after_ref), calls=%async_computation.1 | async-start | bytes 655360 | tf_op jit(solution)/shard_map/all_to_all | solution.py:674
  57.8 22.6 %collective-permute-start.5 = (bf16[1024,256]{1,0:T(8,128)(2,1)}, bf16[1024,256]{1,0:T(8,128)(2,1)S(1)}, u32[]{:S(2)}, u32[]{:S(2)}) collective-permute-start(bf16[1024,256]{1,0:T(8,128)(2,1)} %get-tuple-element.55), channel_id=1, source_target_pairs={{0,1},{1,2},{2,3},{3,0},{4,5},{5,6},{6,7},{7,4},{8,9},{9,10},{10,1... | collective-permute-start | bytes 1572872 | tf_op jit(solution)/shard_map/ppermute | solution.py:652
  59.1 27.7 %collective-permute-start.6 = (bf16[1024,256]{1,0:T(8,128)(2,1)}, bf16[1024,256]{1,0:T(8,128)(2,1)S(1)}, u32[]{:S(2)}, u32[]{:S(2)}) collective-permute-start(bf16[1024,256]{1,0:T(8,128)(2,1)} %get-tuple-element.56), channel_id=1, source_target_pairs={{0,2},{1,3},{2,0},{3,1},{4,6},{5,7},{6,4},{7,5},{8,10},{9,11},{10,... | collective-permute-start | bytes 1572872 | tf_op jit(solution)/shard_map/ppermute | solution.py:652
  61.6 25.2 %collective-permute-start.7 = (bf16[1024,256]{1,0:T(8,128)(2,1)}, bf16[1024,256]{1,0:T(8,128)(2,1)S(1)}, u32[]{:S(2)}, u32[]{:S(2)}) collective-permute-start(bf16[1024,256]{1,0:T(8,128)(2,1)} %get-tuple-element.57), channel_id=1, source_target_pairs={{0,3},{1,0},{2,1},{3,2},{4,7},{5,4},{6,5},{7,6},{8,11},{9,8},{10,9... | collective-permute-start | bytes 1572872 | tf_op jit(solution)/shard_map/ppermute | solution.py:652
  70.1 29.2 %copy-start.3 = (bf16[16,256]{1,0:T(8,128)(2,1)}, bf16[16,256]{1,0:T(8,128)(2,1)S(1)}, u32[]{:S(2)}) copy-start(bf16[16,256]{1,0:T(8,128)(2,1)S(1)} %get-tuple-element.65.refs_6_) | copy-start | bytes 24580
  70.2 18.7 %all-to-all-start.2 = ((bf16[64,8,128]{2,1,0:T(8,128)(2,1)}), bf16[64,8,128]{2,1,0:T(8,128)(2,1)S(1)}, u32[]{:S(2)}, u32[]{:S(2)}) async-start(bf16[64,8,128]{2,1,0:T(8,128)(2,1)} %get-tuple-element.52), calls=%async_computation.2 | async-start | bytes 262144 | tf_op jit(solution)/shard_map/all_to_all | solution.py:677
  77.7 9.1 %collective-permute-start.2 = (bf16[16,256]{1,0:T(8,128)(2,1)S(1)}, bf16[16,256]{1,0:T(8,128)(2,1)S(1)}, u32[]{:S(2)}, u32[]{:S(2)}) collective-permute-start(bf16[16,256]{1,0:T(8,128)(2,1)S(1)} %get-tuple-element.65.refs_6_), channel_id=1, source_target_pairs={{0,1},{1,2},{2,3},{3,0},{4,5},{5,6},{6,7},{7,4},{8,9},{9,10},{10,1... | collective-permute-start | bytes 24584 | tf_op jit(solution)/shard_map/ppermute | solution.py:647
  78.1 9.0 %collective-permute-start.3 = (bf16[16,256]{1,0:T(8,128)(2,1)S(1)}, bf16[16,256]{1,0:T(8,128)(2,1)S(1)}, u32[]{:S(2)}, u32[]{:S(2)}) collective-permute-start(bf16[16,256]{1,0:T(8,128)(2,1)S(1)} %get-tuple-element.65.refs_6_), channel_id=1, source_target_pairs={{0,2},{1,3},{2,0},{3,1},{4,6},{5,7},{6,4},{7,5},{8,10},{9,11},{10,... | collective-permute-start | bytes 24584 | tf_op jit(solution)/shard_map/ppermute | solution.py:647
  80.4 11.8 %copy-start.4 = (bf16[1024,256]{1,0:T(8,128)(2,1)}, bf16[1024,256]{1,0:T(8,128)(2,1)S(1)}, u32[]{:S(2)}) copy-start(bf16[1024,256]{1,0:T(8,128)(2,1)S(1)} %collective-permute-done.5.refs_2_) | copy-start | bytes 1572868
  80.4 6.7 %collective-permute-start.4 = (bf16[16,256]{1,0:T(8,128)(2,1)S(1)}, bf16[16,256]{1,0:T(8,128)(2,1)S(1)}, u32[]{:S(2)}, u32[]{:S(2)}) collective-permute-start(bf16[16,256]{1,0:T(8,128)(2,1)S(1)} %get-tuple-element.65.refs_6_), channel_id=1, source_target_pairs={{0,3},{1,0},{2,1},{3,2},{4,7},{5,4},{6,5},{7,6},{8,11},{9,8},{10,9... | collective-permute-start | bytes 24584 | tf_op jit(solution)/shard_map/ppermute | solution.py:647
  86.8 5.4 %copy-start.5 = (bf16[1024,256]{1,0:T(8,128)(2,1)}, bf16[1024,256]{1,0:T(8,128)(2,1)S(1)}, u32[]{:S(2)}) copy-start(bf16[1024,256]{1,0:T(8,128)(2,1)S(1)} %collective-permute-done.6.refs_3_) | copy-start | bytes 1572868
  86.8 5.4 %copy-start.6 = (bf16[1024,256]{1,0:T(8,128)(2,1)}, bf16[1024,256]{1,0:T(8,128)(2,1)S(1)}, u32[]{:S(2)}) copy-start(bf16[1024,256]{1,0:T(8,128)(2,1)S(1)} %collective-permute-done.7.refs_4_) | copy-start | bytes 1572868
  86.8 12.6 %copy-start.7 = (bf16[16,256]{1,0:T(8,128)(2,1)}, bf16[16,256]{1,0:T(8,128)(2,1)S(1)}, u32[]{:S(2)}) copy-start(bf16[16,256]{1,0:T(8,128)(2,1)S(1)} %collective-permute-done.2.refs_7_) | copy-start | bytes 24580
  87.2 12.2 %copy-start.8 = (bf16[16,256]{1,0:T(8,128)(2,1)}, bf16[16,256]{1,0:T(8,128)(2,1)S(1)}, u32[]{:S(2)}) copy-start(bf16[16,256]{1,0:T(8,128)(2,1)S(1)} %collective-permute-done.3.refs_8_) | copy-start | bytes 24580
  87.2 12.2 %copy-start.9 = (bf16[16,256]{1,0:T(8,128)(2,1)}, bf16[16,256]{1,0:T(8,128)(2,1)S(1)}, u32[]{:S(2)}) copy-start(bf16[16,256]{1,0:T(8,128)(2,1)S(1)} %collective-permute-done.4.refs_9_) | copy-start | bytes 24580
  88.9 6.4 %collective-permute-start.10 = (bf16[64,8,128]{2,1,0:T(8,128)(2,1)S(1)}, bf16[64,8,128]{2,1,0:T(8,128)(2,1)S(1)}, u32[]{:S(2)}, u32[]{:S(2)}) collective-permute-start(bf16[64,8,128]{2,1,0:T(8,128)(2,1)S(1)} %all-to-all-done.2.refs_0_), channel_id=1, source_target_pairs={{0,3},{1,0},{2,1},{3,2},{4,7},{5,4},{6,5},{7,6},{8,11},{9,8},{10,9... | collective-permute-start | bytes 393224 | tf_op jit(solution)/shard_map/ppermute | solution.py:647
  90.5 8.9 %collective-permute-start.8 = (bf16[64,8,128]{2,1,0:T(8,128)(2,1)S(1)}, bf16[64,8,128]{2,1,0:T(8,128)(2,1)S(1)}, u32[]{:S(2)}, u32[]{:S(2)}) collective-permute-start(bf16[64,8,128]{2,1,0:T(8,128)(2,1)S(1)} %all-to-all-done.2.refs_0_), channel_id=1, source_target_pairs={{0,1},{1,2},{2,3},{3,0},{4,5},{5,6},{6,7},{7,4},{8,9},{9,10},{10,1... | collective-permute-start | bytes 393224 | tf_op jit(solution)/shard_map/ppermute | solution.py:647
  90.5 8.9 %collective-permute-start.9 = (bf16[64,8,128]{2,1,0:T(8,128)(2,1)S(1)}, bf16[64,8,128]{2,1,0:T(8,128)(2,1)S(1)}, u32[]{:S(2)}, u32[]{:S(2)}) collective-permute-start(bf16[64,8,128]{2,1,0:T(8,128)(2,1)S(1)} %all-to-all-done.2.refs_0_), channel_id=1, source_target_pairs={{0,2},{1,3},{2,0},{3,1},{4,6},{5,7},{6,4},{7,5},{8,10},{9,11},{10,... | collective-permute-start | bytes 393224 | tf_op jit(solution)/shard_map/ppermute | solution.py:647
  102.5 35.9 %copy-start = (bf16[2048,3,256]{2,0,1:T(8,128)(2,1)S(1)}, bf16[2048,3,256]{2,0,1:T(8,128)(2,1)}, u32[]{:S(2)}) copy-start(bf16[2048,3,256]{2,0,1:T(8,128)(2,1)} %param.33) | copy-start | bytes 9437188
  102.6 8.6 %collective-permute-start.11 = (bf16[256,256]{1,0:T(8,128)(2,1)S(1)}, bf16[256,256]{1,0:T(8,128)(2,1)S(1)}, u32[]{:S(2)}, u32[]{:S(2)}) collective-permute-start(bf16[256,256]{1,0:T(8,128)(2,1)S(1)} %get-tuple-element.69.refs_0_.refs_2_), channel_id=1, source_target_pairs={{0,1},{1,2},{2,3},{3,0},{4,5},{5,6},{6,7},{7,4},{8,9},{9,10},{10,1... | collective-permute-start | bytes 393224 | tf_op jit(solution)/shard_map/ppermute | solution.py:647
  102.6 8.5 %collective-permute-start.12 = (bf16[256,256]{1,0:T(8,128)(2,1)S(1)}, bf16[256,256]{1,0:T(8,128)(2,1)S(1)}, u32[]{:S(2)}, u32[]{:S(2)}) collective-permute-start(bf16[256,256]{1,0:T(8,128)(2,1)S(1)} %get-tuple-element.69.refs_0_.refs_2_), channel_id=1, source_target_pairs={{0,2},{1,3},{2,0},{3,1},{4,6},{5,7},{6,4},{7,5},{8,10},{9,11},{10,... | collective-permute-start | bytes 393224 | tf_op jit(solution)/shard_map/ppermute | solution.py:647
  102.9 8.3 %collective-permute-start.13 = (bf16[256,256]{1,0:T(8,128)(2,1)S(1)}, bf16[256,256]{1,0:T(8,128)(2,1)S(1)}, u32[]{:S(2)}, u32[]{:S(2)}) collective-permute-start(bf16[256,256]{1,0:T(8,128)(2,1)S(1)} %get-tuple-element.69.refs_0_.refs_2_), channel_id=1, source_target_pairs={{0,3},{1,0},{2,1},{3,2},{4,7},{5,4},{6,5},{7,6},{8,11},{9,8},{10,9... | collective-permute-start | bytes 393224 | tf_op jit(solution)/shard_map/ppermute | solution.py:647
  134.7 4.7 %collective-permute-start.14 = (bf16[16,512]{1,0:T(8,128)(2,1)}, bf16[16,512]{1,0:T(8,128)(2,1)S(1)}, u32[]{:S(2)}, u32[]{:S(2)}) collective-permute-start(bf16[16,512]{1,0:T(8,128)(2,1)} %blend.1.refs_2_), channel_id=1, source_target_pairs={{0,1},{1,2},{2,3},{3,0},{4,5},{5,6},{6,7},{7,4},{8,9},{9,10},{10,1... | collective-permute-start | bytes 49160 | tf_op jit(solution)/shard_map/ppermute | solution.py:647
  135.2 4.7 %collective-permute-start.15 = (bf16[16,512]{1,0:T(8,128)(2,1)}, bf16[16,512]{1,0:T(8,128)(2,1)S(1)}, u32[]{:S(2)}, u32[]{:S(2)}) collective-permute-start(bf16[16,512]{1,0:T(8,128)(2,1)} %blend.1.refs_2_), channel_id=1, source_target_pairs={{0,2},{1,3},{2,0},{3,1},{4,6},{5,7},{6,4},{7,5},{8,10},{9,11},{10,... | collective-permute-start | bytes 49160 | tf_op jit(solution)/shard_map/ppermute | solution.py:647
  138.4 2.8 %collective-permute-start.16 = (bf16[16,512]{1,0:T(8,128)(2,1)}, bf16[16,512]{1,0:T(8,128)(2,1)S(1)}, u32[]{:S(2)}, u32[]{:S(2)}) collective-permute-start(bf16[16,512]{1,0:T(8,128)(2,1)} %blend.1.refs_2_), channel_id=1, source_target_pairs={{0,3},{1,0},{2,1},{3,2},{4,7},{5,4},{6,5},{7,6},{8,11},{9,8},{10,9... | collective-permute-start | bytes 49160 | tf_op jit(solution)/shard_map/ppermute | solution.py:647
Sparse Core Ops, SparseCore 0:
  9.8 56.3 all-gather.1
